TPU v7x, 256 devices: a whole 4x4x8 slice. The times are simulated.
256 devices in a mesh: dp: 8 (over y, core), expert: 32 (over x, z).
Axes of the slice: x: 4, y: 4, z: 8, core: 2. Of those that a mesh axis runs over, the one named last changes fastest.
Arguments:
- tokens: bfloat16 [8192, 3584], P('expert', 'dp'), may hold values from -6 to 6
- cotangent: bfloat16 [8192, 3584], P('expert', 'dp'), may hold values from -6 to 6
- slot_tokens: int32 [32, 32, 32], P('expert'), may hold values from 0 to 255
- slot_counts: int32 [32, 32], P('expert'), may hold values from 0 to 32, as said below
- slot_gates: float32 [32, 32, 32], P('expert'), may hold values from 0.1 to 1
- swap_pairs: int32 [16], replicated, may hold values from 0 to 1, as said below
- gate_weight: bfloat16 [32, 3584, 1024], P('expert', 'dp'), may hold values from -0.09375 to 0.09375
- up_weight: bfloat16 [32, 3584, 1024], P('expert', 'dp'), may hold values from -0.09375 to 0.09375
- down_weight: bfloat16 [32, 1024, 3584], P('expert', None, 'dp'), may hold values from -0.1875 to 0.1875
- first_moment: float32 [32, 1024, 3584], P('expert', None, 'dp'), may hold values from -6 to 6
- second_moment: float32 [32, 1024, 3584], P('expert', None, 'dp'), may hold values from 0.5 to 4
Outputs:
- mixed: bfloat16 [8192, 3584], P('expert', 'dp')
- token_grad: bfloat16 [8192, 3584], P('expert', 'dp')
- new_first_moment: float32 [32, 1024, 3584], P('expert', None, 'dp')
- new_second_moment: float32 [32, 1024, 3584], P('expert', None, 'dp')
- adam_step: bfloat16 [32, 1024, 3584], P('expert', None, 'dp')
Inputs may be any that keep to these rules, and one draw needn't show every extreme that they name: `slot_tokens`: slots at or past slot_counts hold arbitrary token numbers and carry nothing. `slot_counts`: every source fills all 32 slots of some expert, and one expert receives 32 live slots from every source. `swap_pairs`: at least one pair trades and at least one pair does not.
All inputs are finite; a program needn't handle non-finite values.
Results may differ from a plain program's by a relative error of at most 0.022.
Values may be sent and summed in bfloat16 or wider, within the bound.
No kernel may reach another device: no remote copies, remote signals or barrier semaphores. Data moves between devices by JAX's collectives and lax.ppermute only.
A program may use at most 128 MiB of HBM per device.

v0:
```python
import jax
import jax.numpy as jnp
from jax import lax
from jax.sharding import PartitionSpec as P

beta_first = 0.9
beta_second = 0.999
adam_eps = 1e-08


def partner(block, axis, bit):
    count = lax.axis_size(axis)
    route = []
    for low in range(count):
        high = low | 1 << bit
        if high != low and high < count:
            route += [(low, high), (high, low)]
    return lax.ppermute(block, axis, route)


def held_order(values, pair_flags):
    half_count = pair_flags.shape[0]
    blocks = values.reshape((2, half_count) + values.shape[1:])
    chosen = pair_flags.reshape((1, half_count) + (1,) * (values.ndim - 1)) > 0
    return jnp.where(chosen, blocks[::-1], blocks).reshape(values.shape)


def preact_grad(hidden_grad, gate_pre, up_pre):
    sigmoid_gate = jax.nn.sigmoid(gate_pre)
    first_half = hidden_grad * up_pre * sigmoid_gate * (1.0 + gate_pre * (1.0 - sigmoid_gate))
    second_half = hidden_grad * gate_pre * sigmoid_gate
    return jnp.concatenate([first_half, second_half], axis=1).astype(jnp.bfloat16)


def shards(
    tokens,
    cotangent,
    slot_tokens,
    slot_counts,
    slot_gates,
    swap_pairs,
    gate_weight,
    up_weight,
    down_weight,
    first_moment,
    second_moment,
):
    tok_count, model_cols = tokens.shape
    experts = slot_counts.shape[1]
    capacity = slot_tokens.shape[2]
    bit_index = lax.axis_size("expert").bit_length() - 2
    position = lax.axis_index("expert")
    half_count = swap_pairs.shape[0]
    own_swap = (
        jnp.sum(jnp.where(jnp.arange(half_count) == position % half_count, swap_pairs, 0)) > 0
    )
    live_slots = (
        (jnp.arange(capacity)[None, :] < slot_counts[0][:, None]).astype(jnp.float32).reshape(-1)
    )
    weighted = live_slots * slot_gates[0].reshape(-1)
    slot_route = slot_tokens[0].reshape(-1)
    matcher = (jnp.arange(tok_count)[:, None] == slot_route[None, :]).astype(jnp.float32)
    gate_up = jnp.concatenate([gate_weight[0], up_weight[0]], axis=1)
    down_proj = down_weight[0]
    moment_one = first_moment[0]
    moment_two = second_moment[0]
    moved_gate_up, moved_down = partner((gate_up, down_proj), "expert", bit_index)
    gate_up = jnp.where(own_swap, moved_gate_up, gate_up)
    down_proj = jnp.where(own_swap, moved_down, down_proj)
    moved_one, moved_two = (
        partner(moment_one.astype(jnp.bfloat16), "expert", bit_index).astype(moment_one.dtype),
        partner(moment_two.astype(jnp.bfloat16), "expert", bit_index).astype(moment_two.dtype),
    )
    moment_one = jnp.where(own_swap, moved_one, moment_one)
    moment_two = jnp.where(own_swap, moved_two, moment_two)

    def to_hosts(slot_rows):
        return held_order(slot_rows, swap_pairs)

    picked = jnp.take(tokens, slot_route, axis=0)
    outgoing = jnp.where(live_slots[:, None] > 0, picked, jnp.zeros_like(picked)).reshape(
        experts, capacity, model_cols
    )
    arrived = lax.all_to_all(
        to_hosts(outgoing), "expert", split_axis=0, concat_axis=0, tiled=True
    ).reshape(-1, model_cols)
    hidden_units = down_proj.shape[0]
    contract_last = (((1,), (1,)), ((), ()))
    preact = lax.psum(
        jnp.dot(arrived, gate_up, preferred_element_type=jnp.float32).astype(jnp.bfloat16), "dp"
    ).astype(jnp.float32)
    gate_pre = preact[:, :hidden_units]
    up_pre = preact[:, hidden_units:]
    hidden = (jax.nn.silu(gate_pre) * up_pre).astype(jnp.bfloat16)
    outputs = (
        jnp.dot(hidden, down_proj, preferred_element_type=jnp.float32)
        .astype(jnp.bfloat16)
        .reshape(-1, capacity, model_cols)
    )
    returned = to_hosts(
        lax.all_to_all(outputs, "expert", split_axis=0, concat_axis=0, tiled=True)
    ).reshape(-1, model_cols)
    mixed = jnp.dot(
        matcher * weighted[None, :], returned.astype(jnp.float32), precision=lax.Precision.HIGHEST
    ).astype(jnp.bfloat16)
    grad_picked = jnp.take(cotangent, slot_route, axis=0).astype(jnp.float32) * weighted[:, None]
    grad_slots = grad_picked.astype(jnp.bfloat16).reshape(experts, capacity, model_cols)
    arrived_grad = lax.all_to_all(
        to_hosts(grad_slots), "expert", split_axis=0, concat_axis=0, tiled=True
    ).reshape(-1, model_cols)
    weight_grad = lax.dot_general(
        hidden, arrived_grad, (((0,), (0,)), ((), ())), preferred_element_type=jnp.float32
    )
    hidden_grad = lax.psum(
        lax.dot_general(
            arrived_grad, down_proj, contract_last, preferred_element_type=jnp.float32
        ).astype(jnp.bfloat16),
        "dp",
    ).astype(jnp.float32)
    back_rows = lax.dot_general(
        preact_grad(hidden_grad, gate_pre, up_pre),
        gate_up,
        contract_last,
        preferred_element_type=jnp.float32,
    ).astype(jnp.bfloat16)
    returned_grad = to_hosts(
        lax.all_to_all(
            back_rows.reshape(-1, capacity, model_cols),
            "expert",
            split_axis=0,
            concat_axis=0,
            tiled=True,
        )
    ).reshape(-1, model_cols)
    token_grad = jnp.dot(
        matcher * live_slots[None, :],
        returned_grad.astype(jnp.float32),
        precision=lax.Precision.HIGHEST,
    ).astype(jnp.bfloat16)
    new_one = beta_first * moment_one + (1.0 - beta_first) * weight_grad
    new_two = beta_second * moment_two + (1.0 - beta_second) * weight_grad * weight_grad
    step_dir = (new_one / (jnp.sqrt(new_two) + adam_eps)).astype(jnp.bfloat16)
    return (mixed, token_grad, new_one[None], new_two[None], step_dir[None])


def solution(mesh):
    return jax.shard_map(
        shards,
        mesh=mesh,
        in_specs=(
            P("expert", "dp"),
            P("expert", "dp"),
            P("expert", None, None),
            P("expert", None),
            P("expert", None, None),
            P(),
            P("expert", "dp", None),
            P("expert", "dp", None),
            P("expert", None, "dp"),
            P("expert", None, "dp"),
            P("expert", None, "dp"),
        ),
        out_specs=(
            P("expert", "dp"),
            P("expert", "dp"),
            P("expert", None, "dp"),
            P("expert", None, "dp"),
            P("expert", None, "dp"),
        ),
        check_vma=False,
    )
```

profile of v0, /device:TPU:1, one launch (start us, length us, event | category | flops | bytes accessed | tf_op | source)
XLA Modules:
  0.0 327.6 jit_solution(159144839303572518)
XLA Ops:
  7.2 0.8 eq.24
  8.0 0.7 iota_compare_fusion.3
  8.7 0.1 lt.50
  8.8 1.1 copy.22
  9.9 1.1 copy.24
  11.0 4.0 %gather_fusion = bf16[1024,448]{1,0:T(8,128)(2,1)S(1)} fusion(bf16[256,448]{1,0:T(8,128)(2,1)S(1)} %copy.22, s32[1024]{0:T(1024)S(1)} %fusion.26), kind=kCustom, calls=%fused_computation.clone | custom fusion | bytes 1839104 | tf_op jit(solution)/shard_map/jit(_take)/gather | solution.py:80
  14.9 0.0 copy-start.6
  14.9 0.0 copy-start.8
  15.0 4.0 %gather_fusion.1 = bf16[1024,448]{1,0:T(8,128)(2,1)S(1)} fusion(bf16[256,448]{1,0:T(8,128)(2,1)S(1)} %copy.24, s32[1024]{0:T(1024)S(1)} %fusion.26), kind=kCustom, calls=%fused_computation.1.clone | custom fusion | bytes 1839104 | tf_op jit(solution)/shard_map/jit(_take)/gather | solution.py:106
  18.9 0.1 reshape_squeeze.4
  19.0 0.8 select_select_fusion
  19.8 0.3 multiply_convert_fusion.1
  20.2 2.2 reverse_select_fusion.1
  22.4 11.9 %all-to-all-start.2 = ((bf16[32,32,448]{2,1,0:T(8,128)(2,1)}), bf16[32,32,448]{2,1,0:T(8,128)(2,1)S(1)}, u32[]{:S(2)}, u32[]{:S(2)}) async-start(bf16[32,32,448]{2,1,0:T(8,128)(2,1)} %bitcast.11), calls=%async_computation.2 | async-start | bytes 2097152 | tf_op jit(solution)/shard_map/all_to_all | solution.py:108
  34.2 1.6 pad_maximum_fusion
  35.8 2.8 collective-permute-start
  38.6 20.5 %all-to-all-done.2 = bf16[32,32,448]{2,1,0:T(8,128)(2,1)S(1)} async-done(((bf16[32,32,448]{2,1,0:T(8,128)(2,1)}), bf16[32,32,448]{2,1,0:T(8,128)(2,1)S(1)}, u32[]{:S(2)}, u32[]{:S(2)}) %all-to-all-start.2) | async-done | bytes 917536 | tf_op jit(solution)/shard_map/all_to_all | solution.py:108
  59.1 8.4 %all-to-all-start = ((bf16[32,32,448]{2,1,0:T(8,128)(2,1)}), bf16[32,32,448]{2,1,0:T(8,128)(2,1)}, u32[]{:S(2)}, u32[]{:S(2)}) async-start(bf16[32,32,448]{2,1,0:T(8,128)(2,1)} %bitcast.2), calls=%async_computation | async-start | bytes 2097152 | tf_op jit(solution)/shard_map/all_to_all | solution.py:84
  67.6 0.0 all-reduce.3.cloned.1.call-start
  67.6 2.8 collective-permute-start.1
  70.4 0.6 fusion.27
  71.6 48.7 %collective-permute-done.1 = bf16[1024,448]{0,1:T(8,128)(2,1)} collective-permute-done((bf16[1024,448]{0,1:T(8,128)(2,1)}, bf16[1024,448]{0,1:T(8,128)(2,1)}, u32[]{:S(2)}, u32[]{:S(2)}) %collective-permute-start.1) | collective-permute-done | bytes 917536 | tf_op jit(solution)/shard_map/ppermute | solution.py:18
  120.3 4.1 %convolution_convert_fusion.1 = bf16[1024,1024]{1,0:T(8,128)(2,1)} fusion(bf16[1024,448]{1,0:T(8,128)(2,1)S(1)} %bitcast.65, bf16[1024,448]{0,1:T(8,128)(2,1)} %collective-permute-done.1, pred[]{:T(512)S(6)} %gt.21, bf16[1,1024,448]{1,2,0:T(8,128)(2,1)} %param.21), kind=kOutput, calls=%fused_computation.18 | convolution fusion | flops 941031424 | bytes 4849665 | tf_op jit(solution)/shard_map/dot_general | solution.py:115
  124.4 6.6 %convolution_convert_fusion = bf16[1024,2048]{1,0:T(8,128)(2,1)} fusion(bf16[1024,448]{1,0:T(8,128)(2,1)} %bitcast.3, bf16[448,2048]{1,0:T(8,128)(2,1)} %collective-permute-done, pred[]{:T(512)S(6)} %gt.21, bf16[448,1024]{1,0:T(8,128)(2,1)} %bitcast.68, bf16[448,1024]{1,0:T(8,128)(2,1)} %bitcast.71), kind=kOutput, calls=%fused_computation.15 | convolution fusion | flops 1885732864 | bytes 8781825 | tf_op jit(solution)/shard_map/dot_general | solution.py:90
  131.1 0.0 all-reduce.3.cloned.1.call-update
  131.1 88.6 %all-reduce.3.cloned.1.call-done = (bf16[1024,2048]{1,0:T(8,128)(2,1)}, bf16[1024,1024]{1,0:T(8,128)(2,1)}) async-done(((bf16[1024,2048]{1,0:T(8,128)(2,1)}, bf16[1024,1024]{1,0:T(8,128)(2,1)}), (bf16[1024,2048]{1,0:T(8,128)(2,1)}, bf16[1024,1024]{1,0:T(8,128)(2,1)})) %all-reduce.3.cloned.1.call-update) | async-done | bytes 6291472 | tf_op jit(solution)/shard_map/psum | solution.py:89
  219.7 3.4 %convert_element_type.69 = f32[1024,2048]{1,0:T(8,128)S(1)} convert(bf16[1024,2048]{1,0:T(8,128)(2,1)} %get-tuple-element.6) | non-fusion elementwise | flops 2097152 | bytes 12582912 | tf_op jit(solution)/shard_map/convert_element_type | solution.py:91
  223.1 0.0 copy-start.7
  223.1 3.7 %fusion.2 = (bf16[1024,1024]{1,0:T(8,128)(2,1)S(1)}, bf16[1024,1024]{1,0:T(8,128)(2,1)}, bf16[1024,1024]{1,0:T(8,128)(2,1)S(1)}) fusion(bf16[1024,1024]{1,0:T(8,128)(2,1)S(1)} %copy-done.3, f32[1024,2048]{1,0:T(8,128)S(1)} %convert_element_type.69), kind=kLoop, calls=%fused_computation.6 | loop fusion | flops 17825792 | bytes 16777216 | tf_op jit(solution)/shard_map/convert
  226.8 1.3 copy-done
  228.2 2.3 convolution_convert_fusion.2
  230.5 1.3 copy.23
  231.8 8.4 %all-to-all-start.1 = ((bf16[32,32,448]{2,1,0:T(8,128)(2,1)}), bf16[32,32,448]{2,1,0:T(8,128)(2,1)S(1)}, u32[]{:S(2)}, u32[]{:S(2)}) async-start(bf16[32,32,448]{2,1,0:T(8,128)(2,1)} %bitcast.7), calls=%async_computation.1 | async-start | bytes 2097152 | tf_op jit(solution)/shard_map/all_to_all | solution.py:101
  240.3 2.7 bitcast_convert_fusion.1
  243.0 2.7 collective-permute-start.2
  245.7 5.2 %fusion.13 = bf16[1024,448]{0,1:T(8,128)(2,1)} fusion(bf16[1024,1024]{1,0:T(8,128)(2,1)S(1)} %copy-done.2, bf16[1024,1024]{1,0:T(8,128)(2,1)S(1)} %get-tuple-element.8, bf16[448,2048]{1,0:T(8,128)(2,1)} %collective-permute-done, pred[]{:T(512)S(6)} %gt.21, bf16[448,1024]{1,0:T(8,128)(2,1)} %bitcast.69, bf16[448,1024]{1,0:T(8,128)(2,1)} %bitcast.72), kind=kOutput, calls=%fused_computation.34 | convolution fusion | flops 1892483072 | bytes 8781825 | tf_op jit(solution)/shard_map/dot_general | solution.py:120
  250.9 2.2 copy.25
  253.1 12.3 %all-to-all-done.1 = bf16[32,32,448]{2,1,0:T(8,128)(2,1)S(1)} async-done(((bf16[32,32,448]{2,1,0:T(8,128)(2,1)}), bf16[32,32,448]{2,1,0:T(8,128)(2,1)S(1)}, u32[]{:S(2)}, u32[]{:S(2)}) %all-to-all-start.1) | async-done | bytes 917536 | tf_op jit(solution)/shard_map/all_to_all | solution.py:101
  265.4 8.2 %all-to-all-start.3 = ((bf16[32,32,448]{2,1,0:T(8,128)(2,1)}), bf16[32,32,448]{2,1,0:T(8,128)(2,1)S(1)}, u32[]{:S(2)}, u32[]{:S(2)}) async-start(bf16[32,32,448]{2,1,0:T(8,128)(2,1)} %bitcast.13), calls=%async_computation.3 | async-start | bytes 2097152 | tf_op jit(solution)/shard_map/all_to_all | solution.py:127
  273.6 1.8 bitcast_convert_fusion
  275.4 2.8 collective-permute-start.3
  278.2 0.0 collective-permute-done.2
  278.2 30.9 %collective-permute-done.3 = bf16[1024,448]{0,1:T(8,128)(2,1)S(1)} collective-permute-done((bf16[1024,448]{0,1:T(8,128)(2,1)S(1)}, bf16[1024,448]{0,1:T(8,128)(2,1)S(1)}, u32[]{:S(2)}, u32[]{:S(2)}) %collective-permute-start.3) | collective-permute-done | bytes 917536 | tf_op jit(solution)/shard_map/ppermute | solution.py:18
  309.1 6.7 %fusion.18 = (bf16[1,1024,448]{1,2,0:T(8,128)(2,1)}, f32[1,1024,448]{1,2,0:T(8,128)}, f32[1,1024,448]{1,2,0:T(8,128)}) fusion(f32[1,1024,448]{1,2,0:T(8,128)} %param.22, bf16[1024,448]{0,1:T(8,128)(2,1)} %collective-permute-done.2, pred[]{:T(512)S(6)} %gt.21, f32[1,1024,448]{1,2,0:T(8,128)} %param.23, bf16[1024,448]{0,1:T(8,128)(2,1)S(1)} %collective-permute-done.3, ...), kind=kOutput, calls=%fused_computation.42 | convolution fusion | flops 945946624 | bytes 13107201 | tf_op jit(solution)/shard_map/dot_general | solution.py:111
  315.8 0.0 all-to-all-done.3
  315.8 0.9 reverse_select_fusion
  316.7 2.0 convolution_convert_fusion.4
  318.7 2.0 convolution_convert_fusion.3
  (20 shorter events, 0.1 us)
Async XLA Ops:
  14.9 4.0 %copy-start.6 = (f32[1,32,32]{2,1,0:T(8,128)S(1)}, f32[1,32,32]{2,1,0:T(8,128)}, u32[]{:S(2)}) copy-start(f32[1,32,32]{2,1,0:T(8,128)} %param.17) | copy-start | bytes 12292
  14.9 4.1 %copy-start.8 = (s32[16]{0:T(128)S(1)}, s32[16]{0:T(128)}, u32[]{:S(2)}) copy-start(s32[16]{0:T(128)} %param.18) | copy-start | bytes 196
  22.4 36.8 %all-to-all-start.2 = ((bf16[32,32,448]{2,1,0:T(8,128)(2,1)}), bf16[32,32,448]{2,1,0:T(8,128)(2,1)S(1)}, u32[]{:S(2)}, u32[]{:S(2)}) async-start(bf16[32,32,448]{2,1,0:T(8,128)(2,1)} %bitcast.11), calls=%async_computation.2 | async-start | bytes 2097152 | tf_op jit(solution)/shard_map/all_to_all | solution.py:108
  35.8 88.6 %collective-permute-start = (bf16[448,2048]{1,0:T(8,128)(2,1)S(1)}, bf16[448,2048]{1,0:T(8,128)(2,1)}, u32[]{:S(2)}, u32[]{:S(2)}) collective-permute-start(bf16[448,2048]{1,0:T(8,128)(2,1)S(1)} %pad_maximum_fusion), channel_id=1, source_target_pairs={{0,16},{16,0},{1,17},{17,1},{2,18},{18,2},{3,19},{19,3},{4,20},{20... | collective-permute-start | bytes 5505032 | tf_op jit(solution)/shard_map/ppermute | solution.py:18
  59.1 65.3 %copy-start.4 = (bf16[32,32,448]{2,1,0:T(8,128)(2,1)}, bf16[32,32,448]{2,1,0:T(8,128)(2,1)S(1)}, u32[]{:S(2)}) copy-start(bf16[32,32,448]{2,1,0:T(8,128)(2,1)S(1)} %all-to-all-done.2) | copy-start | bytes 2752516
  59.1 65.3 %all-to-all-start = ((bf16[32,32,448]{2,1,0:T(8,128)(2,1)}), bf16[32,32,448]{2,1,0:T(8,128)(2,1)}, u32[]{:S(2)}, u32[]{:S(2)}) async-start(bf16[32,32,448]{2,1,0:T(8,128)(2,1)} %bitcast.2), calls=%async_computation | async-start | bytes 2097152 | tf_op jit(solution)/shard_map/all_to_all | solution.py:84
  67.6 152.1 %all-reduce.3.cloned.1.call-start = ((), (), s32[]{:S(2)}) async-start(), calls=%async_computation.4 | async-start | bytes 12582912 | tf_op jit(solution)/shard_map/psum | solution.py:89
  67.6 52.7 %collective-permute-start.1 = (bf16[1024,448]{0,1:T(8,128)(2,1)}, bf16[1024,448]{0,1:T(8,128)(2,1)}, u32[]{:S(2)}, u32[]{:S(2)}) collective-permute-start(bf16[1024,448]{0,1:T(8,128)(2,1)} %bitcast.74), channel_id=1, source_target_pairs={{0,16},{16,0},{1,17},{17,1},{2,18},{18,2},{3,19},{19,3},{4,20},{20... | collective-permute-start | bytes 2752520 | tf_op jit(solution)/shard_map/ppermute | solution.py:18
  219.7 3.4 %copy-start.3 = (bf16[1024,1024]{1,0:T(8,128)(2,1)S(1)}, bf16[1024,1024]{1,0:T(8,128)(2,1)}, u32[]{:S(2)}) copy-start(bf16[1024,1024]{1,0:T(8,128)(2,1)} %get-tuple-element.7) | copy-start | bytes 6291460
  223.1 5.0 %copy-start.7 = (bf16[1,1024,448]{1,2,0:T(8,128)(2,1)S(1)}, bf16[1,1024,448]{1,2,0:T(8,128)(2,1)}, u32[]{:S(2)}) copy-start(bf16[1,1024,448]{1,2,0:T(8,128)(2,1)} %param.21) | copy-start | bytes 2752516
  226.8 1.3 copy-start
  231.8 33.6 %all-to-all-start.1 = ((bf16[32,32,448]{2,1,0:T(8,128)(2,1)}), bf16[32,32,448]{2,1,0:T(8,128)(2,1)S(1)}, u32[]{:S(2)}, u32[]{:S(2)}) async-start(bf16[32,32,448]{2,1,0:T(8,128)(2,1)} %bitcast.7), calls=%async_computation.1 | async-start | bytes 2097152 | tf_op jit(solution)/shard_map/all_to_all | solution.py:101
  240.2 5.5 %copy-start.2 = (bf16[1024,1024]{1,0:T(8,128)(2,1)S(1)}, bf16[1024,1024]{1,0:T(8,128)(2,1)}, u32[]{:S(2)}) copy-start(bf16[1024,1024]{1,0:T(8,128)(2,1)} %get-tuple-element.9) | copy-start | bytes 6291460
  243.0 35.3 %collective-permute-start.2 = (bf16[1024,448]{0,1:T(8,128)(2,1)}, bf16[1024,448]{0,1:T(8,128)(2,1)}, u32[]{:S(2)}, u32[]{:S(2)}) collective-permute-start(bf16[1024,448]{0,1:T(8,128)(2,1)} %bitcast_convert_fusion.1), channel_id=1, source_target_pairs={{0,16},{16,0},{1,17},{17,1},{2,18},{18,2},{3,19},{19,3},{4,20},{20... | collective-permute-start | bytes 2752520 | tf_op jit(solution)/shard_map/ppermute | solution.py:18
  265.4 43.7 %copy-start.5 = (bf16[32,32,448]{2,1,0:T(8,128)(2,1)S(1)}, bf16[32,32,448]{2,1,0:T(8,128)(2,1)}, u32[]{:S(2)}) copy-start(bf16[32,32,448]{2,1,0:T(8,128)(2,1)} %copy-done.4) | copy-start | bytes 2752516
  265.4 50.4 %all-to-all-start.3 = ((bf16[32,32,448]{2,1,0:T(8,128)(2,1)}), bf16[32,32,448]{2,1,0:T(8,128)(2,1)S(1)}, u32[]{:S(2)}, u32[]{:S(2)}) async-start(bf16[32,32,448]{2,1,0:T(8,128)(2,1)} %bitcast.13), calls=%async_computation.3 | async-start | bytes 2097152 | tf_op jit(solution)/shard_map/all_to_all | solution.py:127
  273.6 35.5 %copy-start.1 = (bf16[1024,1024]{1,0:T(8,128)(2,1)S(1)}, bf16[1024,1024]{1,0:T(8,128)(2,1)}, u32[]{:S(2)}) copy-start(bf16[1024,1024]{1,0:T(8,128)(2,1)} %copy-done) | copy-start | bytes 6291460
  275.4 33.7 %collective-permute-start.3 = (bf16[1024,448]{0,1:T(8,128)(2,1)S(1)}, bf16[1024,448]{0,1:T(8,128)(2,1)S(1)}, u32[]{:S(2)}, u32[]{:S(2)}) collective-permute-start(bf16[1024,448]{0,1:T(8,128)(2,1)S(1)} %bitcast_convert_fusion), channel_id=1, source_target_pairs={{0,16},{16,0},{1,17},{17,1},{2,18},{18,2},{3,19},{19,3},{4,20},{20... | collective-permute-start | bytes 2752520 | tf_op jit(solution)/shard_map/ppermute | solution.py:18
Sparse Core Ops, SparseCore 0:
  131.2 88.4 all-reduce.2
where the time goes:
time: 329 us; the launch traced here: 328 us
  waiting for transfers between devices  201 us (61%)
  starting transfers between devices  48.1 us (15%)
  matrix products  29 us (9%)
  other arithmetic  18.7 us (6%)
  local copies, waits for them, and re-layouts  15.9 us (5%)
  between operations  14.9 us (5%)
    psum x1, waiting for transfers between devices, shards(): lax.psum(jnp.dot(arrived, gate_up, preferred_element_type=jnp.float32).as...  88.6 us
    ppermute x4, waiting for transfers between devices, partner(): return lax.ppermute(block, axis, route)  79.5 us
    all_to_all x1, waiting for transfers between devices, shards(): lax.all_to_all(to_hosts(grad_slots), 'expert', split_axis=0, concat_axis=...  20.5 us
    all_to_all x1, waiting for transfers between devices, shards(): lax.all_to_all(outputs, 'expert', split_axis=0, concat_axis=0, tiled=True)  12.3 us
    all_to_all x1, starting transfers between devices, shards(): lax.all_to_all(to_hosts(grad_slots), 'expert', split_axis=0, concat_axis=...  11.9 us
    ppermute x4, starting transfers between devices, partner(): return lax.ppermute(block, axis, route)  11.2 us
    all_to_all x1, starting transfers between devices, shards(): lax.all_to_all(to_hosts(outgoing), 'expert', split_axis=0, concat_axis=0,...  8.45 us
    all_to_all x1, starting transfers between devices, shards(): lax.all_to_all(outputs, 'expert', split_axis=0, concat_axis=0, tiled=True)  8.44 us
  transfers between devices with their start and end apart: 9, of which 5 were waited for; matrix products, arithmetic and copies ran while one was open for 8% of the time, Pallas kernels for 0%

commit v1 on v0

v1 whole, which is shorter than its diff:
```python
import jax
import jax.numpy as jnp
from jax import lax
from jax.sharding import PartitionSpec as P


beta_first = 0.9
beta_second = 0.999
adam_eps = 1e-08
BF = jnp.bfloat16
F32 = jnp.float32


def dot(a, b, ca=1, cb=0):
    return lax.dot_general(a, b, (((ca,), (cb,)), ((), ())), preferred_element_type=F32)


def core_swap(block):
    return lax.ppermute(block, "dp", [(i, i ^ 1) for i in range(lax.axis_size("dp"))])


def chip_shift(block, step):
    count = lax.axis_size("dp")
    return lax.ppermute(block, "dp", [(i, (i + 2 * step) % count) for i in range(count)])


def expert_swap(block):
    count = lax.axis_size("expert")
    return lax.ppermute(block, "expert", [(i, i ^ (count // 2)) for i in range(count)])


def rows_at(block, index, rows):
    return lax.dynamic_slice_in_dim(block, index * rows, rows, 0)


def tie(value, *others):
    return lax.optimization_barrier((value,) + others)[0]


def pieces_of(keep, other, y_pos, chips):
    rows = keep.shape[0] // chips
    found = []
    for step in range(chips):
        at = (y_pos + step) % chips
        found.append(rows_at(keep, at, rows).astype(F32) + rows_at(other, at, rows).astype(F32))
    return found


def scatter_sum(pieces):
    total = pieces[0]
    for step in range(1, len(pieces)):
        came = chip_shift(pieces[step].astype(BF), step)
        total = total + came.astype(F32)
    return total


def gather_rows(shard, y_pos, core, chips):
    rows = shard.shape[0]
    half = jnp.zeros((chips * rows,) + shard.shape[1:], shard.dtype)
    half = lax.dynamic_update_slice_in_dim(half, shard, y_pos * rows, 0)
    for step in range(1, chips):
        piece = chip_shift(shard, step)
        half = lax.dynamic_update_slice_in_dim(half, piece, ((y_pos - step) % chips) * rows, 0)
    far = core_swap(half)
    full = jnp.where(core == 0, jnp.concatenate([half, far]), jnp.concatenate([far, half]))
    return half, full


def shards(
    tokens,
    cotangent,
    slot_tokens,
    slot_counts,
    slot_gates,
    swap_pairs,
    gate_weight,
    up_weight,
    down_weight,
    first_moment,
    second_moment,
):
    tok_count, model_cols = tokens.shape
    experts = slot_counts.shape[1]
    capacity = slot_tokens.shape[2]
    rows = experts * capacity
    half_rows = rows // 2
    chips = lax.axis_size("dp") // 2
    dp_pos = lax.axis_index("dp")
    core, y_pos = dp_pos % 2, dp_pos // 2
    position = lax.axis_index("expert")
    half_count = swap_pairs.shape[0]
    own_swap = (
        jnp.sum(jnp.where(jnp.arange(half_count) == position % half_count, swap_pairs, 0)) > 0
    )
    down_w = down_weight[0]
    live = (jnp.arange(capacity)[None, :] < slot_counts[0][:, None]).reshape(-1)
    route = slot_tokens[0].reshape(-1)
    weighted = jnp.where(live, slot_gates[0].reshape(-1), 0.0)
    masked_route = jnp.where(live, route, -1)
    token_ids = jnp.arange(tok_count)

    def exchange(block):
        return lax.all_to_all(
            block.reshape(experts, capacity, model_cols), "expert", 0, 0, tiled=True
        ).reshape(rows, model_cols)

    pick = (masked_route[:, None] == token_ids[None, :]).astype(BF)
    arrived = exchange(dot(pick, tokens).astype(BF))
    grad_rows = (dot(pick, cotangent) * weighted[:, None]).astype(BF)
    arrived_grad = exchange(grad_rows)
    far_one = expert_swap(first_moment[0].astype(BF))
    far_two = expert_swap(second_moment[0].astype(BF))
    gate_up = lax.optimization_barrier(jnp.concatenate([gate_weight[0], up_weight[0]], axis=1))

    pre_far = core_swap(dot(rows_at(arrived, 1 - core, half_rows), gate_up).astype(BF))
    pre_own = dot(rows_at(arrived, core, half_rows), gate_up).astype(BF)
    preact = scatter_sum(pieces_of(pre_own, pre_far, y_pos, chips))
    hidden_units = down_w.shape[0]
    gate_pre, up_pre = preact[:, :hidden_units], preact[:, hidden_units:]
    sig = jax.nn.sigmoid(gate_pre)
    hidden_shard = (gate_pre * sig * up_pre).astype(BF)
    hidden_half, hidden = gather_rows(hidden_shard, y_pos, core, chips)

    returned = exchange(dot(hidden, down_w).astype(BF))

    arrived_grad = tie(arrived_grad, hidden_shard)
    hid_far = core_swap(dot(rows_at(arrived_grad, 1 - core, half_rows), down_w, 1, 1).astype(BF))
    hid_own = dot(rows_at(arrived_grad, core, half_rows), down_w, 1, 1).astype(BF)
    hid_far = tie(hid_far, hidden_half)
    hidden_grad = scatter_sum(pieces_of(hid_own, hid_far, y_pos, chips))
    gate_grad = hidden_grad * up_pre * sig * (1.0 + gate_pre * (1.0 - sig))
    up_grad = hidden_grad * gate_pre * sig
    pre_shard = jnp.concatenate([gate_grad, up_grad], axis=1).astype(BF)
    _, pre_grad = gather_rows(pre_shard, y_pos, core, chips)
    returned_grad = exchange(dot(pre_grad, gate_up, 1, 1).astype(BF))

    weight_grad = dot(hidden, arrived_grad, 0, 0)
    far_grad = expert_swap(weight_grad.astype(BF))
    one = jnp.where(own_swap, far_one.astype(F32), first_moment[0])
    two = jnp.where(own_swap, far_two.astype(F32), second_moment[0])
    grad = jnp.where(own_swap, far_grad.astype(F32), weight_grad)
    new_one = beta_first * one + (1.0 - beta_first) * grad
    new_two = beta_second * two + (1.0 - beta_second) * grad * grad
    step_dir = (new_one / (jnp.sqrt(new_two) + adam_eps)).astype(BF)

    match = token_ids[:, None] == masked_route[None, :]
    top = lax.reduce_precision(weighted, 8, 7)
    rest = weighted - top
    mixed = (
        dot(jnp.where(match, top[None, :], 0.0).astype(BF), returned)
        + dot(jnp.where(match, rest[None, :], 0.0).astype(BF), returned)
    ).astype(BF)
    token_grad = dot(match.astype(BF), returned_grad).astype(BF)
    return (mixed, token_grad, new_one[None], new_two[None], step_dir[None])


def solution(mesh):
    return jax.shard_map(
        shards,
        mesh=mesh,
        in_specs=(
            P("expert", "dp"),
            P("expert", "dp"),
            P("expert", None, None),
            P("expert", None),
            P("expert", None, None),
            P(),
            P("expert", "dp", None),
            P("expert", "dp", None),
            P("expert", None, "dp"),
            P("expert", None, "dp"),
            P("expert", None, "dp"),
        ),
        out_specs=(
            P("expert", "dp"),
            P("expert", "dp"),
            P("expert", None, "dp"),
            P("expert", None, "dp"),
            P("expert", None, "dp"),
        ),
        check_vma=False,
    )
```

time: 329 us -> 280 us (0.85)
  waiting for transfers between devices: 201 us -> 147 us
  between operations: 14.9 us -> 1.62 us
  starting transfers between devices: 48.1 us -> 59.3 us
  matrix products: 29 us -> 35.8 us
    psum x1 -> x0, waiting for transfers between devices: 88.6 us -> none  [shards(): lax.psum(jnp.dot(arrived, gate_up, preferred_element_type=jnp.float32).as...]
    ppermute x4 -> x19, waiting for transfers between devices: 79.5 us -> 120 us  [the longest x12 71.2 us: chip_shift(): lax.ppermute(block, 'dp', [(i, (i + 2 * step) % count) for i in range(cou...]
    ppermute x4 -> x19, starting transfers between devices: 11.2 us -> 25 us  [the longest x12 11.1 us: chip_shift(): lax.ppermute(block, 'dp', [(i, (i + 2 * step) % count) for i in range(cou...]
    gather x2 -> x0, local copies, waits for them, and re-layouts: 7.93 us -> none  [the longest x1 3.97 us: shards(): picked = jnp.take(tokens, slot_route, axis=0)]
    dot_general x7 -> x12, matrix products: 29 us -> 35.8 us  [dot(): lax.dot_general(a, b, (((ca,), (cb,)), ((), ())), preferred_element_type=...]
    broadcast_in_dim x0 -> x1, other arithmetic: none -> 5.93 us  [shards(): return (mixed, token_grad, new_one[None], new_two[None], step_dir[None])]
    all_to_all x4, waiting for transfers between devices: 32.7 us -> 27.1 us  [exchange(): lax.all_to_all(block.reshape(experts, capacity, model_cols), 'expert', 0,...]
    dynamic_update_slice x0 -> x6, local copies, waits for them, and re-layouts: none -> 4.76 us  [gather_rows(): lax.dynamic_update_slice_in_dim(half, piece, (y_pos - step) % chips * row...]
  transfers between devices with their start and end apart: 9 -> 23, of which waited for: 5 -> 11; matrix products, arithmetic and copies ran while one was open for 8% -> 19% of each run, Pallas kernels for 0% -> 0%
where the time goes in v1:
time: 280 us; the launch traced here: 279 us
  waiting for transfers between devices  147 us (52%)
  starting transfers between devices  59.3 us (21%)
  matrix products  35.8 us (13%)
  local copies, waits for them, and re-layouts  18.2 us (6%)
  other arithmetic  17.2 us (6%)
    ppermute x12, waiting for transfers between devices, chip_shift(): lax.ppermute(block, 'dp', [(i, (i + 2 * step) % count) for i in range(cou...  71.2 us
    ppermute x3, waiting for transfers between devices, expert_swap(): lax.ppermute(block, 'expert', [(i, i ^ count // 2) for i in range(count)])  48.7 us
    dot_general x12, matrix products, dot(): lax.dot_general(a, b, (((ca,), (cb,)), ((), ())), preferred_element_type=...  35.8 us
    all_to_all x4, starting transfers between devices, exchange(): lax.all_to_all(block.reshape(experts, capacity, model_cols), 'expert', 0,...  34.3 us
    all_to_all x4, waiting for transfers between devices, exchange(): lax.all_to_all(block.reshape(experts, capacity, model_cols), 'expert', 0,...  27.1 us
    ppermute x12, starting transfers between devices, chip_shift(): lax.ppermute(block, 'dp', [(i, (i + 2 * step) % count) for i in range(cou...  11.1 us
    ppermute x4, starting transfers between devices, core_swap(): lax.ppermute(block, 'dp', [(i, i ^ 1) for i in range(lax.axis_size('dp'))])  8.18 us
    broadcast_in_dim x1, other arithmetic, shards(): return (mixed, token_grad, new_one[None], new_two[None], step_dir[None])  5.93 us
  transfers between devices with their start and end apart: 23, of which 11 were waited for; matrix products, arithmetic and copies ran while one was open for 19% of the time, Pallas kernels for 0%

profile of v1, /device:TPU:1, one launch (start us, length us, event | category | flops | bytes accessed | tf_op | source)
XLA Modules:
  0.0 279.2 jit_solution(6442806941235867561)
XLA Ops:
  2.3 1.5 convolution_convert_fusion.4
  3.8 1.3 copy.16
  5.1 12.0 %all-to-all-start = ((bf16[32,32,448]{2,1,0:T(8,128)(2,1)}), bf16[32,32,448]{2,1,0:T(8,128)(2,1)}, u32[]{:S(2)}, u32[]{:S(2)}) async-start(bf16[32,32,448]{2,1,0:T(8,128)(2,1)} %bitcast.1), calls=%async_computation | async-start | bytes 2097152 | tf_op jit(solution)/shard_map/all_to_all | solution.py:103
  17.1 1.6 pad_maximum_fusion
  18.8 23.2 %all-to-all-done = bf16[32,32,448]{2,1,0:T(8,128)(2,1)} async-done(((bf16[32,32,448]{2,1,0:T(8,128)(2,1)}), bf16[32,32,448]{2,1,0:T(8,128)(2,1)}, u32[]{:S(2)}, u32[]{:S(2)}) %all-to-all-start) | async-done | bytes 917536 | tf_op jit(solution)/shard_map/all_to_all | solution.py:103
  42.0 3.7 %convolution_convert_fusion = bf16[512,2048]{1,0:T(8,128)(2,1)} fusion(bf16[448,2048]{1,0:T(8,128)(2,1)S(1)} %pad_maximum_fusion, bf16[1024,448]{1,0:T(8,128)(2,1)} %bitcast.2, s32[]{:T(128)S(6)} %select_n.184), kind=kOutput, calls=%fused_computation.8 | convolution fusion | flops 940572672 | bytes 4456452 | tf_op jit(solution)/shard_map/dot_general | solution.py:15
  45.6 4.7 %collective-permute-start = (bf16[512,2048]{1,0:T(8,128)(2,1)}, bf16[512,2048]{1,0:T(8,128)(2,1)S(1)}, u32[]{:S(2)}, u32[]{:S(2)}) collective-permute-start(bf16[512,2048]{1,0:T(8,128)(2,1)} %convolution_convert_fusion), channel_id=1, source_target_pairs={{0,32},{32,0},{64,96},{96,64},{128,160},{160,128},{192,224},{224,1... | collective-permute-start | bytes 6291464 | tf_op jit(solution)/shard_map/ppermute | solution.py:19
  50.4 1.5 multiply_convert_fusion
  51.9 2.2 copy.18
  54.1 4.9 %all-to-all-start.2 = ((bf16[32,32,448]{2,1,0:T(8,128)(2,1)}), bf16[32,32,448]{2,1,0:T(8,128)(2,1)}, u32[]{:S(2)}, u32[]{:S(2)}) async-start(bf16[32,32,448]{2,1,0:T(8,128)(2,1)} %bitcast.8), calls=%async_computation.2 | async-start | bytes 2097152 | tf_op jit(solution)/shard_map/all_to_all | solution.py:103
  59.1 2.9 %convolution_convert_fusion.1 = bf16[512,2048]{1,0:T(8,128)(2,1)S(1)} fusion(bf16[448,2048]{1,0:T(8,128)(2,1)} %copy-done.5, bf16[1024,448]{1,0:T(8,128)(2,1)} %bitcast.2, s32[]{:T(128)S(6)} %select_n.180), kind=kOutput, calls=%fused_computation.9 | convolution fusion | flops 940572672 | bytes 4456452 | tf_op jit(solution)/shard_map/dot_general | solution.py:15
  62.1 1.9 add_convert_fusion.2
  64.5 2.7 collective-permute-start.3
  68.3 21.4 %collective-permute-done.3 = bf16[128,2048]{1,0:T(8,128)(2,1)S(1)} collective-permute-done((bf16[128,2048]{1,0:T(8,128)(2,1)}, bf16[128,2048]{1,0:T(8,128)(2,1)S(1)}, u32[]{:S(2)}, u32[]{:S(2)}) %collective-permute-start.3) | collective-permute-done | bytes 524320 | tf_op jit(solution)/shard_map/ppermute | solution.py:24
  89.7 4.4 %collective-permute-done.1 = bf16[128,2048]{1,0:T(8,128)(2,1)S(1)} collective-permute-done((bf16[128,2048]{1,0:T(8,128)(2,1)}, bf16[128,2048]{1,0:T(8,128)(2,1)S(1)}, u32[]{:S(2)}, u32[]{:S(2)}) %collective-permute-start.1) | collective-permute-done | bytes 524320 | tf_op jit(solution)/shard_map/ppermute | solution.py:24
  94.1 1.6 convert_add_fusion
  95.7 1.2 broadcast_in_dim.57
  97.8 2.7 convolution_convert_fusion.2
  101.0 1.5 collective-permute-start.5
  102.5 1.1 collective-permute-start.6
  103.7 1.7 convolution_convert_fusion.3
  105.4 10.2 %collective-permute-done.4 = bf16[128,1024]{1,0:T(8,128)(2,1)S(1)} collective-permute-done((bf16[128,1024]{1,0:T(8,128)(2,1)S(1)}, bf16[128,1024]{1,0:T(8,128)(2,1)S(1)}, u32[]{:S(2)}, u32[]{:S(2)}) %collective-permute-start.4) | collective-permute-done | bytes 262176 | tf_op jit(solution)/shard_map/ppermute | solution.py:24
  118.2 1.3 collective-permute-start.11
  120.2 5.1 %collective-permute-done.11 = bf16[128,1024]{1,0:T(8,128)(2,1)S(1)} collective-permute-done((bf16[128,1024]{1,0:T(8,128)(2,1)S(1)}, bf16[128,1024]{1,0:T(8,128)(2,1)S(1)}, u32[]{:S(2)}, u32[]{:S(2)}) %collective-permute-start.11) | collective-permute-done | bytes 262176 | tf_op jit(solution)/shard_map/ppermute | solution.py:24
  125.3 2.7 collective-permute-done.10
  127.9 6.4 %collective-permute-done.9 = bf16[128,1024]{1,0:T(8,128)(2,1)S(1)} collective-permute-done((bf16[128,1024]{1,0:T(8,128)(2,1)S(1)}, bf16[128,1024]{1,0:T(8,128)(2,1)S(1)}, u32[]{:S(2)}, u32[]{:S(2)}) %collective-permute-start.9) | collective-permute-done | bytes 262176 | tf_op jit(solution)/shard_map/ppermute | solution.py:24
  134.7 1.6 broadcast_in_dim.59
  137.9 2.0 collective-permute-start.14
  139.9 1.3 collective-permute-start.7
  141.3 21.1 %collective-permute-done.12 = bf16[128,2048]{1,0:T(8,128)(2,1)S(1)} collective-permute-done((bf16[128,2048]{1,0:T(8,128)(2,1)S(1)}, bf16[128,2048]{1,0:T(8,128)(2,1)S(1)}, u32[]{:S(2)}, u32[]{:S(2)}) %collective-permute-start.12) | collective-permute-done | bytes 524320 | tf_op jit(solution)/shard_map/ppermute | solution.py:24
  164.9 1.6 collective-permute-start.15
  167.5 3.8 %convolution_convert_fusion.5 = bf16[1024,448]{0,1:T(8,128)(2,1)} fusion(bf16[1,1024,448]{1,2,0:T(8,128)(2,1)S(1)} %copy-done, bf16[512,1024]{1,0:T(8,128)(2,1)S(1)} %collective-permute-done.7, bf16[512,1024]{1,0:T(8,128)(2,1)} %constant_dynamic-update-slice_fusion.4, pred[]{:T(512)S(6)} %eq.56), kind=kOutput, calls=%fused_computation.27 | convolution fusion | flops 949420032 | bytes 3932161 | tf_op jit(solution)/shard_map/dot_general | solution.py:15
  171.3 2.4 copy.17
  173.7 9.3 %all-to-all-start.1 = ((bf16[32,32,448]{2,1,0:T(8,128)(2,1)}), bf16[32,32,448]{2,1,0:T(8,128)(2,1)}, u32[]{:S(2)}, u32[]{:S(2)}) async-start(bf16[32,32,448]{2,1,0:T(8,128)(2,1)} %bitcast.48), calls=%async_computation.1 | async-start | bytes 2097152 | tf_op jit(solution)/shard_map/all_to_all | solution.py:103
  184.1 2.7 collective-permute-start.18
  186.7 1.1 bitcast_convert_fusion.1
  188.6 4.8 %fusion.44 = (bf16[1024,448]{0,1:T(8,128)(2,1)}, f32[1024,448]{0,1:T(8,128)}) fusion(bf16[1024,448]{1,0:T(8,128)(2,1)} %bitcast.9, bf16[512,1024]{1,0:T(8,128)(2,1)S(1)} %copy-done.9, bf16[512,1024]{1,0:T(8,128)(2,1)} %constant_dynamic-update-slice_fusion.4, pred[]{:T(512)S(6)} %eq.56), kind=kOutput, calls=%fused_computation.91 | convolution fusion | flops 949420032 | bytes 5767169 | tf_op jit(solution)/shard_map/dot_general | solution.py:15
  193.4 2.2 collective-permute-start.17
  195.6 6.5 %fusion.11 = bf16[1024,448]{0,1:T(8,128)(2,1)} fusion(bf16[448,2048]{1,0:T(8,128)(2,1)S(1)} %copy-done.6, bf16[512,2048]{1,0:T(8,128)(2,1)} %collective-permute-done.15, bf16[512,2048]{1,0:T(8,128)(2,1)} %constant_dynamic-update-slice_fusion.2, pred[]{:T(512)S(6)} %eq.56), kind=kOutput, calls=%fused_computation.28 | convolution fusion | flops 1898381312 | bytes 6946817 | tf_op jit(solution)/shard_map/dot_general | solution.py:15
  202.2 2.3 copy.19
  204.4 3.9 %all-to-all-done.1 = bf16[32,32,448]{2,1,0:T(8,128)(2,1)} async-done(((bf16[32,32,448]{2,1,0:T(8,128)(2,1)}), bf16[32,32,448]{2,1,0:T(8,128)(2,1)}, u32[]{:S(2)}, u32[]{:S(2)}) %all-to-all-start.1) | async-done | bytes 917536 | tf_op jit(solution)/shard_map/all_to_all | solution.py:103
  208.4 8.1 %all-to-all-start.3 = ((bf16[32,32,448]{2,1,0:T(8,128)(2,1)}), bf16[32,32,448]{2,1,0:T(8,128)(2,1)}, u32[]{:S(2)}, u32[]{:S(2)}) async-start(bf16[32,32,448]{2,1,0:T(8,128)(2,1)} %bitcast.47), calls=%async_computation.3 | async-start | bytes 2097152 | tf_op jit(solution)/shard_map/all_to_all | solution.py:103
  217.8 29.0 %collective-permute-done.16 = bf16[1024,448]{0,1:T(8,128)(2,1)} collective-permute-done((bf16[1024,448]{0,1:T(8,128)(2,1)}, bf16[1024,448]{0,1:T(8,128)(2,1)}, u32[]{:S(2)}, u32[]{:S(2)}) %collective-permute-start.16) | collective-permute-done | bytes 917536 | tf_op jit(solution)/shard_map/ppermute | solution.py:29
  246.8 19.7 %collective-permute-done.17 = bf16[1024,448]{0,1:T(8,128)(2,1)} collective-permute-done((bf16[1024,448]{0,1:T(8,128)(2,1)}, bf16[1024,448]{0,1:T(8,128)(2,1)}, u32[]{:S(2)}, u32[]{:S(2)}) %collective-permute-start.17) | collective-permute-done | bytes 917536 | tf_op jit(solution)/shard_map/ppermute | solution.py:29
  266.5 5.9 %fusion.16 = (bf16[1,1024,448]{1,2,0:T(8,128)(2,1)}, f32[1024,448]{0,1:T(8,128)}, f32[1024,448]{0,1:T(8,128)}) fusion(f32[1024,448]{0,1:T(8,128)} %get-tuple-element.27, bf16[1024,448]{0,1:T(8,128)(2,1)} %collective-permute-done.17, f32[1,1024,448]{1,2,0:T(8,128)S(1)} %copy-done.1, bf16[1024,448]{0,1:T(8,128)(2,1)} %collective-permute-done.18, pred[]{:T(512)S(6)} %gt.3, ...), kind=kLoop, calls=%fused_computation.43 | loop fusion | flops 7340032 | bytes 12845057 | tf_op jit(solution)/shard_map/broadcast_in_dim | solution.py:154
  272.4 1.8 fusion.17
  274.2 2.5 fusion.12
  276.7 2.5 convolution_convert_fusion.6
  (64 shorter events, 16.0 us)
Async XLA Ops:
  0.6 97.1 %copy-start = (bf16[1,1024,448]{1,2,0:T(8,128)(2,1)S(1)}, bf16[1,1024,448]{1,2,0:T(8,128)(2,1)}, u32[]{:S(2)}) copy-start(bf16[1,1024,448]{1,2,0:T(8,128)(2,1)} %param.19) | copy-start | bytes 2752516
  5.1 36.8 %all-to-all-start = ((bf16[32,32,448]{2,1,0:T(8,128)(2,1)}), bf16[32,32,448]{2,1,0:T(8,128)(2,1)}, u32[]{:S(2)}, u32[]{:S(2)}) async-start(bf16[32,32,448]{2,1,0:T(8,128)(2,1)} %bitcast.1), calls=%async_computation | async-start | bytes 2097152 | tf_op jit(solution)/shard_map/all_to_all | solution.py:103
  18.7 23.2 %copy-start.5 = (bf16[448,2048]{1,0:T(8,128)(2,1)}, bf16[448,2048]{1,0:T(8,128)(2,1)S(1)}, u32[]{:S(2)}) copy-start(bf16[448,2048]{1,0:T(8,128)(2,1)S(1)} %pad_maximum_fusion) | copy-start | bytes 5505028
  42.0 8.4 %copy-start.7 = (f32[1,32,32]{2,1,0:T(8,128)S(1)}, f32[1,32,32]{2,1,0:T(8,128)}, u32[]{:S(2)}) copy-start(f32[1,32,32]{2,1,0:T(8,128)} %param.15) | copy-start | bytes 12292
  42.0 8.5 %copy-start.10 = (bf16[256,448]{0,1:T(8,128)(2,1)S(1)}, bf16[256,448]{0,1:T(8,128)(2,1)}, u32[]{:S(2)}) copy-start(bf16[256,448]{0,1:T(8,128)(2,1)} %param.12) | copy-start | bytes 688132
  45.6 16.5 %collective-permute-start = (bf16[512,2048]{1,0:T(8,128)(2,1)}, bf16[512,2048]{1,0:T(8,128)(2,1)S(1)}, u32[]{:S(2)}, u32[]{:S(2)}) collective-permute-start(bf16[512,2048]{1,0:T(8,128)(2,1)} %convolution_convert_fusion), channel_id=1, source_target_pairs={{0,32},{32,0},{64,96},{96,64},{128,160},{160,128},{192,224},{224,1... | collective-permute-start | bytes 6291464 | tf_op jit(solution)/shard_map/ppermute | solution.py:19
  54.1 43.6 %all-to-all-start.2 = ((bf16[32,32,448]{2,1,0:T(8,128)(2,1)}), bf16[32,32,448]{2,1,0:T(8,128)(2,1)}, u32[]{:S(2)}, u32[]{:S(2)}) async-start(bf16[32,32,448]{2,1,0:T(8,128)(2,1)} %bitcast.8), calls=%async_computation.2 | async-start | bytes 2097152 | tf_op jit(solution)/shard_map/all_to_all | solution.py:103
  62.1 1.9 copy-start.4
  62.1 2.4 copy-start.3
  64.5 25.1 %collective-permute-start.3 = (bf16[128,2048]{1,0:T(8,128)(2,1)}, bf16[128,2048]{1,0:T(8,128)(2,1)S(1)}, u32[]{:S(2)}, u32[]{:S(2)}) collective-permute-start(bf16[128,2048]{1,0:T(8,128)(2,1)} %get-tuple-element.17), channel_id=1, source_target_pairs={{0,192},{32,224},{64,0},{96,32},{128,64},{160,96},{192,128},{224,1... | collective-permute-start | bytes 1572872 | tf_op jit(solution)/shard_map/ppermute | solution.py:24
  67.3 22.4 %collective-permute-start.2 = (bf16[128,2048]{1,0:T(8,128)(2,1)}, bf16[128,2048]{1,0:T(8,128)(2,1)S(1)}, u32[]{:S(2)}, u32[]{:S(2)}) collective-permute-start(bf16[128,2048]{1,0:T(8,128)(2,1)} %get-tuple-element.18), channel_id=1, source_target_pairs={{0,128},{32,160},{64,192},{96,224},{128,0},{160,32},{192,64},{224,... | collective-permute-start | bytes 1572872 | tf_op jit(solution)/shard_map/ppermute | solution.py:24
  67.6 26.4 %collective-permute-start.1 = (bf16[128,2048]{1,0:T(8,128)(2,1)}, bf16[128,2048]{1,0:T(8,128)(2,1)S(1)}, u32[]{:S(2)}, u32[]{:S(2)}) collective-permute-start(bf16[128,2048]{1,0:T(8,128)(2,1)} %get-tuple-element.16), channel_id=1, source_target_pairs={{0,64},{32,96},{64,128},{96,160},{128,192},{160,224},{192,0},{224,... | collective-permute-start | bytes 1572872 | tf_op jit(solution)/shard_map/ppermute | solution.py:24
  100.5 17.4 %collective-permute-start.8 = (bf16[512,1024]{1,0:T(8,128)(2,1)}, bf16[512,1024]{1,0:T(8,128)(2,1)S(1)}, u32[]{:S(2)}, u32[]{:S(2)}) collective-permute-start(bf16[512,1024]{1,0:T(8,128)(2,1)} %convolution_convert_fusion.2), channel_id=1, source_target_pairs={{0,32},{32,0},{64,96},{96,64},{128,160},{160,128},{192,224},{224,1... | collective-permute-start | bytes 3145736 | tf_op jit(solution)/shard_map/ppermute | solution.py:19
  101.0 14.7 %collective-permute-start.4 = (bf16[128,1024]{1,0:T(8,128)(2,1)S(1)}, bf16[128,1024]{1,0:T(8,128)(2,1)S(1)}, u32[]{:S(2)}, u32[]{:S(2)}) collective-permute-start(bf16[128,1024]{1,0:T(8,128)(2,1)S(1)} %get-tuple-element.15), channel_id=1, source_target_pairs={{0,64},{32,96},{64,128},{96,160},{128,192},{160,224},{192,0},{224,... | collective-permute-start | bytes 786440 | tf_op jit(solution)/shard_map/ppermute | solution.py:24
  101.0 15.4 %collective-permute-start.5 = (bf16[128,1024]{1,0:T(8,128)(2,1)S(1)}, bf16[128,1024]{1,0:T(8,128)(2,1)S(1)}, u32[]{:S(2)}, u32[]{:S(2)}) collective-permute-start(bf16[128,1024]{1,0:T(8,128)(2,1)S(1)} %get-tuple-element.15), channel_id=1, source_target_pairs={{0,128},{32,160},{64,192},{96,224},{128,0},{160,32},{192,64},{224,... | collective-permute-start | bytes 786440 | tf_op jit(solution)/shard_map/ppermute | solution.py:24
  102.5 14.7 %collective-permute-start.6 = (bf16[128,1024]{1,0:T(8,128)(2,1)S(1)}, bf16[128,1024]{1,0:T(8,128)(2,1)S(1)}, u32[]{:S(2)}, u32[]{:S(2)}) collective-permute-start(bf16[128,1024]{1,0:T(8,128)(2,1)S(1)} %get-tuple-element.15), channel_id=1, source_target_pairs={{0,192},{32,224},{64,0},{96,32},{128,64},{160,96},{192,128},{224,1... | collective-permute-start | bytes 786440 | tf_op jit(solution)/shard_map/ppermute | solution.py:24
  118.2 7.1 %collective-permute-start.11 = (bf16[128,1024]{1,0:T(8,128)(2,1)S(1)}, bf16[128,1024]{1,0:T(8,128)(2,1)S(1)}, u32[]{:S(2)}, u32[]{:S(2)}) collective-permute-start(bf16[128,1024]{1,0:T(8,128)(2,1)S(1)} %get-tuple-element.22), channel_id=1, source_target_pairs={{0,192},{32,224},{64,0},{96,32},{128,64},{160,96},{192,128},{224,1... | collective-permute-start | bytes 786440 | tf_op jit(solution)/shard_map/ppermute | solution.py:24
  119.5 8.4 %collective-permute-start.10 = (bf16[128,1024]{1,0:T(8,128)(2,1)S(1)}, bf16[128,1024]{1,0:T(8,128)(2,1)S(1)}, u32[]{:S(2)}, u32[]{:S(2)}) collective-permute-start(bf16[128,1024]{1,0:T(8,128)(2,1)S(1)} %get-tuple-element.23), channel_id=1, source_target_pairs={{0,128},{32,160},{64,192},{96,224},{128,0},{160,32},{192,64},{224,... | collective-permute-start | bytes 786440 | tf_op jit(solution)/shard_map/ppermute | solution.py:24
  119.5 14.8 %collective-permute-start.9 = (bf16[128,1024]{1,0:T(8,128)(2,1)S(1)}, bf16[128,1024]{1,0:T(8,128)(2,1)S(1)}, u32[]{:S(2)}, u32[]{:S(2)}) collective-permute-start(bf16[128,1024]{1,0:T(8,128)(2,1)S(1)} %get-tuple-element.21), channel_id=1, source_target_pairs={{0,64},{32,96},{64,128},{96,160},{128,192},{160,224},{192,0},{224,... | collective-permute-start | bytes 786440 | tf_op jit(solution)/shard_map/ppermute | solution.py:24
  137.2 25.1 %collective-permute-start.12 = (bf16[128,2048]{1,0:T(8,128)(2,1)S(1)}, bf16[128,2048]{1,0:T(8,128)(2,1)S(1)}, u32[]{:S(2)}, u32[]{:S(2)}) collective-permute-start(bf16[128,2048]{1,0:T(8,128)(2,1)S(1)} %get-tuple-element.24), channel_id=1, source_target_pairs={{0,64},{32,96},{64,128},{96,160},{128,192},{160,224},{192,0},{224,... | collective-permute-start | bytes 1572872 | tf_op jit(solution)/shard_map/ppermute | solution.py:24
  137.2 26.0 %collective-permute-start.13 = (bf16[128,2048]{1,0:T(8,128)(2,1)S(1)}, bf16[128,2048]{1,0:T(8,128)(2,1)S(1)}, u32[]{:S(2)}, u32[]{:S(2)}) collective-permute-start(bf16[128,2048]{1,0:T(8,128)(2,1)S(1)} %get-tuple-element.24), channel_id=1, source_target_pairs={{0,128},{32,160},{64,192},{96,224},{128,0},{160,32},{192,64},{224,... | collective-permute-start | bytes 1572872 | tf_op jit(solution)/shard_map/ppermute | solution.py:24
  137.9 26.1 %collective-permute-start.14 = (bf16[128,2048]{1,0:T(8,128)(2,1)S(1)}, bf16[128,2048]{1,0:T(8,128)(2,1)S(1)}, u32[]{:S(2)}, u32[]{:S(2)}) collective-permute-start(bf16[128,2048]{1,0:T(8,128)(2,1)S(1)} %get-tuple-element.24), channel_id=1, source_target_pairs={{0,192},{32,224},{64,0},{96,32},{128,64},{160,96},{192,128},{224,1... | collective-permute-start | bytes 1572872 | tf_op jit(solution)/shard_map/ppermute | solution.py:24
  139.9 26.6 %collective-permute-start.7 = (bf16[512,1024]{1,0:T(8,128)(2,1)}, bf16[512,1024]{1,0:T(8,128)(2,1)S(1)}, u32[]{:S(2)}, u32[]{:S(2)}) collective-permute-start(bf16[512,1024]{1,0:T(8,128)(2,1)} %constant_dynamic-update-slice_fusion.4), channel_id=1, source_target_pairs={{0,32},{32,0},{64,96},{96,64},{128,160},{160,128},{192,224},{224,1... | collective-permute-start | bytes 3145736 | tf_op jit(solution)/shard_map/ppermute | solution.py:19
  164.9 30.7 %collective-permute-start.15 = (bf16[512,2048]{1,0:T(8,128)(2,1)}, bf16[512,2048]{1,0:T(8,128)(2,1)}, u32[]{:S(2)}, u32[]{:S(2)}) collective-permute-start(bf16[512,2048]{1,0:T(8,128)(2,1)} %constant_dynamic-update-slice_fusion.2), channel_id=1, source_target_pairs={{0,32},{32,0},{64,96},{96,64},{128,160},{160,128},{192,224},{224,1... | collective-permute-start | bytes 6291464 | tf_op jit(solution)/shard_map/ppermute | solution.py:19
  166.5 1.0 copy-start.8
  171.3 11.7 %copy-start.1 = (f32[1,1024,448]{1,2,0:T(8,128)S(1)}, f32[1,1024,448]{1,2,0:T(8,128)}, u32[]{:S(2)}) copy-start(f32[1,1024,448]{1,2,0:T(8,128)} %param.21) | copy-start | bytes 5505028
  173.7 34.7 %all-to-all-start.1 = ((bf16[32,32,448]{2,1,0:T(8,128)(2,1)}), bf16[32,32,448]{2,1,0:T(8,128)(2,1)}, u32[]{:S(2)}, u32[]{:S(2)}) async-start(bf16[32,32,448]{2,1,0:T(8,128)(2,1)} %bitcast.48), calls=%async_computation.1 | async-start | bytes 2097152 | tf_op jit(solution)/shard_map/all_to_all | solution.py:103
  183.0 3.8 %copy-start.2 = (f32[1,1024,448]{1,2,0:T(8,128)S(1)}, f32[1,1024,448]{1,2,0:T(8,128)}, u32[]{:S(2)}) copy-start(f32[1,1024,448]{1,2,0:T(8,128)} %param.20) | copy-start | bytes 5505028
  183.0 5.6 %copy-start.9 = (bf16[512,1024]{1,0:T(8,128)(2,1)S(1)}, bf16[512,1024]{1,0:T(8,128)(2,1)}, u32[]{:S(2)}) copy-start(bf16[512,1024]{1,0:T(8,128)(2,1)} %copy-done.8) | copy-start | bytes 3145732
  184.1 33.8 %collective-permute-start.18 = (bf16[1024,448]{0,1:T(8,128)(2,1)}, bf16[1024,448]{0,1:T(8,128)(2,1)}, u32[]{:S(2)}, u32[]{:S(2)}) collective-permute-start(bf16[1024,448]{0,1:T(8,128)(2,1)} %bitcast_convert_fusion), channel_id=1, source_target_pairs={{0,16},{1,17},{2,18},{3,19},{4,20},{5,21},{6,22},{7,23},{8,24},{9,... | collective-permute-start | bytes 2752520 | tf_op jit(solution)/shard_map/ppermute | solution.py:29
  187.8 7.8 %copy-start.6 = (bf16[448,2048]{1,0:T(8,128)(2,1)S(1)}, bf16[448,2048]{1,0:T(8,128)(2,1)}, u32[]{:S(2)}) copy-start(bf16[448,2048]{1,0:T(8,128)(2,1)} %copy-done.5) | copy-start | bytes 5505028
  187.8 59.0 %collective-permute-start.16 = (bf16[1024,448]{0,1:T(8,128)(2,1)}, bf16[1024,448]{0,1:T(8,128)(2,1)}, u32[]{:S(2)}, u32[]{:S(2)}) collective-permute-start(bf16[1024,448]{0,1:T(8,128)(2,1)} %bitcast_convert_fusion.1), channel_id=1, source_target_pairs={{0,16},{1,17},{2,18},{3,19},{4,20},{5,21},{6,22},{7,23},{8,24},{9,... | collective-permute-start | bytes 2752520 | tf_op jit(solution)/shard_map/ppermute | solution.py:29
  193.4 73.1 %collective-permute-start.17 = (bf16[1024,448]{0,1:T(8,128)(2,1)}, bf16[1024,448]{0,1:T(8,128)(2,1)}, u32[]{:S(2)}, u32[]{:S(2)}) collective-permute-start(bf16[1024,448]{0,1:T(8,128)(2,1)} %get-tuple-element.26), channel_id=1, source_target_pairs={{0,16},{1,17},{2,18},{3,19},{4,20},{5,21},{6,22},{7,23},{8,24},{9,... | collective-permute-start | bytes 2752520 | tf_op jit(solution)/shard_map/ppermute | solution.py:29
  202.2 14.4 %copy-start.11 = (s32[16]{0:T(128)S(1)}, s32[16]{0:T(128)}, u32[]{:S(2)}) copy-start(s32[16]{0:T(128)} %param.16) | copy-start | bytes 196
  208.4 68.3 %all-to-all-start.3 = ((bf16[32,32,448]{2,1,0:T(8,128)(2,1)}), bf16[32,32,448]{2,1,0:T(8,128)(2,1)}, u32[]{:S(2)}, u32[]{:S(2)}) async-start(bf16[32,32,448]{2,1,0:T(8,128)(2,1)} %bitcast.47), calls=%async_computation.3 | async-start | bytes 2097152 | tf_op jit(solution)/shard_map/all_to_all | solution.py:103

commit v2 on v1

v2 whole, which is shorter than its diff:
```python
import jax
import jax.numpy as jnp
from jax import lax
from jax.sharding import PartitionSpec as P


beta_first = 0.9
beta_second = 0.999
adam_eps = 1e-08
BF = jnp.bfloat16
F32 = jnp.float32


def dot(a, b, ca=1, cb=0):
    return lax.dot_general(a, b, (((ca,), (cb,)), ((), ())), preferred_element_type=F32)


def core_swap(block):
    return lax.ppermute(block, "dp", [(i, i ^ 1) for i in range(lax.axis_size("dp"))])


def chip_shift(block, step):
    count = lax.axis_size("dp")
    return lax.ppermute(block, "dp", [(i, (i + 2 * step) % count) for i in range(count)])


def expert_swap(block):
    count = lax.axis_size("expert")
    return lax.ppermute(block, "expert", [(i, i ^ (count // 2)) for i in range(count)])


def rows_at(block, index, rows):
    return lax.dynamic_slice_in_dim(block, index * rows, rows, 0)


def tie(value, *others):
    return lax.optimization_barrier((value,) + others)[0]


def scatter_sum(partial, y_pos, chips):
    rows = partial.shape[0] // chips
    total = rows_at(partial, y_pos, rows).astype(F32)
    for step in (2, 1, 3):
        piece = rows_at(partial, (y_pos + step) % chips, rows)
        came = chip_shift(piece, step)
        total = total + came.astype(F32)
    return total


def gather_rows(shard, y_pos, chips):
    rows = shard.shape[0]
    full = jnp.zeros((chips * rows,) + shard.shape[1:], shard.dtype)
    full = lax.dynamic_update_slice_in_dim(full, shard, y_pos * rows, 0)
    for step in (1, 3, 2):
        piece = chip_shift(shard, step)
        full = lax.dynamic_update_slice_in_dim(full, piece, ((y_pos - step) % chips) * rows, 0)
    return full


def pair_rows(block):
    far = core_swap(block)
    return jnp.concatenate([block, far], axis=0)


def pair_sum(partial):
    split = partial.shape[0] // 2
    far = core_swap(partial[split:].astype(BF))
    return partial[:split] + far.astype(F32)


def shards(
    tokens,
    cotangent,
    slot_tokens,
    slot_counts,
    slot_gates,
    swap_pairs,
    gate_weight,
    up_weight,
    down_weight,
    first_moment,
    second_moment,
):
    tok_count, model_cols = tokens.shape
    experts = slot_counts.shape[1]
    capacity = slot_tokens.shape[2]
    own_slots = capacity // 2
    rows = experts * own_slots
    pair_cols = 2 * model_cols
    chips = lax.axis_size("dp") // 2
    dp_pos = lax.axis_index("dp")
    core, y_pos = dp_pos % 2, dp_pos // 2
    position = lax.axis_index("expert")
    half_count = swap_pairs.shape[0]
    own_swap = (
        jnp.sum(jnp.where(jnp.arange(half_count) == position % half_count, swap_pairs, 0)) > 0
    )

    def own_part(table):
        return lax.dynamic_slice_in_dim(table, core * own_slots, own_slots, 1)

    live = (own_part(jnp.arange(capacity)[None, :]) < slot_counts[0][:, None]).reshape(-1)
    route = own_part(slot_tokens[0]).reshape(-1)
    weighted = jnp.where(live, own_part(slot_gates[0]).reshape(-1), 0.0)
    masked_route = jnp.where(live, route, -1)
    token_ids = jnp.arange(tok_count)

    def exchange(block):
        return lax.all_to_all(
            block.reshape(experts, own_slots, pair_cols), "expert", 0, 0, tiled=True
        ).reshape(rows, pair_cols)

    token_cols = pair_rows(tokens.T)
    pick = (masked_route[:, None] == token_ids[None, :]).astype(BF)
    arrived = exchange(dot(pick, token_cols, 1, 1).astype(BF))
    grad_cols = pair_rows(cotangent.T)
    grad_rows = (dot(pick, grad_cols, 1, 1) * weighted[:, None]).astype(BF)
    gate_up = jnp.concatenate([pair_rows(gate_weight[0]), pair_rows(up_weight[0])], axis=1)
    down_cols = pair_rows(down_weight[0].T)
    moment_one = first_moment[0].T
    moment_two = second_moment[0].T
    gate_up, down_cols, grad_rows, arrived = lax.optimization_barrier(
        (gate_up, down_cols, grad_rows, arrived)
    )
    arrived_grad = exchange(grad_rows)
    far_one = expert_swap(moment_one.astype(BF))
    far_two = expert_swap(moment_two.astype(BF))

    preact = scatter_sum(dot(arrived, gate_up).astype(BF), y_pos, chips)
    hidden_units = down_weight.shape[1]
    gate_pre, up_pre = preact[:, :hidden_units], preact[:, hidden_units:]
    sig = jax.nn.sigmoid(gate_pre)
    hidden_shard = (gate_pre * sig * up_pre).astype(BF)
    hidden = gather_rows(hidden_shard, y_pos, chips)
    returned = exchange(dot(hidden, down_cols, 1, 1).astype(BF))

    arrived_grad = tie(arrived_grad, hidden_shard)
    hidden_part = tie(dot(arrived_grad, down_cols).astype(BF), hidden)
    hidden_grad = scatter_sum(hidden_part, y_pos, chips)
    gate_grad = hidden_grad * up_pre * sig * (1.0 + gate_pre * (1.0 - sig))
    up_grad = hidden_grad * gate_pre * sig
    pre_shard = jnp.concatenate([gate_grad, up_grad], axis=1).astype(BF)
    pre_grad = gather_rows(pre_shard, y_pos, chips)
    returned_grad = exchange(dot(pre_grad, gate_up, 1, 1).astype(BF))

    weight_grad = pair_sum(dot(tie(arrived_grad, pre_shard), hidden, 0, 0))
    far_grad = expert_swap(weight_grad.astype(BF))
    one = jnp.where(own_swap, far_one.astype(F32), moment_one)
    two = jnp.where(own_swap, far_two.astype(F32), moment_two)
    grad = jnp.where(own_swap, far_grad.astype(F32), weight_grad)
    new_one = beta_first * one + (1.0 - beta_first) * grad
    new_two = beta_second * two + (1.0 - beta_second) * grad * grad
    step_dir = (new_one / (jnp.sqrt(new_two) + adam_eps)).astype(BF)

    match = masked_route[:, None] == token_ids[None, :]
    top = lax.reduce_precision(weighted, 8, 7)
    rest = weighted - top
    mixed = pair_sum(
        dot(returned, jnp.where(match, top[:, None], 0.0).astype(BF), 0, 0)
        + dot(returned, jnp.where(match, rest[:, None], 0.0).astype(BF), 0, 0),
    ).astype(BF)
    returned_grad = tie(returned_grad, mixed, step_dir)
    token_grad = pair_sum(dot(returned_grad, match.astype(BF), 0, 0)).astype(BF)
    return (mixed.T, token_grad.T, new_one.T[None], new_two.T[None], step_dir.T[None])


def solution(mesh):
    return jax.shard_map(
        shards,
        mesh=mesh,
        in_specs=(
            P("expert", "dp"),
            P("expert", "dp"),
            P("expert", None, None),
            P("expert", None),
            P("expert", None, None),
            P(),
            P("expert", "dp", None),
            P("expert", "dp", None),
            P("expert", None, "dp"),
            P("expert", None, "dp"),
            P("expert", None, "dp"),
        ),
        out_specs=(
            P("expert", "dp"),
            P("expert", "dp"),
            P("expert", None, "dp"),
            P("expert", None, "dp"),
            P("expert", None, "dp"),
        ),
        check_vma=False,
    )
```

time: 280 us -> 193 us (0.69)
  waiting for transfers between devices: 147 us -> 31.6 us
  starting transfers between devices: 59.3 us -> 89.1 us
  other arithmetic: 17.2 us -> 31.9 us
  matrix products: 35.8 us -> 26.2 us
  local copies, waits for them, and re-layouts: 18.2 us -> 11.2 us
    ppermute x12, waiting for transfers between devices: 71.2 us -> 13 us  [chip_shift(): lax.ppermute(block, 'dp', [(i, (i + 2 * step) % count) for i in range(cou...]
    ppermute x3, waiting for transfers between devices: 48.7 us -> 10.7 us  [expert_swap(): lax.ppermute(block, 'expert', [(i, i ^ count // 2) for i in range(count)])]
    all_to_all x4, waiting for transfers between devices: 27.1 us -> 2.22 us  [exchange(): lax.all_to_all(block.reshape(experts, own_slots, pair_cols), 'expert', 0,...]
    ppermute x4 -> x8, starting transfers between devices: 8.18 us -> 25.1 us  [core_swap(): lax.ppermute(block, 'dp', [(i, i ^ 1) for i in range(lax.axis_size('dp'))])]
    concatenate x1 -> x2, other arithmetic: 1.59 us -> 12.8 us  [the longest x1 10.3 us: shards(): jnp.concatenate([pair_rows(gate_weight[0]), pair_rows(up_weight[0])], axi...]
    dot_general x12 -> x10, matrix products: 35.8 us -> 26.2 us  [dot(): lax.dot_general(a, b, (((ca,), (cb,)), ((), ())), preferred_element_type=...]
    convert_element_type x4 -> x5, other arithmetic: 4.35 us -> 12.7 us  [the longest x1 6.04 us: shards(): step_dir = (new_one / (jnp.sqrt(new_two) + adam_eps)).astype(BF)]
    convert_element_type x4 -> x0, local copies, waits for them, and re-layouts: 8.19 us -> none  [the longest x1 2.37 us: shards(): returned = exchange(dot(hidden, down_w).astype(BF))]
  transfers between devices with their start and end apart: 23 -> 27, of which waited for: 11 -> 11; matrix products, arithmetic and copies ran while one was open for 19% -> 29% of each run, Pallas kernels for 0% -> 0%
where the time goes in v2:
time: 193 us; the launch traced here: 192 us
  starting transfers between devices  89.1 us (46%)
  other arithmetic  31.9 us (17%)
  waiting for transfers between devices  31.6 us (16%)
  matrix products  26.2 us (14%)
  local copies, waits for them, and re-layouts  11.2 us (6%)
    all_to_all x4, starting transfers between devices, exchange(): lax.all_to_all(block.reshape(experts, own_slots, pair_cols), 'expert', 0,...  40 us
    dot_general x10, matrix products, dot(): lax.dot_general(a, b, (((ca,), (cb,)), ((), ())), preferred_element_type=...  26.2 us
    ppermute x8, starting transfers between devices, core_swap(): lax.ppermute(block, 'dp', [(i, i ^ 1) for i in range(lax.axis_size('dp'))])  25.1 us
    ppermute x12, starting transfers between devices, chip_shift(): lax.ppermute(block, 'dp', [(i, (i + 2 * step) % count) for i in range(cou...  16.7 us
    ppermute x12, waiting for transfers between devices, chip_shift(): lax.ppermute(block, 'dp', [(i, (i + 2 * step) % count) for i in range(cou...  13 us
    ppermute x3, waiting for transfers between devices, expert_swap(): lax.ppermute(block, 'expert', [(i, i ^ count // 2) for i in range(count)])  10.7 us
    concatenate x1, other arithmetic, shards(): jnp.concatenate([pair_rows(gate_weight[0]), pair_rows(up_weight[0])], axi...  10.3 us
    ppermute x3, starting transfers between devices, expert_swap(): lax.ppermute(block, 'expert', [(i, i ^ count // 2) for i in range(count)])  7.34 us
  transfers between devices with their start and end apart: 27, of which 11 were waited for; matrix products, arithmetic and copies ran while one was open for 29% of the time, Pallas kernels for 0%

profile of v2, /device:TPU:1, one launch (start us, length us, event | category | flops | bytes accessed | tf_op | source)
XLA Modules:
  0.0 191.7 jit_solution(14097563229535627022)
XLA Ops:
  0.7 3.3 %collective-permute-start.4 = (bf16[448,256]{1,0:T(8,128)(2,1)}, bf16[448,256]{1,0:T(8,128)(2,1)S(1)}, u32[]{:S(2)}, u32[]{:S(2)}) collective-permute-start(bf16[448,256]{1,0:T(8,128)(2,1)} %bitcast.77), channel_id=1, source_target_pairs={{0,32},{32,0},{64,96},{96,64},{128,160},{160,128},{192,224},{224,1... | collective-permute-start | bytes 688136 | tf_op jit(solution)/shard_map/ppermute | solution.py:19
  5.3 2.3 %convolution_convert_fusion.2 = bf16[512,896]{1,0:T(8,128)(2,1)} fusion(bf16[448,256]{1,0:T(8,128)(2,1)S(1)} %collective-permute-done.4, bf16[448,256]{1,0:T(8,128)(2,1)} %bitcast.78, s32[512]{0:T(512)S(1)} %broadcast_select_fusion.1), kind=kOutput, calls=%fused_computation.18 | convolution fusion | flops 236388352 | bytes 1378304 | tf_op jit(solution)/shard_map/dot_general | solution.py:15
  7.7 9.4 %all-to-all-start = ((bf16[32,16,896]{2,1,0:T(8,128)(2,1)}), bf16[32,16,896]{2,1,0:T(8,128)(2,1)}, u32[]{:S(2)}, u32[]{:S(2)}) async-start(bf16[32,16,896]{2,1,0:T(8,128)(2,1)} %bitcast.71), calls=%async_computation | async-start | bytes 1835008 | tf_op jit(solution)/shard_map/all_to_all | solution.py:109
  18.7 4.2 %collective-permute-done.3 = bf16[448,256]{1,0:T(8,128)(2,1)S(1)} collective-permute-done((bf16[448,256]{1,0:T(8,128)(2,1)S(1)}, bf16[448,256]{1,0:T(8,128)(2,1)S(1)}, u32[]{:S(2)}, u32[]{:S(2)}) %collective-permute-start.3) | collective-permute-done | bytes 229408 | tf_op jit(solution)/shard_map/ppermute | solution.py:19
  22.9 1.4 multiply_convert_fusion
  24.4 2.6 %pad_maximum_fusion = bf16[896,1024]{1,0:T(8,128)(2,1)} fusion(bf16[448,1024]{1,0:T(8,128)(2,1)} %collective-permute-done.2, bf16[448,1024]{1,0:T(8,128)(2,1)S(1)} %bitcast.66), kind=kLoop, calls=%fused_computation.6 | loop fusion | flops 3670016 | bytes 3670016 | tf_op jit(solution)/shard_map/concatenate | solution.py:62
  26.9 10.3 %maximum_maximum_fusion = bf16[896,2048]{1,0:T(8,128)(2,1)} fusion(bf16[448,1024]{1,0:T(8,128)(2,1)} %collective-permute-done.1, bf16[448,1024]{1,0:T(8,128)(2,1)S(1)} %bitcast.68, bf16[448,1024]{1,0:T(8,128)(2,1)} %collective-permute-done, bf16[448,1024]{1,0:T(8,128)(2,1)S(1)} %bitcast.70), kind=kLoop, calls=%fused_computation | loop fusion | flops 14680064 | bytes 7340032 | tf_op jit(solution)/shard_map/concatenate | solution.py:118
  37.2 2.2 %all-to-all-done = bf16[32,16,896]{2,1,0:T(8,128)(2,1)} async-done(((bf16[32,16,896]{2,1,0:T(8,128)(2,1)}), bf16[32,16,896]{2,1,0:T(8,128)(2,1)}, u32[]{:S(2)}, u32[]{:S(2)}) %all-to-all-start) | async-done | bytes 917536 | tf_op jit(solution)/shard_map/all_to_all | solution.py:109
  39.4 4.7 %convolution_convert_fusion = bf16[512,2048]{1,0:T(8,128)(2,1)S(1)} fusion(bf16[512,896]{1,0:T(8,128)(2,1)} %bitcast.10, bf16[896,2048]{1,0:T(8,128)(2,1)} %maximum_maximum_fusion), kind=kOutput, calls=%fused_computation.1 | convolution fusion | flops 1880096768 | bytes 6684672 | tf_op jit(solution)/shard_map/dot_general | solution.py:15
  44.1 1.3 copy-done.6
  45.5 2.8 %collective-permute-start.7 = (bf16[128,2048]{1,0:T(8,128)(2,1)S(1)}, bf16[128,2048]{1,0:T(8,128)(2,1)S(1)}, u32[]{:S(2)}, u32[]{:S(2)}) collective-permute-start(bf16[128,2048]{1,0:T(8,128)(2,1)S(1)} %get-tuple-element.31), channel_id=1, source_target_pairs={{0,192},{32,224},{64,0},{96,32},{128,64},{160,96},{192,128},{224,1... | collective-permute-start | bytes 1572872 | tf_op jit(solution)/shard_map/ppermute | solution.py:24
  48.4 1.6 collective-permute-start.5
  50.0 8.2 %all-to-all-start.2 = ((bf16[32,16,896]{2,1,0:T(8,128)(2,1)}), bf16[32,16,896]{2,1,0:T(8,128)(2,1)}, u32[]{:S(2)}, u32[]{:S(2)}) async-start(bf16[32,16,896]{2,1,0:T(8,128)(2,1)} %bitcast.14), calls=%async_computation.2 | async-start | bytes 1835008 | tf_op jit(solution)/shard_map/all_to_all | solution.py:109
  58.3 1.3 collective-permute-done.6
  60.4 8.1 %collective-permute-done.5 = bf16[128,2048]{1,0:T(8,128)(2,1)} collective-permute-done((bf16[128,2048]{1,0:T(8,128)(2,1)S(1)}, bf16[128,2048]{1,0:T(8,128)(2,1)}, u32[]{:S(2)}, u32[]{:S(2)}) %collective-permute-start.5) | collective-permute-done | bytes 524320 | tf_op jit(solution)/shard_map/ppermute | solution.py:24
  68.5 1.7 convert_add_fusion
  70.2 1.1 broadcast_in_dim.53
  72.3 2.7 %collective-permute-start.9 = (bf16[128,1024]{1,0:T(8,128)(2,1)}, bf16[128,1024]{1,0:T(8,128)(2,1)S(1)}, u32[]{:S(2)}, u32[]{:S(2)}) collective-permute-start(bf16[128,1024]{1,0:T(8,128)(2,1)} %get-tuple-element.27), channel_id=1, source_target_pairs={{0,192},{32,224},{64,0},{96,32},{128,64},{160,96},{192,128},{224,1... | collective-permute-start | bytes 786440 | tf_op jit(solution)/shard_map/ppermute | solution.py:24
  75.3 1.1 bitcast_convert_fusion
  76.4 2.0 %collective-permute-start.21 = (bf16[448,1024]{1,0:T(8,128)(2,1)}, bf16[448,1024]{1,0:T(8,128)(2,1)}, u32[]{:S(2)}, u32[]{:S(2)}) collective-permute-start(bf16[448,1024]{1,0:T(8,128)(2,1)} %bitcast_convert_fusion), channel_id=1, source_target_pairs={{0,16},{1,17},{2,18},{3,19},{4,20},{5,21},{6,22},{7,23},{8,24},{9,... | collective-permute-start | bytes 2752520 | tf_op jit(solution)/shard_map/ppermute | solution.py:29
  79.3 1.7 constant_dynamic-update-slice_fusion.6
  83.0 3.2 %convolution_convert_fusion.1 = bf16[512,1024]{1,0:T(8,128)(2,1)S(1)} fusion(bf16[512,896]{1,0:T(8,128)(2,1)} %bitcast.15, bf16[896,1024]{1,0:T(8,128)(2,1)} %pad_maximum_fusion), kind=kOutput, calls=%fused_computation.17 | convolution fusion | flops 940048384 | bytes 3801088 | tf_op jit(solution)/shard_map/dot_general | solution.py:15
  87.9 3.2 %collective-permute-start.14 = (bf16[128,1024]{1,0:T(8,128)(2,1)}, bf16[128,1024]{1,0:T(8,128)(2,1)}, u32[]{:S(2)}, u32[]{:S(2)}) collective-permute-start(bf16[128,1024]{1,0:T(8,128)(2,1)} %get-tuple-element.34), channel_id=1, source_target_pairs={{0,192},{32,224},{64,0},{96,32},{128,64},{160,96},{192,128},{224,1... | collective-permute-start | bytes 786440 | tf_op jit(solution)/shard_map/ppermute | solution.py:24
  91.2 1.2 collective-permute-start.12
  92.4 3.4 %convolution_convert_fusion.3 = bf16[512,896]{1,0:T(8,128)(2,1)} fusion(bf16[512,1024]{1,0:T(8,128)(2,1)} %constant_dynamic-update-slice_fusion.4, bf16[896,1024]{1,0:T(8,128)(2,1)S(1)} %copy-done.7), kind=kOutput, calls=%fused_computation.19 | convolution fusion | flops 939982848 | bytes 3801088 | tf_op jit(solution)/shard_map/dot_general | solution.py:15
  95.8 13.6 %all-to-all-start.1 = ((bf16[32,16,896]{2,1,0:T(8,128)(2,1)}), bf16[32,16,896]{2,1,0:T(8,128)(2,1)}, u32[]{:S(2)}, u32[]{:S(2)}) async-start(bf16[32,16,896]{2,1,0:T(8,128)(2,1)} %bitcast.73), calls=%async_computation.1 | async-start | bytes 1835008 | tf_op jit(solution)/shard_map/all_to_all | solution.py:109
  109.4 1.6 multiply_convert_fusion.2
  111.4 1.9 collective-permute-start.15
  113.2 1.1 bitcast_convert_fusion.1
  114.3 2.7 %collective-permute-start.18 = (bf16[448,1024]{1,0:T(8,128)(2,1)}, bf16[448,1024]{1,0:T(8,128)(2,1)}, u32[]{:S(2)}, u32[]{:S(2)}) collective-permute-start(bf16[448,1024]{1,0:T(8,128)(2,1)} %bitcast_convert_fusion.1), channel_id=1, source_target_pairs={{0,16},{1,17},{2,18},{3,19},{4,20},{5,21},{6,22},{7,23},{8,24},{9,... | collective-permute-start | bytes 2752520 | tf_op jit(solution)/shard_map/ppermute | solution.py:29
  117.0 1.7 collective-permute-start.16
  118.7 1.2 collective-permute-start.17
  119.8 2.6 %fusion.33 = f32[896,1024]{1,0:T(8,128)S(1)} fusion(bf16[512,896]{1,0:T(8,128)(2,1)} %bitcast.15, bf16[512,1024]{1,0:T(8,128)(2,1)} %constant_dynamic-update-slice_fusion.4), kind=kOutput, calls=%fused_computation.85 | convolution fusion | flops 939524096 | bytes 5636096 | tf_op jit(solution)/shard_map/dot_general | solution.py:15
  123.6 8.4 %collective-permute-start.19 = (bf16[448,1024]{1,0:T(8,128)(2,1)}, bf16[448,1024]{1,0:T(8,128)(2,1)S(1)}, u32[]{:S(2)}, u32[]{:S(2)}) collective-permute-start(bf16[448,1024]{1,0:T(8,128)(2,1)} %slice.66), channel_id=1, source_target_pairs={{0,32},{32,0},{64,96},{96,64},{128,160},{160,128},{192,224},{224,1... | collective-permute-start | bytes 2752520 | tf_op jit(solution)/shard_map/ppermute | solution.py:19
  132.2 2.0 %collective-permute-done.17 = bf16[128,2048]{1,0:T(8,128)(2,1)S(1)} collective-permute-done((bf16[128,2048]{1,0:T(8,128)(2,1)S(1)}, bf16[128,2048]{1,0:T(8,128)(2,1)S(1)}, u32[]{:S(2)}, u32[]{:S(2)}) %collective-permute-start.17) | collective-permute-done | bytes 524320 | tf_op jit(solution)/shard_map/ppermute | solution.py:24
  134.3 3.3 %convolution_convert_fusion.4 = bf16[512,896]{1,0:T(8,128)(2,1)} fusion(bf16[512,2048]{1,0:T(8,128)(2,1)S(1)} %constant_dynamic-update-slice_fusion, bf16[896,2048]{1,0:T(8,128)(2,1)S(1)} %copy-done.4), kind=kOutput, calls=%fused_computation.20 | convolution fusion | flops 1879506944 | bytes 6684672 | tf_op jit(solution)/shard_map/dot_general | solution.py:15
  137.6 8.7 %all-to-all-start.3 = ((bf16[32,16,896]{2,1,0:T(8,128)(2,1)}), bf16[32,16,896]{2,1,0:T(8,128)(2,1)}, u32[]{:S(2)}, u32[]{:S(2)}) async-start(bf16[32,16,896]{2,1,0:T(8,128)(2,1)} %bitcast.72), calls=%async_computation.3 | async-start | bytes 1835008 | tf_op jit(solution)/shard_map/all_to_all | solution.py:109
  146.3 2.7 %fusion.5 = bf16[448,1024]{1,0:T(8,128)(2,1)} fusion(bf16[448,1024]{1,0:T(8,128)(2,1)S(1)} %collective-permute-done.19, f32[896,1024]{1,0:T(8,128)} %copy-done.1), kind=kLoop, calls=%fused_computation.33 | loop fusion | flops 1376256 | bytes 3670016 | tf_op jit(solution)/shard_map/convert_element_type | solution.py:147
  149.0 2.7 %collective-permute-start.20 = (bf16[448,1024]{1,0:T(8,128)(2,1)}, bf16[448,1024]{1,0:T(8,128)(2,1)}, u32[]{:S(2)}, u32[]{:S(2)}) collective-permute-start(bf16[448,1024]{1,0:T(8,128)(2,1)} %fusion.5), channel_id=1, source_target_pairs={{0,16},{1,17},{2,18},{3,19},{4,20},{5,21},{6,22},{7,23},{8,24},{9,... | collective-permute-start | bytes 2752520 | tf_op jit(solution)/shard_map/ppermute | solution.py:29
  151.7 1.8 fusion.14
  153.5 1.8 convolution_add_fusion
  156.3 7.6 %collective-permute-start.11 = (bf16[448,256]{1,0:T(8,128)(2,1)S(1)}, bf16[448,256]{1,0:T(8,128)(2,1)S(1)}, u32[]{:S(2)}, u32[]{:S(2)}) collective-permute-start(bf16[448,256]{1,0:T(8,128)(2,1)S(1)} %slice.68), channel_id=1, source_target_pairs={{0,32},{32,0},{64,96},{96,64},{128,160},{160,128},{192,224},{224,1... | collective-permute-start | bytes 688136 | tf_op jit(solution)/shard_map/ppermute | solution.py:19
  165.2 1.8 fusion.7
  166.9 10.7 %collective-permute-done.20 = bf16[448,1024]{1,0:T(8,128)(2,1)} collective-permute-done((bf16[448,1024]{1,0:T(8,128)(2,1)}, bf16[448,1024]{1,0:T(8,128)(2,1)}, u32[]{:S(2)}, u32[]{:S(2)}) %collective-permute-start.20) | collective-permute-done | bytes 917536 | tf_op jit(solution)/shard_map/ppermute | solution.py:29
  177.6 6.0 %divide_convert_fusion = (bf16[448,1024]{1,0:T(8,128)(2,1)}, f32[448,1024]{1,0:T(8,128)}, f32[448,1024]{1,0:T(8,128)}) fusion(bf16[448,1024]{1,0:T(8,128)(2,1)S(1)} %collective-permute-done.19, f32[896,1024]{1,0:T(8,128)} %copy-done.1, bf16[448,1024]{1,0:T(8,128)(2,1)} %collective-permute-done.20, f32[1,1024,448]{1,2,0:T(8,128)S(1)} %copy-done.2, ...), kind=kLoop, calls=%fused_computation.14 | loop fusion | flops 8257536 | bytes 13762561 | tf_op jit(solution)/shard_map/convert_element_type | solution.py:153
  183.7 1.7 fusion.4
  185.4 4.4 %collective-permute-start.22 = (bf16[448,256]{1,0:T(8,128)(2,1)S(1)}, bf16[448,256]{1,0:T(8,128)(2,1)S(1)}, u32[]{:S(2)}, u32[]{:S(2)}) collective-permute-start(bf16[448,256]{1,0:T(8,128)(2,1)S(1)} %slice.67), channel_id=1, source_target_pairs={{0,32},{32,0},{64,96},{96,64},{128,160},{160,128},{192,224},{224,1... | collective-permute-start | bytes 688136 | tf_op jit(solution)/shard_map/ppermute | solution.py:19
  189.8 1.1 collective-permute-done.22
  (85 shorter events, 13.7 us)
Async XLA Ops:
  0.6 4.2 %copy-start = (s32[1,32,32]{2,1,0:T(8,128)S(1)}, s32[1,32,32]{2,1,0:T(8,128)}, u32[]{:S(2)}) copy-start(s32[1,32,32]{2,1,0:T(8,128)} %param.13) | copy-start | bytes 12292
  0.6 16.5 %copy-start.9 = (bf16[1,1024,448]{1,2,0:T(8,128)(2,1)S(1)}, bf16[1,1024,448]{1,2,0:T(8,128)(2,1)}, u32[]{:S(2)}) copy-start(bf16[1,1024,448]{1,2,0:T(8,128)(2,1)} %param.19) | copy-start | bytes 2752516
  0.7 17.2 %copy-start.10 = (bf16[1,448,1024]{2,1,0:T(8,128)(2,1)S(1)}, bf16[1,448,1024]{2,1,0:T(8,128)(2,1)}, u32[]{:S(2)}) copy-start(bf16[1,448,1024]{2,1,0:T(8,128)(2,1)} %param.18) | copy-start | bytes 2752516
  0.7 17.3 %copy-start.11 = (bf16[1,448,1024]{2,1,0:T(8,128)(2,1)S(1)}, bf16[1,448,1024]{2,1,0:T(8,128)(2,1)}, u32[]{:S(2)}) copy-start(bf16[1,448,1024]{2,1,0:T(8,128)(2,1)} %param.17) | copy-start | bytes 2752516
  0.7 17.7 %copy-start.14 = (bf16[256,448]{0,1:T(8,128)(2,1)S(1)}, bf16[256,448]{0,1:T(8,128)(2,1)}, u32[]{:S(2)}) copy-start(bf16[256,448]{0,1:T(8,128)(2,1)} %param.12) | copy-start | bytes 688132
  0.7 17.8 %copy-start.13 = (f32[1,32,32]{2,1,0:T(8,128)S(1)}, f32[1,32,32]{2,1,0:T(8,128)}, u32[]{:S(2)}) copy-start(f32[1,32,32]{2,1,0:T(8,128)} %param.15) | copy-start | bytes 12292
  0.7 4.6 %collective-permute-start.4 = (bf16[448,256]{1,0:T(8,128)(2,1)}, bf16[448,256]{1,0:T(8,128)(2,1)S(1)}, u32[]{:S(2)}, u32[]{:S(2)}) collective-permute-start(bf16[448,256]{1,0:T(8,128)(2,1)} %bitcast.77), channel_id=1, source_target_pairs={{0,32},{32,0},{64,96},{96,64},{128,160},{160,128},{192,224},{224,1... | collective-permute-start | bytes 688136 | tf_op jit(solution)/shard_map/ppermute | solution.py:19
  7.7 31.8 %all-to-all-start = ((bf16[32,16,896]{2,1,0:T(8,128)(2,1)}), bf16[32,16,896]{2,1,0:T(8,128)(2,1)}, u32[]{:S(2)}, u32[]{:S(2)}) async-start(bf16[32,16,896]{2,1,0:T(8,128)(2,1)} %bitcast.71), calls=%async_computation | async-start | bytes 1835008 | tf_op jit(solution)/shard_map/all_to_all | solution.py:109
  17.1 7.2 %collective-permute-start.2 = (bf16[448,1024]{1,0:T(8,128)(2,1)S(1)}, bf16[448,1024]{1,0:T(8,128)(2,1)}, u32[]{:S(2)}, u32[]{:S(2)}) collective-permute-start(bf16[448,1024]{1,0:T(8,128)(2,1)S(1)} %bitcast.65), channel_id=1, source_target_pairs={{0,32},{32,0},{64,96},{96,64},{128,160},{160,128},{192,224},{224,1... | collective-permute-start | bytes 2752520 | tf_op jit(solution)/shard_map/ppermute | solution.py:19
  17.9 9.0 %collective-permute-start.1 = (bf16[448,1024]{1,0:T(8,128)(2,1)S(1)}, bf16[448,1024]{1,0:T(8,128)(2,1)}, u32[]{:S(2)}, u32[]{:S(2)}) collective-permute-start(bf16[448,1024]{1,0:T(8,128)(2,1)S(1)} %bitcast.67), channel_id=1, source_target_pairs={{0,32},{32,0},{64,96},{96,64},{128,160},{160,128},{192,224},{224,1... | collective-permute-start | bytes 2752520 | tf_op jit(solution)/shard_map/ppermute | solution.py:19
  18.0 8.9 %collective-permute-start = (bf16[448,1024]{1,0:T(8,128)(2,1)S(1)}, bf16[448,1024]{1,0:T(8,128)(2,1)}, u32[]{:S(2)}, u32[]{:S(2)}) collective-permute-start(bf16[448,1024]{1,0:T(8,128)(2,1)S(1)} %bitcast.69), channel_id=1, source_target_pairs={{0,32},{32,0},{64,96},{96,64},{128,160},{160,128},{192,224},{224,1... | collective-permute-start | bytes 2752520 | tf_op jit(solution)/shard_map/ppermute | solution.py:19
  18.4 4.5 %collective-permute-start.3 = (bf16[448,256]{1,0:T(8,128)(2,1)S(1)}, bf16[448,256]{1,0:T(8,128)(2,1)S(1)}, u32[]{:S(2)}, u32[]{:S(2)}) collective-permute-start(bf16[448,256]{1,0:T(8,128)(2,1)S(1)} %bitcast.79), channel_id=1, source_target_pairs={{0,32},{32,0},{64,96},{96,64},{128,160},{160,128},{192,224},{224,1... | collective-permute-start | bytes 688136 | tf_op jit(solution)/shard_map/ppermute | solution.py:19
  44.1 1.4 copy-start.6
  45.5 12.7 %collective-permute-start.7 = (bf16[128,2048]{1,0:T(8,128)(2,1)S(1)}, bf16[128,2048]{1,0:T(8,128)(2,1)S(1)}, u32[]{:S(2)}, u32[]{:S(2)}) collective-permute-start(bf16[128,2048]{1,0:T(8,128)(2,1)S(1)} %get-tuple-element.31), channel_id=1, source_target_pairs={{0,192},{32,224},{64,0},{96,32},{128,64},{160,96},{192,128},{224,1... | collective-permute-start | bytes 1572872 | tf_op jit(solution)/shard_map/ppermute | solution.py:24
  48.4 11.3 %collective-permute-start.6 = (bf16[128,2048]{1,0:T(8,128)(2,1)S(1)}, bf16[128,2048]{1,0:T(8,128)(2,1)S(1)}, u32[]{:S(2)}, u32[]{:S(2)}) collective-permute-start(bf16[128,2048]{1,0:T(8,128)(2,1)S(1)} %get-tuple-element.32), channel_id=1, source_target_pairs={{0,64},{32,96},{64,128},{96,160},{128,192},{160,224},{192,0},{224,... | collective-permute-start | bytes 1572872 | tf_op jit(solution)/shard_map/ppermute | solution.py:24
  48.4 20.2 %collective-permute-start.5 = (bf16[128,2048]{1,0:T(8,128)(2,1)S(1)}, bf16[128,2048]{1,0:T(8,128)(2,1)}, u32[]{:S(2)}, u32[]{:S(2)}) collective-permute-start(bf16[128,2048]{1,0:T(8,128)(2,1)S(1)} %get-tuple-element.30), channel_id=1, source_target_pairs={{0,128},{32,160},{64,192},{96,224},{128,0},{160,32},{192,64},{224,... | collective-permute-start | bytes 1572872 | tf_op jit(solution)/shard_map/ppermute | solution.py:24
  50.0 33.0 %all-to-all-start.2 = ((bf16[32,16,896]{2,1,0:T(8,128)(2,1)}), bf16[32,16,896]{2,1,0:T(8,128)(2,1)}, u32[]{:S(2)}, u32[]{:S(2)}) async-start(bf16[32,16,896]{2,1,0:T(8,128)(2,1)} %bitcast.14), calls=%async_computation.2 | async-start | bytes 1835008 | tf_op jit(solution)/shard_map/all_to_all | solution.py:109
  59.6 0.8 copy-start.12
  70.2 5.1 %copy-start.2 = (f32[1,1024,448]{1,2,0:T(8,128)S(1)}, f32[1,1024,448]{1,2,0:T(8,128)}, u32[]{:S(2)}) copy-start(f32[1,1024,448]{1,2,0:T(8,128)} %param.21) | copy-start | bytes 5505028
  72.3 7.0 %collective-permute-start.8 = (bf16[128,1024]{1,0:T(8,128)(2,1)}, bf16[128,1024]{1,0:T(8,128)(2,1)}, u32[]{:S(2)}, u32[]{:S(2)}) collective-permute-start(bf16[128,1024]{1,0:T(8,128)(2,1)} %get-tuple-element.27), channel_id=1, source_target_pairs={{0,64},{32,96},{64,128},{96,160},{128,192},{160,224},{192,0},{224,... | collective-permute-start | bytes 786440 | tf_op jit(solution)/shard_map/ppermute | solution.py:24
  72.3 9.1 %collective-permute-start.9 = (bf16[128,1024]{1,0:T(8,128)(2,1)}, bf16[128,1024]{1,0:T(8,128)(2,1)S(1)}, u32[]{:S(2)}, u32[]{:S(2)}) collective-permute-start(bf16[128,1024]{1,0:T(8,128)(2,1)} %get-tuple-element.27), channel_id=1, source_target_pairs={{0,192},{32,224},{64,0},{96,32},{128,64},{160,96},{192,128},{224,1... | collective-permute-start | bytes 786440 | tf_op jit(solution)/shard_map/ppermute | solution.py:24
  74.9 7.3 %collective-permute-start.10 = (bf16[128,1024]{1,0:T(8,128)(2,1)}, bf16[128,1024]{1,0:T(8,128)(2,1)S(1)}, u32[]{:S(2)}, u32[]{:S(2)}) collective-permute-start(bf16[128,1024]{1,0:T(8,128)(2,1)} %get-tuple-element.27), channel_id=1, source_target_pairs={{0,128},{32,160},{64,192},{96,224},{128,0},{160,32},{192,64},{224,... | collective-permute-start | bytes 786440 | tf_op jit(solution)/shard_map/ppermute | solution.py:24
  76.4 90.5 %collective-permute-start.21 = (bf16[448,1024]{1,0:T(8,128)(2,1)}, bf16[448,1024]{1,0:T(8,128)(2,1)}, u32[]{:S(2)}, u32[]{:S(2)}) collective-permute-start(bf16[448,1024]{1,0:T(8,128)(2,1)} %bitcast_convert_fusion), channel_id=1, source_target_pairs={{0,16},{1,17},{2,18},{3,19},{4,20},{5,21},{6,22},{7,23},{8,24},{9,... | collective-permute-start | bytes 2752520 | tf_op jit(solution)/shard_map/ppermute | solution.py:29
  83.0 9.3 %copy-start.7 = (bf16[896,1024]{1,0:T(8,128)(2,1)S(1)}, bf16[896,1024]{1,0:T(8,128)(2,1)}, u32[]{:S(2)}) copy-start(bf16[896,1024]{1,0:T(8,128)(2,1)} %pad_maximum_fusion) | copy-start | bytes 5505028
  86.2 1.0 copy-start.8
  87.9 21.5 %collective-permute-start.14 = (bf16[128,1024]{1,0:T(8,128)(2,1)}, bf16[128,1024]{1,0:T(8,128)(2,1)}, u32[]{:S(2)}, u32[]{:S(2)}) collective-permute-start(bf16[128,1024]{1,0:T(8,128)(2,1)} %get-tuple-element.34), channel_id=1, source_target_pairs={{0,192},{32,224},{64,0},{96,32},{128,64},{160,96},{192,128},{224,1... | collective-permute-start | bytes 786440 | tf_op jit(solution)/shard_map/ppermute | solution.py:24
  91.2 18.3 %collective-permute-start.13 = (bf16[128,1024]{1,0:T(8,128)(2,1)S(1)}, bf16[128,1024]{1,0:T(8,128)(2,1)}, u32[]{:S(2)}, u32[]{:S(2)}) collective-permute-start(bf16[128,1024]{1,0:T(8,128)(2,1)S(1)} %get-tuple-element.35), channel_id=1, source_target_pairs={{0,64},{32,96},{64,128},{96,160},{128,192},{160,224},{192,0},{224,... | collective-permute-start | bytes 786440 | tf_op jit(solution)/shard_map/ppermute | solution.py:24
  91.2 18.3 %collective-permute-start.12 = (bf16[128,1024]{1,0:T(8,128)(2,1)S(1)}, bf16[128,1024]{1,0:T(8,128)(2,1)}, u32[]{:S(2)}, u32[]{:S(2)}) collective-permute-start(bf16[128,1024]{1,0:T(8,128)(2,1)S(1)} %get-tuple-element.33), channel_id=1, source_target_pairs={{0,128},{32,160},{64,192},{96,224},{128,0},{160,32},{192,64},{224,... | collective-permute-start | bytes 786440 | tf_op jit(solution)/shard_map/ppermute | solution.py:24
  95.8 41.8 %all-to-all-start.1 = ((bf16[32,16,896]{2,1,0:T(8,128)(2,1)}), bf16[32,16,896]{2,1,0:T(8,128)(2,1)}, u32[]{:S(2)}, u32[]{:S(2)}) async-start(bf16[32,16,896]{2,1,0:T(8,128)(2,1)} %bitcast.73), calls=%async_computation.1 | async-start | bytes 1835008 | tf_op jit(solution)/shard_map/all_to_all | solution.py:109
  111.0 2.2 %copy-start.3 = (f32[1,1024,448]{1,2,0:T(8,128)S(1)}, f32[1,1024,448]{1,2,0:T(8,128)}, u32[]{:S(2)}) copy-start(f32[1,1024,448]{1,2,0:T(8,128)} %param.20) | copy-start | bytes 5505028
  111.4 12.2 %collective-permute-start.15 = (bf16[128,2048]{1,0:T(8,128)(2,1)S(1)}, bf16[128,2048]{1,0:T(8,128)(2,1)S(1)}, u32[]{:S(2)}, u32[]{:S(2)}) collective-permute-start(bf16[128,2048]{1,0:T(8,128)(2,1)S(1)} %get-tuple-element.36), channel_id=1, source_target_pairs={{0,64},{32,96},{64,128},{96,160},{128,192},{160,224},{192,0},{224,... | collective-permute-start | bytes 1572872 | tf_op jit(solution)/shard_map/ppermute | solution.py:24
  114.3 52.6 %collective-permute-start.18 = (bf16[448,1024]{1,0:T(8,128)(2,1)}, bf16[448,1024]{1,0:T(8,128)(2,1)}, u32[]{:S(2)}, u32[]{:S(2)}) collective-permute-start(bf16[448,1024]{1,0:T(8,128)(2,1)} %bitcast_convert_fusion.1), channel_id=1, source_target_pairs={{0,16},{1,17},{2,18},{3,19},{4,20},{5,21},{6,22},{7,23},{8,24},{9,... | collective-permute-start | bytes 2752520 | tf_op jit(solution)/shard_map/ppermute | solution.py:29
  117.0 15.1 %collective-permute-start.16 = (bf16[128,2048]{1,0:T(8,128)(2,1)S(1)}, bf16[128,2048]{1,0:T(8,128)(2,1)S(1)}, u32[]{:S(2)}, u32[]{:S(2)}) collective-permute-start(bf16[128,2048]{1,0:T(8,128)(2,1)S(1)} %get-tuple-element.36), channel_id=1, source_target_pairs={{0,192},{32,224},{64,0},{96,32},{128,64},{160,96},{192,128},{224,1... | collective-permute-start | bytes 1572872 | tf_op jit(solution)/shard_map/ppermute | solution.py:24
  118.7 15.6 %collective-permute-start.17 = (bf16[128,2048]{1,0:T(8,128)(2,1)S(1)}, bf16[128,2048]{1,0:T(8,128)(2,1)S(1)}, u32[]{:S(2)}, u32[]{:S(2)}) collective-permute-start(bf16[128,2048]{1,0:T(8,128)(2,1)S(1)} %get-tuple-element.36), channel_id=1, source_target_pairs={{0,128},{32,160},{64,192},{96,224},{128,0},{160,32},{192,64},{224,... | collective-permute-start | bytes 1572872 | tf_op jit(solution)/shard_map/ppermute | solution.py:24
  122.5 9.7 %copy-start.1 = (f32[896,1024]{1,0:T(8,128)}, f32[896,1024]{1,0:T(8,128)S(1)}, u32[]{:S(2)}) copy-start(f32[896,1024]{1,0:T(8,128)S(1)} %fusion.33) | copy-start | bytes 11010052
  122.5 11.8 %copy-start.4 = (bf16[896,2048]{1,0:T(8,128)(2,1)S(1)}, bf16[896,2048]{1,0:T(8,128)(2,1)}, u32[]{:S(2)}) copy-start(bf16[896,2048]{1,0:T(8,128)(2,1)} %maximum_maximum_fusion) | copy-start | bytes 11010052
  123.6 22.7 %collective-permute-start.19 = (bf16[448,1024]{1,0:T(8,128)(2,1)}, bf16[448,1024]{1,0:T(8,128)(2,1)S(1)}, u32[]{:S(2)}, u32[]{:S(2)}) collective-permute-start(bf16[448,1024]{1,0:T(8,128)(2,1)} %slice.66), channel_id=1, source_target_pairs={{0,32},{32,0},{64,96},{96,64},{128,160},{160,128},{192,224},{224,1... | collective-permute-start | bytes 2752520 | tf_op jit(solution)/shard_map/ppermute | solution.py:19
  137.6 46.1 %all-to-all-start.3 = ((bf16[32,16,896]{2,1,0:T(8,128)(2,1)}), bf16[32,16,896]{2,1,0:T(8,128)(2,1)}, u32[]{:S(2)}, u32[]{:S(2)}) async-start(bf16[32,16,896]{2,1,0:T(8,128)(2,1)} %bitcast.72), calls=%async_computation.3 | async-start | bytes 1835008 | tf_op jit(solution)/shard_map/all_to_all | solution.py:109
  149.0 28.6 %collective-permute-start.20 = (bf16[448,1024]{1,0:T(8,128)(2,1)}, bf16[448,1024]{1,0:T(8,128)(2,1)}, u32[]{:S(2)}, u32[]{:S(2)}) collective-permute-start(bf16[448,1024]{1,0:T(8,128)(2,1)} %fusion.5), channel_id=1, source_target_pairs={{0,16},{1,17},{2,18},{3,19},{4,20},{5,21},{6,22},{7,23},{8,24},{9,... | collective-permute-start | bytes 2752520 | tf_op jit(solution)/shard_map/ppermute | solution.py:29
  153.5 10.4 %copy-start.15 = (s32[16]{0:T(128)S(1)}, s32[16]{0:T(128)}, u32[]{:S(2)}) copy-start(s32[16]{0:T(128)} %param.16) | copy-start | bytes 196
  155.3 0.9 copy-start.5
  156.3 8.9 %collective-permute-start.11 = (bf16[448,256]{1,0:T(8,128)(2,1)S(1)}, bf16[448,256]{1,0:T(8,128)(2,1)S(1)}, u32[]{:S(2)}, u32[]{:S(2)}) collective-permute-start(bf16[448,256]{1,0:T(8,128)(2,1)S(1)} %slice.68), channel_id=1, source_target_pairs={{0,32},{32,0},{64,96},{96,64},{128,160},{160,128},{192,224},{224,1... | collective-permute-start | bytes 688136 | tf_op jit(solution)/shard_map/ppermute | solution.py:19
  185.4 5.5 %collective-permute-start.22 = (bf16[448,256]{1,0:T(8,128)(2,1)S(1)}, bf16[448,256]{1,0:T(8,128)(2,1)S(1)}, u32[]{:S(2)}, u32[]{:S(2)}) collective-permute-start(bf16[448,256]{1,0:T(8,128)(2,1)S(1)} %slice.67), channel_id=1, source_target_pairs={{0,32},{32,0},{64,96},{96,64},{128,160},{160,128},{192,224},{224,1... | collective-permute-start | bytes 688136 | tf_op jit(solution)/shard_map/ppermute | solution.py:19

commit v3 on v2

--- a/solution.py
+++ b/solution.py
@@ -1,6 +1,8 @@
 import jax
 import jax.numpy as jnp
 from jax import lax
+from jax.experimental import pallas as pl
+from jax.experimental.pallas import tpu as pltpu
 from jax.sharding import PartitionSpec as P
 
 
@@ -35,6 +37,10 @@
 
 def tie(value, *others):
     return lax.optimization_barrier((value,) + others)[0]
+
+
+def tie_all(values, *others):
+    return lax.optimization_barrier(tuple(values) + others)[: len(values)]
 
 
 def scatter_sum(partial, y_pos, chips):
@@ -47,12 +53,15 @@
     return total
 
 
-def gather_rows(shard, y_pos, chips):
+def gather_rows(shard, y_pos, chips, after=()):
     rows = shard.shape[0]
-    full = jnp.zeros((chips * rows,) + shard.shape[1:], shard.dtype)
-    full = lax.dynamic_update_slice_in_dim(full, shard, y_pos * rows, 0)
+    full = jnp.broadcast_to(shard[None], (chips,) + shard.shape).reshape(-1, shard.shape[1])
+    pieces = []
     for step in (1, 3, 2):
         piece = chip_shift(shard, step)
+        pieces.append((step, piece))
+    held = tie_all([piece for _, piece in pieces], *after)
+    for (step, _), piece in zip(pieces, held):
         full = lax.dynamic_update_slice_in_dim(full, piece, ((y_pos - step) % chips) * rows, 0)
     return full
 
@@ -60,6 +69,38 @@
 def pair_rows(block):
     far = core_swap(block)
     return jnp.concatenate([block, far], axis=0)
+
+
+def join_weights(gate_own, up_own, gate_far, up_far):
+    rows, units = gate_own.shape
+    steps = 4
+    block = rows // steps
+
+    def body(gate_a, up_a, gate_b, up_b, out):
+        first = pl.program_id(0) < steps
+
+        @pl.when(first)
+        def _():
+            out[:, :units] = gate_a[...]
+            out[:, units:] = up_a[...]
+
+        @pl.when(jnp.logical_not(first))
+        def _():
+            out[:, :units] = gate_b[...]
+            out[:, units:] = up_b[...]
+
+    near = pl.BlockSpec((block, units), lambda i: (jnp.minimum(i, steps - 1), 0))
+    far = pl.BlockSpec((block, units), lambda i: (jnp.maximum(i - steps, 0), 0))
+    moved = 8 * rows * units
+    return pl.pallas_call(
+        body,
+        out_shape=jax.ShapeDtypeStruct((2 * rows, 2 * units), gate_own.dtype),
+        grid=(2 * steps,),
+        in_specs=[near, near, far, far],
+        out_specs=pl.BlockSpec((block, 2 * units), lambda i: (i, 0)),
+        compiler_params=pltpu.CompilerParams(vmem_limit_bytes=8 << 20),
+        cost_estimate=pl.CostEstimate(flops=0, bytes_accessed=2 * moved, transcendentals=0),
+    )(gate_own, up_own, gate_far, up_far)
 
 
 def pair_sum(partial):
@@ -85,7 +126,6 @@
     experts = slot_counts.shape[1]
     capacity = slot_tokens.shape[2]
     own_slots = capacity // 2
-    rows = experts * own_slots
     pair_cols = 2 * model_cols
     chips = lax.axis_size("dp") // 2
     dp_pos = lax.axis_index("dp")
@@ -105,46 +145,72 @@
     masked_route = jnp.where(live, route, -1)
     token_ids = jnp.arange(tok_count)
 
-    def exchange(block):
+    def exchange(block, slots):
         return lax.all_to_all(
-            block.reshape(experts, own_slots, pair_cols), "expert", 0, 0, tiled=True
-        ).reshape(rows, pair_cols)
+            block.reshape(experts, slots, pair_cols), "expert", 0, 0, tiled=True
+        ).reshape(experts * slots, pair_cols)
 
     token_cols = pair_rows(tokens.T)
+    part_slots = own_slots // 2
+    blocks = []
+    for part in range(2):
+        ids = masked_route.reshape(experts, own_slots)[:, part * part_slots :][:, :part_slots]
+        picked = (ids.reshape(-1)[:, None] == token_ids[None, :]).astype(BF)
+        blocks.append(dot(picked, token_cols, 1, 1).astype(BF))
     pick = (masked_route[:, None] == token_ids[None, :]).astype(BF)
-    arrived = exchange(dot(pick, token_cols, 1, 1).astype(BF))
     grad_cols = pair_rows(cotangent.T)
     grad_rows = (dot(pick, grad_cols, 1, 1) * weighted[:, None]).astype(BF)
-    gate_up = jnp.concatenate([pair_rows(gate_weight[0]), pair_rows(up_weight[0])], axis=1)
+    far_gate = core_swap(gate_weight[0])
+    far_up = core_swap(up_weight[0])
+    gate_up = join_weights(gate_weight[0], up_weight[0], far_gate, far_up)
     down_cols = pair_rows(down_weight[0].T)
+    arrived = [exchange(blocks[0], part_slots)]
+    later, gate_up, down_cols, grad_rows = lax.optimization_barrier(
+        (blocks[1], gate_up, down_cols, grad_rows)
+    )
+    arrived.append(exchange(later, part_slots))
     moment_one = first_moment[0].T
     moment_two = second_moment[0].T
-    gate_up, down_cols, grad_rows, arrived = lax.optimization_barrier(
-        (gate_up, down_cols, grad_rows, arrived)
-    )
-    arrived_grad = exchange(grad_rows)
-    far_one = expert_swap(moment_one.astype(BF))
-    far_two = expert_swap(moment_two.astype(BF))
-
-    preact = scatter_sum(dot(arrived, gate_up).astype(BF), y_pos, chips)
+    arrived_grad = exchange(grad_rows, own_slots)
+    far_one = expert_swap(tie(moment_one, arrived[0]).astype(BF))
+    far_two = expert_swap(tie(moment_two, arrived[0]).astype(BF))
+
     hidden_units = down_weight.shape[1]
-    gate_pre, up_pre = preact[:, :hidden_units], preact[:, hidden_units:]
-    sig = jax.nn.sigmoid(gate_pre)
-    hidden_shard = (gate_pre * sig * up_pre).astype(BF)
-    hidden = gather_rows(hidden_shard, y_pos, chips)
-    returned = exchange(dot(hidden, down_cols, 1, 1).astype(BF))
-
+    groups = experts // chips
+
+    def merge(parts):
+        split = [part.reshape(groups, 1, part_slots, -1) for part in parts]
+        return jnp.concatenate(split, axis=1).reshape(groups * own_slots, -1)
+
+    gates, hidden_parts = [], []
+    for x in arrived:
+        preact = scatter_sum(dot(x, gate_up).astype(BF), y_pos, chips)
+        gate_pre, up_pre = preact[:, :hidden_units], preact[:, hidden_units:]
+        sig = jax.nn.sigmoid(gate_pre)
+        gates.append((gate_pre, up_pre, sig))
+        hidden_parts.append((gate_pre * sig * up_pre).astype(BF))
+    hidden_shard = merge(hidden_parts)
     arrived_grad = tie(arrived_grad, hidden_shard)
-    hidden_part = tie(dot(arrived_grad, down_cols).astype(BF), hidden)
+    hidden_part = dot(arrived_grad, down_cols).astype(BF)
+    hidden = gather_rows(hidden_shard, y_pos, chips, (hidden_part,))
+    returned = exchange(dot(hidden, down_cols, 1, 1).astype(BF), own_slots)
+
+    hidden_part = tie(hidden_part, hidden)
     hidden_grad = scatter_sum(hidden_part, y_pos, chips)
-    gate_grad = hidden_grad * up_pre * sig * (1.0 + gate_pre * (1.0 - sig))
-    up_grad = hidden_grad * gate_pre * sig
-    pre_shard = jnp.concatenate([gate_grad, up_grad], axis=1).astype(BF)
-    pre_grad = gather_rows(pre_shard, y_pos, chips)
-    returned_grad = exchange(dot(pre_grad, gate_up, 1, 1).astype(BF))
-
+    grad_parts = []
+    for part, (gate_pre, up_pre, sig) in enumerate(gates):
+        grad = hidden_grad.reshape(groups, 2, part_slots, hidden_units)[:, part]
+        grad = grad.reshape(-1, hidden_units)
+        gate_grad = grad * up_pre * sig * (1.0 + gate_pre * (1.0 - sig))
+        up_grad = grad * gate_pre * sig
+        grad_parts.append(jnp.concatenate([gate_grad, up_grad], axis=1).astype(BF))
+    pre_shard = merge(grad_parts)
     weight_grad = pair_sum(dot(tie(arrived_grad, pre_shard), hidden, 0, 0))
-    far_grad = expert_swap(weight_grad.astype(BF))
+    sent_grad = weight_grad.astype(BF)
+    far_grad = expert_swap(sent_grad)
+    pre_grad = gather_rows(pre_shard, y_pos, chips, (sent_grad,))
+    returned_grad = exchange(dot(pre_grad, gate_up, 1, 1).astype(BF), own_slots)
+
     one = jnp.where(own_swap, far_one.astype(F32), moment_one)
     two = jnp.where(own_swap, far_two.astype(F32), moment_two)
     grad = jnp.where(own_swap, far_grad.astype(F32), weight_grad)

time: 193 us -> 249 us (1.29)
  waiting for transfers between devices: 31.6 us -> 99.8 us
  other arithmetic: 31.9 us -> 22.2 us
  starting transfers between devices: 89.1 us -> 81.4 us
  Pallas kernels: 0 us -> 3.23 us
    ppermute x3, waiting for transfers between devices: 10.7 us -> 57.1 us  [expert_swap(): lax.ppermute(block, 'expert', [(i, i ^ count // 2) for i in range(count)])]
    ppermute x12 -> x15, waiting for transfers between devices: 13 us -> 31.9 us  [chip_shift(): lax.ppermute(block, 'dp', [(i, (i + 2 * step) % count) for i in range(cou...]
    concatenate x2 -> x3, other arithmetic: 10.4 us -> 0.38 us  [the longest x1 0.32 us: shards(): grad_parts.append(jnp.concatenate([gate_grad, up_grad], axis=1).astype(BF))]
    ppermute x8, starting transfers between devices: 25.1 us -> 15.4 us  [core_swap(): lax.ppermute(block, 'dp', [(i, i ^ 1) for i in range(lax.axis_size('dp'))])]
    all_to_all x4 -> x5, waiting for transfers between devices: 2.22 us -> 9.64 us  [exchange(): lax.all_to_all(block.reshape(experts, slots, pair_cols), 'expert', 0, 0,...]
    ppermute x8, waiting for transfers between devices: 5.64 us -> 1.13 us  [core_swap(): lax.ppermute(block, 'dp', [(i, i ^ 1) for i in range(lax.axis_size('dp'))])]
    all_to_all x4 -> x5, starting transfers between devices: 40 us -> 43.8 us  [exchange(): lax.all_to_all(block.reshape(experts, slots, pair_cols), 'expert', 0, 0,...]
    pallas_call x0 -> x1, Pallas kernels: none -> 3.23 us  [join_weights(): pl.pallas_call(body, out_shape=jax.ShapeDtypeStruct((2 * rows, 2 * units)...]
  transfers between devices with their start and end apart: 27 -> 31, of which waited for: 11 -> 17; matrix products, arithmetic and copies ran while one was open for 29% -> 19% of each run, Pallas kernels for 0% -> 1%
where the time goes in v3:
time: 249 us; the launch traced here: 247 us
  waiting for transfers between devices  99.8 us (40%)
  starting transfers between devices  81.4 us (33%)
  matrix products  25.5 us (10%)
  other arithmetic  22.2 us (9%)
  local copies, waits for them, and re-layouts  13.2 us (5%)
  Pallas kernels  3.23 us (1%)
    ppermute x3, waiting for transfers between devices, expert_swap(): lax.ppermute(block, 'expert', [(i, i ^ count // 2) for i in range(count)])  57.1 us
    all_to_all x5, starting transfers between devices, exchange(): lax.all_to_all(block.reshape(experts, slots, pair_cols), 'expert', 0, 0,...  43.8 us
    ppermute x15, waiting for transfers between devices, chip_shift(): lax.ppermute(block, 'dp', [(i, (i + 2 * step) % count) for i in range(cou...  31.9 us
    dot_general x12, matrix products, dot(): lax.dot_general(a, b, (((ca,), (cb,)), ((), ())), preferred_element_type=...  25.5 us
    ppermute x15, starting transfers between devices, chip_shift(): lax.ppermute(block, 'dp', [(i, (i + 2 * step) % count) for i in range(cou...  16.6 us
    ppermute x8, starting transfers between devices, core_swap(): lax.ppermute(block, 'dp', [(i, i ^ 1) for i in range(lax.axis_size('dp'))])  15.4 us
    all_to_all x5, waiting for transfers between devices, exchange(): lax.all_to_all(block.reshape(experts, slots, pair_cols), 'expert', 0, 0,...  9.64 us
    unnamed x48, local copies, waits for them, and re-layouts  6.76 us
  transfers between devices with their start and end apart: 31, of which 17 were waited for; matrix products, arithmetic and copies ran while one was open for 19% of the time, Pallas kernels for 1%

profile of v3, /device:TPU:1, one launch (start us, length us, event | category | flops | bytes accessed | tf_op | source)
XLA Modules:
  0.0 247.3 jit_solution(16027854209269526612)
XLA Ops:
  0.7 3.3 %collective-permute-start = (bf16[448,256]{1,0:T(8,128)(2,1)}, bf16[448,256]{1,0:T(8,128)(2,1)S(1)}, u32[]{:S(2)}, u32[]{:S(2)}) collective-permute-start(bf16[448,256]{1,0:T(8,128)(2,1)} %bitcast.146), channel_id=1, source_target_pairs={{0,32},{32,0},{64,96},{96,64},{128,160},{160,128},{192,224},{224,1... | collective-permute-start | bytes 688136 | tf_op jit(solution)/shard_map/ppermute | solution.py:21
  7.6 2.1 fusion.1
  9.7 9.5 %all-to-all-start = ((bf16[32,8,896]{2,1,0:T(8,128)(2,1)}), bf16[32,8,896]{2,1,0:T(8,128)(2,1)S(1)}, u32[]{:S(2)}, u32[]{:S(2)}) async-start(bf16[32,8,896]{2,1,0:T(8,128)(2,1)} %fusion.1), calls=%async_computation | async-start | bytes 917504 | tf_op jit(solution)/shard_map/all_to_all | solution.py:149
  20.0 2.1 convolution_convert_fusion.5
  22.1 2.5 multiply_convert_fusion
  24.6 3.2 %shard_map.146 = bf16[896,2048]{1,0:T(8,128)(2,1)S(1)} custom-call(bf16[448,1024]{1,0:T(8,128)(2,1)S(1)} %bitcast.116, bf16[448,1024]{1,0:T(8,128)(2,1)S(1)} %bitcast.118, bf16[448,1024]{1,0:T(8,128)(2,1)S(1)} %collective-permute-done.1.gate_b, bf16[448,1024]{1,0:T(8,128)(2,1)} %collective-permute-done.2.up_b), custom_call_target="tpu_custom_call" | custom-call | bytes 7340032 | tf_op jit(solution)/shard_map/pallas_call | solution.py:95
  27.8 1.8 copy-done.1
  29.6 2.6 %pad_maximum_fusion = bf16[896,1024]{1,0:T(8,128)(2,1)} fusion(bf16[448,1024]{1,0:T(8,128)(2,1)} %collective-permute-done.3, bf16[448,1024]{1,0:T(8,128)(2,1)S(1)} %bitcast.139), kind=kLoop, calls=%fused_computation.6 | loop fusion | flops 3670016 | bytes 3670016 | tf_op jit(solution)/shard_map/concatenate | solution.py:71
  32.3 9.1 %all-to-all-start.1 = ((bf16[32,8,896]{2,1,0:T(8,128)(2,1)}), bf16[32,8,896]{2,1,0:T(8,128)(2,1)S(1)}, u32[]{:S(2)}, u32[]{:S(2)}) async-start(bf16[32,8,896]{2,1,0:T(8,128)(2,1)} %bitcast.14), calls=%async_computation.1 | async-start | bytes 917504 | tf_op jit(solution)/shard_map/all_to_all | solution.py:149
  41.6 3.3 %convolution_convert_fusion.1 = bf16[256,2048]{1,0:T(8,128)(2,1)S(1)} fusion(bf16[896,2048]{1,0:T(8,128)(2,1)} %copy-done.1, bf16[32,8,896]{2,1,0:T(8,128)(2,1)S(1)} %all-to-all-done), kind=kOutput, calls=%fused_computation.2 | convolution fusion | flops 940048384 | bytes 5177344 | tf_op jit(solution)/shard_map/dot_general | solution.py:17
  44.9 2.8 %collective-permute-start.7 = (bf16[64,2048]{1,0:T(8,128)(2,1)S(1)}, bf16[64,2048]{1,0:T(8,128)(2,1)S(1)}, u32[]{:S(2)}, u32[]{:S(2)}) collective-permute-start(bf16[64,2048]{1,0:T(8,128)(2,1)S(1)} %get-tuple-element.52), channel_id=1, source_target_pairs={{0,192},{32,224},{64,0},{96,32},{128,64},{160,96},{192,128},{224,1... | collective-permute-start | bytes 786440 | tf_op jit(solution)/shard_map/ppermute | solution.py:26
  47.8 1.6 collective-permute-start.5
  49.4 5.0 %all-to-all-done.1 = bf16[32,8,896]{2,1,0:T(8,128)(2,1)S(1)} async-done(((bf16[32,8,896]{2,1,0:T(8,128)(2,1)}), bf16[32,8,896]{2,1,0:T(8,128)(2,1)S(1)}, u32[]{:S(2)}, u32[]{:S(2)}) %all-to-all-start.1) | async-done | bytes 458784 | tf_op jit(solution)/shard_map/all_to_all | solution.py:149
  54.4 7.7 %all-to-all-start.2 = ((bf16[32,16,896]{2,1,0:T(8,128)(2,1)}), bf16[32,16,896]{2,1,0:T(8,128)(2,1)S(1)}, u32[]{:S(2)}, u32[]{:S(2)}) async-start(bf16[32,16,896]{2,1,0:T(8,128)(2,1)} %bitcast.20), calls=%async_computation.2 | async-start | bytes 1835008 | tf_op jit(solution)/shard_map/all_to_all | solution.py:149
  62.1 3.3 %convolution_convert_fusion = bf16[256,2048]{1,0:T(8,128)(2,1)S(1)} fusion(bf16[896,2048]{1,0:T(8,128)(2,1)} %copy-done.1, bf16[32,8,896]{2,1,0:T(8,128)(2,1)S(1)} %all-to-all-done.1), kind=kOutput, calls=%fused_computation.1 | convolution fusion | flops 940048384 | bytes 5177344 | tf_op jit(solution)/shard_map/dot_general | solution.py:17
  65.5 2.8 %collective-permute-start.10 = (bf16[64,2048]{1,0:T(8,128)(2,1)S(1)}, bf16[64,2048]{1,0:T(8,128)(2,1)S(1)}, u32[]{:S(2)}, u32[]{:S(2)}) collective-permute-start(bf16[64,2048]{1,0:T(8,128)(2,1)S(1)} %get-tuple-element.55), channel_id=1, source_target_pairs={{0,192},{32,224},{64,0},{96,32},{128,64},{160,96},{192,128},{224,1... | collective-permute-start | bytes 786440 | tf_op jit(solution)/shard_map/ppermute | solution.py:26
  68.3 1.6 collective-permute-start.8
  71.2 1.8 collective-permute-done.10
  73.0 3.8 %collective-permute-done.9 = bf16[64,2048]{1,0:T(8,128)(2,1)S(1)} collective-permute-done((bf16[64,2048]{1,0:T(8,128)(2,1)S(1)}, bf16[64,2048]{1,0:T(8,128)(2,1)S(1)}, u32[]{:S(2)}, u32[]{:S(2)}) %collective-permute-start.9) | collective-permute-done | bytes 262176 | tf_op jit(solution)/shard_map/ppermute | solution.py:26
  76.8 3.6 %collective-permute-done.8 = bf16[64,2048]{1,0:T(8,128)(2,1)S(1)} collective-permute-done((bf16[64,2048]{1,0:T(8,128)(2,1)S(1)}, bf16[64,2048]{1,0:T(8,128)(2,1)S(1)}, u32[]{:S(2)}, u32[]{:S(2)}) %collective-permute-start.8) | collective-permute-done | bytes 262176 | tf_op jit(solution)/shard_map/ppermute | solution.py:26
  80.7 2.7 %collective-permute-start.12 = (bf16[128,1024]{1,0:T(8,128)(2,1)S(1)}, bf16[128,1024]{1,0:T(8,128)(2,1)S(1)}, u32[]{:S(2)}, u32[]{:S(2)}) collective-permute-start(bf16[128,1024]{1,0:T(8,128)(2,1)S(1)} %bitcast.135), channel_id=1, source_target_pairs={{0,192},{32,224},{64,0},{96,32},{128,64},{160,96},{192,128},{224,1... | collective-permute-start | bytes 786440 | tf_op jit(solution)/shard_map/ppermute | solution.py:26
  84.2 2.7 %convolution_convert_fusion.2 = bf16[512,1024]{1,0:T(8,128)(2,1)S(1)} fusion(bf16[512,896]{1,0:T(8,128)(2,1)S(1)} %bitcast.121, bf16[896,1024]{1,0:T(8,128)(2,1)} %pad_maximum_fusion), kind=kOutput, calls=%fused_computation.11 | convolution fusion | flops 940048384 | bytes 3801088 | tf_op jit(solution)/shard_map/dot_general | solution.py:17
  87.4 2.2 collective-permute-done.12
  90.3 3.0 %collective-permute-done.13 = bf16[128,1024]{1,0:T(8,128)(2,1)} collective-permute-done((bf16[128,1024]{1,0:T(8,128)(2,1)S(1)}, bf16[128,1024]{1,0:T(8,128)(2,1)}, u32[]{:S(2)}, u32[]{:S(2)}) %collective-permute-start.13) | collective-permute-done | bytes 262176 | tf_op jit(solution)/shard_map/ppermute | solution.py:26
  98.1 3.6 %collective-permute-done.17 = bf16[128,1024]{1,0:T(8,128)(2,1)} collective-permute-done((bf16[128,1024]{1,0:T(8,128)(2,1)}, bf16[128,1024]{1,0:T(8,128)(2,1)}, u32[]{:S(2)}, u32[]{:S(2)}) %collective-permute-start.17) | collective-permute-done | bytes 262176 | tf_op jit(solution)/shard_map/ppermute | solution.py:26
  101.6 4.6 %collective-permute-done.16 = bf16[128,1024]{1,0:T(8,128)(2,1)} collective-permute-done((bf16[128,1024]{1,0:T(8,128)(2,1)S(1)}, bf16[128,1024]{1,0:T(8,128)(2,1)}, u32[]{:S(2)}, u32[]{:S(2)}) %collective-permute-start.16) | collective-permute-done | bytes 262176 | tf_op jit(solution)/shard_map/ppermute | solution.py:26
  106.2 1.3 convert_add_fusion
  109.1 1.8 copy-done.5
  112.0 6.9 %collective-permute-start.21 = (bf16[448,1024]{1,0:T(8,128)(2,1)}, bf16[448,1024]{1,0:T(8,128)(2,1)S(1)}, u32[]{:S(2)}, u32[]{:S(2)}) collective-permute-start(bf16[448,1024]{1,0:T(8,128)(2,1)} %slice.139), channel_id=1, source_target_pairs={{0,32},{32,0},{64,96},{96,64},{128,160},{160,128},{192,224},{224,1... | collective-permute-start | bytes 2752520 | tf_op jit(solution)/shard_map/ppermute | solution.py:21
  118.9 2.7 %collective-permute-start.19 = (bf16[128,2048]{1,0:T(8,128)(2,1)S(1)}, bf16[128,2048]{1,0:T(8,128)(2,1)}, u32[]{:S(2)}, u32[]{:S(2)}) collective-permute-start(bf16[128,2048]{1,0:T(8,128)(2,1)S(1)} %bitcast.128), channel_id=1, source_target_pairs={{0,192},{32,224},{64,0},{96,32},{128,64},{160,96},{192,128},{224,1... | collective-permute-start | bytes 1572872 | tf_op jit(solution)/shard_map/ppermute | solution.py:26
  121.6 2.2 convolution_convert_fusion.3
  123.8 9.1 %all-to-all-start.3 = ((bf16[32,16,896]{2,1,0:T(8,128)(2,1)}), bf16[32,16,896]{2,1,0:T(8,128)(2,1)S(1)}, u32[]{:S(2)}, u32[]{:S(2)}) async-start(bf16[32,16,896]{2,1,0:T(8,128)(2,1)} %bitcast.141), calls=%async_computation.3 | async-start | bytes 1835008 | tf_op jit(solution)/shard_map/all_to_all | solution.py:149
  133.0 3.1 %fusion.3 = bf16[448,1024]{1,0:T(8,128)(2,1)} fusion(bf16[448,1024]{1,0:T(8,128)(2,1)S(1)} %collective-permute-done.21, f32[896,1024]{1,0:T(8,128)} %copy-done.5), kind=kLoop, calls=%fused_computation.26 | loop fusion | flops 1376256 | bytes 3670016 | tf_op jit(solution)/shard_map/convert_element_type | solution.py:209
  136.0 8.8 %collective-permute-done.18 = bf16[128,2048]{1,0:T(8,128)(2,1)S(1)} collective-permute-done((bf16[128,2048]{1,0:T(8,128)(2,1)S(1)}, bf16[128,2048]{1,0:T(8,128)(2,1)S(1)}, u32[]{:S(2)}, u32[]{:S(2)}) %collective-permute-start.18) | collective-permute-done | bytes 524320 | tf_op jit(solution)/shard_map/ppermute | solution.py:26
  145.2 1.2 constant_dynamic-update-slice_fusion.1
  147.5 3.3 %convolution_convert_fusion.4 = bf16[512,896]{1,0:T(8,128)(2,1)} fusion(bf16[512,2048]{1,0:T(8,128)(2,1)S(1)} %constant_dynamic-update-slice_fusion, bf16[896,2048]{1,0:T(8,128)(2,1)S(1)} %copy-done.2), kind=kOutput, calls=%fused_computation.13 | convolution fusion | flops 1879506944 | bytes 6684672 | tf_op jit(solution)/shard_map/dot_general | solution.py:17
  150.9 4.0 %all-to-all-done.3 = bf16[32,16,896]{2,1,0:T(8,128)(2,1)S(1)} async-done(((bf16[32,16,896]{2,1,0:T(8,128)(2,1)}), bf16[32,16,896]{2,1,0:T(8,128)(2,1)S(1)}, u32[]{:S(2)}, u32[]{:S(2)}) %all-to-all-start.3) | async-done | bytes 917536 | tf_op jit(solution)/shard_map/all_to_all | solution.py:149
  154.9 8.4 %all-to-all-start.4 = ((bf16[32,16,896]{2,1,0:T(8,128)(2,1)}), bf16[32,16,896]{2,1,0:T(8,128)(2,1)}, u32[]{:S(2)}, u32[]{:S(2)}) async-start(bf16[32,16,896]{2,1,0:T(8,128)(2,1)} %bitcast.140), calls=%async_computation.4 | async-start | bytes 1835008 | tf_op jit(solution)/shard_map/all_to_all | solution.py:149
  164.4 2.7 %collective-permute-start.24 = (bf16[448,1024]{1,0:T(8,128)(2,1)}, bf16[448,1024]{1,0:T(8,128)(2,1)}, u32[]{:S(2)}, u32[]{:S(2)}) collective-permute-start(bf16[448,1024]{1,0:T(8,128)(2,1)} %convert_element_type.162), channel_id=1, source_target_pairs={{0,16},{1,17},{2,18},{3,19},{4,20},{5,21},{6,22},{7,23},{8,24},{9,... | collective-permute-start | bytes 2752520 | tf_op jit(solution)/shard_map/ppermute | solution.py:31
  168.9 2.2 collective-permute-start.23
  173.4 2.6 %collective-permute-start.14 = (bf16[448,256]{1,0:T(8,128)(2,1)S(1)}, bf16[448,256]{1,0:T(8,128)(2,1)S(1)}, u32[]{:S(2)}, u32[]{:S(2)}) collective-permute-start(bf16[448,256]{1,0:T(8,128)(2,1)S(1)} %slice.141), channel_id=1, source_target_pairs={{0,32},{32,0},{64,96},{96,64},{128,160},{160,128},{192,224},{224,1... | collective-permute-start | bytes 688136 | tf_op jit(solution)/shard_map/ppermute | solution.py:21
  177.3 1.8 fusion.5
  179.0 17.8 %collective-permute-done.24 = bf16[448,1024]{1,0:T(8,128)(2,1)} collective-permute-done((bf16[448,1024]{1,0:T(8,128)(2,1)}, bf16[448,1024]{1,0:T(8,128)(2,1)}, u32[]{:S(2)}, u32[]{:S(2)}) %collective-permute-start.24) | collective-permute-done | bytes 917536 | tf_op jit(solution)/shard_map/ppermute | solution.py:31
  196.8 19.7 %collective-permute-done.22 = bf16[448,1024]{1,0:T(8,128)(2,1)} collective-permute-done((bf16[448,1024]{1,0:T(8,128)(2,1)}, bf16[448,1024]{1,0:T(8,128)(2,1)}, u32[]{:S(2)}, u32[]{:S(2)}) %collective-permute-start.22) | collective-permute-done | bytes 917536 | tf_op jit(solution)/shard_map/ppermute | solution.py:31
  216.5 19.7 %collective-permute-done.23 = bf16[448,1024]{1,0:T(8,128)(2,1)} collective-permute-done((bf16[448,1024]{1,0:T(8,128)(2,1)}, bf16[448,1024]{1,0:T(8,128)(2,1)}, u32[]{:S(2)}, u32[]{:S(2)}) %collective-permute-start.23) | collective-permute-done | bytes 917536 | tf_op jit(solution)/shard_map/ppermute | solution.py:31
  236.2 6.1 %divide_convert_fusion = (bf16[448,1024]{1,0:T(8,128)(2,1)}, f32[448,1024]{1,0:T(8,128)}, f32[448,1024]{1,0:T(8,128)}) fusion(bf16[448,1024]{1,0:T(8,128)(2,1)S(1)} %copy-done.9, f32[896,1024]{1,0:T(8,128)} %copy-done.5, bf16[448,1024]{1,0:T(8,128)(2,1)} %collective-permute-done.23, f32[1,1024,448]{1,2,0:T(8,128)S(1)} %copy-done.6, ...), kind=kLoop, calls=%fused_computation.7 | loop fusion | flops 8257536 | bytes 13762561 | tf_op jit(solution)/shard_map/convert_element_type | solution.py:219
  242.2 1.7 fusion.2
  244.0 1.5 collective-permute-start.25
  (119 shorter events, 24.6 us)
Async XLA Ops:
  0.6 18.6 %copy-start = (f32[1,32,32]{2,1,0:T(8,128)S(1)}, f32[1,32,32]{2,1,0:T(8,128)}, u32[]{:S(2)}) copy-start(f32[1,32,32]{2,1,0:T(8,128)} %param.15) | copy-start | bytes 12292
  0.6 19.4 %copy-start.21 = (bf16[256,448]{0,1:T(8,128)(2,1)S(1)}, bf16[256,448]{0,1:T(8,128)(2,1)}, u32[]{:S(2)}) copy-start(bf16[256,448]{0,1:T(8,128)(2,1)} %param.11) | copy-start | bytes 688132
  0.7 6.3 %collective-permute-start = (bf16[448,256]{1,0:T(8,128)(2,1)}, bf16[448,256]{1,0:T(8,128)(2,1)S(1)}, u32[]{:S(2)}, u32[]{:S(2)}) collective-permute-start(bf16[448,256]{1,0:T(8,128)(2,1)} %bitcast.146), channel_id=1, source_target_pairs={{0,32},{32,0},{64,96},{96,64},{128,160},{160,128},{192,224},{224,1... | collective-permute-start | bytes 688136 | tf_op jit(solution)/shard_map/ppermute | solution.py:21
  3.9 20.6 %collective-permute-start.1 = (bf16[448,1024]{1,0:T(8,128)(2,1)}, bf16[448,1024]{1,0:T(8,128)(2,1)S(1)}, u32[]{:S(2)}, u32[]{:S(2)}) collective-permute-start(bf16[448,1024]{1,0:T(8,128)(2,1)} %bitcast.115), channel_id=1, source_target_pairs={{0,32},{32,0},{64,96},{96,64},{128,160},{160,128},{192,224},{224,1... | collective-permute-start | bytes 2752520 | tf_op jit(solution)/shard_map/ppermute | solution.py:21
  4.0 20.5 %collective-permute-start.2 = (bf16[448,1024]{1,0:T(8,128)(2,1)}, bf16[448,1024]{1,0:T(8,128)(2,1)}, u32[]{:S(2)}, u32[]{:S(2)}) collective-permute-start(bf16[448,1024]{1,0:T(8,128)(2,1)} %bitcast.117), channel_id=1, source_target_pairs={{0,32},{32,0},{64,96},{96,64},{128,160},{160,128},{192,224},{224,1... | collective-permute-start | bytes 2752520 | tf_op jit(solution)/shard_map/ppermute | solution.py:21
  4.5 25.1 %collective-permute-start.3 = (bf16[448,1024]{1,0:T(8,128)(2,1)}, bf16[448,1024]{1,0:T(8,128)(2,1)}, u32[]{:S(2)}, u32[]{:S(2)}) collective-permute-start(bf16[448,1024]{1,0:T(8,128)(2,1)} %bitcast.138), channel_id=1, source_target_pairs={{0,32},{32,0},{64,96},{96,64},{128,160},{160,128},{192,224},{224,1... | collective-permute-start | bytes 2752520 | tf_op jit(solution)/shard_map/ppermute | solution.py:21
  4.6 17.5 %collective-permute-start.4 = (bf16[448,256]{1,0:T(8,128)(2,1)}, bf16[448,256]{1,0:T(8,128)(2,1)}, u32[]{:S(2)}, u32[]{:S(2)}) collective-permute-start(bf16[448,256]{1,0:T(8,128)(2,1)} %bitcast.149), channel_id=1, source_target_pairs={{0,32},{32,0},{64,96},{96,64},{128,160},{160,128},{192,224},{224,1... | collective-permute-start | bytes 688136 | tf_op jit(solution)/shard_map/ppermute | solution.py:21
  6.9 17.6 %copy-start.18 = (s32[512]{0:T(512)}, s32[512]{0:T(512)S(1)}, u32[]{:S(2)}) copy-start(s32[512]{0:T(512)S(1)} %broadcast_select_fusion.1) | copy-start | bytes 6148
  9.7 14.8 %copy-start.3 = (bf16[1,448,1024]{2,1,0:T(8,128)(2,1)S(1)}, bf16[1,448,1024]{2,1,0:T(8,128)(2,1)}, u32[]{:S(2)}) copy-start(bf16[1,448,1024]{2,1,0:T(8,128)(2,1)} %param.17) | copy-start | bytes 2752516
  9.7 14.8 %copy-start.4 = (bf16[1,448,1024]{2,1,0:T(8,128)(2,1)S(1)}, bf16[1,448,1024]{2,1,0:T(8,128)(2,1)}, u32[]{:S(2)}) copy-start(bf16[1,448,1024]{2,1,0:T(8,128)(2,1)} %param.18) | copy-start | bytes 2752516
  9.7 22.6 %all-to-all-start = ((bf16[32,8,896]{2,1,0:T(8,128)(2,1)}), bf16[32,8,896]{2,1,0:T(8,128)(2,1)S(1)}, u32[]{:S(2)}, u32[]{:S(2)}) async-start(bf16[32,8,896]{2,1,0:T(8,128)(2,1)} %fusion.1), calls=%async_computation | async-start | bytes 917504 | tf_op jit(solution)/shard_map/all_to_all | solution.py:149
  20.0 7.8 %copy-start.16 = (f32[512]{0:T(512)}, f32[512]{0:T(512)S(1)}, u32[]{:S(2)}) copy-start(f32[512]{0:T(512)S(1)} %get-tuple-element.41) | copy-start | bytes 6148
  24.5 5.1 %copy-start.13 = (bf16[1,1024,448]{1,2,0:T(8,128)(2,1)S(1)}, bf16[1,1024,448]{1,2,0:T(8,128)(2,1)}, u32[]{:S(2)}) copy-start(bf16[1,1024,448]{1,2,0:T(8,128)(2,1)} %param.19) | copy-start | bytes 2752516
  32.3 22.1 %all-to-all-start.1 = ((bf16[32,8,896]{2,1,0:T(8,128)(2,1)}), bf16[32,8,896]{2,1,0:T(8,128)(2,1)S(1)}, u32[]{:S(2)}, u32[]{:S(2)}) async-start(bf16[32,8,896]{2,1,0:T(8,128)(2,1)} %bitcast.14), calls=%async_computation.1 | async-start | bytes 917504 | tf_op jit(solution)/shard_map/all_to_all | solution.py:149
  44.9 23.3 %collective-permute-start.7 = (bf16[64,2048]{1,0:T(8,128)(2,1)S(1)}, bf16[64,2048]{1,0:T(8,128)(2,1)S(1)}, u32[]{:S(2)}, u32[]{:S(2)}) collective-permute-start(bf16[64,2048]{1,0:T(8,128)(2,1)S(1)} %get-tuple-element.52), channel_id=1, source_target_pairs={{0,192},{32,224},{64,0},{96,32},{128,64},{160,96},{192,128},{224,1... | collective-permute-start | bytes 786440 | tf_op jit(solution)/shard_map/ppermute | solution.py:26
  47.7 22.2 %collective-permute-start.6 = (bf16[64,2048]{1,0:T(8,128)(2,1)S(1)}, bf16[64,2048]{1,0:T(8,128)(2,1)}, u32[]{:S(2)}, u32[]{:S(2)}) collective-permute-start(bf16[64,2048]{1,0:T(8,128)(2,1)S(1)} %get-tuple-element.53), channel_id=1, source_target_pairs={{0,64},{32,96},{64,128},{96,160},{128,192},{160,224},{192,0},{224,... | collective-permute-start | bytes 786440 | tf_op jit(solution)/shard_map/ppermute | solution.py:26
  47.8 22.2 %collective-permute-start.5 = (bf16[64,2048]{1,0:T(8,128)(2,1)S(1)}, bf16[64,2048]{1,0:T(8,128)(2,1)}, u32[]{:S(2)}, u32[]{:S(2)}) collective-permute-start(bf16[64,2048]{1,0:T(8,128)(2,1)S(1)} %get-tuple-element.51), channel_id=1, source_target_pairs={{0,128},{32,160},{64,192},{96,224},{128,0},{160,32},{192,64},{224,... | collective-permute-start | bytes 786440 | tf_op jit(solution)/shard_map/ppermute | solution.py:26
  54.4 29.8 %all-to-all-start.2 = ((bf16[32,16,896]{2,1,0:T(8,128)(2,1)}), bf16[32,16,896]{2,1,0:T(8,128)(2,1)S(1)}, u32[]{:S(2)}, u32[]{:S(2)}) async-start(bf16[32,16,896]{2,1,0:T(8,128)(2,1)} %bitcast.20), calls=%async_computation.2 | async-start | bytes 1835008 | tf_op jit(solution)/shard_map/all_to_all | solution.py:149
  65.5 7.5 %collective-permute-start.10 = (bf16[64,2048]{1,0:T(8,128)(2,1)S(1)}, bf16[64,2048]{1,0:T(8,128)(2,1)S(1)}, u32[]{:S(2)}, u32[]{:S(2)}) collective-permute-start(bf16[64,2048]{1,0:T(8,128)(2,1)S(1)} %get-tuple-element.55), channel_id=1, source_target_pairs={{0,192},{32,224},{64,0},{96,32},{128,64},{160,96},{192,128},{224,1... | collective-permute-start | bytes 786440 | tf_op jit(solution)/shard_map/ppermute | solution.py:26
  68.3 8.5 %collective-permute-start.9 = (bf16[64,2048]{1,0:T(8,128)(2,1)S(1)}, bf16[64,2048]{1,0:T(8,128)(2,1)S(1)}, u32[]{:S(2)}, u32[]{:S(2)}) collective-permute-start(bf16[64,2048]{1,0:T(8,128)(2,1)S(1)} %get-tuple-element.56), channel_id=1, source_target_pairs={{0,64},{32,96},{64,128},{96,160},{128,192},{160,224},{192,0},{224,... | collective-permute-start | bytes 786440 | tf_op jit(solution)/shard_map/ppermute | solution.py:26
  68.3 12.1 %collective-permute-start.8 = (bf16[64,2048]{1,0:T(8,128)(2,1)S(1)}, bf16[64,2048]{1,0:T(8,128)(2,1)S(1)}, u32[]{:S(2)}, u32[]{:S(2)}) collective-permute-start(bf16[64,2048]{1,0:T(8,128)(2,1)S(1)} %get-tuple-element.54), channel_id=1, source_target_pairs={{0,128},{32,160},{64,192},{96,224},{128,0},{160,32},{192,64},{224,... | collective-permute-start | bytes 786440 | tf_op jit(solution)/shard_map/ppermute | solution.py:26
  80.6 6.8 %collective-permute-start.11 = (bf16[128,1024]{1,0:T(8,128)(2,1)S(1)}, bf16[128,1024]{1,0:T(8,128)(2,1)S(1)}, u32[]{:S(2)}, u32[]{:S(2)}) collective-permute-start(bf16[128,1024]{1,0:T(8,128)(2,1)S(1)} %bitcast.134), channel_id=1, source_target_pairs={{0,64},{32,96},{64,128},{96,160},{128,192},{160,224},{192,0},{224,... | collective-permute-start | bytes 786440 | tf_op jit(solution)/shard_map/ppermute | solution.py:26
  80.7 8.9 %collective-permute-start.12 = (bf16[128,1024]{1,0:T(8,128)(2,1)S(1)}, bf16[128,1024]{1,0:T(8,128)(2,1)S(1)}, u32[]{:S(2)}, u32[]{:S(2)}) collective-permute-start(bf16[128,1024]{1,0:T(8,128)(2,1)S(1)} %bitcast.135), channel_id=1, source_target_pairs={{0,192},{32,224},{64,0},{96,32},{128,64},{160,96},{192,128},{224,1... | collective-permute-start | bytes 786440 | tf_op jit(solution)/shard_map/ppermute | solution.py:26
  83.4 10.0 %collective-permute-start.13 = (bf16[128,1024]{1,0:T(8,128)(2,1)S(1)}, bf16[128,1024]{1,0:T(8,128)(2,1)}, u32[]{:S(2)}, u32[]{:S(2)}) collective-permute-start(bf16[128,1024]{1,0:T(8,128)(2,1)S(1)} %bitcast.136), channel_id=1, source_target_pairs={{0,128},{32,160},{64,192},{96,224},{128,0},{160,32},{192,64},{224,... | collective-permute-start | bytes 786440 | tf_op jit(solution)/shard_map/ppermute | solution.py:26
  87.0 9.1 %copy-start.12 = (bf16[512,1024]{1,0:T(8,128)(2,1)}, bf16[512,1024]{1,0:T(8,128)(2,1)S(1)}, u32[]{:S(2)}) copy-start(bf16[512,1024]{1,0:T(8,128)(2,1)S(1)} %convolution_convert_fusion.2) | copy-start | bytes 3145732
  96.1 5.5 %collective-permute-start.17 = (bf16[128,1024]{1,0:T(8,128)(2,1)}, bf16[128,1024]{1,0:T(8,128)(2,1)}, u32[]{:S(2)}, u32[]{:S(2)}) collective-permute-start(bf16[128,1024]{1,0:T(8,128)(2,1)} %get-tuple-element.49), channel_id=1, source_target_pairs={{0,192},{32,224},{64,0},{96,32},{128,64},{160,96},{192,128},{224,1... | collective-permute-start | bytes 786440 | tf_op jit(solution)/shard_map/ppermute | solution.py:26
  96.9 9.3 %collective-permute-start.16 = (bf16[128,1024]{1,0:T(8,128)(2,1)S(1)}, bf16[128,1024]{1,0:T(8,128)(2,1)}, u32[]{:S(2)}, u32[]{:S(2)}) collective-permute-start(bf16[128,1024]{1,0:T(8,128)(2,1)S(1)} %get-tuple-element.50), channel_id=1, source_target_pairs={{0,64},{32,96},{64,128},{96,160},{128,192},{160,224},{192,0},{224,... | collective-permute-start | bytes 786440 | tf_op jit(solution)/shard_map/ppermute | solution.py:26
  97.6 8.7 %collective-permute-start.15 = (bf16[128,1024]{1,0:T(8,128)(2,1)S(1)}, bf16[128,1024]{1,0:T(8,128)(2,1)}, u32[]{:S(2)}, u32[]{:S(2)}) collective-permute-start(bf16[128,1024]{1,0:T(8,128)(2,1)S(1)} %get-tuple-element.48), channel_id=1, source_target_pairs={{0,128},{32,160},{64,192},{96,224},{128,0},{160,32},{192,64},{224,... | collective-permute-start | bytes 786440 | tf_op jit(solution)/shard_map/ppermute | solution.py:26
  110.9 10.7 %copy-start.11 = (bf16[896,1024]{1,0:T(8,128)(2,1)S(1)}, bf16[896,1024]{1,0:T(8,128)(2,1)}, u32[]{:S(2)}) copy-start(bf16[896,1024]{1,0:T(8,128)(2,1)} %pad_maximum_fusion) | copy-start | bytes 5505028
  112.0 21.0 %collective-permute-start.21 = (bf16[448,1024]{1,0:T(8,128)(2,1)}, bf16[448,1024]{1,0:T(8,128)(2,1)S(1)}, u32[]{:S(2)}, u32[]{:S(2)}) collective-permute-start(bf16[448,1024]{1,0:T(8,128)(2,1)} %slice.139), channel_id=1, source_target_pairs={{0,32},{32,0},{64,96},{96,64},{128,160},{160,128},{192,224},{224,1... | collective-permute-start | bytes 2752520 | tf_op jit(solution)/shard_map/ppermute | solution.py:21
  118.9 25.9 %collective-permute-start.18 = (bf16[128,2048]{1,0:T(8,128)(2,1)S(1)}, bf16[128,2048]{1,0:T(8,128)(2,1)S(1)}, u32[]{:S(2)}, u32[]{:S(2)}) collective-permute-start(bf16[128,2048]{1,0:T(8,128)(2,1)S(1)} %bitcast.127), channel_id=1, source_target_pairs={{0,64},{32,96},{64,128},{96,160},{128,192},{160,224},{192,0},{224,... | collective-permute-start | bytes 1572872 | tf_op jit(solution)/shard_map/ppermute | solution.py:26
  118.9 25.9 %collective-permute-start.19 = (bf16[128,2048]{1,0:T(8,128)(2,1)S(1)}, bf16[128,2048]{1,0:T(8,128)(2,1)}, u32[]{:S(2)}, u32[]{:S(2)}) collective-permute-start(bf16[128,2048]{1,0:T(8,128)(2,1)S(1)} %bitcast.128), channel_id=1, source_target_pairs={{0,192},{32,224},{64,0},{96,32},{128,64},{160,96},{192,128},{224,1... | collective-permute-start | bytes 1572872 | tf_op jit(solution)/shard_map/ppermute | solution.py:26
  121.6 23.3 %collective-permute-start.20 = (bf16[128,2048]{1,0:T(8,128)(2,1)S(1)}, bf16[128,2048]{1,0:T(8,128)(2,1)}, u32[]{:S(2)}, u32[]{:S(2)}) collective-permute-start(bf16[128,2048]{1,0:T(8,128)(2,1)S(1)} %bitcast.129), channel_id=1, source_target_pairs={{0,128},{32,160},{64,192},{96,224},{128,0},{160,32},{192,64},{224,... | collective-permute-start | bytes 1572872 | tf_op jit(solution)/shard_map/ppermute | solution.py:26
  123.8 31.1 %all-to-all-start.3 = ((bf16[32,16,896]{2,1,0:T(8,128)(2,1)}), bf16[32,16,896]{2,1,0:T(8,128)(2,1)S(1)}, u32[]{:S(2)}, u32[]{:S(2)}) async-start(bf16[32,16,896]{2,1,0:T(8,128)(2,1)} %bitcast.141), calls=%async_computation.3 | async-start | bytes 1835008 | tf_op jit(solution)/shard_map/all_to_all | solution.py:149
  133.0 3.1 %copy-start.8 = (bf16[448,1024]{1,0:T(8,128)(2,1)}, bf16[448,1024]{1,0:T(8,128)(2,1)S(1)}, u32[]{:S(2)}) copy-start(bf16[448,1024]{1,0:T(8,128)(2,1)S(1)} %collective-permute-done.21) | copy-start | bytes 2752516
  147.5 15.8 %copy-start.17 = (f32[512]{0:T(512)S(1)}, f32[512]{0:T(512)}, u32[]{:S(2)}) copy-start(f32[512]{0:T(512)} %copy-done.16) | copy-start | bytes 6148
  150.9 12.5 %copy-start.6 = (f32[1,1024,448]{1,2,0:T(8,128)S(1)}, f32[1,1024,448]{1,2,0:T(8,128)}, u32[]{:S(2)}) copy-start(f32[1,1024,448]{1,2,0:T(8,128)} %param.21) | copy-start | bytes 5505028
  154.9 87.3 %all-to-all-start.4 = ((bf16[32,16,896]{2,1,0:T(8,128)(2,1)}), bf16[32,16,896]{2,1,0:T(8,128)(2,1)}, u32[]{:S(2)}, u32[]{:S(2)}) async-start(bf16[32,16,896]{2,1,0:T(8,128)(2,1)} %bitcast.140), calls=%async_computation.4 | async-start | bytes 1835008 | tf_op jit(solution)/shard_map/all_to_all | solution.py:149
  163.3 3.8 %copy-start.7 = (f32[1,1024,448]{1,2,0:T(8,128)S(1)}, f32[1,1024,448]{1,2,0:T(8,128)}, u32[]{:S(2)}) copy-start(f32[1,1024,448]{1,2,0:T(8,128)} %param.20) | copy-start | bytes 5505028
  164.4 6.7 %copy-start.19 = (s32[512]{0:T(512)S(1)}, s32[512]{0:T(512)}, u32[]{:S(2)}) copy-start(s32[512]{0:T(512)} %copy-done.18) | copy-start | bytes 6148
  164.4 32.4 %collective-permute-start.24 = (bf16[448,1024]{1,0:T(8,128)(2,1)}, bf16[448,1024]{1,0:T(8,128)(2,1)}, u32[]{:S(2)}, u32[]{:S(2)}) collective-permute-start(bf16[448,1024]{1,0:T(8,128)(2,1)} %convert_element_type.162), channel_id=1, source_target_pairs={{0,16},{1,17},{2,18},{3,19},{4,20},{5,21},{6,22},{7,23},{8,24},{9,... | collective-permute-start | bytes 2752520 | tf_op jit(solution)/shard_map/ppermute | solution.py:31
  167.1 4.7 %copy-start.20 = (bf16[512]{0:T(512)(128)(2,1)S(1)}, bf16[512]{0:T(512)(128)(2,1)}, u32[]{:S(2)}) copy-start(bf16[512]{0:T(512)(128)(2,1)} %get-tuple-element.40) | copy-start | bytes 3076
  168.2 48.3 %collective-permute-start.22 = (bf16[448,1024]{1,0:T(8,128)(2,1)}, bf16[448,1024]{1,0:T(8,128)(2,1)}, u32[]{:S(2)}, u32[]{:S(2)}) collective-permute-start(bf16[448,1024]{1,0:T(8,128)(2,1)} %convert_element_type.159), channel_id=1, source_target_pairs={{0,16},{1,17},{2,18},{3,19},{4,20},{5,21},{6,22},{7,23},{8,24},{9,... | collective-permute-start | bytes 2752520 | tf_op jit(solution)/shard_map/ppermute | solution.py:31
  168.9 67.2 %collective-permute-start.23 = (bf16[448,1024]{1,0:T(8,128)(2,1)}, bf16[448,1024]{1,0:T(8,128)(2,1)}, u32[]{:S(2)}, u32[]{:S(2)}) collective-permute-start(bf16[448,1024]{1,0:T(8,128)(2,1)} %fusion.3), channel_id=1, source_target_pairs={{0,16},{1,17},{2,18},{3,19},{4,20},{5,21},{6,22},{7,23},{8,24},{9,... | collective-permute-start | bytes 2752520 | tf_op jit(solution)/shard_map/ppermute | solution.py:31
  171.8 4.2 %copy-start.23 = (s32[16]{0:T(128)S(1)}, s32[16]{0:T(128)}, u32[]{:S(2)}) copy-start(s32[16]{0:T(128)} %param.16) | copy-start | bytes 196
  173.3 62.8 %copy-start.9 = (bf16[448,1024]{1,0:T(8,128)(2,1)S(1)}, bf16[448,1024]{1,0:T(8,128)(2,1)}, u32[]{:S(2)}) copy-start(bf16[448,1024]{1,0:T(8,128)(2,1)} %copy-done.8) | copy-start | bytes 2752516
  173.4 3.9 %collective-permute-start.14 = (bf16[448,256]{1,0:T(8,128)(2,1)S(1)}, bf16[448,256]{1,0:T(8,128)(2,1)S(1)}, u32[]{:S(2)}, u32[]{:S(2)}) collective-permute-start(bf16[448,256]{1,0:T(8,128)(2,1)S(1)} %slice.141), channel_id=1, source_target_pairs={{0,32},{32,0},{64,96},{96,64},{128,160},{160,128},{192,224},{224,1... | collective-permute-start | bytes 688136 | tf_op jit(solution)/shard_map/ppermute | solution.py:21
  244.0 2.6 %collective-permute-start.25 = (bf16[448,256]{1,0:T(8,128)(2,1)S(1)}, bf16[448,256]{1,0:T(8,128)(2,1)S(1)}, u32[]{:S(2)}, u32[]{:S(2)}) collective-permute-start(bf16[448,256]{1,0:T(8,128)(2,1)S(1)} %slice.140), channel_id=1, source_target_pairs={{0,32},{32,0},{64,96},{96,64},{128,160},{160,128},{192,224},{224,1... | collective-permute-start | bytes 688136 | tf_op jit(solution)/shard_map/ppermute | solution.py:21
  (7 other events, 9.5 us)

commit v4 on v2

--- a/solution.py
+++ b/solution.py
@@ -1,6 +1,8 @@
 import jax
 import jax.numpy as jnp
 from jax import lax
+from jax.experimental import pallas as pl
+from jax.experimental.pallas import tpu as pltpu
 from jax.sharding import PartitionSpec as P
 
 
@@ -35,6 +37,10 @@
 
 def tie(value, *others):
     return lax.optimization_barrier((value,) + others)[0]
+
+
+def tie_all(values, *others):
+    return lax.optimization_barrier(tuple(values) + others)[: len(values)]
 
 
 def scatter_sum(partial, y_pos, chips):
@@ -47,19 +53,75 @@
     return total
 
 
-def gather_rows(shard, y_pos, chips):
+def ring_sum(partial, y_pos, chips):
+    rows = partial.shape[0] // (2 * chips)
+
+    def half(step, part):
+        return rows_at(partial, 2 * ((y_pos + step) % chips) + part, rows)
+
+    from_left = chip_shift(jnp.concatenate([half(2, 0), half(1, 1)]), 1)
+    from_right = chip_shift(jnp.concatenate([half(2, 1), half(3, 0)]), chips - 1)
+    on_right = (half(1, 0).astype(F32) + from_left[:rows].astype(F32)).astype(BF)
+    on_left = (half(3, 1).astype(F32) + from_right[:rows].astype(F32)).astype(BF)
+    on_right, on_left = lax.optimization_barrier((on_right, on_left))
+    far_left = chip_shift(on_right, 1)
+    far_right = chip_shift(on_left, chips - 1)
+    top = half(0, 0).astype(F32) + from_right[rows:].astype(F32) + far_left.astype(F32)
+    low = half(0, 1).astype(F32) + from_left[rows:].astype(F32) + far_right.astype(F32)
+    return jnp.concatenate([top, low])
+
+
+def ring_gather(shard, y_pos, chips, after=()):
     rows = shard.shape[0]
-    full = jnp.zeros((chips * rows,) + shard.shape[1:], shard.dtype)
-    full = lax.dynamic_update_slice_in_dim(full, shard, y_pos * rows, 0)
-    for step in (1, 3, 2):
-        piece = chip_shift(shard, step)
-        full = lax.dynamic_update_slice_in_dim(full, piece, ((y_pos - step) % chips) * rows, 0)
+    mid = rows // 2
+    left = chip_shift(shard, 1)
+    right = chip_shift(shard, chips - 1)
+    far_top = chip_shift(left[:mid], 1)
+    far_low = chip_shift(right[mid:], chips - 1)
+    full = jnp.broadcast_to(shard[None], (chips,) + shard.shape).reshape(-1, shard.shape[1])
+    pieces = tie_all([left, right, far_top, far_low], *after)
+    spots = ((3, 0), (1, 0), (2, 0), (2, mid))
+    for (step, offset), piece in zip(spots, pieces):
+        at = ((y_pos + step) % chips) * rows + offset
+        full = lax.dynamic_update_slice_in_dim(full, piece, at, 0)
     return full
 
 
 def pair_rows(block):
     far = core_swap(block)
     return jnp.concatenate([block, far], axis=0)
+
+
+def join_weights(gate_own, up_own, gate_far, up_far):
+    rows, units = gate_own.shape
+    steps = 4
+    block = rows // steps
+
+    def body(gate_a, up_a, gate_b, up_b, out):
+        first = pl.program_id(0) < steps
+
+        @pl.when(first)
+        def _():
+            out[:, :units] = gate_a[...]
+            out[:, units:] = up_a[...]
+
+        @pl.when(jnp.logical_not(first))
+        def _():
+            out[:, :units] = gate_b[...]
+            out[:, units:] = up_b[...]
+
+    near = pl.BlockSpec((block, units), lambda i: (jnp.minimum(i, steps - 1), 0))
+    far = pl.BlockSpec((block, units), lambda i: (jnp.maximum(i - steps, 0), 0))
+    moved = 8 * rows * units
+    return pl.pallas_call(
+        body,
+        out_shape=jax.ShapeDtypeStruct((2 * rows, 2 * units), gate_own.dtype),
+        grid=(2 * steps,),
+        in_specs=[near, near, far, far],
+        out_specs=pl.BlockSpec((block, 2 * units), lambda i: (i, 0)),
+        compiler_params=pltpu.CompilerParams(vmem_limit_bytes=8 << 20),
+        cost_estimate=pl.CostEstimate(flops=0, bytes_accessed=2 * moved, transcendentals=0),
+    )(gate_own, up_own, gate_far, up_far)
 
 
 def pair_sum(partial):
@@ -115,36 +177,41 @@
     arrived = exchange(dot(pick, token_cols, 1, 1).astype(BF))
     grad_cols = pair_rows(cotangent.T)
     grad_rows = (dot(pick, grad_cols, 1, 1) * weighted[:, None]).astype(BF)
-    gate_up = jnp.concatenate([pair_rows(gate_weight[0]), pair_rows(up_weight[0])], axis=1)
+    far_gate = core_swap(gate_weight[0])
+    far_up = core_swap(up_weight[0])
+    gate_up = join_weights(gate_weight[0], up_weight[0], far_gate, far_up)
     down_cols = pair_rows(down_weight[0].T)
+    arrived, gate_up, down_cols, grad_rows = lax.optimization_barrier(
+        (arrived, gate_up, down_cols, grad_rows)
+    )
     moment_one = first_moment[0].T
     moment_two = second_moment[0].T
-    gate_up, down_cols, grad_rows, arrived = lax.optimization_barrier(
-        (gate_up, down_cols, grad_rows, arrived)
-    )
     arrived_grad = exchange(grad_rows)
-    far_one = expert_swap(moment_one.astype(BF))
-    far_two = expert_swap(moment_two.astype(BF))
-
-    preact = scatter_sum(dot(arrived, gate_up).astype(BF), y_pos, chips)
+    far_one = expert_swap(tie(moment_one, arrived).astype(BF))
+    far_two = expert_swap(tie(moment_two, arrived).astype(BF))
+
     hidden_units = down_weight.shape[1]
+    preact = ring_sum(dot(arrived, gate_up).astype(BF), y_pos, chips)
     gate_pre, up_pre = preact[:, :hidden_units], preact[:, hidden_units:]
     sig = jax.nn.sigmoid(gate_pre)
     hidden_shard = (gate_pre * sig * up_pre).astype(BF)
-    hidden = gather_rows(hidden_shard, y_pos, chips)
-    returned = exchange(dot(hidden, down_cols, 1, 1).astype(BF))
-
-    arrived_grad = tie(arrived_grad, hidden_shard)
-    hidden_part = tie(dot(arrived_grad, down_cols).astype(BF), hidden)
+    hidden = ring_gather(hidden_shard, y_pos, chips)
+    out_rows, arrived_grad = lax.optimization_barrier(
+        (dot(hidden, down_cols, 1, 1).astype(BF), arrived_grad)
+    )
+    returned = exchange(out_rows)
+
+    hidden_part = dot(arrived_grad, down_cols).astype(BF)
     hidden_grad = scatter_sum(hidden_part, y_pos, chips)
     gate_grad = hidden_grad * up_pre * sig * (1.0 + gate_pre * (1.0 - sig))
     up_grad = hidden_grad * gate_pre * sig
     pre_shard = jnp.concatenate([gate_grad, up_grad], axis=1).astype(BF)
-    pre_grad = gather_rows(pre_shard, y_pos, chips)
+    weight_grad = pair_sum(dot(tie(arrived_grad, pre_shard), hidden, 0, 0))
+    sent_grad = weight_grad.astype(BF)
+    far_grad = expert_swap(sent_grad)
+    pre_grad = ring_gather(pre_shard, y_pos, chips, (sent_grad,))
     returned_grad = exchange(dot(pre_grad, gate_up, 1, 1).astype(BF))
 
-    weight_grad = pair_sum(dot(tie(arrived_grad, pre_shard), hidden, 0, 0))
-    far_grad = expert_swap(weight_grad.astype(BF))
     one = jnp.where(own_swap, far_one.astype(F32), moment_one)
     two = jnp.where(own_swap, far_two.astype(F32), moment_two)
     grad = jnp.where(own_swap, far_grad.astype(F32), weight_grad)

time: 193 us -> 249 us (1.29)
  waiting for transfers between devices: 31.6 us -> 106 us
  starting transfers between devices: 89.1 us -> 77.5 us
  other arithmetic: 31.9 us -> 24.1 us
  matrix products: 26.2 us -> 20.8 us
  Pallas kernels: 0 us -> 3.23 us
  local copies, waits for them, and re-layouts: 11.2 us -> 13.9 us
    ppermute x3, waiting for transfers between devices: 10.7 us -> 57.1 us  [expert_swap(): lax.ppermute(block, 'expert', [(i, i ^ count // 2) for i in range(count)])]
    ppermute x12 -> x15, waiting for transfers between devices: 13 us -> 29.3 us  [chip_shift(): lax.ppermute(block, 'dp', [(i, (i + 2 * step) % count) for i in range(cou...]
    all_to_all x4, waiting for transfers between devices: 2.22 us -> 14.9 us  [exchange(): lax.all_to_all(block.reshape(experts, own_slots, pair_cols), 'expert', 0,...]
    ppermute x8, starting transfers between devices: 25.1 us -> 15.2 us  [core_swap(): lax.ppermute(block, 'dp', [(i, i ^ 1) for i in range(lax.axis_size('dp'))])]
    concatenate x1 -> x2, other arithmetic: 10.3 us -> 1.84 us  [the longest x1 0.97 us: ring_sum(): jnp.concatenate([half(2, 1), half(3, 0)])]
    dot_general x10, matrix products: 26.2 us -> 20.8 us  [dot(): lax.dot_general(a, b, (((ca,), (cb,)), ((), ())), preferred_element_type=...]
    pallas_call x0 -> x1, Pallas kernels: none -> 3.23 us  [join_weights(): pl.pallas_call(body, out_shape=jax.ShapeDtypeStruct((2 * rows, 2 * units)...]
    unnamed x32 -> x52, local copies, waits for them, and re-layouts: 4.09 us -> 6.79 us
  transfers between devices with their start and end apart: 27 -> 30, of which waited for: 11 -> 18; matrix products, arithmetic and copies ran while one was open for 29% -> 13% of each run, Pallas kernels for 0% -> 1%
where the time goes in v4:
time: 249 us; the launch traced here: 248 us
  waiting for transfers between devices  106 us (43%)
  starting transfers between devices  77.5 us (31%)
  other arithmetic  24.1 us (10%)
  matrix products  20.8 us (8%)
  local copies, waits for them, and re-layouts  13.9 us (6%)
  Pallas kernels  3.23 us (1%)
    ppermute x3, waiting for transfers between devices, expert_swap(): lax.ppermute(block, 'expert', [(i, i ^ count // 2) for i in range(count)])  57.1 us
    all_to_all x4, starting transfers between devices, exchange(): lax.all_to_all(block.reshape(experts, own_slots, pair_cols), 'expert', 0,...  38.3 us
    ppermute x15, waiting for transfers between devices, chip_shift(): lax.ppermute(block, 'dp', [(i, (i + 2 * step) % count) for i in range(cou...  29.3 us
    dot_general x10, matrix products, dot(): lax.dot_general(a, b, (((ca,), (cb,)), ((), ())), preferred_element_type=...  20.8 us
    ppermute x15, starting transfers between devices, chip_shift(): lax.ppermute(block, 'dp', [(i, (i + 2 * step) % count) for i in range(cou...  18.3 us
    ppermute x8, starting transfers between devices, core_swap(): lax.ppermute(block, 'dp', [(i, i ^ 1) for i in range(lax.axis_size('dp'))])  15.2 us
    all_to_all x4, waiting for transfers between devices, exchange(): lax.all_to_all(block.reshape(experts, own_slots, pair_cols), 'expert', 0,...  14.9 us
    unnamed x52, local copies, waits for them, and re-layouts  6.79 us
  transfers between devices with their start and end apart: 30, of which 18 were waited for; matrix products, arithmetic and copies ran while one was open for 13% of the time, Pallas kernels for 1%

profile of v4, /device:TPU:1, one launch (start us, length us, event | category | flops | bytes accessed | tf_op | source)
XLA Modules:
  0.0 247.7 jit_solution(9509900734640752792)
XLA Ops:
  0.7 3.3 %collective-permute-start = (bf16[448,256]{1,0:T(8,128)(2,1)}, bf16[448,256]{1,0:T(8,128)(2,1)S(1)}, u32[]{:S(2)}, u32[]{:S(2)}) collective-permute-start(bf16[448,256]{1,0:T(8,128)(2,1)} %bitcast.76), channel_id=1, source_target_pairs={{0,32},{32,0},{64,96},{96,64},{128,160},{160,128},{192,224},{224,1... | collective-permute-start | bytes 688136 | tf_op jit(solution)/shard_map/ppermute | solution.py:21
  5.3 2.3 convolution_convert_fusion.2
  7.6 9.4 %all-to-all-start = ((bf16[32,16,896]{2,1,0:T(8,128)(2,1)}), bf16[32,16,896]{2,1,0:T(8,128)(2,1)}, u32[]{:S(2)}, u32[]{:S(2)}) async-start(bf16[32,16,896]{2,1,0:T(8,128)(2,1)} %bitcast.3), calls=%async_computation | async-start | bytes 1835008 | tf_op jit(solution)/shard_map/all_to_all | solution.py:171
  19.2 3.7 %collective-permute-done.4 = bf16[448,256]{1,0:T(8,128)(2,1)S(1)} collective-permute-done((bf16[448,256]{1,0:T(8,128)(2,1)S(1)}, bf16[448,256]{1,0:T(8,128)(2,1)S(1)}, u32[]{:S(2)}, u32[]{:S(2)}) %collective-permute-start.4) | collective-permute-done | bytes 229408 | tf_op jit(solution)/shard_map/ppermute | solution.py:21
  22.9 1.4 multiply_convert_fusion
  24.3 3.2 %shard_map.146 = bf16[896,2048]{1,0:T(8,128)(2,1)S(1)} custom-call(bf16[448,1024]{1,0:T(8,128)(2,1)S(1)} %bitcast.56, bf16[448,1024]{1,0:T(8,128)(2,1)S(1)} %bitcast.58, bf16[448,1024]{1,0:T(8,128)(2,1)S(1)} %collective-permute-done.1.gate_b, bf16[448,1024]{1,0:T(8,128)(2,1)} %collective-permute-done.2.up_b), custom_call_target="tpu_custom_call" | custom-call | bytes 7340032 | tf_op jit(solution)/shard_map/pallas_call | solution.py:116
  27.6 1.8 copy-done.1
  29.4 2.6 %pad_maximum_fusion = bf16[896,1024]{1,0:T(8,128)(2,1)} fusion(bf16[448,1024]{1,0:T(8,128)(2,1)} %collective-permute-done.3, bf16[448,1024]{1,0:T(8,128)(2,1)S(1)} %bitcast.70), kind=kLoop, calls=%fused_computation.5 | loop fusion | flops 3670016 | bytes 3670016 | tf_op jit(solution)/shard_map/concatenate | solution.py:92
  31.9 7.5 %all-to-all-done = bf16[32,16,896]{2,1,0:T(8,128)(2,1)} async-done(((bf16[32,16,896]{2,1,0:T(8,128)(2,1)}), bf16[32,16,896]{2,1,0:T(8,128)(2,1)}, u32[]{:S(2)}, u32[]{:S(2)}) %all-to-all-start) | async-done | bytes 917536 | tf_op jit(solution)/shard_map/all_to_all | solution.py:171
  39.4 4.7 %convolution_convert_fusion = bf16[512,2048]{1,0:T(8,128)(2,1)S(1)} fusion(bf16[512,896]{1,0:T(8,128)(2,1)} %bitcast.4, bf16[896,2048]{1,0:T(8,128)(2,1)} %copy-done.1), kind=kOutput, calls=%fused_computation | convolution fusion | flops 1880096768 | bytes 6684672 | tf_op jit(solution)/shard_map/dot_general | solution.py:17
  45.1 2.7 %collective-permute-start.5 = (bf16[128,2048]{1,0:T(8,128)(2,1)}, bf16[128,2048]{1,0:T(8,128)(2,1)S(1)}, u32[]{:S(2)}, u32[]{:S(2)}) collective-permute-start(bf16[128,2048]{1,0:T(8,128)(2,1)} %pad_maximum_fusion.2), channel_id=1, source_target_pairs={{0,192},{32,224},{64,0},{96,32},{128,64},{160,96},{192,128},{224,1... | collective-permute-start | bytes 1572872 | tf_op jit(solution)/shard_map/ppermute | solution.py:26
  48.7 6.2 %collective-permute-done.5 = bf16[128,2048]{1,0:T(8,128)(2,1)S(1)} collective-permute-done((bf16[128,2048]{1,0:T(8,128)(2,1)}, bf16[128,2048]{1,0:T(8,128)(2,1)S(1)}, u32[]{:S(2)}, u32[]{:S(2)}) %collective-permute-start.5) | collective-permute-done | bytes 524320 | tf_op jit(solution)/shard_map/ppermute | solution.py:26
  54.9 3.9 %collective-permute-done.6 = bf16[128,2048]{1,0:T(8,128)(2,1)S(1)} collective-permute-done((bf16[128,2048]{1,0:T(8,128)(2,1)}, bf16[128,2048]{1,0:T(8,128)(2,1)S(1)}, u32[]{:S(2)}, u32[]{:S(2)}) %collective-permute-start.6) | collective-permute-done | bytes 524320 | tf_op jit(solution)/shard_map/ppermute | solution.py:26
  59.7 2.7 %collective-permute-start.8 = (bf16[64,2048]{1,0:T(8,128)(2,1)}, bf16[64,2048]{1,0:T(8,128)(2,1)}, u32[]{:S(2)}, u32[]{:S(2)}) collective-permute-start(bf16[64,2048]{1,0:T(8,128)(2,1)} %get-tuple-element.28), channel_id=1, source_target_pairs={{0,192},{32,224},{64,0},{96,32},{128,64},{160,96},{192,128},{224,1... | collective-permute-start | bytes 786440 | tf_op jit(solution)/shard_map/ppermute | solution.py:26
  62.4 12.2 %all-to-all-start.1 = ((bf16[32,16,896]{2,1,0:T(8,128)(2,1)}), bf16[32,16,896]{2,1,0:T(8,128)(2,1)S(1)}, u32[]{:S(2)}, u32[]{:S(2)}) async-start(bf16[32,16,896]{2,1,0:T(8,128)(2,1)} %bitcast.12), calls=%async_computation.1 | async-start | bytes 1835008 | tf_op jit(solution)/shard_map/all_to_all | solution.py:171
  74.6 1.3 convert_add_fusion.2
  76.2 2.7 %collective-permute-start.10 = (bf16[128,1024]{1,0:T(8,128)(2,1)S(1)}, bf16[128,1024]{1,0:T(8,128)(2,1)S(1)}, u32[]{:S(2)}, u32[]{:S(2)}) collective-permute-start(bf16[128,1024]{1,0:T(8,128)(2,1)S(1)} %multiply_convert_fusion.3), channel_id=1, source_target_pairs={{0,192},{32,224},{64,0},{96,32},{128,64},{160,96},{192,128},{224,1... | collective-permute-start | bytes 786440 | tf_op jit(solution)/shard_map/ppermute | solution.py:26
  78.8 3.8 %collective-permute-done.9 = bf16[128,1024]{1,0:T(8,128)(2,1)S(1)} collective-permute-done((bf16[128,1024]{1,0:T(8,128)(2,1)S(1)}, bf16[128,1024]{1,0:T(8,128)(2,1)S(1)}, u32[]{:S(2)}, u32[]{:S(2)}) %collective-permute-start.9) | collective-permute-done | bytes 262176 | tf_op jit(solution)/shard_map/ppermute | solution.py:26
  82.7 2.9 %collective-permute-start.12 = (bf16[64,1024]{1,0:T(8,128)(2,1)S(1)}, bf16[64,1024]{1,0:T(8,128)(2,1)}, u32[]{:S(2)}, u32[]{:S(2)}) collective-permute-start(bf16[64,1024]{1,0:T(8,128)(2,1)S(1)} %slice.74), channel_id=1, source_target_pairs={{0,192},{32,224},{64,0},{96,32},{128,64},{160,96},{192,128},{224,1... | collective-permute-start | bytes 393224 | tf_op jit(solution)/shard_map/ppermute | solution.py:26
  85.7 2.3 collective-permute-done.11
  90.8 2.2 convolution_convert_fusion.3
  93.0 3.1 %all-to-all-done.1 = bf16[32,16,896]{2,1,0:T(8,128)(2,1)S(1)} async-done(((bf16[32,16,896]{2,1,0:T(8,128)(2,1)}), bf16[32,16,896]{2,1,0:T(8,128)(2,1)S(1)}, u32[]{:S(2)}, u32[]{:S(2)}) %all-to-all-start.1) | async-done | bytes 917536 | tf_op jit(solution)/shard_map/all_to_all | solution.py:171
  96.1 2.7 %convolution_convert_fusion.1 = bf16[512,1024]{1,0:T(8,128)(2,1)S(1)} fusion(bf16[512,896]{1,0:T(8,128)(2,1)S(1)} %bitcast.61, bf16[896,1024]{1,0:T(8,128)(2,1)} %pad_maximum_fusion), kind=kOutput, calls=%fused_computation.10 | convolution fusion | flops 940048384 | bytes 3801088 | tf_op jit(solution)/shard_map/dot_general | solution.py:17
  100.7 1.4 collective-permute-start.15
  102.0 4.1 %collective-permute-done.16 = bf16[128,1024]{1,0:T(8,128)(2,1)} collective-permute-done((bf16[128,1024]{1,0:T(8,128)(2,1)}, bf16[128,1024]{1,0:T(8,128)(2,1)}, u32[]{:S(2)}, u32[]{:S(2)}) %collective-permute-start.16) | collective-permute-done | bytes 262176 | tf_op jit(solution)/shard_map/ppermute | solution.py:26
  106.1 3.9 %collective-permute-done.15 = bf16[128,1024]{1,0:T(8,128)(2,1)} collective-permute-done((bf16[128,1024]{1,0:T(8,128)(2,1)S(1)}, bf16[128,1024]{1,0:T(8,128)(2,1)}, u32[]{:S(2)}, u32[]{:S(2)}) %collective-permute-start.15) | collective-permute-done | bytes 262176 | tf_op jit(solution)/shard_map/ppermute | solution.py:26
  110.0 1.5 multiply_convert_fusion.2
  112.8 1.8 copy-done.5
  115.6 6.4 %collective-permute-start.21 = (bf16[448,1024]{1,0:T(8,128)(2,1)}, bf16[448,1024]{1,0:T(8,128)(2,1)S(1)}, u32[]{:S(2)}, u32[]{:S(2)}) collective-permute-start(bf16[448,1024]{1,0:T(8,128)(2,1)} %slice.123), channel_id=1, source_target_pairs={{0,32},{32,0},{64,96},{96,64},{128,160},{160,128},{192,224},{224,1... | collective-permute-start | bytes 2752520 | tf_op jit(solution)/shard_map/ppermute | solution.py:21
  122.1 2.7 %collective-permute-start.18 = (bf16[128,2048]{1,0:T(8,128)(2,1)S(1)}, bf16[128,2048]{1,0:T(8,128)(2,1)}, u32[]{:S(2)}, u32[]{:S(2)}) collective-permute-start(bf16[128,2048]{1,0:T(8,128)(2,1)S(1)} %pad_maximum_fusion.4), channel_id=1, source_target_pairs={{0,192},{32,224},{64,0},{96,32},{128,64},{160,96},{192,128},{224,1... | collective-permute-start | bytes 1572872 | tf_op jit(solution)/shard_map/ppermute | solution.py:26
  124.7 8.3 %all-to-all-start.2 = ((bf16[32,16,896]{2,1,0:T(8,128)(2,1)}), bf16[32,16,896]{2,1,0:T(8,128)(2,1)S(1)}, u32[]{:S(2)}, u32[]{:S(2)}) async-start(bf16[32,16,896]{2,1,0:T(8,128)(2,1)} %bitcast.71), calls=%async_computation.2 | async-start | bytes 1835008 | tf_op jit(solution)/shard_map/all_to_all | solution.py:171
  133.1 3.7 %collective-permute-done.17 = bf16[128,2048]{1,0:T(8,128)(2,1)S(1)} collective-permute-done((bf16[128,2048]{1,0:T(8,128)(2,1)S(1)}, bf16[128,2048]{1,0:T(8,128)(2,1)S(1)}, u32[]{:S(2)}, u32[]{:S(2)}) %collective-permute-start.17) | collective-permute-done | bytes 524320 | tf_op jit(solution)/shard_map/ppermute | solution.py:26
  137.9 3.0 %collective-permute-start.20 = (bf16[64,2048]{1,0:T(8,128)(2,1)S(1)}, bf16[64,2048]{1,0:T(8,128)(2,1)S(1)}, u32[]{:S(2)}, u32[]{:S(2)}) collective-permute-start(bf16[64,2048]{1,0:T(8,128)(2,1)S(1)} %slice.78), channel_id=1, source_target_pairs={{0,192},{32,224},{64,0},{96,32},{128,64},{160,96},{192,128},{224,1... | collective-permute-start | bytes 786440 | tf_op jit(solution)/shard_map/ppermute | solution.py:26
  140.8 3.1 %fusion.3 = bf16[448,1024]{1,0:T(8,128)(2,1)} fusion(bf16[448,1024]{1,0:T(8,128)(2,1)S(1)} %collective-permute-done.21, f32[896,1024]{1,0:T(8,128)} %copy-done.5), kind=kLoop, calls=%fused_computation.35 | loop fusion | flops 1376256 | bytes 3670016 | tf_op jit(solution)/shard_map/convert_element_type | solution.py:210
  145.6 1.2 constant_dynamic-update-slice_fusion.2
  147.5 3.3 %convolution_convert_fusion.4 = bf16[512,896]{1,0:T(8,128)(2,1)} fusion(bf16[512,2048]{1,0:T(8,128)(2,1)S(1)} %constant_dynamic-update-slice_fusion, bf16[896,2048]{1,0:T(8,128)(2,1)S(1)} %copy-done.2), kind=kOutput, calls=%fused_computation.13 | convolution fusion | flops 1879506944 | bytes 6684672 | tf_op jit(solution)/shard_map/dot_general | solution.py:17
  150.9 4.4 %all-to-all-done.2 = bf16[32,16,896]{2,1,0:T(8,128)(2,1)S(1)} async-done(((bf16[32,16,896]{2,1,0:T(8,128)(2,1)}), bf16[32,16,896]{2,1,0:T(8,128)(2,1)S(1)}, u32[]{:S(2)}, u32[]{:S(2)}) %all-to-all-start.2) | async-done | bytes 917536 | tf_op jit(solution)/shard_map/all_to_all | solution.py:171
  155.2 8.4 %all-to-all-start.3 = ((bf16[32,16,896]{2,1,0:T(8,128)(2,1)}), bf16[32,16,896]{2,1,0:T(8,128)(2,1)}, u32[]{:S(2)}, u32[]{:S(2)}) async-start(bf16[32,16,896]{2,1,0:T(8,128)(2,1)} %bitcast.72), calls=%async_computation.3 | async-start | bytes 1835008 | tf_op jit(solution)/shard_map/all_to_all | solution.py:171
  164.8 2.7 %collective-permute-start.24 = (bf16[448,1024]{1,0:T(8,128)(2,1)}, bf16[448,1024]{1,0:T(8,128)(2,1)}, u32[]{:S(2)}, u32[]{:S(2)}) collective-permute-start(bf16[448,1024]{1,0:T(8,128)(2,1)} %convert_element_type.153), channel_id=1, source_target_pairs={{0,16},{1,17},{2,18},{3,19},{4,20},{5,21},{6,22},{7,23},{8,24},{9,... | collective-permute-start | bytes 2752520 | tf_op jit(solution)/shard_map/ppermute | solution.py:31
  169.3 2.3 collective-permute-start.23
  173.7 2.6 %collective-permute-start.13 = (bf16[448,256]{1,0:T(8,128)(2,1)S(1)}, bf16[448,256]{1,0:T(8,128)(2,1)S(1)}, u32[]{:S(2)}, u32[]{:S(2)}) collective-permute-start(bf16[448,256]{1,0:T(8,128)(2,1)S(1)} %slice.125), channel_id=1, source_target_pairs={{0,32},{32,0},{64,96},{96,64},{128,160},{160,128},{192,224},{224,1... | collective-permute-start | bytes 688136 | tf_op jit(solution)/shard_map/ppermute | solution.py:21
  177.6 1.8 fusion.5
  179.4 17.8 %collective-permute-done.24 = bf16[448,1024]{1,0:T(8,128)(2,1)} collective-permute-done((bf16[448,1024]{1,0:T(8,128)(2,1)}, bf16[448,1024]{1,0:T(8,128)(2,1)}, u32[]{:S(2)}, u32[]{:S(2)}) %collective-permute-start.24) | collective-permute-done | bytes 917536 | tf_op jit(solution)/shard_map/ppermute | solution.py:31
  197.2 19.7 %collective-permute-done.22 = bf16[448,1024]{1,0:T(8,128)(2,1)} collective-permute-done((bf16[448,1024]{1,0:T(8,128)(2,1)}, bf16[448,1024]{1,0:T(8,128)(2,1)}, u32[]{:S(2)}, u32[]{:S(2)}) %collective-permute-start.22) | collective-permute-done | bytes 917536 | tf_op jit(solution)/shard_map/ppermute | solution.py:31
  216.8 19.7 %collective-permute-done.23 = bf16[448,1024]{1,0:T(8,128)(2,1)} collective-permute-done((bf16[448,1024]{1,0:T(8,128)(2,1)}, bf16[448,1024]{1,0:T(8,128)(2,1)}, u32[]{:S(2)}, u32[]{:S(2)}) %collective-permute-start.23) | collective-permute-done | bytes 917536 | tf_op jit(solution)/shard_map/ppermute | solution.py:31
  236.5 6.1 %divide_convert_fusion = (bf16[448,1024]{1,0:T(8,128)(2,1)}, f32[448,1024]{1,0:T(8,128)}, f32[448,1024]{1,0:T(8,128)}) fusion(bf16[448,1024]{1,0:T(8,128)(2,1)S(1)} %copy-done.9, f32[896,1024]{1,0:T(8,128)} %copy-done.5, bf16[448,1024]{1,0:T(8,128)(2,1)} %collective-permute-done.23, f32[1,1024,448]{1,2,0:T(8,128)S(1)} %copy-done.6, ...), kind=kLoop, calls=%fused_computation.6 | loop fusion | flops 8257536 | bytes 13762561 | tf_op jit(solution)/shard_map/convert_element_type | solution.py:220
  242.6 1.7 fusion.2
  244.3 1.5 collective-permute-start.25
  (120 shorter events, 24.5 us)
Async XLA Ops:
  0.6 4.2 %copy-start = (s32[1,32,32]{2,1,0:T(8,128)S(1)}, s32[1,32,32]{2,1,0:T(8,128)}, u32[]{:S(2)}) copy-start(s32[1,32,32]{2,1,0:T(8,128)} %param.13) | copy-start | bytes 12292
  0.6 16.5 %copy-start.3 = (bf16[1,448,1024]{2,1,0:T(8,128)(2,1)S(1)}, bf16[1,448,1024]{2,1,0:T(8,128)(2,1)}, u32[]{:S(2)}) copy-start(bf16[1,448,1024]{2,1,0:T(8,128)(2,1)} %param.17) | copy-start | bytes 2752516
  0.7 17.2 %copy-start.4 = (bf16[1,448,1024]{2,1,0:T(8,128)(2,1)S(1)}, bf16[1,448,1024]{2,1,0:T(8,128)(2,1)}, u32[]{:S(2)}) copy-start(bf16[1,448,1024]{2,1,0:T(8,128)(2,1)} %param.18) | copy-start | bytes 2752516
  0.7 17.7 %copy-start.24 = (bf16[256,448]{0,1:T(8,128)(2,1)S(1)}, bf16[256,448]{0,1:T(8,128)(2,1)}, u32[]{:S(2)}) copy-start(bf16[256,448]{0,1:T(8,128)(2,1)} %param.12) | copy-start | bytes 688132
  0.7 17.8 %copy-start.18 = (f32[1,32,32]{2,1,0:T(8,128)S(1)}, f32[1,32,32]{2,1,0:T(8,128)}, u32[]{:S(2)}) copy-start(f32[1,32,32]{2,1,0:T(8,128)} %param.15) | copy-start | bytes 12292
  0.7 4.6 %collective-permute-start = (bf16[448,256]{1,0:T(8,128)(2,1)}, bf16[448,256]{1,0:T(8,128)(2,1)S(1)}, u32[]{:S(2)}, u32[]{:S(2)}) collective-permute-start(bf16[448,256]{1,0:T(8,128)(2,1)} %bitcast.76), channel_id=1, source_target_pairs={{0,32},{32,0},{64,96},{96,64},{128,160},{160,128},{192,224},{224,1... | collective-permute-start | bytes 688136 | tf_op jit(solution)/shard_map/ppermute | solution.py:21
  5.0 19.3 %copy-start.21 = (s32[512]{0:T(512)}, s32[512]{0:T(512)S(1)}, u32[]{:S(2)}) copy-start(s32[512]{0:T(512)S(1)} %broadcast_select_fusion.1) | copy-start | bytes 6148
  7.6 31.7 %all-to-all-start = ((bf16[32,16,896]{2,1,0:T(8,128)(2,1)}), bf16[32,16,896]{2,1,0:T(8,128)(2,1)}, u32[]{:S(2)}, u32[]{:S(2)}) async-start(bf16[32,16,896]{2,1,0:T(8,128)(2,1)} %bitcast.3), calls=%async_computation | async-start | bytes 1835008 | tf_op jit(solution)/shard_map/all_to_all | solution.py:171
  17.1 7.2 %collective-permute-start.1 = (bf16[448,1024]{1,0:T(8,128)(2,1)S(1)}, bf16[448,1024]{1,0:T(8,128)(2,1)S(1)}, u32[]{:S(2)}, u32[]{:S(2)}) collective-permute-start(bf16[448,1024]{1,0:T(8,128)(2,1)S(1)} %bitcast.55), channel_id=1, source_target_pairs={{0,32},{32,0},{64,96},{96,64},{128,160},{160,128},{192,224},{224,1... | collective-permute-start | bytes 2752520 | tf_op jit(solution)/shard_map/ppermute | solution.py:21
  17.9 6.5 %collective-permute-start.2 = (bf16[448,1024]{1,0:T(8,128)(2,1)S(1)}, bf16[448,1024]{1,0:T(8,128)(2,1)}, u32[]{:S(2)}, u32[]{:S(2)}) collective-permute-start(bf16[448,1024]{1,0:T(8,128)(2,1)S(1)} %bitcast.57), channel_id=1, source_target_pairs={{0,32},{32,0},{64,96},{96,64},{128,160},{160,128},{192,224},{224,1... | collective-permute-start | bytes 2752520 | tf_op jit(solution)/shard_map/ppermute | solution.py:21
  18.0 11.4 %collective-permute-start.3 = (bf16[448,1024]{1,0:T(8,128)(2,1)}, bf16[448,1024]{1,0:T(8,128)(2,1)}, u32[]{:S(2)}, u32[]{:S(2)}) collective-permute-start(bf16[448,1024]{1,0:T(8,128)(2,1)} %bitcast.69), channel_id=1, source_target_pairs={{0,32},{32,0},{64,96},{96,64},{128,160},{160,128},{192,224},{224,1... | collective-permute-start | bytes 2752520 | tf_op jit(solution)/shard_map/ppermute | solution.py:21
  18.4 4.5 %collective-permute-start.4 = (bf16[448,256]{1,0:T(8,128)(2,1)S(1)}, bf16[448,256]{1,0:T(8,128)(2,1)S(1)}, u32[]{:S(2)}, u32[]{:S(2)}) collective-permute-start(bf16[448,256]{1,0:T(8,128)(2,1)S(1)} %bitcast.78), channel_id=1, source_target_pairs={{0,32},{32,0},{64,96},{96,64},{128,160},{160,128},{192,224},{224,1... | collective-permute-start | bytes 688136 | tf_op jit(solution)/shard_map/ppermute | solution.py:21
  19.2 8.4 %copy-start.19 = (f32[512]{0:T(512)}, f32[512]{0:T(512)S(1)}, u32[]{:S(2)}) copy-start(f32[512]{0:T(512)S(1)} %get-tuple-element.49) | copy-start | bytes 6148
  24.3 5.1 %copy-start.14 = (bf16[1,1024,448]{1,2,0:T(8,128)(2,1)S(1)}, bf16[1,1024,448]{1,2,0:T(8,128)(2,1)}, u32[]{:S(2)}) copy-start(bf16[1,1024,448]{1,2,0:T(8,128)(2,1)} %param.19) | copy-start | bytes 2752516
  44.1 14.8 %copy-start.11 = (bf16[512,2048]{1,0:T(8,128)(2,1)}, bf16[512,2048]{1,0:T(8,128)(2,1)S(1)}, u32[]{:S(2)}) copy-start(bf16[512,2048]{1,0:T(8,128)(2,1)S(1)} %convolution_convert_fusion) | copy-start | bytes 6291460
  45.1 9.8 %collective-permute-start.5 = (bf16[128,2048]{1,0:T(8,128)(2,1)}, bf16[128,2048]{1,0:T(8,128)(2,1)S(1)}, u32[]{:S(2)}, u32[]{:S(2)}) collective-permute-start(bf16[128,2048]{1,0:T(8,128)(2,1)} %pad_maximum_fusion.2), channel_id=1, source_target_pairs={{0,192},{32,224},{64,0},{96,32},{128,64},{160,96},{192,128},{224,1... | collective-permute-start | bytes 1572872 | tf_op jit(solution)/shard_map/ppermute | solution.py:26
  48.7 10.1 %collective-permute-start.6 = (bf16[128,2048]{1,0:T(8,128)(2,1)}, bf16[128,2048]{1,0:T(8,128)(2,1)S(1)}, u32[]{:S(2)}, u32[]{:S(2)}) collective-permute-start(bf16[128,2048]{1,0:T(8,128)(2,1)} %pad_maximum_fusion.3), channel_id=1, source_target_pairs={{0,64},{32,96},{64,128},{96,160},{128,192},{160,224},{192,0},{224,... | collective-permute-start | bytes 1572872 | tf_op jit(solution)/shard_map/ppermute | solution.py:26
  59.7 14.8 %collective-permute-start.7 = (bf16[64,2048]{1,0:T(8,128)(2,1)}, bf16[64,2048]{1,0:T(8,128)(2,1)S(1)}, u32[]{:S(2)}, u32[]{:S(2)}) collective-permute-start(bf16[64,2048]{1,0:T(8,128)(2,1)} %get-tuple-element.27), channel_id=1, source_target_pairs={{0,64},{32,96},{64,128},{96,160},{128,192},{160,224},{192,0},{224,... | collective-permute-start | bytes 786440 | tf_op jit(solution)/shard_map/ppermute | solution.py:26
  59.7 14.8 %collective-permute-start.8 = (bf16[64,2048]{1,0:T(8,128)(2,1)}, bf16[64,2048]{1,0:T(8,128)(2,1)}, u32[]{:S(2)}, u32[]{:S(2)}) collective-permute-start(bf16[64,2048]{1,0:T(8,128)(2,1)} %get-tuple-element.28), channel_id=1, source_target_pairs={{0,192},{32,224},{64,0},{96,32},{128,64},{160,96},{192,128},{224,1... | collective-permute-start | bytes 786440 | tf_op jit(solution)/shard_map/ppermute | solution.py:26
  62.4 33.6 %all-to-all-start.1 = ((bf16[32,16,896]{2,1,0:T(8,128)(2,1)}), bf16[32,16,896]{2,1,0:T(8,128)(2,1)S(1)}, u32[]{:S(2)}, u32[]{:S(2)}) async-start(bf16[32,16,896]{2,1,0:T(8,128)(2,1)} %bitcast.12), calls=%async_computation.1 | async-start | bytes 1835008 | tf_op jit(solution)/shard_map/all_to_all | solution.py:171
  76.1 6.5 %collective-permute-start.9 = (bf16[128,1024]{1,0:T(8,128)(2,1)S(1)}, bf16[128,1024]{1,0:T(8,128)(2,1)S(1)}, u32[]{:S(2)}, u32[]{:S(2)}) collective-permute-start(bf16[128,1024]{1,0:T(8,128)(2,1)S(1)} %multiply_convert_fusion.3), channel_id=1, source_target_pairs={{0,64},{32,96},{64,128},{96,160},{128,192},{160,224},{192,0},{224,... | collective-permute-start | bytes 786440 | tf_op jit(solution)/shard_map/ppermute | solution.py:26
  76.2 6.5 %collective-permute-start.10 = (bf16[128,1024]{1,0:T(8,128)(2,1)S(1)}, bf16[128,1024]{1,0:T(8,128)(2,1)S(1)}, u32[]{:S(2)}, u32[]{:S(2)}) collective-permute-start(bf16[128,1024]{1,0:T(8,128)(2,1)S(1)} %multiply_convert_fusion.3), channel_id=1, source_target_pairs={{0,192},{32,224},{64,0},{96,32},{128,64},{160,96},{192,128},{224,1... | collective-permute-start | bytes 786440 | tf_op jit(solution)/shard_map/ppermute | solution.py:26
  82.6 5.4 %collective-permute-start.11 = (bf16[64,1024]{1,0:T(8,128)(2,1)S(1)}, bf16[64,1024]{1,0:T(8,128)(2,1)S(1)}, u32[]{:S(2)}, u32[]{:S(2)}) collective-permute-start(bf16[64,1024]{1,0:T(8,128)(2,1)S(1)} %slice.73), channel_id=1, source_target_pairs={{0,64},{32,96},{64,128},{96,160},{128,192},{160,224},{192,0},{224,... | collective-permute-start | bytes 393224 | tf_op jit(solution)/shard_map/ppermute | solution.py:26
  82.7 5.3 %copy-start.15 = (bf16[128,1024]{1,0:T(8,128)(2,1)}, bf16[128,1024]{1,0:T(8,128)(2,1)S(1)}, u32[]{:S(2)}) copy-start(bf16[128,1024]{1,0:T(8,128)(2,1)S(1)} %collective-permute-done.10) | copy-start | bytes 786436
  82.7 5.9 %collective-permute-start.12 = (bf16[64,1024]{1,0:T(8,128)(2,1)S(1)}, bf16[64,1024]{1,0:T(8,128)(2,1)}, u32[]{:S(2)}, u32[]{:S(2)}) collective-permute-start(bf16[64,1024]{1,0:T(8,128)(2,1)S(1)} %slice.74), channel_id=1, source_target_pairs={{0,192},{32,224},{64,0},{96,32},{128,64},{160,96},{192,128},{224,1... | collective-permute-start | bytes 393224 | tf_op jit(solution)/shard_map/ppermute | solution.py:26
  85.7 5.1 %copy-start.12 = (bf16[896,1024]{1,0:T(8,128)(2,1)S(1)}, bf16[896,1024]{1,0:T(8,128)(2,1)}, u32[]{:S(2)}) copy-start(bf16[896,1024]{1,0:T(8,128)(2,1)} %pad_maximum_fusion) | copy-start | bytes 5505028
  100.6 5.5 %collective-permute-start.16 = (bf16[128,1024]{1,0:T(8,128)(2,1)}, bf16[128,1024]{1,0:T(8,128)(2,1)}, u32[]{:S(2)}, u32[]{:S(2)}) collective-permute-start(bf16[128,1024]{1,0:T(8,128)(2,1)} %get-tuple-element.61), channel_id=1, source_target_pairs={{0,192},{32,224},{64,0},{96,32},{128,64},{160,96},{192,128},{224,1... | collective-permute-start | bytes 786440 | tf_op jit(solution)/shard_map/ppermute | solution.py:26
  100.7 9.3 %collective-permute-start.15 = (bf16[128,1024]{1,0:T(8,128)(2,1)S(1)}, bf16[128,1024]{1,0:T(8,128)(2,1)}, u32[]{:S(2)}, u32[]{:S(2)}) collective-permute-start(bf16[128,1024]{1,0:T(8,128)(2,1)S(1)} %get-tuple-element.62), channel_id=1, source_target_pairs={{0,64},{32,96},{64,128},{96,160},{128,192},{160,224},{192,0},{224,... | collective-permute-start | bytes 786440 | tf_op jit(solution)/shard_map/ppermute | solution.py:26
  102.0 8.0 %collective-permute-start.14 = (bf16[128,1024]{1,0:T(8,128)(2,1)S(1)}, bf16[128,1024]{1,0:T(8,128)(2,1)}, u32[]{:S(2)}, u32[]{:S(2)}) collective-permute-start(bf16[128,1024]{1,0:T(8,128)(2,1)S(1)} %get-tuple-element.60), channel_id=1, source_target_pairs={{0,128},{32,160},{64,192},{96,224},{128,0},{160,32},{192,64},{224,... | collective-permute-start | bytes 786440 | tf_op jit(solution)/shard_map/ppermute | solution.py:26
  115.6 25.2 %collective-permute-start.21 = (bf16[448,1024]{1,0:T(8,128)(2,1)}, bf16[448,1024]{1,0:T(8,128)(2,1)S(1)}, u32[]{:S(2)}, u32[]{:S(2)}) collective-permute-start(bf16[448,1024]{1,0:T(8,128)(2,1)} %slice.123), channel_id=1, source_target_pairs={{0,32},{32,0},{64,96},{96,64},{128,160},{160,128},{192,224},{224,1... | collective-permute-start | bytes 2752520 | tf_op jit(solution)/shard_map/ppermute | solution.py:21
  122.1 14.7 %collective-permute-start.17 = (bf16[128,2048]{1,0:T(8,128)(2,1)S(1)}, bf16[128,2048]{1,0:T(8,128)(2,1)S(1)}, u32[]{:S(2)}, u32[]{:S(2)}) collective-permute-start(bf16[128,2048]{1,0:T(8,128)(2,1)S(1)} %pad_maximum_fusion.4), channel_id=1, source_target_pairs={{0,64},{32,96},{64,128},{96,160},{128,192},{160,224},{192,0},{224,... | collective-permute-start | bytes 1572872 | tf_op jit(solution)/shard_map/ppermute | solution.py:26
  122.1 14.8 %collective-permute-start.18 = (bf16[128,2048]{1,0:T(8,128)(2,1)S(1)}, bf16[128,2048]{1,0:T(8,128)(2,1)}, u32[]{:S(2)}, u32[]{:S(2)}) collective-permute-start(bf16[128,2048]{1,0:T(8,128)(2,1)S(1)} %pad_maximum_fusion.4), channel_id=1, source_target_pairs={{0,192},{32,224},{64,0},{96,32},{128,64},{160,96},{192,128},{224,1... | collective-permute-start | bytes 1572872 | tf_op jit(solution)/shard_map/ppermute | solution.py:26
  124.7 30.5 %all-to-all-start.2 = ((bf16[32,16,896]{2,1,0:T(8,128)(2,1)}), bf16[32,16,896]{2,1,0:T(8,128)(2,1)S(1)}, u32[]{:S(2)}, u32[]{:S(2)}) async-start(bf16[32,16,896]{2,1,0:T(8,128)(2,1)} %bitcast.71), calls=%async_computation.2 | async-start | bytes 1835008 | tf_op jit(solution)/shard_map/all_to_all | solution.py:171
  136.8 8.3 %collective-permute-start.19 = (bf16[64,2048]{1,0:T(8,128)(2,1)S(1)}, bf16[64,2048]{1,0:T(8,128)(2,1)S(1)}, u32[]{:S(2)}, u32[]{:S(2)}) collective-permute-start(bf16[64,2048]{1,0:T(8,128)(2,1)S(1)} %slice.77), channel_id=1, source_target_pairs={{0,64},{32,96},{64,128},{96,160},{128,192},{160,224},{192,0},{224,... | collective-permute-start | bytes 786440 | tf_op jit(solution)/shard_map/ppermute | solution.py:26
  137.9 7.5 %collective-permute-start.20 = (bf16[64,2048]{1,0:T(8,128)(2,1)S(1)}, bf16[64,2048]{1,0:T(8,128)(2,1)S(1)}, u32[]{:S(2)}, u32[]{:S(2)}) collective-permute-start(bf16[64,2048]{1,0:T(8,128)(2,1)S(1)} %slice.78), channel_id=1, source_target_pairs={{0,192},{32,224},{64,0},{96,32},{128,64},{160,96},{192,128},{224,1... | collective-permute-start | bytes 786440 | tf_op jit(solution)/shard_map/ppermute | solution.py:26
  147.5 16.1 %copy-start.20 = (f32[512]{0:T(512)S(1)}, f32[512]{0:T(512)}, u32[]{:S(2)}) copy-start(f32[512]{0:T(512)} %copy-done.19) | copy-start | bytes 6148
  150.9 12.8 %copy-start.6 = (f32[1,1024,448]{1,2,0:T(8,128)S(1)}, f32[1,1024,448]{1,2,0:T(8,128)}, u32[]{:S(2)}) copy-start(f32[1,1024,448]{1,2,0:T(8,128)} %param.21) | copy-start | bytes 5505028
  155.2 87.3 %all-to-all-start.3 = ((bf16[32,16,896]{2,1,0:T(8,128)(2,1)}), bf16[32,16,896]{2,1,0:T(8,128)(2,1)}, u32[]{:S(2)}, u32[]{:S(2)}) async-start(bf16[32,16,896]{2,1,0:T(8,128)(2,1)} %bitcast.72), calls=%async_computation.3 | async-start | bytes 1835008 | tf_op jit(solution)/shard_map/all_to_all | solution.py:171
  163.7 3.8 %copy-start.7 = (f32[1,1024,448]{1,2,0:T(8,128)S(1)}, f32[1,1024,448]{1,2,0:T(8,128)}, u32[]{:S(2)}) copy-start(f32[1,1024,448]{1,2,0:T(8,128)} %param.20) | copy-start | bytes 5505028
  164.8 6.7 %copy-start.22 = (s32[512]{0:T(512)S(1)}, s32[512]{0:T(512)}, u32[]{:S(2)}) copy-start(s32[512]{0:T(512)} %copy-done.21) | copy-start | bytes 6148
  164.8 32.4 %collective-permute-start.24 = (bf16[448,1024]{1,0:T(8,128)(2,1)}, bf16[448,1024]{1,0:T(8,128)(2,1)}, u32[]{:S(2)}, u32[]{:S(2)}) collective-permute-start(bf16[448,1024]{1,0:T(8,128)(2,1)} %convert_element_type.153), channel_id=1, source_target_pairs={{0,16},{1,17},{2,18},{3,19},{4,20},{5,21},{6,22},{7,23},{8,24},{9,... | collective-permute-start | bytes 2752520 | tf_op jit(solution)/shard_map/ppermute | solution.py:31
  167.5 4.7 %copy-start.23 = (bf16[512]{0:T(512)(128)(2,1)S(1)}, bf16[512]{0:T(512)(128)(2,1)}, u32[]{:S(2)}) copy-start(bf16[512]{0:T(512)(128)(2,1)} %get-tuple-element.48) | copy-start | bytes 3076
  168.5 48.3 %collective-permute-start.22 = (bf16[448,1024]{1,0:T(8,128)(2,1)}, bf16[448,1024]{1,0:T(8,128)(2,1)}, u32[]{:S(2)}, u32[]{:S(2)}) collective-permute-start(bf16[448,1024]{1,0:T(8,128)(2,1)} %convert_element_type.150), channel_id=1, source_target_pairs={{0,16},{1,17},{2,18},{3,19},{4,20},{5,21},{6,22},{7,23},{8,24},{9,... | collective-permute-start | bytes 2752520 | tf_op jit(solution)/shard_map/ppermute | solution.py:31
  169.3 67.2 %collective-permute-start.23 = (bf16[448,1024]{1,0:T(8,128)(2,1)}, bf16[448,1024]{1,0:T(8,128)(2,1)}, u32[]{:S(2)}, u32[]{:S(2)}) collective-permute-start(bf16[448,1024]{1,0:T(8,128)(2,1)} %fusion.3), channel_id=1, source_target_pairs={{0,16},{1,17},{2,18},{3,19},{4,20},{5,21},{6,22},{7,23},{8,24},{9,... | collective-permute-start | bytes 2752520 | tf_op jit(solution)/shard_map/ppermute | solution.py:31
  172.1 4.2 %copy-start.25 = (s32[16]{0:T(128)S(1)}, s32[16]{0:T(128)}, u32[]{:S(2)}) copy-start(s32[16]{0:T(128)} %param.16) | copy-start | bytes 196
  173.7 62.8 %copy-start.9 = (bf16[448,1024]{1,0:T(8,128)(2,1)S(1)}, bf16[448,1024]{1,0:T(8,128)(2,1)}, u32[]{:S(2)}) copy-start(bf16[448,1024]{1,0:T(8,128)(2,1)} %copy-done.8) | copy-start | bytes 2752516
  173.7 3.9 %collective-permute-start.13 = (bf16[448,256]{1,0:T(8,128)(2,1)S(1)}, bf16[448,256]{1,0:T(8,128)(2,1)S(1)}, u32[]{:S(2)}, u32[]{:S(2)}) collective-permute-start(bf16[448,256]{1,0:T(8,128)(2,1)S(1)} %slice.125), channel_id=1, source_target_pairs={{0,32},{32,0},{64,96},{96,64},{128,160},{160,128},{192,224},{224,1... | collective-permute-start | bytes 688136 | tf_op jit(solution)/shard_map/ppermute | solution.py:21
  244.3 2.6 %collective-permute-start.25 = (bf16[448,256]{1,0:T(8,128)(2,1)S(1)}, bf16[448,256]{1,0:T(8,128)(2,1)S(1)}, u32[]{:S(2)}, u32[]{:S(2)}) collective-permute-start(bf16[448,256]{1,0:T(8,128)(2,1)S(1)} %slice.124), channel_id=1, source_target_pairs={{0,32},{32,0},{64,96},{96,64},{128,160},{160,128},{192,224},{224,1... | collective-permute-start | bytes 688136 | tf_op jit(solution)/shard_map/ppermute | solution.py:21
  (8 other events, 12.6 us)

commit v5 on v4

--- a/solution.py
+++ b/solution.py
@@ -31,10 +31,6 @@
     return lax.ppermute(block, "expert", [(i, i ^ (count // 2)) for i in range(count)])
 
 
-def rows_at(block, index, rows):
-    return lax.dynamic_slice_in_dim(block, index * rows, rows, 0)
-
-
 def tie(value, *others):
     return lax.optimization_barrier((value,) + others)[0]
 
@@ -43,48 +39,151 @@
     return lax.optimization_barrier(tuple(values) + others)[: len(values)]
 
 
-def scatter_sum(partial, y_pos, chips):
-    rows = partial.shape[0] // chips
-    total = rows_at(partial, y_pos, rows).astype(F32)
-    for step in (2, 1, 3):
-        piece = rows_at(partial, (y_pos + step) % chips, rows)
-        came = chip_shift(piece, step)
-        total = total + came.astype(F32)
-    return total
-
-
-def ring_sum(partial, y_pos, chips):
-    rows = partial.shape[0] // (2 * chips)
-
-    def half(step, part):
-        return rows_at(partial, 2 * ((y_pos + step) % chips) + part, rows)
-
-    from_left = chip_shift(jnp.concatenate([half(2, 0), half(1, 1)]), 1)
-    from_right = chip_shift(jnp.concatenate([half(2, 1), half(3, 0)]), chips - 1)
-    on_right = (half(1, 0).astype(F32) + from_left[:rows].astype(F32)).astype(BF)
-    on_left = (half(3, 1).astype(F32) + from_right[:rows].astype(F32)).astype(BF)
+def ordered_dot(y_pos, left, right, units, sizes):
+    rows, depth = left.shape
+    width = right.shape[1]
+    unit = rows // len(units)
+    per_block = len(units) // 4
+    tile = 512
+
+    def body(pos, left_ref, right_ref, *refs):
+        outs, ordered = refs[:-1], refs[-1]
+
+        @pl.when(pl.program_id(0) == 0)
+        def _():
+            for place, (step, part) in enumerate(units):
+                at = (lax.rem(pos[0] + step, 4) * per_block + part) * unit
+                ordered[place * unit : (place + 1) * unit, :] = left_ref[
+                    pl.ds(pl.multiple_of(at, unit), unit), :
+                ]
+
+        start = 0
+        for out in outs:
+            size = out.shape[0]
+            out[...] = dot(ordered[start : start + size, :], right_ref[...]).astype(BF)
+            start += size
+
+    return pl.pallas_call(
+        body,
+        out_shape=[pltpu.HBM((size, width), BF) for size in sizes],
+        grid_spec=pltpu.PrefetchScalarGridSpec(
+            num_scalar_prefetch=1,
+            grid=(width // tile,),
+            in_specs=[
+                pl.BlockSpec((rows, depth), lambda i, pos: (0, 0)),
+                pl.BlockSpec((depth, tile), lambda i, pos: (0, i)),
+            ],
+            out_specs=[pl.BlockSpec((size, tile), lambda i, pos: (0, i)) for size in sizes],
+            scratch_shapes=[pltpu.VMEM((rows, depth), BF)],
+        ),
+        compiler_params=pltpu.CompilerParams(vmem_limit_bytes=16 << 20),
+        cost_estimate=pl.CostEstimate(
+            flops=2 * rows * depth * width,
+            bytes_accessed=2 * (rows * depth + depth * width + rows * width),
+            transcendentals=0,
+        ),
+    )(y_pos.reshape(1), left, pltpu.with_memory_space_constraint(right, pltpu.HBM))
+
+
+def gathered_dot(y_pos, parts, right, keep):
+    own, _, _, _, _ = parts
+    rows, depth = own.shape
+    width = right.shape[0]
+    total = 4 * rows
+    mid = rows // 2
+    tile = 512
+    steps = depth // tile
+
+    def body(pos, own_ref, left_ref, right_ref, top_ref, low_ref, w_ref, out, *refs):
+        full, acc = refs[-2:]
+        k = pl.program_id(0)
+
+        @pl.when(k == 0)
+        def _():
+            for step, offset, ref in (
+                (0, 0, own_ref),
+                (3, 0, left_ref),
+                (1, 0, right_ref),
+                (2, 0, top_ref),
+                (2, mid, low_ref),
+            ):
+                at = lax.rem(pos[0] + step, 4) * rows + offset
+                size = ref.shape[0]
+                if keep:
+                    refs[0][pl.ds(pl.multiple_of(at, mid), size), :] = ref[...]
+                for t in range(steps):
+                    full[t, pl.ds(pl.multiple_of(at, mid), size), :] = ref[
+                        :, t * tile : (t + 1) * tile
+                    ]
+
+        term = dot(full[k], w_ref[...], 1, 1)
+
+        @pl.when(k == 0)
+        def _():
+            acc[...] = term
+
+        @pl.when(jnp.logical_and(k > 0, k < steps - 1))
+        def _():
+            acc[...] += term
+
+        @pl.when(k == steps - 1)
+        def _():
+            out[...] = (acc[...] + term).astype(BF)
+
+    def whole(shape):
+        return pl.BlockSpec(shape, lambda k, pos: (0,) * len(shape))
+
+    out_shape = [pltpu.HBM((total, width), BF)]
+    out_specs = [whole((total, width))]
+    if keep:
+        out_shape.append(pltpu.HBM((total, depth), BF))
+        out_specs.append(whole((total, depth)))
+    scratch = [pltpu.VMEM((steps, total, tile), BF), pltpu.VMEM((total, width), F32)]
+    return pl.pallas_call(
+        body,
+        out_shape=out_shape,
+        grid_spec=pltpu.PrefetchScalarGridSpec(
+            num_scalar_prefetch=1,
+            grid=(steps,),
+            in_specs=[whole(part.shape) for part in parts]
+            + [pl.BlockSpec((width, tile), lambda k, pos: (0, k))],
+            out_specs=out_specs,
+            scratch_shapes=scratch,
+        ),
+        compiler_params=pltpu.CompilerParams(vmem_limit_bytes=24 << 20),
+        cost_estimate=pl.CostEstimate(
+            flops=2 * total * depth * width,
+            bytes_accessed=2 * (total * depth + depth * width + total * width),
+            transcendentals=0,
+        ),
+    )(y_pos.reshape(1), *parts, pltpu.with_memory_space_constraint(right, pltpu.HBM))
+
+
+RING_UNITS = ((2, 0), (1, 1), (2, 1), (3, 0), (0, 0), (0, 1), (1, 0), (3, 1))
+
+
+def ring_sum(to_right, to_left, rest, chips):
+    rows = rest.shape[0] // 4
+    own_top, own_low, pass_right, pass_left = (rest[i * rows :][:rows] for i in range(4))
+    from_left = chip_shift(to_right, 1)
+    from_right = chip_shift(to_left, chips - 1)
+    on_right = (pass_right.astype(F32) + from_left[:rows].astype(F32)).astype(BF)
+    on_left = (pass_left.astype(F32) + from_right[:rows].astype(F32)).astype(BF)
     on_right, on_left = lax.optimization_barrier((on_right, on_left))
     far_left = chip_shift(on_right, 1)
     far_right = chip_shift(on_left, chips - 1)
-    top = half(0, 0).astype(F32) + from_right[rows:].astype(F32) + far_left.astype(F32)
-    low = half(0, 1).astype(F32) + from_left[rows:].astype(F32) + far_right.astype(F32)
+    top = own_top.astype(F32) + from_right[rows:].astype(F32) + far_left.astype(F32)
+    low = own_low.astype(F32) + from_left[rows:].astype(F32) + far_right.astype(F32)
     return jnp.concatenate([top, low])
 
 
-def ring_gather(shard, y_pos, chips, after=()):
-    rows = shard.shape[0]
-    mid = rows // 2
+def ring_gather(shard, chips):
+    mid = shard.shape[0] // 2
     left = chip_shift(shard, 1)
     right = chip_shift(shard, chips - 1)
     far_top = chip_shift(left[:mid], 1)
     far_low = chip_shift(right[mid:], chips - 1)
-    full = jnp.broadcast_to(shard[None], (chips,) + shard.shape).reshape(-1, shard.shape[1])
-    pieces = tie_all([left, right, far_top, far_low], *after)
-    spots = ((3, 0), (1, 0), (2, 0), (2, mid))
-    for (step, offset), piece in zip(spots, pieces):
-        at = ((y_pos + step) % chips) * rows + offset
-        full = lax.dynamic_update_slice_in_dim(full, piece, at, 0)
-    return full
+    return shard, left, right, far_top, far_low
 
 
 def pair_rows(block):
@@ -115,7 +214,7 @@
     moved = 8 * rows * units
     return pl.pallas_call(
         body,
-        out_shape=jax.ShapeDtypeStruct((2 * rows, 2 * units), gate_own.dtype),
+        out_shape=pltpu.HBM((2 * rows, 2 * units), gate_own.dtype),
         grid=(2 * steps,),
         in_specs=[near, near, far, far],
         out_specs=pl.BlockSpec((block, 2 * units), lambda i: (i, 0)),
@@ -191,26 +290,35 @@
     far_two = expert_swap(tie(moment_two, arrived).astype(BF))
 
     hidden_units = down_weight.shape[1]
-    preact = ring_sum(dot(arrived, gate_up).astype(BF), y_pos, chips)
+    half = rows // (2 * chips)
+    products = ordered_dot(y_pos, arrived, gate_up, RING_UNITS, (2 * half, 2 * half, 4 * half))
+    preact = ring_sum(*products, chips)
     gate_pre, up_pre = preact[:, :hidden_units], preact[:, hidden_units:]
     sig = jax.nn.sigmoid(gate_pre)
     hidden_shard = (gate_pre * sig * up_pre).astype(BF)
-    hidden = ring_gather(hidden_shard, y_pos, chips)
-    out_rows, arrived_grad = lax.optimization_barrier(
-        (dot(hidden, down_cols, 1, 1).astype(BF), arrived_grad)
+    arrived_grad = tie(arrived_grad, hidden_shard)
+    terms = ordered_dot(
+        y_pos, arrived_grad, down_cols, ((2, 0), (1, 0), (3, 0), (0, 0)), (2 * half,) * 4
     )
+    gathered = ring_gather(hidden_shard, chips)
+    gathered = tie_all(gathered, *terms)
+    out_rows, hidden = gathered_dot(y_pos, gathered, down_cols, True)
     returned = exchange(out_rows)
 
-    hidden_part = dot(arrived_grad, down_cols).astype(BF)
-    hidden_grad = scatter_sum(hidden_part, y_pos, chips)
+    hidden_grad = terms[3].astype(F32)
+    for step, term in zip((2, 1, 3), terms):
+        came = chip_shift(term, step)
+        hidden_grad = hidden_grad + came.astype(F32)
     gate_grad = hidden_grad * up_pre * sig * (1.0 + gate_pre * (1.0 - sig))
     up_grad = hidden_grad * gate_pre * sig
     pre_shard = jnp.concatenate([gate_grad, up_grad], axis=1).astype(BF)
     weight_grad = pair_sum(dot(tie(arrived_grad, pre_shard), hidden, 0, 0))
     sent_grad = weight_grad.astype(BF)
+    gathered = ring_gather(pre_shard, chips)
+    gathered = tie_all(gathered, sent_grad)
     far_grad = expert_swap(sent_grad)
-    pre_grad = ring_gather(pre_shard, y_pos, chips, (sent_grad,))
-    returned_grad = exchange(dot(pre_grad, gate_up, 1, 1).astype(BF))
+    (back,) = gathered_dot(y_pos, gathered, gate_up, False)
+    returned_grad = exchange(back)
 
     one = jnp.where(own_swap, far_one.astype(F32), moment_one)
     two = jnp.where(own_swap, far_two.astype(F32), moment_two)

time: 249 us -> 242 us (0.972)
  Pallas kernels: 3.23 us -> 25.6 us
  local copies, waits for them, and re-layouts: 13.9 us -> 1.72 us
  matrix products: 20.8 us -> 10.2 us
  other arithmetic: 24.1 us -> 19.2 us
    pallas_call x1 -> x5, Pallas kernels: 3.23 us -> 25.6 us  [the longest x2 10.6 us: gathered_dot(): pl.pallas_call(body, out_shape=out_shape, grid_spec=pltpu.PrefetchScalarG...]
    dot_general x10 -> x6, matrix products: 20.8 us -> 10.2 us  [dot(): lax.dot_general(a, b, (((ca,), (cb,)), ((), ())), preferred_element_type=...]
    unnamed x52 -> x40, local copies, waits for them, and re-layouts: 6.79 us -> 1.01 us
    ppermute x3, waiting for transfers between devices: 57.1 us -> 53.8 us  [expert_swap(): lax.ppermute(block, 'expert', [(i, i ^ count // 2) for i in range(count)])]
    dynamic_update_slice x8 -> x0, local copies, waits for them, and re-layouts: 3.28 us -> none  [ring_gather(): full = lax.dynamic_update_slice_in_dim(full, piece, at, 0)]
    ppermute x8, starting transfers between devices: 15.2 us -> 12.5 us  [core_swap(): lax.ppermute(block, 'dp', [(i, i ^ 1) for i in range(lax.axis_size('dp'))])]
  transfers between devices with their start and end apart: 30 -> 30, of which waited for: 18 -> 13; matrix products, arithmetic and copies ran while one was open for 13% -> 11% of each run, Pallas kernels for 1% -> 8%
where the time goes in v5:
time: 242 us; the launch traced here: 241 us
  waiting for transfers between devices  105 us (43%)
  starting transfers between devices  77.3 us (32%)
  Pallas kernels  25.6 us (11%)
  other arithmetic  19.2 us (8%)
  matrix products  10.2 us (4%)
    ppermute x3, waiting for transfers between devices, expert_swap(): lax.ppermute(block, 'expert', [(i, i ^ count // 2) for i in range(count)])  53.8 us
    all_to_all x4, starting transfers between devices, exchange(): lax.all_to_all(block.reshape(experts, own_slots, pair_cols), 'expert', 0,...  39.1 us
    ppermute x15, waiting for transfers between devices, chip_shift(): lax.ppermute(block, 'dp', [(i, (i + 2 * step) % count) for i in range(cou...  31.6 us
    ppermute x15, starting transfers between devices, chip_shift(): lax.ppermute(block, 'dp', [(i, (i + 2 * step) % count) for i in range(cou...  20.1 us
    all_to_all x4, waiting for transfers between devices, exchange(): lax.all_to_all(block.reshape(experts, own_slots, pair_cols), 'expert', 0,...  14.6 us
    ppermute x8, starting transfers between devices, core_swap(): lax.ppermute(block, 'dp', [(i, i ^ 1) for i in range(lax.axis_size('dp'))])  12.5 us
    pallas_call x2, Pallas kernels, gathered_dot(): pl.pallas_call(body, out_shape=out_shape, grid_spec=pltpu.PrefetchScalarG...  10.6 us
    dot_general x6, matrix products, dot(): lax.dot_general(a, b, (((ca,), (cb,)), ((), ())), preferred_element_type=...  10.2 us
  transfers between devices with their start and end apart: 30, of which 13 were waited for; matrix products, arithmetic and copies ran while one was open for 11% of the time, Pallas kernels for 8%

profile of v5, /device:TPU:1, one launch (start us, length us, event | category | flops | bytes accessed | tf_op | source)
XLA Modules:
  0.0 240.9 jit_solution(17018163280947738386)
XLA Ops:
  0.7 3.3 %collective-permute-start = (bf16[448,256]{1,0:T(8,128)(2,1)}, bf16[448,256]{1,0:T(8,128)(2,1)S(1)}, u32[]{:S(2)}, u32[]{:S(2)}) collective-permute-start(bf16[448,256]{1,0:T(8,128)(2,1)} %bitcast.63), channel_id=1, source_target_pairs={{0,32},{32,0},{64,96},{96,64},{128,160},{160,128},{192,224},{224,1... | collective-permute-start | bytes 688136 | tf_op jit(solution)/shard_map/ppermute | solution.py:21
  5.3 2.3 convolution_convert_fusion
  7.6 9.4 %all-to-all-start = ((bf16[32,16,896]{2,1,0:T(8,128)(2,1)}), bf16[32,16,896]{2,1,0:T(8,128)(2,1)}, u32[]{:S(2)}, u32[]{:S(2)}) async-start(bf16[32,16,896]{2,1,0:T(8,128)(2,1)} %bitcast.4), calls=%async_computation | async-start | bytes 1835008 | tf_op jit(solution)/shard_map/all_to_all | solution.py:270
  19.2 3.7 %collective-permute-done.4 = bf16[448,256]{1,0:T(8,128)(2,1)S(1)} collective-permute-done((bf16[448,256]{1,0:T(8,128)(2,1)S(1)}, bf16[448,256]{1,0:T(8,128)(2,1)S(1)}, u32[]{:S(2)}, u32[]{:S(2)}) %collective-permute-start.4) | collective-permute-done | bytes 229408 | tf_op jit(solution)/shard_map/ppermute | solution.py:21
  22.9 1.4 multiply_convert_fusion
  24.3 5.8 %shard_map.146.right_ref.w_ref = bf16[896,2048]{1,0:T(8,128)(2,1)} custom-call(bf16[448,1024]{1,0:T(8,128)(2,1)S(1)} %bitcast.49, bf16[448,1024]{1,0:T(8,128)(2,1)S(1)} %bitcast.51, bf16[448,1024]{1,0:T(8,128)(2,1)S(1)} %collective-permute-done.1.gate_b, bf16[448,1024]{1,0:T(8,128)(2,1)} %collective-permute-done.2.up_b), custom_call_target="tpu_custom_call" | custom-call | bytes 7340032 | tf_op jit(solution)/shard_map/pallas_call | solution.py:215
  30.2 2.6 %pad_maximum_fusion.right_ref.w_ref = bf16[896,1024]{1,0:T(8,128)(2,1)} fusion(bf16[448,1024]{1,0:T(8,128)(2,1)} %collective-permute-done.3, bf16[448,1024]{1,0:T(8,128)(2,1)S(1)} %bitcast.57), kind=kLoop, calls=%fused_computation.4 | loop fusion | flops 3670016 | bytes 3670016 | tf_op jit(solution)/shard_map/concatenate | solution.py:191
  32.8 6.6 %all-to-all-done = bf16[32,16,896]{2,1,0:T(8,128)(2,1)} async-done(((bf16[32,16,896]{2,1,0:T(8,128)(2,1)}), bf16[32,16,896]{2,1,0:T(8,128)(2,1)}, u32[]{:S(2)}, u32[]{:S(2)}) %all-to-all-start) | async-done | bytes 917536 | tf_op jit(solution)/shard_map/all_to_all | solution.py:270
  39.4 5.8 %shard_map.147 = (bf16[128,2048]{1,0:T(8,128)(2,1)}, bf16[128,2048]{1,0:T(8,128)(2,1)}, bf16[256,2048]{1,0:T(8,128)(2,1)}) custom-call(s32[1]{0:T(128)} %bitcast.pos, bf16[512,896]{1,0:T(8,128)(2,1)} %bitcast.5.left_ref, bf16[896,2048]{1,0:T(8,128)(2,1)} %shard_map.146.right_ref.w_ref), custom_call_target="tpu_custom_call" | custom-call | flops 1879048192 | bytes 6684672 | tf_op jit(solution)/shard_map/pallas_call | solution.py:66
  45.2 2.7 %collective-permute-start.5 = (bf16[128,2048]{1,0:T(8,128)(2,1)}, bf16[128,2048]{1,0:T(8,128)(2,1)S(1)}, u32[]{:S(2)}, u32[]{:S(2)}) collective-permute-start(bf16[128,2048]{1,0:T(8,128)(2,1)} %get-tuple-element.38), channel_id=1, source_target_pairs={{0,192},{32,224},{64,0},{96,32},{128,64},{160,96},{192,128},{224,1... | collective-permute-start | bytes 1572872 | tf_op jit(solution)/shard_map/ppermute | solution.py:26
  47.9 8.1 %all-to-all-start.1 = ((bf16[32,16,896]{2,1,0:T(8,128)(2,1)}), bf16[32,16,896]{2,1,0:T(8,128)(2,1)S(1)}, u32[]{:S(2)}, u32[]{:S(2)}) async-start(bf16[32,16,896]{2,1,0:T(8,128)(2,1)} %bitcast.12), calls=%async_computation.1 | async-start | bytes 1835008 | tf_op jit(solution)/shard_map/all_to_all | solution.py:270
  56.1 1.9 collective-permute-done.6
  58.2 2.7 %collective-permute-start.8 = (bf16[64,2048]{1,0:T(8,128)(2,1)S(1)}, bf16[64,2048]{1,0:T(8,128)(2,1)S(1)}, u32[]{:S(2)}, u32[]{:S(2)}) collective-permute-start(bf16[64,2048]{1,0:T(8,128)(2,1)S(1)} %get-tuple-element.41), channel_id=1, source_target_pairs={{0,192},{32,224},{64,0},{96,32},{128,64},{160,96},{192,128},{224,1... | collective-permute-start | bytes 786440 | tf_op jit(solution)/shard_map/ppermute | solution.py:26
  60.9 5.2 %collective-permute-done.7 = bf16[64,2048]{1,0:T(8,128)(2,1)S(1)} collective-permute-done((bf16[64,2048]{1,0:T(8,128)(2,1)S(1)}, bf16[64,2048]{1,0:T(8,128)(2,1)S(1)}, u32[]{:S(2)}, u32[]{:S(2)}) %collective-permute-start.7) | collective-permute-done | bytes 262176 | tf_op jit(solution)/shard_map/ppermute | solution.py:26
  66.1 1.2 convert_add_fusion.2
  67.5 2.7 %collective-permute-start.10 = (bf16[128,1024]{1,0:T(8,128)(2,1)S(1)}, bf16[128,1024]{1,0:T(8,128)(2,1)S(1)}, u32[]{:S(2)}, u32[]{:S(2)}) collective-permute-start(bf16[128,1024]{1,0:T(8,128)(2,1)S(1)} %multiply_convert_fusion.3.own_ref), channel_id=1, source_target_pairs={{0,192},{32,224},{64,0},{96,32},{128,64},{160,96},{192,128},{224,1... | collective-permute-start | bytes 786440 | tf_op jit(solution)/shard_map/ppermute | solution.py:26
  70.2 8.0 %all-to-all-done.1 = bf16[32,16,896]{2,1,0:T(8,128)(2,1)S(1)} async-done(((bf16[32,16,896]{2,1,0:T(8,128)(2,1)}), bf16[32,16,896]{2,1,0:T(8,128)(2,1)S(1)}, u32[]{:S(2)}, u32[]{:S(2)}) %all-to-all-start.1) | async-done | bytes 917536 | tf_op jit(solution)/shard_map/all_to_all | solution.py:270
  78.2 3.4 %shard_map.148 = (bf16[128,1024]{1,0:T(8,128)(2,1)}, bf16[128,1024]{1,0:T(8,128)(2,1)}, bf16[128,1024]{1,0:T(8,128)(2,1)}, bf16[128,1024]{1,0:T(8,128)(2,1)}) custom-call(s32[1]{0:T(128)} %bitcast.pos, bf16[512,896]{1,0:T(8,128)(2,1)S(1)} %bitcast.46, bf16[896,1024]{1,0:T(8,128)(2,1)} %pad_maximum_fusion.right_ref.w_ref), custom_call_target="tpu_custom_call" | custom-call | flops 939524096 | bytes 3801088 | tf_op jit(solution)/shard_map/pallas_call | solution.py:66
  81.5 2.3 collective-permute-start.16
  83.8 1.2 collective-permute-start.14
  85.1 2.1 collective-permute-start.11
  87.9 8.2 %collective-permute-done.11.top_ref = bf16[64,1024]{1,0:T(8,128)(2,1)S(1)} collective-permute-done((bf16[64,1024]{1,0:T(8,128)(2,1)S(1)}, bf16[64,1024]{1,0:T(8,128)(2,1)S(1)}, u32[]{:S(2)}, u32[]{:S(2)}) %collective-permute-start.11) | collective-permute-done | bytes 131104 | tf_op jit(solution)/shard_map/ppermute | solution.py:26
  96.2 4.4 %shard_map.149 = (bf16[512,896]{1,0:T(8,128)(2,1)}, bf16[512,1024]{1,0:T(8,128)(2,1)}) custom-call(s32[1]{0:T(128)} %bitcast.pos, bf16[128,1024]{1,0:T(8,128)(2,1)S(1)} %multiply_convert_fusion.3.own_ref, bf16[128,1024]{1,0:T(8,128)(2,1)S(1)} %collective-permute-done.9.left_ref, bf16[128,1024]{1,0:T(8,128)(2,1)S(1)} %collective-permute-done.10.right_ref, ...), custom_call_target="tpu_custom_call" | custom-call | flops 939524096 | bytes 3801088 | tf_op jit(solution)/shard_map/pallas_call | solution.py:142
  100.5 11.9 %all-to-all-start.2 = ((bf16[32,16,896]{2,1,0:T(8,128)(2,1)}), bf16[32,16,896]{2,1,0:T(8,128)(2,1)}, u32[]{:S(2)}, u32[]{:S(2)}) async-start(bf16[32,16,896]{2,1,0:T(8,128)(2,1)} %bitcast.59), calls=%async_computation.2 | async-start | bytes 1835008 | tf_op jit(solution)/shard_map/all_to_all | solution.py:270
  112.5 1.4 multiply_convert_fusion.2
  113.9 1.2 fusion.30
  115.2 2.8 %collective-permute-start.21 = (bf16[448,1024]{1,0:T(8,128)(2,1)S(1)}, bf16[448,1024]{1,0:T(8,128)(2,1)S(1)}, u32[]{:S(2)}, u32[]{:S(2)}) collective-permute-start(bf16[448,1024]{1,0:T(8,128)(2,1)S(1)} %slice.147), channel_id=1, source_target_pairs={{0,32},{32,0},{64,96},{96,64},{128,160},{160,128},{192,224},{224,1... | collective-permute-start | bytes 2752520 | tf_op jit(solution)/shard_map/ppermute | solution.py:21
  118.0 2.7 %collective-permute-start.18 = (bf16[128,2048]{1,0:T(8,128)(2,1)S(1)}, bf16[128,2048]{1,0:T(8,128)(2,1)S(1)}, u32[]{:S(2)}, u32[]{:S(2)}) collective-permute-start(bf16[128,2048]{1,0:T(8,128)(2,1)S(1)} %pad_maximum_fusion.2.own_ref), channel_id=1, source_target_pairs={{0,192},{32,224},{64,0},{96,32},{128,64},{160,96},{192,128},{224,1... | collective-permute-start | bytes 1572872 | tf_op jit(solution)/shard_map/ppermute | solution.py:26
  120.7 12.0 %collective-permute-done.17.left_ref = bf16[128,2048]{1,0:T(8,128)(2,1)S(1)} collective-permute-done((bf16[128,2048]{1,0:T(8,128)(2,1)S(1)}, bf16[128,2048]{1,0:T(8,128)(2,1)S(1)}, u32[]{:S(2)}, u32[]{:S(2)}) %collective-permute-start.17) | collective-permute-done | bytes 524320 | tf_op jit(solution)/shard_map/ppermute | solution.py:26
  132.9 2.7 %collective-permute-start.20 = (bf16[64,2048]{1,0:T(8,128)(2,1)S(1)}, bf16[64,2048]{1,0:T(8,128)(2,1)S(1)}, u32[]{:S(2)}, u32[]{:S(2)}) collective-permute-start(bf16[64,2048]{1,0:T(8,128)(2,1)S(1)} %slice.98), channel_id=1, source_target_pairs={{0,192},{32,224},{64,0},{96,32},{128,64},{160,96},{192,128},{224,1... | collective-permute-start | bytes 786440 | tf_op jit(solution)/shard_map/ppermute | solution.py:26
  135.6 1.3 fusion.3
  136.9 4.2 %collective-permute-done.19.top_ref = bf16[64,2048]{1,0:T(8,128)(2,1)S(1)} collective-permute-done((bf16[64,2048]{1,0:T(8,128)(2,1)S(1)}, bf16[64,2048]{1,0:T(8,128)(2,1)S(1)}, u32[]{:S(2)}, u32[]{:S(2)}) %collective-permute-start.19) | collective-permute-done | bytes 262176 | tf_op jit(solution)/shard_map/ppermute | solution.py:26
  141.0 6.2 %shard_map.150 = bf16[512,896]{1,0:T(8,128)(2,1)} custom-call(s32[1]{0:T(128)} %bitcast.pos, bf16[128,2048]{1,0:T(8,128)(2,1)S(1)} %pad_maximum_fusion.2.own_ref, bf16[128,2048]{1,0:T(8,128)(2,1)S(1)} %collective-permute-done.17.left_ref, bf16[128,2048]{1,0:T(8,128)(2,1)S(1)} %collective-permute-done.18.right_ref, ...), custom_call_target="tpu_custom_call" | custom-call | flops 1879048192 | bytes 6684672 | tf_op jit(solution)/shard_map/pallas_call | solution.py:142
  147.2 9.7 %all-to-all-start.3 = ((bf16[32,16,896]{2,1,0:T(8,128)(2,1)}), bf16[32,16,896]{2,1,0:T(8,128)(2,1)}, u32[]{:S(2)}, u32[]{:S(2)}) async-start(bf16[32,16,896]{2,1,0:T(8,128)(2,1)} %bitcast.58), calls=%async_computation.3 | async-start | bytes 1835008 | tf_op jit(solution)/shard_map/all_to_all | solution.py:270
  158.0 2.7 %collective-permute-start.24 = (bf16[448,1024]{1,0:T(8,128)(2,1)}, bf16[448,1024]{1,0:T(8,128)(2,1)}, u32[]{:S(2)}, u32[]{:S(2)}) collective-permute-start(bf16[448,1024]{1,0:T(8,128)(2,1)} %convert_element_type.133), channel_id=1, source_target_pairs={{0,16},{1,17},{2,18},{3,19},{4,20},{5,21},{6,22},{7,23},{8,24},{9,... | collective-permute-start | bytes 2752520 | tf_op jit(solution)/shard_map/ppermute | solution.py:31
  160.7 1.1 convert_element_type.130
  162.5 2.2 collective-permute-start.23
  164.8 1.8 fusion.12
  166.6 1.8 convolution_add_fusion
  169.3 3.2 %collective-permute-start.13 = (bf16[448,256]{1,0:T(8,128)(2,1)S(1)}, bf16[448,256]{1,0:T(8,128)(2,1)S(1)}, u32[]{:S(2)}, u32[]{:S(2)}) collective-permute-start(bf16[448,256]{1,0:T(8,128)(2,1)S(1)} %slice.149), channel_id=1, source_target_pairs={{0,32},{32,0},{64,96},{96,64},{128,160},{160,128},{192,224},{224,1... | collective-permute-start | bytes 688136 | tf_op jit(solution)/shard_map/ppermute | solution.py:21
  173.8 1.8 fusion.5
  175.6 14.5 %collective-permute-done.24 = bf16[448,1024]{1,0:T(8,128)(2,1)} collective-permute-done((bf16[448,1024]{1,0:T(8,128)(2,1)}, bf16[448,1024]{1,0:T(8,128)(2,1)}, u32[]{:S(2)}, u32[]{:S(2)}) %collective-permute-start.24) | collective-permute-done | bytes 917536 | tf_op jit(solution)/shard_map/ppermute | solution.py:31
  190.0 19.7 %collective-permute-done.22 = bf16[448,1024]{1,0:T(8,128)(2,1)} collective-permute-done((bf16[448,1024]{1,0:T(8,128)(2,1)}, bf16[448,1024]{1,0:T(8,128)(2,1)}, u32[]{:S(2)}, u32[]{:S(2)}) %collective-permute-start.22) | collective-permute-done | bytes 917536 | tf_op jit(solution)/shard_map/ppermute | solution.py:31
  209.7 19.7 %collective-permute-done.23 = bf16[448,1024]{1,0:T(8,128)(2,1)} collective-permute-done((bf16[448,1024]{1,0:T(8,128)(2,1)}, bf16[448,1024]{1,0:T(8,128)(2,1)}, u32[]{:S(2)}, u32[]{:S(2)}) %collective-permute-start.23) | collective-permute-done | bytes 917536 | tf_op jit(solution)/shard_map/ppermute | solution.py:31
  229.4 6.0 %divide_convert_fusion = (bf16[448,1024]{1,0:T(8,128)(2,1)}, f32[448,1024]{1,0:T(8,128)}, f32[448,1024]{1,0:T(8,128)}) fusion(bf16[448,1024]{1,0:T(8,128)(2,1)S(1)} %collective-permute-done.21, f32[896,1024]{1,0:T(8,128)} %copy-done.3, bf16[448,1024]{1,0:T(8,128)(2,1)} %collective-permute-done.23, f32[1,1024,448]{1,2,0:T(8,128)S(1)} %copy-done.4, ...), kind=kLoop, calls=%fused_computation.5 | loop fusion | flops 8257536 | bytes 13762561 | tf_op jit(solution)/shard_map/convert_element_type | solution.py:328
  235.4 1.7 fusion.2
  237.1 1.9 collective-permute-start.25
  239.0 1.1 collective-permute-done.25
  (94 shorter events, 9.1 us)
Async XLA Ops:
  0.6 4.2 %copy-start = (s32[1,32,32]{2,1,0:T(8,128)S(1)}, s32[1,32,32]{2,1,0:T(8,128)}, u32[]{:S(2)}) copy-start(s32[1,32,32]{2,1,0:T(8,128)} %param.13) | copy-start | bytes 12292
  0.6 16.5 %copy-start.1 = (bf16[1,448,1024]{2,1,0:T(8,128)(2,1)S(1)}, bf16[1,448,1024]{2,1,0:T(8,128)(2,1)}, u32[]{:S(2)}) copy-start(bf16[1,448,1024]{2,1,0:T(8,128)(2,1)} %param.17) | copy-start | bytes 2752516
  0.7 17.2 %copy-start.2 = (bf16[1,448,1024]{2,1,0:T(8,128)(2,1)S(1)}, bf16[1,448,1024]{2,1,0:T(8,128)(2,1)}, u32[]{:S(2)}) copy-start(bf16[1,448,1024]{2,1,0:T(8,128)(2,1)} %param.18) | copy-start | bytes 2752516
  0.7 17.7 %copy-start.18 = (bf16[256,448]{0,1:T(8,128)(2,1)S(1)}, bf16[256,448]{0,1:T(8,128)(2,1)}, u32[]{:S(2)}) copy-start(bf16[256,448]{0,1:T(8,128)(2,1)} %param.12) | copy-start | bytes 688132
  0.7 17.8 %copy-start.12 = (f32[1,32,32]{2,1,0:T(8,128)S(1)}, f32[1,32,32]{2,1,0:T(8,128)}, u32[]{:S(2)}) copy-start(f32[1,32,32]{2,1,0:T(8,128)} %param.15) | copy-start | bytes 12292
  0.7 4.6 %collective-permute-start = (bf16[448,256]{1,0:T(8,128)(2,1)}, bf16[448,256]{1,0:T(8,128)(2,1)S(1)}, u32[]{:S(2)}, u32[]{:S(2)}) collective-permute-start(bf16[448,256]{1,0:T(8,128)(2,1)} %bitcast.63), channel_id=1, source_target_pairs={{0,32},{32,0},{64,96},{96,64},{128,160},{160,128},{192,224},{224,1... | collective-permute-start | bytes 688136 | tf_op jit(solution)/shard_map/ppermute | solution.py:21
  5.0 19.3 %copy-start.15 = (s32[512]{0:T(512)}, s32[512]{0:T(512)S(1)}, u32[]{:S(2)}) copy-start(s32[512]{0:T(512)S(1)} %broadcast_select_fusion.1) | copy-start | bytes 6148
  7.6 31.7 %all-to-all-start = ((bf16[32,16,896]{2,1,0:T(8,128)(2,1)}), bf16[32,16,896]{2,1,0:T(8,128)(2,1)}, u32[]{:S(2)}, u32[]{:S(2)}) async-start(bf16[32,16,896]{2,1,0:T(8,128)(2,1)} %bitcast.4), calls=%async_computation | async-start | bytes 1835008 | tf_op jit(solution)/shard_map/all_to_all | solution.py:270
  17.1 7.2 %collective-permute-start.1 = (bf16[448,1024]{1,0:T(8,128)(2,1)S(1)}, bf16[448,1024]{1,0:T(8,128)(2,1)S(1)}, u32[]{:S(2)}, u32[]{:S(2)}) collective-permute-start(bf16[448,1024]{1,0:T(8,128)(2,1)S(1)} %bitcast.48), channel_id=1, source_target_pairs={{0,32},{32,0},{64,96},{96,64},{128,160},{160,128},{192,224},{224,1... | collective-permute-start | bytes 2752520 | tf_op jit(solution)/shard_map/ppermute | solution.py:21
  17.9 6.5 %collective-permute-start.2 = (bf16[448,1024]{1,0:T(8,128)(2,1)S(1)}, bf16[448,1024]{1,0:T(8,128)(2,1)}, u32[]{:S(2)}, u32[]{:S(2)}) collective-permute-start(bf16[448,1024]{1,0:T(8,128)(2,1)S(1)} %bitcast.50), channel_id=1, source_target_pairs={{0,32},{32,0},{64,96},{96,64},{128,160},{160,128},{192,224},{224,1... | collective-permute-start | bytes 2752520 | tf_op jit(solution)/shard_map/ppermute | solution.py:21
  18.0 12.2 %collective-permute-start.3 = (bf16[448,1024]{1,0:T(8,128)(2,1)}, bf16[448,1024]{1,0:T(8,128)(2,1)}, u32[]{:S(2)}, u32[]{:S(2)}) collective-permute-start(bf16[448,1024]{1,0:T(8,128)(2,1)} %bitcast.56), channel_id=1, source_target_pairs={{0,32},{32,0},{64,96},{96,64},{128,160},{160,128},{192,224},{224,1... | collective-permute-start | bytes 2752520 | tf_op jit(solution)/shard_map/ppermute | solution.py:21
  18.4 4.5 %collective-permute-start.4 = (bf16[448,256]{1,0:T(8,128)(2,1)S(1)}, bf16[448,256]{1,0:T(8,128)(2,1)S(1)}, u32[]{:S(2)}, u32[]{:S(2)}) collective-permute-start(bf16[448,256]{1,0:T(8,128)(2,1)S(1)} %bitcast.65), channel_id=1, source_target_pairs={{0,32},{32,0},{64,96},{96,64},{128,160},{160,128},{192,224},{224,1... | collective-permute-start | bytes 688136 | tf_op jit(solution)/shard_map/ppermute | solution.py:21
  19.2 11.0 %copy-start.13 = (f32[512]{0:T(512)}, f32[512]{0:T(512)S(1)}, u32[]{:S(2)}) copy-start(f32[512]{0:T(512)S(1)} %get-tuple-element.69) | copy-start | bytes 6148
  24.3 5.9 %copy-start.9 = (bf16[1,1024,448]{1,2,0:T(8,128)(2,1)S(1)}, bf16[1,1024,448]{1,2,0:T(8,128)(2,1)}, u32[]{:S(2)}) copy-start(bf16[1,1024,448]{1,2,0:T(8,128)(2,1)} %param.19) | copy-start | bytes 2752516
  45.2 12.8 %copy-start.7 = (bf16[256,2048]{1,0:T(8,128)(2,1)S(1)}, bf16[256,2048]{1,0:T(8,128)(2,1)}, u32[]{:S(2)}) copy-start(bf16[256,2048]{1,0:T(8,128)(2,1)} %get-tuple-element.37) | copy-start | bytes 3145732
  45.2 10.9 %collective-permute-start.5 = (bf16[128,2048]{1,0:T(8,128)(2,1)}, bf16[128,2048]{1,0:T(8,128)(2,1)S(1)}, u32[]{:S(2)}, u32[]{:S(2)}) collective-permute-start(bf16[128,2048]{1,0:T(8,128)(2,1)} %get-tuple-element.38), channel_id=1, source_target_pairs={{0,192},{32,224},{64,0},{96,32},{128,64},{160,96},{192,128},{224,1... | collective-permute-start | bytes 1572872 | tf_op jit(solution)/shard_map/ppermute | solution.py:26
  47.9 10.1 %collective-permute-start.6 = (bf16[128,2048]{1,0:T(8,128)(2,1)}, bf16[128,2048]{1,0:T(8,128)(2,1)S(1)}, u32[]{:S(2)}, u32[]{:S(2)}) collective-permute-start(bf16[128,2048]{1,0:T(8,128)(2,1)} %get-tuple-element.39), channel_id=1, source_target_pairs={{0,64},{32,96},{64,128},{96,160},{128,192},{160,224},{192,0},{224,... | collective-permute-start | bytes 1572872 | tf_op jit(solution)/shard_map/ppermute | solution.py:26
  47.9 30.2 %all-to-all-start.1 = ((bf16[32,16,896]{2,1,0:T(8,128)(2,1)}), bf16[32,16,896]{2,1,0:T(8,128)(2,1)S(1)}, u32[]{:S(2)}, u32[]{:S(2)}) async-start(bf16[32,16,896]{2,1,0:T(8,128)(2,1)} %bitcast.12), calls=%async_computation.1 | async-start | bytes 1835008 | tf_op jit(solution)/shard_map/all_to_all | solution.py:270
  58.0 8.1 %copy-start.10 = (bf16[128,2048]{1,0:T(8,128)(2,1)}, bf16[128,2048]{1,0:T(8,128)(2,1)S(1)}, u32[]{:S(2)}) copy-start(bf16[128,2048]{1,0:T(8,128)(2,1)S(1)} %collective-permute-done.6) | copy-start | bytes 1572868
  58.1 8.0 %collective-permute-start.7 = (bf16[64,2048]{1,0:T(8,128)(2,1)S(1)}, bf16[64,2048]{1,0:T(8,128)(2,1)S(1)}, u32[]{:S(2)}, u32[]{:S(2)}) collective-permute-start(bf16[64,2048]{1,0:T(8,128)(2,1)S(1)} %get-tuple-element.40), channel_id=1, source_target_pairs={{0,64},{32,96},{64,128},{96,160},{128,192},{160,224},{192,0},{224,... | collective-permute-start | bytes 786440 | tf_op jit(solution)/shard_map/ppermute | solution.py:26
  58.2 7.9 %collective-permute-start.8 = (bf16[64,2048]{1,0:T(8,128)(2,1)S(1)}, bf16[64,2048]{1,0:T(8,128)(2,1)S(1)}, u32[]{:S(2)}, u32[]{:S(2)}) collective-permute-start(bf16[64,2048]{1,0:T(8,128)(2,1)S(1)} %get-tuple-element.41), channel_id=1, source_target_pairs={{0,192},{32,224},{64,0},{96,32},{128,64},{160,96},{192,128},{224,1... | collective-permute-start | bytes 786440 | tf_op jit(solution)/shard_map/ppermute | solution.py:26
  67.4 17.7 %collective-permute-start.9 = (bf16[128,1024]{1,0:T(8,128)(2,1)S(1)}, bf16[128,1024]{1,0:T(8,128)(2,1)S(1)}, u32[]{:S(2)}, u32[]{:S(2)}) collective-permute-start(bf16[128,1024]{1,0:T(8,128)(2,1)S(1)} %multiply_convert_fusion.3.own_ref), channel_id=1, source_target_pairs={{0,64},{32,96},{64,128},{96,160},{128,192},{160,224},{192,0},{224,... | collective-permute-start | bytes 786440 | tf_op jit(solution)/shard_map/ppermute | solution.py:26
  67.5 19.7 %collective-permute-start.10 = (bf16[128,1024]{1,0:T(8,128)(2,1)S(1)}, bf16[128,1024]{1,0:T(8,128)(2,1)S(1)}, u32[]{:S(2)}, u32[]{:S(2)}) collective-permute-start(bf16[128,1024]{1,0:T(8,128)(2,1)S(1)} %multiply_convert_fusion.3.own_ref), channel_id=1, source_target_pairs={{0,192},{32,224},{64,0},{96,32},{128,64},{160,96},{192,128},{224,1... | collective-permute-start | bytes 786440 | tf_op jit(solution)/shard_map/ppermute | solution.py:26
  81.5 30.9 %collective-permute-start.16 = (bf16[128,1024]{1,0:T(8,128)(2,1)}, bf16[128,1024]{1,0:T(8,128)(2,1)S(1)}, u32[]{:S(2)}, u32[]{:S(2)}) collective-permute-start(bf16[128,1024]{1,0:T(8,128)(2,1)} %get-tuple-element.47), channel_id=1, source_target_pairs={{0,192},{32,224},{64,0},{96,32},{128,64},{160,96},{192,128},{224,1... | collective-permute-start | bytes 786440 | tf_op jit(solution)/shard_map/ppermute | solution.py:26
  83.8 28.6 %collective-permute-start.15 = (bf16[128,1024]{1,0:T(8,128)(2,1)}, bf16[128,1024]{1,0:T(8,128)(2,1)S(1)}, u32[]{:S(2)}, u32[]{:S(2)}) collective-permute-start(bf16[128,1024]{1,0:T(8,128)(2,1)} %get-tuple-element.46), channel_id=1, source_target_pairs={{0,64},{32,96},{64,128},{96,160},{128,192},{160,224},{192,0},{224,... | collective-permute-start | bytes 786440 | tf_op jit(solution)/shard_map/ppermute | solution.py:26
  83.8 28.6 %collective-permute-start.14 = (bf16[128,1024]{1,0:T(8,128)(2,1)}, bf16[128,1024]{1,0:T(8,128)(2,1)}, u32[]{:S(2)}, u32[]{:S(2)}) collective-permute-start(bf16[128,1024]{1,0:T(8,128)(2,1)} %get-tuple-element.45), channel_id=1, source_target_pairs={{0,128},{32,160},{64,192},{96,224},{128,0},{160,32},{192,64},{224,... | collective-permute-start | bytes 786440 | tf_op jit(solution)/shard_map/ppermute | solution.py:26
  85.1 11.1 %collective-permute-start.11 = (bf16[64,1024]{1,0:T(8,128)(2,1)S(1)}, bf16[64,1024]{1,0:T(8,128)(2,1)S(1)}, u32[]{:S(2)}, u32[]{:S(2)}) collective-permute-start(bf16[64,1024]{1,0:T(8,128)(2,1)S(1)} %slice.93), channel_id=1, source_target_pairs={{0,64},{32,96},{64,128},{96,160},{128,192},{160,224},{192,0},{224,... | collective-permute-start | bytes 393224 | tf_op jit(solution)/shard_map/ppermute | solution.py:26
  87.2 9.0 %collective-permute-start.12 = (bf16[64,1024]{1,0:T(8,128)(2,1)S(1)}, bf16[64,1024]{1,0:T(8,128)(2,1)S(1)}, u32[]{:S(2)}, u32[]{:S(2)}) collective-permute-start(bf16[64,1024]{1,0:T(8,128)(2,1)S(1)} %slice.94), channel_id=1, source_target_pairs={{0,192},{32,224},{64,0},{96,32},{128,64},{160,96},{192,128},{224,1... | collective-permute-start | bytes 393224 | tf_op jit(solution)/shard_map/ppermute | solution.py:26
  96.2 16.3 %copy-start.11 = (bf16[128,1024]{1,0:T(8,128)(2,1)S(1)}, bf16[128,1024]{1,0:T(8,128)(2,1)}, u32[]{:S(2)}) copy-start(bf16[128,1024]{1,0:T(8,128)(2,1)} %get-tuple-element.48) | copy-start | bytes 786436
  100.5 46.7 %all-to-all-start.2 = ((bf16[32,16,896]{2,1,0:T(8,128)(2,1)}), bf16[32,16,896]{2,1,0:T(8,128)(2,1)}, u32[]{:S(2)}, u32[]{:S(2)}) async-start(bf16[32,16,896]{2,1,0:T(8,128)(2,1)} %bitcast.59), calls=%async_computation.2 | async-start | bytes 1835008 | tf_op jit(solution)/shard_map/all_to_all | solution.py:270
  115.1 21.8 %copy-start.3 = (f32[896,1024]{1,0:T(8,128)}, f32[896,1024]{1,0:T(8,128)S(1)}, u32[]{:S(2)}) copy-start(f32[896,1024]{1,0:T(8,128)S(1)} %fusion.30) | copy-start | bytes 11010052
  115.2 20.4 %collective-permute-start.21 = (bf16[448,1024]{1,0:T(8,128)(2,1)S(1)}, bf16[448,1024]{1,0:T(8,128)(2,1)S(1)}, u32[]{:S(2)}, u32[]{:S(2)}) collective-permute-start(bf16[448,1024]{1,0:T(8,128)(2,1)S(1)} %slice.147), channel_id=1, source_target_pairs={{0,32},{32,0},{64,96},{96,64},{128,160},{160,128},{192,224},{224,1... | collective-permute-start | bytes 2752520 | tf_op jit(solution)/shard_map/ppermute | solution.py:21
  118.0 14.7 %collective-permute-start.17 = (bf16[128,2048]{1,0:T(8,128)(2,1)S(1)}, bf16[128,2048]{1,0:T(8,128)(2,1)S(1)}, u32[]{:S(2)}, u32[]{:S(2)}) collective-permute-start(bf16[128,2048]{1,0:T(8,128)(2,1)S(1)} %pad_maximum_fusion.2.own_ref), channel_id=1, source_target_pairs={{0,64},{32,96},{64,128},{96,160},{128,192},{160,224},{192,0},{224,... | collective-permute-start | bytes 1572872 | tf_op jit(solution)/shard_map/ppermute | solution.py:26
  118.0 14.8 %collective-permute-start.18 = (bf16[128,2048]{1,0:T(8,128)(2,1)S(1)}, bf16[128,2048]{1,0:T(8,128)(2,1)S(1)}, u32[]{:S(2)}, u32[]{:S(2)}) collective-permute-start(bf16[128,2048]{1,0:T(8,128)(2,1)S(1)} %pad_maximum_fusion.2.own_ref), channel_id=1, source_target_pairs={{0,192},{32,224},{64,0},{96,32},{128,64},{160,96},{192,128},{224,1... | collective-permute-start | bytes 1572872 | tf_op jit(solution)/shard_map/ppermute | solution.py:26
  132.7 8.3 %collective-permute-start.19 = (bf16[64,2048]{1,0:T(8,128)(2,1)S(1)}, bf16[64,2048]{1,0:T(8,128)(2,1)S(1)}, u32[]{:S(2)}, u32[]{:S(2)}) collective-permute-start(bf16[64,2048]{1,0:T(8,128)(2,1)S(1)} %slice.97), channel_id=1, source_target_pairs={{0,64},{32,96},{64,128},{96,160},{128,192},{160,224},{192,0},{224,... | collective-permute-start | bytes 786440 | tf_op jit(solution)/shard_map/ppermute | solution.py:26
  132.9 8.2 %collective-permute-start.20 = (bf16[64,2048]{1,0:T(8,128)(2,1)S(1)}, bf16[64,2048]{1,0:T(8,128)(2,1)S(1)}, u32[]{:S(2)}, u32[]{:S(2)}) collective-permute-start(bf16[64,2048]{1,0:T(8,128)(2,1)S(1)} %slice.98), channel_id=1, source_target_pairs={{0,192},{32,224},{64,0},{96,32},{128,64},{160,96},{192,128},{224,1... | collective-permute-start | bytes 786440 | tf_op jit(solution)/shard_map/ppermute | solution.py:26
  141.0 15.9 %copy-start.14 = (f32[512]{0:T(512)S(1)}, f32[512]{0:T(512)}, u32[]{:S(2)}) copy-start(f32[512]{0:T(512)} %copy-done.13) | copy-start | bytes 6148
  147.2 9.7 %copy-start.4 = (f32[1,1024,448]{1,2,0:T(8,128)S(1)}, f32[1,1024,448]{1,2,0:T(8,128)}, u32[]{:S(2)}) copy-start(f32[1,1024,448]{1,2,0:T(8,128)} %param.21) | copy-start | bytes 5505028
  147.2 88.2 %all-to-all-start.3 = ((bf16[32,16,896]{2,1,0:T(8,128)(2,1)}), bf16[32,16,896]{2,1,0:T(8,128)(2,1)}, u32[]{:S(2)}, u32[]{:S(2)}) async-start(bf16[32,16,896]{2,1,0:T(8,128)(2,1)} %bitcast.58), calls=%async_computation.3 | async-start | bytes 1835008 | tf_op jit(solution)/shard_map/all_to_all | solution.py:270
  156.9 3.8 %copy-start.5 = (f32[1,1024,448]{1,2,0:T(8,128)S(1)}, f32[1,1024,448]{1,2,0:T(8,128)}, u32[]{:S(2)}) copy-start(f32[1,1024,448]{1,2,0:T(8,128)} %param.20) | copy-start | bytes 5505028
  158.0 6.7 %copy-start.16 = (s32[512]{0:T(512)S(1)}, s32[512]{0:T(512)}, u32[]{:S(2)}) copy-start(s32[512]{0:T(512)} %copy-done.15) | copy-start | bytes 6148
  158.0 32.0 %collective-permute-start.24 = (bf16[448,1024]{1,0:T(8,128)(2,1)}, bf16[448,1024]{1,0:T(8,128)(2,1)}, u32[]{:S(2)}, u32[]{:S(2)}) collective-permute-start(bf16[448,1024]{1,0:T(8,128)(2,1)} %convert_element_type.133), channel_id=1, source_target_pairs={{0,16},{1,17},{2,18},{3,19},{4,20},{5,21},{6,22},{7,23},{8,24},{9,... | collective-permute-start | bytes 2752520 | tf_op jit(solution)/shard_map/ppermute | solution.py:31
  160.7 5.8 %copy-start.17 = (bf16[512]{0:T(512)(128)(2,1)S(1)}, bf16[512]{0:T(512)(128)(2,1)}, u32[]{:S(2)}) copy-start(bf16[512]{0:T(512)(128)(2,1)} %get-tuple-element.68) | copy-start | bytes 3076
  161.8 47.9 %collective-permute-start.22 = (bf16[448,1024]{1,0:T(8,128)(2,1)}, bf16[448,1024]{1,0:T(8,128)(2,1)}, u32[]{:S(2)}, u32[]{:S(2)}) collective-permute-start(bf16[448,1024]{1,0:T(8,128)(2,1)} %convert_element_type.130), channel_id=1, source_target_pairs={{0,16},{1,17},{2,18},{3,19},{4,20},{5,21},{6,22},{7,23},{8,24},{9,... | collective-permute-start | bytes 2752520 | tf_op jit(solution)/shard_map/ppermute | solution.py:31
  162.5 66.8 %collective-permute-start.23 = (bf16[448,1024]{1,0:T(8,128)(2,1)}, bf16[448,1024]{1,0:T(8,128)(2,1)}, u32[]{:S(2)}, u32[]{:S(2)}) collective-permute-start(bf16[448,1024]{1,0:T(8,128)(2,1)} %fusion.3), channel_id=1, source_target_pairs={{0,16},{1,17},{2,18},{3,19},{4,20},{5,21},{6,22},{7,23},{8,24},{9,... | collective-permute-start | bytes 2752520 | tf_op jit(solution)/shard_map/ppermute | solution.py:31
  166.5 6.0 %copy-start.19 = (s32[16]{0:T(128)S(1)}, s32[16]{0:T(128)}, u32[]{:S(2)}) copy-start(s32[16]{0:T(128)} %param.16) | copy-start | bytes 196
  169.3 4.5 %collective-permute-start.13 = (bf16[448,256]{1,0:T(8,128)(2,1)S(1)}, bf16[448,256]{1,0:T(8,128)(2,1)S(1)}, u32[]{:S(2)}, u32[]{:S(2)}) collective-permute-start(bf16[448,256]{1,0:T(8,128)(2,1)S(1)} %slice.149), channel_id=1, source_target_pairs={{0,32},{32,0},{64,96},{96,64},{128,160},{160,128},{192,224},{224,1... | collective-permute-start | bytes 688136 | tf_op jit(solution)/shard_map/ppermute | solution.py:21
  237.1 3.0 %collective-permute-start.25 = (bf16[448,256]{1,0:T(8,128)(2,1)S(1)}, bf16[448,256]{1,0:T(8,128)(2,1)S(1)}, u32[]{:S(2)}, u32[]{:S(2)}) collective-permute-start(bf16[448,256]{1,0:T(8,128)(2,1)S(1)} %slice.148), channel_id=1, source_target_pairs={{0,32},{32,0},{64,96},{96,64},{128,160},{160,128},{192,224},{224,1... | collective-permute-start | bytes 688136 | tf_op jit(solution)/shard_map/ppermute | solution.py:21
  (2 other events, 2.4 us)

commit v6 on v5

--- a/solution.py
+++ b/solution.py
@@ -91,72 +91,42 @@
     width = right.shape[0]
     total = 4 * rows
     mid = rows // 2
-    tile = 512
-    steps = depth // tile
-
-    def body(pos, own_ref, left_ref, right_ref, top_ref, low_ref, w_ref, out, *refs):
-        full, acc = refs[-2:]
-        k = pl.program_id(0)
-
-        @pl.when(k == 0)
-        def _():
-            for step, offset, ref in (
-                (0, 0, own_ref),
-                (3, 0, left_ref),
-                (1, 0, right_ref),
-                (2, 0, top_ref),
-                (2, mid, low_ref),
-            ):
-                at = lax.rem(pos[0] + step, 4) * rows + offset
-                size = ref.shape[0]
-                if keep:
-                    refs[0][pl.ds(pl.multiple_of(at, mid), size), :] = ref[...]
-                for t in range(steps):
-                    full[t, pl.ds(pl.multiple_of(at, mid), size), :] = ref[
-                        :, t * tile : (t + 1) * tile
-                    ]
-
-        term = dot(full[k], w_ref[...], 1, 1)
-
-        @pl.when(k == 0)
-        def _():
-            acc[...] = term
-
-        @pl.when(jnp.logical_and(k > 0, k < steps - 1))
-        def _():
-            acc[...] += term
-
-        @pl.when(k == steps - 1)
-        def _():
-            out[...] = (acc[...] + term).astype(BF)
-
-    def whole(shape):
-        return pl.BlockSpec(shape, lambda k, pos: (0,) * len(shape))
-
+
+    def body(pos, own_ref, left_ref, right_ref, top_ref, low_ref, w_ref, out, full):
+        for step, offset, ref in (
+            (0, 0, own_ref),
+            (3, 0, left_ref),
+            (1, 0, right_ref),
+            (2, 0, top_ref),
+            (2, mid, low_ref),
+        ):
+            at = lax.rem(pos[0] + step, 4) * rows + offset
+            full[pl.ds(pl.multiple_of(at, mid), ref.shape[0]), :] = ref[...]
+        out[...] = dot(full[...], w_ref[...], 1, 1).astype(BF)
+
+    vmem = pl.BlockSpec(memory_space=pltpu.VMEM)
     out_shape = [pltpu.HBM((total, width), BF)]
-    out_specs = [whole((total, width))]
+    out_specs = [pl.BlockSpec((total, width), lambda k: (0, 0))]
+    scratch = []
     if keep:
         out_shape.append(pltpu.HBM((total, depth), BF))
-        out_specs.append(whole((total, depth)))
-    scratch = [pltpu.VMEM((steps, total, tile), BF), pltpu.VMEM((total, width), F32)]
+        out_specs.append(pl.BlockSpec((total, depth), lambda k: (0, 0)))
+    else:
+        scratch.append(pltpu.VMEM((total, depth), BF))
     return pl.pallas_call(
         body,
         out_shape=out_shape,
-        grid_spec=pltpu.PrefetchScalarGridSpec(
-            num_scalar_prefetch=1,
-            grid=(steps,),
-            in_specs=[whole(part.shape) for part in parts]
-            + [pl.BlockSpec((width, tile), lambda k, pos: (0, k))],
-            out_specs=out_specs,
-            scratch_shapes=scratch,
-        ),
+        grid=(1,),
+        in_specs=[pl.BlockSpec(memory_space=pltpu.SMEM)] + [vmem] * 6,
+        out_specs=out_specs,
+        scratch_shapes=scratch,
         compiler_params=pltpu.CompilerParams(vmem_limit_bytes=24 << 20),
         cost_estimate=pl.CostEstimate(
             flops=2 * total * depth * width,
             bytes_accessed=2 * (total * depth + depth * width + total * width),
             transcendentals=0,
         ),
-    )(y_pos.reshape(1), *parts, pltpu.with_memory_space_constraint(right, pltpu.HBM))
+    )(y_pos.reshape(1), *parts, right)
 
 
 RING_UNITS = ((2, 0), (1, 1), (2, 1), (3, 0), (0, 0), (0, 1), (1, 0), (3, 1))
@@ -280,15 +250,15 @@
     far_up = core_swap(up_weight[0])
     gate_up = join_weights(gate_weight[0], up_weight[0], far_gate, far_up)
     down_cols = pair_rows(down_weight[0].T)
+    moment_one = first_moment[0].T
+    moment_two = second_moment[0].T
+    far_one = expert_swap(tie(moment_one, grad_cols).astype(BF))
+    far_two = expert_swap(tie(moment_two, grad_cols).astype(BF))
+
     arrived, gate_up, down_cols, grad_rows = lax.optimization_barrier(
         (arrived, gate_up, down_cols, grad_rows)
     )
-    moment_one = first_moment[0].T
-    moment_two = second_moment[0].T
     arrived_grad = exchange(grad_rows)
-    far_one = expert_swap(tie(moment_one, arrived).astype(BF))
-    far_two = expert_swap(tie(moment_two, arrived).astype(BF))
-
     hidden_units = down_weight.shape[1]
     half = rows // (2 * chips)
     products = ordered_dot(y_pos, arrived, gate_up, RING_UNITS, (2 * half, 2 * half, 4 * half))

time: 242 us -> 237 us (0.979)
  Pallas kernels: 25.6 us -> 21 us
    pallas_call x2, Pallas kernels: 10.6 us -> 5.8 us  [gathered_dot(): pl.pallas_call(body, out_shape=out_shape, grid=(1,), in_specs=[pl.BlockSp...]
  transfers between devices with their start and end apart: 30 -> 30, of which waited for: 13 -> 13; matrix products, arithmetic and copies ran while one was open for 11% -> 11% of each run, Pallas kernels for 8% -> 6%
where the time goes in v6:
time: 237 us; the launch traced here: 236 us
  waiting for transfers between devices  105 us (44%)
  starting transfers between devices  77.3 us (33%)
  Pallas kernels  21 us (9%)
  other arithmetic  19.3 us (8%)
  matrix products  10.2 us (4%)
    ppermute x3, waiting for transfers between devices, expert_swap(): lax.ppermute(block, 'expert', [(i, i ^ count // 2) for i in range(count)])  53.8 us
    all_to_all x4, starting transfers between devices, exchange(): lax.all_to_all(block.reshape(experts, own_slots, pair_cols), 'expert', 0,...  39.1 us
    ppermute x15, waiting for transfers between devices, chip_shift(): lax.ppermute(block, 'dp', [(i, (i + 2 * step) % count) for i in range(cou...  31.6 us
    ppermute x15, starting transfers between devices, chip_shift(): lax.ppermute(block, 'dp', [(i, (i + 2 * step) % count) for i in range(cou...  20.1 us
    all_to_all x4, waiting for transfers between devices, exchange(): lax.all_to_all(block.reshape(experts, own_slots, pair_cols), 'expert', 0,...  14.6 us
    ppermute x8, starting transfers between devices, core_swap(): lax.ppermute(block, 'dp', [(i, i ^ 1) for i in range(lax.axis_size('dp'))])  12.5 us
    dot_general x6, matrix products, dot(): lax.dot_general(a, b, (((ca,), (cb,)), ((), ())), preferred_element_type=...  10.2 us
    pallas_call x2, Pallas kernels, ordered_dot(): pl.pallas_call(body, out_shape=[pltpu.HBM((size, width), BF) for size in...  9.3 us
  transfers between devices with their start and end apart: 30, of which 13 were waited for; matrix products, arithmetic and copies ran while one was open for 11% of the time, Pallas kernels for 6%

profile of v6, /device:TPU:1, one launch (start us, length us, event | category | flops | bytes accessed | tf_op | source)
XLA Modules:
  0.0 236.3 jit_solution(995777506648311021)
XLA Ops:
  0.7 3.3 %collective-permute-start = (bf16[448,256]{1,0:T(8,128)(2,1)}, bf16[448,256]{1,0:T(8,128)(2,1)S(1)}, u32[]{:S(2)}, u32[]{:S(2)}) collective-permute-start(bf16[448,256]{1,0:T(8,128)(2,1)} %bitcast.63), channel_id=1, source_target_pairs={{0,32},{32,0},{64,96},{96,64},{128,160},{160,128},{192,224},{224,1... | collective-permute-start | bytes 688136 | tf_op jit(solution)/shard_map/ppermute | solution.py:21
  5.3 2.3 convolution_convert_fusion
  7.6 9.4 %all-to-all-start = ((bf16[32,16,896]{2,1,0:T(8,128)(2,1)}), bf16[32,16,896]{2,1,0:T(8,128)(2,1)}, u32[]{:S(2)}, u32[]{:S(2)}) async-start(bf16[32,16,896]{2,1,0:T(8,128)(2,1)} %bitcast.4), calls=%async_computation | async-start | bytes 1835008 | tf_op jit(solution)/shard_map/all_to_all | solution.py:240
  19.2 3.7 %collective-permute-done.4 = bf16[448,256]{1,0:T(8,128)(2,1)S(1)} collective-permute-done((bf16[448,256]{1,0:T(8,128)(2,1)S(1)}, bf16[448,256]{1,0:T(8,128)(2,1)S(1)}, u32[]{:S(2)}, u32[]{:S(2)}) %collective-permute-start.4) | collective-permute-done | bytes 229408 | tf_op jit(solution)/shard_map/ppermute | solution.py:21
  22.9 1.4 multiply_convert_fusion
  24.3 5.8 %shard_map.146.right_ref.w_ref = bf16[896,2048]{1,0:T(8,128)(2,1)} custom-call(bf16[448,1024]{1,0:T(8,128)(2,1)S(1)} %bitcast.49, bf16[448,1024]{1,0:T(8,128)(2,1)S(1)} %bitcast.51, bf16[448,1024]{1,0:T(8,128)(2,1)S(1)} %collective-permute-done.1.gate_b, bf16[448,1024]{1,0:T(8,128)(2,1)} %collective-permute-done.2.up_b), custom_call_target="tpu_custom_call" | custom-call | bytes 7340032 | tf_op jit(solution)/shard_map/pallas_call | solution.py:185
  30.2 2.6 %pad_maximum_fusion.right_ref.w_ref = bf16[896,1024]{1,0:T(8,128)(2,1)} fusion(bf16[448,1024]{1,0:T(8,128)(2,1)} %collective-permute-done.3, bf16[448,1024]{1,0:T(8,128)(2,1)S(1)} %bitcast.57), kind=kLoop, calls=%fused_computation.4 | loop fusion | flops 3670016 | bytes 3670016 | tf_op jit(solution)/shard_map/concatenate | solution.py:161
  32.8 6.6 %all-to-all-done = bf16[32,16,896]{2,1,0:T(8,128)(2,1)} async-done(((bf16[32,16,896]{2,1,0:T(8,128)(2,1)}), bf16[32,16,896]{2,1,0:T(8,128)(2,1)}, u32[]{:S(2)}, u32[]{:S(2)}) %all-to-all-start) | async-done | bytes 917536 | tf_op jit(solution)/shard_map/all_to_all | solution.py:240
  39.4 5.8 %shard_map.147 = (bf16[128,2048]{1,0:T(8,128)(2,1)}, bf16[128,2048]{1,0:T(8,128)(2,1)}, bf16[256,2048]{1,0:T(8,128)(2,1)}) custom-call(s32[1]{0:T(128)} %bitcast.pos, bf16[512,896]{1,0:T(8,128)(2,1)} %bitcast.5.left_ref, bf16[896,2048]{1,0:T(8,128)(2,1)} %shard_map.146.right_ref.w_ref), custom_call_target="tpu_custom_call" | custom-call | flops 1879048192 | bytes 6684672 | tf_op jit(solution)/shard_map/pallas_call | solution.py:66
  45.2 2.7 %collective-permute-start.5 = (bf16[128,2048]{1,0:T(8,128)(2,1)}, bf16[128,2048]{1,0:T(8,128)(2,1)S(1)}, u32[]{:S(2)}, u32[]{:S(2)}) collective-permute-start(bf16[128,2048]{1,0:T(8,128)(2,1)} %get-tuple-element.38), channel_id=1, source_target_pairs={{0,192},{32,224},{64,0},{96,32},{128,64},{160,96},{192,128},{224,1... | collective-permute-start | bytes 1572872 | tf_op jit(solution)/shard_map/ppermute | solution.py:26
  47.9 8.1 %all-to-all-start.1 = ((bf16[32,16,896]{2,1,0:T(8,128)(2,1)}), bf16[32,16,896]{2,1,0:T(8,128)(2,1)S(1)}, u32[]{:S(2)}, u32[]{:S(2)}) async-start(bf16[32,16,896]{2,1,0:T(8,128)(2,1)} %bitcast.12), calls=%async_computation.1 | async-start | bytes 1835008 | tf_op jit(solution)/shard_map/all_to_all | solution.py:240
  56.1 1.9 collective-permute-done.6
  58.2 2.7 %collective-permute-start.8 = (bf16[64,2048]{1,0:T(8,128)(2,1)S(1)}, bf16[64,2048]{1,0:T(8,128)(2,1)S(1)}, u32[]{:S(2)}, u32[]{:S(2)}) collective-permute-start(bf16[64,2048]{1,0:T(8,128)(2,1)S(1)} %get-tuple-element.41), channel_id=1, source_target_pairs={{0,192},{32,224},{64,0},{96,32},{128,64},{160,96},{192,128},{224,1... | collective-permute-start | bytes 786440 | tf_op jit(solution)/shard_map/ppermute | solution.py:26
  60.9 5.2 %collective-permute-done.7 = bf16[64,2048]{1,0:T(8,128)(2,1)S(1)} collective-permute-done((bf16[64,2048]{1,0:T(8,128)(2,1)S(1)}, bf16[64,2048]{1,0:T(8,128)(2,1)S(1)}, u32[]{:S(2)}, u32[]{:S(2)}) %collective-permute-start.7) | collective-permute-done | bytes 262176 | tf_op jit(solution)/shard_map/ppermute | solution.py:26
  66.1 1.2 convert_add_fusion.2
  67.5 2.7 %collective-permute-start.10 = (bf16[128,1024]{1,0:T(8,128)(2,1)S(1)}, bf16[128,1024]{1,0:T(8,128)(2,1)S(1)}, u32[]{:S(2)}, u32[]{:S(2)}) collective-permute-start(bf16[128,1024]{1,0:T(8,128)(2,1)S(1)} %multiply_convert_fusion.3.own_ref), channel_id=1, source_target_pairs={{0,192},{32,224},{64,0},{96,32},{128,64},{160,96},{192,128},{224,1... | collective-permute-start | bytes 786440 | tf_op jit(solution)/shard_map/ppermute | solution.py:26
  70.2 8.0 %all-to-all-done.1 = bf16[32,16,896]{2,1,0:T(8,128)(2,1)S(1)} async-done(((bf16[32,16,896]{2,1,0:T(8,128)(2,1)}), bf16[32,16,896]{2,1,0:T(8,128)(2,1)S(1)}, u32[]{:S(2)}, u32[]{:S(2)}) %all-to-all-start.1) | async-done | bytes 917536 | tf_op jit(solution)/shard_map/all_to_all | solution.py:240
  78.2 3.5 %shard_map.148 = (bf16[128,1024]{1,0:T(8,128)(2,1)}, bf16[128,1024]{1,0:T(8,128)(2,1)}, bf16[128,1024]{1,0:T(8,128)(2,1)}, bf16[128,1024]{1,0:T(8,128)(2,1)}) custom-call(s32[1]{0:T(128)} %bitcast.pos, bf16[512,896]{1,0:T(8,128)(2,1)S(1)} %bitcast.46, bf16[896,1024]{1,0:T(8,128)(2,1)} %pad_maximum_fusion.right_ref.w_ref), custom_call_target="tpu_custom_call" | custom-call | flops 939524096 | bytes 3801088 | tf_op jit(solution)/shard_map/pallas_call | solution.py:66
  81.7 2.3 collective-permute-start.16
  84.0 1.2 collective-permute-start.14
  85.2 2.1 collective-permute-start.11
  88.1 8.3 %collective-permute-done.11.top_ref = bf16[64,1024]{1,0:T(8,128)(2,1)S(1)} collective-permute-done((bf16[64,1024]{1,0:T(8,128)(2,1)S(1)}, bf16[64,1024]{1,0:T(8,128)(2,1)S(1)}, u32[]{:S(2)}, u32[]{:S(2)}) %collective-permute-start.11) | collective-permute-done | bytes 131104 | tf_op jit(solution)/shard_map/ppermute | solution.py:26
  96.3 2.3 shard_map.149
  98.6 11.9 %all-to-all-start.2 = ((bf16[32,16,896]{2,1,0:T(8,128)(2,1)}), bf16[32,16,896]{2,1,0:T(8,128)(2,1)}, u32[]{:S(2)}, u32[]{:S(2)}) async-start(bf16[32,16,896]{2,1,0:T(8,128)(2,1)} %bitcast.59), calls=%async_computation.2 | async-start | bytes 1835008 | tf_op jit(solution)/shard_map/all_to_all | solution.py:240
  110.5 1.4 multiply_convert_fusion.2
  112.0 1.2 fusion.26
  113.3 2.7 %collective-permute-start.21 = (bf16[448,1024]{1,0:T(8,128)(2,1)S(1)}, bf16[448,1024]{1,0:T(8,128)(2,1)S(1)}, u32[]{:S(2)}, u32[]{:S(2)}) collective-permute-start(bf16[448,1024]{1,0:T(8,128)(2,1)S(1)} %slice.147), channel_id=1, source_target_pairs={{0,32},{32,0},{64,96},{96,64},{128,160},{160,128},{192,224},{224,1... | collective-permute-start | bytes 2752520 | tf_op jit(solution)/shard_map/ppermute | solution.py:21
  116.0 2.7 %collective-permute-start.18 = (bf16[128,2048]{1,0:T(8,128)(2,1)S(1)}, bf16[128,2048]{1,0:T(8,128)(2,1)S(1)}, u32[]{:S(2)}, u32[]{:S(2)}) collective-permute-start(bf16[128,2048]{1,0:T(8,128)(2,1)S(1)} %pad_maximum_fusion.2.own_ref), channel_id=1, source_target_pairs={{0,192},{32,224},{64,0},{96,32},{128,64},{160,96},{192,128},{224,1... | collective-permute-start | bytes 1572872 | tf_op jit(solution)/shard_map/ppermute | solution.py:26
  118.7 12.0 %collective-permute-done.17.left_ref = bf16[128,2048]{1,0:T(8,128)(2,1)S(1)} collective-permute-done((bf16[128,2048]{1,0:T(8,128)(2,1)S(1)}, bf16[128,2048]{1,0:T(8,128)(2,1)S(1)}, u32[]{:S(2)}, u32[]{:S(2)}) %collective-permute-start.17) | collective-permute-done | bytes 524320 | tf_op jit(solution)/shard_map/ppermute | solution.py:26
  130.9 2.7 %collective-permute-start.20 = (bf16[64,2048]{1,0:T(8,128)(2,1)S(1)}, bf16[64,2048]{1,0:T(8,128)(2,1)S(1)}, u32[]{:S(2)}, u32[]{:S(2)}) collective-permute-start(bf16[64,2048]{1,0:T(8,128)(2,1)S(1)} %slice.98), channel_id=1, source_target_pairs={{0,192},{32,224},{64,0},{96,32},{128,64},{160,96},{192,128},{224,1... | collective-permute-start | bytes 786440 | tf_op jit(solution)/shard_map/ppermute | solution.py:26
  133.6 1.3 fusion.3
  134.9 4.2 %collective-permute-done.19.top_ref = bf16[64,2048]{1,0:T(8,128)(2,1)S(1)} collective-permute-done((bf16[64,2048]{1,0:T(8,128)(2,1)S(1)}, bf16[64,2048]{1,0:T(8,128)(2,1)S(1)}, u32[]{:S(2)}, u32[]{:S(2)}) %collective-permute-start.19) | collective-permute-done | bytes 262176 | tf_op jit(solution)/shard_map/ppermute | solution.py:26
  139.1 3.5 %shard_map.150 = bf16[512,896]{1,0:T(8,128)(2,1)} custom-call(s32[1]{0:T(128)} %bitcast.pos, bf16[128,2048]{1,0:T(8,128)(2,1)S(1)} %pad_maximum_fusion.2.own_ref, bf16[128,2048]{1,0:T(8,128)(2,1)S(1)} %collective-permute-done.17.left_ref, bf16[128,2048]{1,0:T(8,128)(2,1)S(1)} %collective-permute-done.18.right_ref, ...), custom_call_target="tpu_custom_call" | custom-call | flops 1879048192 | bytes 6684672 | tf_op jit(solution)/shard_map/pallas_call | solution.py:116
  142.6 9.7 %all-to-all-start.3 = ((bf16[32,16,896]{2,1,0:T(8,128)(2,1)}), bf16[32,16,896]{2,1,0:T(8,128)(2,1)}, u32[]{:S(2)}, u32[]{:S(2)}) async-start(bf16[32,16,896]{2,1,0:T(8,128)(2,1)} %bitcast.58), calls=%async_computation.3 | async-start | bytes 1835008 | tf_op jit(solution)/shard_map/all_to_all | solution.py:240
  153.4 2.7 %collective-permute-start.24 = (bf16[448,1024]{1,0:T(8,128)(2,1)}, bf16[448,1024]{1,0:T(8,128)(2,1)}, u32[]{:S(2)}, u32[]{:S(2)}) collective-permute-start(bf16[448,1024]{1,0:T(8,128)(2,1)} %convert_element_type.133), channel_id=1, source_target_pairs={{0,16},{1,17},{2,18},{3,19},{4,20},{5,21},{6,22},{7,23},{8,24},{9,... | collective-permute-start | bytes 2752520 | tf_op jit(solution)/shard_map/ppermute | solution.py:31
  156.1 1.1 convert_element_type.130
  157.9 2.2 collective-permute-start.23
  160.2 1.8 fusion.9
  162.0 1.8 convolution_add_fusion
  164.7 3.2 %collective-permute-start.13 = (bf16[448,256]{1,0:T(8,128)(2,1)S(1)}, bf16[448,256]{1,0:T(8,128)(2,1)S(1)}, u32[]{:S(2)}, u32[]{:S(2)}) collective-permute-start(bf16[448,256]{1,0:T(8,128)(2,1)S(1)} %slice.149), channel_id=1, source_target_pairs={{0,32},{32,0},{64,96},{96,64},{128,160},{160,128},{192,224},{224,1... | collective-permute-start | bytes 688136 | tf_op jit(solution)/shard_map/ppermute | solution.py:21
  169.2 1.8 fusion.5
  170.9 14.5 %collective-permute-done.24 = bf16[448,1024]{1,0:T(8,128)(2,1)} collective-permute-done((bf16[448,1024]{1,0:T(8,128)(2,1)}, bf16[448,1024]{1,0:T(8,128)(2,1)}, u32[]{:S(2)}, u32[]{:S(2)}) %collective-permute-start.24) | collective-permute-done | bytes 917536 | tf_op jit(solution)/shard_map/ppermute | solution.py:31
  185.4 19.7 %collective-permute-done.22 = bf16[448,1024]{1,0:T(8,128)(2,1)} collective-permute-done((bf16[448,1024]{1,0:T(8,128)(2,1)}, bf16[448,1024]{1,0:T(8,128)(2,1)}, u32[]{:S(2)}, u32[]{:S(2)}) %collective-permute-start.22) | collective-permute-done | bytes 917536 | tf_op jit(solution)/shard_map/ppermute | solution.py:31
  205.1 19.7 %collective-permute-done.23 = bf16[448,1024]{1,0:T(8,128)(2,1)} collective-permute-done((bf16[448,1024]{1,0:T(8,128)(2,1)}, bf16[448,1024]{1,0:T(8,128)(2,1)}, u32[]{:S(2)}, u32[]{:S(2)}) %collective-permute-start.23) | collective-permute-done | bytes 917536 | tf_op jit(solution)/shard_map/ppermute | solution.py:31
  224.7 6.0 %divide_convert_fusion = (bf16[448,1024]{1,0:T(8,128)(2,1)}, f32[448,1024]{1,0:T(8,128)}, f32[448,1024]{1,0:T(8,128)}) fusion(bf16[448,1024]{1,0:T(8,128)(2,1)S(1)} %collective-permute-done.21, f32[896,1024]{1,0:T(8,128)} %copy-done.5, bf16[448,1024]{1,0:T(8,128)(2,1)} %collective-permute-done.23, f32[1,1024,448]{1,2,0:T(8,128)S(1)} %copy-done.6, ...), kind=kLoop, calls=%fused_computation.5 | loop fusion | flops 8257536 | bytes 13762561 | tf_op jit(solution)/shard_map/convert_element_type | solution.py:298
  230.8 1.7 fusion.2
  232.5 1.9 collective-permute-start.25
  234.4 1.1 collective-permute-done.25
  (98 shorter events, 9.1 us)
Async XLA Ops:
  0.6 16.5 %copy-start.3 = (bf16[1,448,1024]{2,1,0:T(8,128)(2,1)S(1)}, bf16[1,448,1024]{2,1,0:T(8,128)(2,1)}, u32[]{:S(2)}) copy-start(bf16[1,448,1024]{2,1,0:T(8,128)(2,1)} %param.17) | copy-start | bytes 2752516
  0.7 17.2 %copy-start.4 = (bf16[1,448,1024]{2,1,0:T(8,128)(2,1)S(1)}, bf16[1,448,1024]{2,1,0:T(8,128)(2,1)}, u32[]{:S(2)}) copy-start(bf16[1,448,1024]{2,1,0:T(8,128)(2,1)} %param.18) | copy-start | bytes 2752516
  0.7 17.7 %copy-start.20 = (bf16[256,448]{0,1:T(8,128)(2,1)S(1)}, bf16[256,448]{0,1:T(8,128)(2,1)}, u32[]{:S(2)}) copy-start(bf16[256,448]{0,1:T(8,128)(2,1)} %param.12) | copy-start | bytes 688132
  0.7 17.8 %copy-start.14 = (f32[1,32,32]{2,1,0:T(8,128)S(1)}, f32[1,32,32]{2,1,0:T(8,128)}, u32[]{:S(2)}) copy-start(f32[1,32,32]{2,1,0:T(8,128)} %param.15) | copy-start | bytes 12292
  0.7 4.6 %collective-permute-start = (bf16[448,256]{1,0:T(8,128)(2,1)}, bf16[448,256]{1,0:T(8,128)(2,1)S(1)}, u32[]{:S(2)}, u32[]{:S(2)}) collective-permute-start(bf16[448,256]{1,0:T(8,128)(2,1)} %bitcast.63), channel_id=1, source_target_pairs={{0,32},{32,0},{64,96},{96,64},{128,160},{160,128},{192,224},{224,1... | collective-permute-start | bytes 688136 | tf_op jit(solution)/shard_map/ppermute | solution.py:21
  5.0 19.3 %copy-start.17 = (s32[512]{0:T(512)}, s32[512]{0:T(512)S(1)}, u32[]{:S(2)}) copy-start(s32[512]{0:T(512)S(1)} %broadcast_select_fusion.1) | copy-start | bytes 6148
  7.6 31.7 %all-to-all-start = ((bf16[32,16,896]{2,1,0:T(8,128)(2,1)}), bf16[32,16,896]{2,1,0:T(8,128)(2,1)}, u32[]{:S(2)}, u32[]{:S(2)}) async-start(bf16[32,16,896]{2,1,0:T(8,128)(2,1)} %bitcast.4), calls=%async_computation | async-start | bytes 1835008 | tf_op jit(solution)/shard_map/all_to_all | solution.py:240
  17.1 7.2 %collective-permute-start.1 = (bf16[448,1024]{1,0:T(8,128)(2,1)S(1)}, bf16[448,1024]{1,0:T(8,128)(2,1)S(1)}, u32[]{:S(2)}, u32[]{:S(2)}) collective-permute-start(bf16[448,1024]{1,0:T(8,128)(2,1)S(1)} %bitcast.48), channel_id=1, source_target_pairs={{0,32},{32,0},{64,96},{96,64},{128,160},{160,128},{192,224},{224,1... | collective-permute-start | bytes 2752520 | tf_op jit(solution)/shard_map/ppermute | solution.py:21
  17.9 6.5 %collective-permute-start.2 = (bf16[448,1024]{1,0:T(8,128)(2,1)S(1)}, bf16[448,1024]{1,0:T(8,128)(2,1)}, u32[]{:S(2)}, u32[]{:S(2)}) collective-permute-start(bf16[448,1024]{1,0:T(8,128)(2,1)S(1)} %bitcast.50), channel_id=1, source_target_pairs={{0,32},{32,0},{64,96},{96,64},{128,160},{160,128},{192,224},{224,1... | collective-permute-start | bytes 2752520 | tf_op jit(solution)/shard_map/ppermute | solution.py:21
  18.0 12.2 %collective-permute-start.3 = (bf16[448,1024]{1,0:T(8,128)(2,1)}, bf16[448,1024]{1,0:T(8,128)(2,1)}, u32[]{:S(2)}, u32[]{:S(2)}) collective-permute-start(bf16[448,1024]{1,0:T(8,128)(2,1)} %bitcast.56), channel_id=1, source_target_pairs={{0,32},{32,0},{64,96},{96,64},{128,160},{160,128},{192,224},{224,1... | collective-permute-start | bytes 2752520 | tf_op jit(solution)/shard_map/ppermute | solution.py:21
  18.4 4.5 %collective-permute-start.4 = (bf16[448,256]{1,0:T(8,128)(2,1)S(1)}, bf16[448,256]{1,0:T(8,128)(2,1)S(1)}, u32[]{:S(2)}, u32[]{:S(2)}) collective-permute-start(bf16[448,256]{1,0:T(8,128)(2,1)S(1)} %bitcast.65), channel_id=1, source_target_pairs={{0,32},{32,0},{64,96},{96,64},{128,160},{160,128},{192,224},{224,1... | collective-permute-start | bytes 688136 | tf_op jit(solution)/shard_map/ppermute | solution.py:21
  19.2 11.0 %copy-start.15 = (f32[512]{0:T(512)}, f32[512]{0:T(512)S(1)}, u32[]{:S(2)}) copy-start(f32[512]{0:T(512)S(1)} %get-tuple-element.69) | copy-start | bytes 6148
  24.3 5.9 %copy-start.11 = (bf16[1,1024,448]{1,2,0:T(8,128)(2,1)S(1)}, bf16[1,1024,448]{1,2,0:T(8,128)(2,1)}, u32[]{:S(2)}) copy-start(bf16[1,1024,448]{1,2,0:T(8,128)(2,1)} %param.19) | copy-start | bytes 2752516
  45.2 12.8 %copy-start.9 = (bf16[256,2048]{1,0:T(8,128)(2,1)S(1)}, bf16[256,2048]{1,0:T(8,128)(2,1)}, u32[]{:S(2)}) copy-start(bf16[256,2048]{1,0:T(8,128)(2,1)} %get-tuple-element.37) | copy-start | bytes 3145732
  45.2 10.9 %collective-permute-start.5 = (bf16[128,2048]{1,0:T(8,128)(2,1)}, bf16[128,2048]{1,0:T(8,128)(2,1)S(1)}, u32[]{:S(2)}, u32[]{:S(2)}) collective-permute-start(bf16[128,2048]{1,0:T(8,128)(2,1)} %get-tuple-element.38), channel_id=1, source_target_pairs={{0,192},{32,224},{64,0},{96,32},{128,64},{160,96},{192,128},{224,1... | collective-permute-start | bytes 1572872 | tf_op jit(solution)/shard_map/ppermute | solution.py:26
  47.9 10.1 %collective-permute-start.6 = (bf16[128,2048]{1,0:T(8,128)(2,1)}, bf16[128,2048]{1,0:T(8,128)(2,1)S(1)}, u32[]{:S(2)}, u32[]{:S(2)}) collective-permute-start(bf16[128,2048]{1,0:T(8,128)(2,1)} %get-tuple-element.39), channel_id=1, source_target_pairs={{0,64},{32,96},{64,128},{96,160},{128,192},{160,224},{192,0},{224,... | collective-permute-start | bytes 1572872 | tf_op jit(solution)/shard_map/ppermute | solution.py:26
  47.9 30.2 %all-to-all-start.1 = ((bf16[32,16,896]{2,1,0:T(8,128)(2,1)}), bf16[32,16,896]{2,1,0:T(8,128)(2,1)S(1)}, u32[]{:S(2)}, u32[]{:S(2)}) async-start(bf16[32,16,896]{2,1,0:T(8,128)(2,1)} %bitcast.12), calls=%async_computation.1 | async-start | bytes 1835008 | tf_op jit(solution)/shard_map/all_to_all | solution.py:240
  58.0 8.1 %copy-start.12 = (bf16[128,2048]{1,0:T(8,128)(2,1)}, bf16[128,2048]{1,0:T(8,128)(2,1)S(1)}, u32[]{:S(2)}) copy-start(bf16[128,2048]{1,0:T(8,128)(2,1)S(1)} %collective-permute-done.6) | copy-start | bytes 1572868
  58.1 8.0 %collective-permute-start.7 = (bf16[64,2048]{1,0:T(8,128)(2,1)S(1)}, bf16[64,2048]{1,0:T(8,128)(2,1)S(1)}, u32[]{:S(2)}, u32[]{:S(2)}) collective-permute-start(bf16[64,2048]{1,0:T(8,128)(2,1)S(1)} %get-tuple-element.40), channel_id=1, source_target_pairs={{0,64},{32,96},{64,128},{96,160},{128,192},{160,224},{192,0},{224,... | collective-permute-start | bytes 786440 | tf_op jit(solution)/shard_map/ppermute | solution.py:26
  58.2 7.9 %collective-permute-start.8 = (bf16[64,2048]{1,0:T(8,128)(2,1)S(1)}, bf16[64,2048]{1,0:T(8,128)(2,1)S(1)}, u32[]{:S(2)}, u32[]{:S(2)}) collective-permute-start(bf16[64,2048]{1,0:T(8,128)(2,1)S(1)} %get-tuple-element.41), channel_id=1, source_target_pairs={{0,192},{32,224},{64,0},{96,32},{128,64},{160,96},{192,128},{224,1... | collective-permute-start | bytes 786440 | tf_op jit(solution)/shard_map/ppermute | solution.py:26
  67.4 17.8 %collective-permute-start.9 = (bf16[128,1024]{1,0:T(8,128)(2,1)S(1)}, bf16[128,1024]{1,0:T(8,128)(2,1)S(1)}, u32[]{:S(2)}, u32[]{:S(2)}) collective-permute-start(bf16[128,1024]{1,0:T(8,128)(2,1)S(1)} %multiply_convert_fusion.3.own_ref), channel_id=1, source_target_pairs={{0,64},{32,96},{64,128},{96,160},{128,192},{160,224},{192,0},{224,... | collective-permute-start | bytes 786440 | tf_op jit(solution)/shard_map/ppermute | solution.py:26
  67.5 19.8 %collective-permute-start.10 = (bf16[128,1024]{1,0:T(8,128)(2,1)S(1)}, bf16[128,1024]{1,0:T(8,128)(2,1)S(1)}, u32[]{:S(2)}, u32[]{:S(2)}) collective-permute-start(bf16[128,1024]{1,0:T(8,128)(2,1)S(1)} %multiply_convert_fusion.3.own_ref), channel_id=1, source_target_pairs={{0,192},{32,224},{64,0},{96,32},{128,64},{160,96},{192,128},{224,1... | collective-permute-start | bytes 786440 | tf_op jit(solution)/shard_map/ppermute | solution.py:26
  78.2 18.2 %copy-start.2 = (bf16[896,1024]{1,0:T(8,128)(2,1)S(1)}, bf16[896,1024]{1,0:T(8,128)(2,1)}, u32[]{:S(2)}) copy-start(bf16[896,1024]{1,0:T(8,128)(2,1)} %pad_maximum_fusion.right_ref.w_ref) | copy-start | bytes 5505028
  81.7 28.8 %collective-permute-start.16 = (bf16[128,1024]{1,0:T(8,128)(2,1)}, bf16[128,1024]{1,0:T(8,128)(2,1)S(1)}, u32[]{:S(2)}, u32[]{:S(2)}) collective-permute-start(bf16[128,1024]{1,0:T(8,128)(2,1)} %get-tuple-element.47), channel_id=1, source_target_pairs={{0,192},{32,224},{64,0},{96,32},{128,64},{160,96},{192,128},{224,1... | collective-permute-start | bytes 786440 | tf_op jit(solution)/shard_map/ppermute | solution.py:26
  84.0 26.5 %collective-permute-start.15 = (bf16[128,1024]{1,0:T(8,128)(2,1)}, bf16[128,1024]{1,0:T(8,128)(2,1)S(1)}, u32[]{:S(2)}, u32[]{:S(2)}) collective-permute-start(bf16[128,1024]{1,0:T(8,128)(2,1)} %get-tuple-element.46), channel_id=1, source_target_pairs={{0,64},{32,96},{64,128},{96,160},{128,192},{160,224},{192,0},{224,... | collective-permute-start | bytes 786440 | tf_op jit(solution)/shard_map/ppermute | solution.py:26
  84.0 26.5 %collective-permute-start.14 = (bf16[128,1024]{1,0:T(8,128)(2,1)}, bf16[128,1024]{1,0:T(8,128)(2,1)}, u32[]{:S(2)}, u32[]{:S(2)}) collective-permute-start(bf16[128,1024]{1,0:T(8,128)(2,1)} %get-tuple-element.45), channel_id=1, source_target_pairs={{0,128},{32,160},{64,192},{96,224},{128,0},{160,32},{192,64},{224,... | collective-permute-start | bytes 786440 | tf_op jit(solution)/shard_map/ppermute | solution.py:26
  85.2 11.1 %collective-permute-start.11 = (bf16[64,1024]{1,0:T(8,128)(2,1)S(1)}, bf16[64,1024]{1,0:T(8,128)(2,1)S(1)}, u32[]{:S(2)}, u32[]{:S(2)}) collective-permute-start(bf16[64,1024]{1,0:T(8,128)(2,1)S(1)} %slice.93), channel_id=1, source_target_pairs={{0,64},{32,96},{64,128},{96,160},{128,192},{160,224},{192,0},{224,... | collective-permute-start | bytes 393224 | tf_op jit(solution)/shard_map/ppermute | solution.py:26
  87.3 9.0 %collective-permute-start.12 = (bf16[64,1024]{1,0:T(8,128)(2,1)S(1)}, bf16[64,1024]{1,0:T(8,128)(2,1)S(1)}, u32[]{:S(2)}, u32[]{:S(2)}) collective-permute-start(bf16[64,1024]{1,0:T(8,128)(2,1)S(1)} %slice.94), channel_id=1, source_target_pairs={{0,192},{32,224},{64,0},{96,32},{128,64},{160,96},{192,128},{224,1... | collective-permute-start | bytes 393224 | tf_op jit(solution)/shard_map/ppermute | solution.py:26
  96.3 14.2 %copy-start.13 = (bf16[128,1024]{1,0:T(8,128)(2,1)S(1)}, bf16[128,1024]{1,0:T(8,128)(2,1)}, u32[]{:S(2)}) copy-start(bf16[128,1024]{1,0:T(8,128)(2,1)} %get-tuple-element.48) | copy-start | bytes 786436
  98.6 44.0 %all-to-all-start.2 = ((bf16[32,16,896]{2,1,0:T(8,128)(2,1)}), bf16[32,16,896]{2,1,0:T(8,128)(2,1)}, u32[]{:S(2)}, u32[]{:S(2)}) async-start(bf16[32,16,896]{2,1,0:T(8,128)(2,1)} %bitcast.59), calls=%async_computation.2 | async-start | bytes 1835008 | tf_op jit(solution)/shard_map/all_to_all | solution.py:240
  113.1 21.8 %copy-start.5 = (f32[896,1024]{1,0:T(8,128)}, f32[896,1024]{1,0:T(8,128)S(1)}, u32[]{:S(2)}) copy-start(f32[896,1024]{1,0:T(8,128)S(1)} %fusion.26) | copy-start | bytes 11010052
  113.1 5.6 %copy-start.16 = (f32[512]{0:T(512)S(1)}, f32[512]{0:T(512)}, u32[]{:S(2)}) copy-start(f32[512]{0:T(512)} %copy-done.15) | copy-start | bytes 6148
  113.3 20.3 %collective-permute-start.21 = (bf16[448,1024]{1,0:T(8,128)(2,1)S(1)}, bf16[448,1024]{1,0:T(8,128)(2,1)S(1)}, u32[]{:S(2)}, u32[]{:S(2)}) collective-permute-start(bf16[448,1024]{1,0:T(8,128)(2,1)S(1)} %slice.147), channel_id=1, source_target_pairs={{0,32},{32,0},{64,96},{96,64},{128,160},{160,128},{192,224},{224,1... | collective-permute-start | bytes 2752520 | tf_op jit(solution)/shard_map/ppermute | solution.py:21
  116.0 14.7 %collective-permute-start.17 = (bf16[128,2048]{1,0:T(8,128)(2,1)S(1)}, bf16[128,2048]{1,0:T(8,128)(2,1)S(1)}, u32[]{:S(2)}, u32[]{:S(2)}) collective-permute-start(bf16[128,2048]{1,0:T(8,128)(2,1)S(1)} %pad_maximum_fusion.2.own_ref), channel_id=1, source_target_pairs={{0,64},{32,96},{64,128},{96,160},{128,192},{160,224},{192,0},{224,... | collective-permute-start | bytes 1572872 | tf_op jit(solution)/shard_map/ppermute | solution.py:26
  116.0 14.8 %collective-permute-start.18 = (bf16[128,2048]{1,0:T(8,128)(2,1)S(1)}, bf16[128,2048]{1,0:T(8,128)(2,1)S(1)}, u32[]{:S(2)}, u32[]{:S(2)}) collective-permute-start(bf16[128,2048]{1,0:T(8,128)(2,1)S(1)} %pad_maximum_fusion.2.own_ref), channel_id=1, source_target_pairs={{0,192},{32,224},{64,0},{96,32},{128,64},{160,96},{192,128},{224,1... | collective-permute-start | bytes 1572872 | tf_op jit(solution)/shard_map/ppermute | solution.py:26
  130.8 8.3 %collective-permute-start.19 = (bf16[64,2048]{1,0:T(8,128)(2,1)S(1)}, bf16[64,2048]{1,0:T(8,128)(2,1)S(1)}, u32[]{:S(2)}, u32[]{:S(2)}) collective-permute-start(bf16[64,2048]{1,0:T(8,128)(2,1)S(1)} %slice.97), channel_id=1, source_target_pairs={{0,64},{32,96},{64,128},{96,160},{128,192},{160,224},{192,0},{224,... | collective-permute-start | bytes 786440 | tf_op jit(solution)/shard_map/ppermute | solution.py:26
  130.9 8.2 %copy-start.1 = (bf16[896,2048]{1,0:T(8,128)(2,1)S(1)}, bf16[896,2048]{1,0:T(8,128)(2,1)}, u32[]{:S(2)}) copy-start(bf16[896,2048]{1,0:T(8,128)(2,1)} %shard_map.146.right_ref.w_ref) | copy-start | bytes 11010052
  130.9 8.2 %collective-permute-start.20 = (bf16[64,2048]{1,0:T(8,128)(2,1)S(1)}, bf16[64,2048]{1,0:T(8,128)(2,1)S(1)}, u32[]{:S(2)}, u32[]{:S(2)}) collective-permute-start(bf16[64,2048]{1,0:T(8,128)(2,1)S(1)} %slice.98), channel_id=1, source_target_pairs={{0,192},{32,224},{64,0},{96,32},{128,64},{160,96},{192,128},{224,1... | collective-permute-start | bytes 786440 | tf_op jit(solution)/shard_map/ppermute | solution.py:26
  142.6 9.7 %copy-start.6 = (f32[1,1024,448]{1,2,0:T(8,128)S(1)}, f32[1,1024,448]{1,2,0:T(8,128)}, u32[]{:S(2)}) copy-start(f32[1,1024,448]{1,2,0:T(8,128)} %param.21) | copy-start | bytes 5505028
  142.6 88.1 %all-to-all-start.3 = ((bf16[32,16,896]{2,1,0:T(8,128)(2,1)}), bf16[32,16,896]{2,1,0:T(8,128)(2,1)}, u32[]{:S(2)}, u32[]{:S(2)}) async-start(bf16[32,16,896]{2,1,0:T(8,128)(2,1)} %bitcast.58), calls=%async_computation.3 | async-start | bytes 1835008 | tf_op jit(solution)/shard_map/all_to_all | solution.py:240
  153.4 6.7 %copy-start.18 = (s32[512]{0:T(512)S(1)}, s32[512]{0:T(512)}, u32[]{:S(2)}) copy-start(s32[512]{0:T(512)} %copy-done.17) | copy-start | bytes 6148
  153.4 32.0 %collective-permute-start.24 = (bf16[448,1024]{1,0:T(8,128)(2,1)}, bf16[448,1024]{1,0:T(8,128)(2,1)}, u32[]{:S(2)}, u32[]{:S(2)}) collective-permute-start(bf16[448,1024]{1,0:T(8,128)(2,1)} %convert_element_type.133), channel_id=1, source_target_pairs={{0,16},{1,17},{2,18},{3,19},{4,20},{5,21},{6,22},{7,23},{8,24},{9,... | collective-permute-start | bytes 2752520 | tf_op jit(solution)/shard_map/ppermute | solution.py:31
  156.1 5.9 %copy-start.19 = (bf16[512]{0:T(512)(128)(2,1)S(1)}, bf16[512]{0:T(512)(128)(2,1)}, u32[]{:S(2)}) copy-start(bf16[512]{0:T(512)(128)(2,1)} %get-tuple-element.68) | copy-start | bytes 3076
  157.2 47.9 %collective-permute-start.22 = (bf16[448,1024]{1,0:T(8,128)(2,1)}, bf16[448,1024]{1,0:T(8,128)(2,1)}, u32[]{:S(2)}, u32[]{:S(2)}) collective-permute-start(bf16[448,1024]{1,0:T(8,128)(2,1)} %convert_element_type.130), channel_id=1, source_target_pairs={{0,16},{1,17},{2,18},{3,19},{4,20},{5,21},{6,22},{7,23},{8,24},{9,... | collective-permute-start | bytes 2752520 | tf_op jit(solution)/shard_map/ppermute | solution.py:31
  157.9 66.8 %collective-permute-start.23 = (bf16[448,1024]{1,0:T(8,128)(2,1)}, bf16[448,1024]{1,0:T(8,128)(2,1)}, u32[]{:S(2)}, u32[]{:S(2)}) collective-permute-start(bf16[448,1024]{1,0:T(8,128)(2,1)} %fusion.3), channel_id=1, source_target_pairs={{0,16},{1,17},{2,18},{3,19},{4,20},{5,21},{6,22},{7,23},{8,24},{9,... | collective-permute-start | bytes 2752520 | tf_op jit(solution)/shard_map/ppermute | solution.py:31
  161.9 6.0 %copy-start.21 = (s32[16]{0:T(128)S(1)}, s32[16]{0:T(128)}, u32[]{:S(2)}) copy-start(s32[16]{0:T(128)} %param.16) | copy-start | bytes 196
  164.7 4.5 %collective-permute-start.13 = (bf16[448,256]{1,0:T(8,128)(2,1)S(1)}, bf16[448,256]{1,0:T(8,128)(2,1)S(1)}, u32[]{:S(2)}, u32[]{:S(2)}) collective-permute-start(bf16[448,256]{1,0:T(8,128)(2,1)S(1)} %slice.149), channel_id=1, source_target_pairs={{0,32},{32,0},{64,96},{96,64},{128,160},{160,128},{192,224},{224,1... | collective-permute-start | bytes 688136 | tf_op jit(solution)/shard_map/ppermute | solution.py:21
  232.5 3.0 %collective-permute-start.25 = (bf16[448,256]{1,0:T(8,128)(2,1)S(1)}, bf16[448,256]{1,0:T(8,128)(2,1)S(1)}, u32[]{:S(2)}, u32[]{:S(2)}) collective-permute-start(bf16[448,256]{1,0:T(8,128)(2,1)S(1)} %slice.148), channel_id=1, source_target_pairs={{0,32},{32,0},{64,96},{96,64},{128,160},{160,128},{192,224},{224,1... | collective-permute-start | bytes 688136 | tf_op jit(solution)/shard_map/ppermute | solution.py:21
  (4 other events, 10.3 us)

commit v7 on v6

--- a/solution.py
+++ b/solution.py
@@ -57,11 +57,11 @@
                     pl.ds(pl.multiple_of(at, unit), unit), :
                 ]
 
+        product = dot(ordered[...], right_ref[...]).astype(BF)
         start = 0
         for out in outs:
-            size = out.shape[0]
-            out[...] = dot(ordered[start : start + size, :], right_ref[...]).astype(BF)
-            start += size
+            out[...] = product[start : start + out.shape[0], :]
+            start += out.shape[0]
 
     return pl.pallas_call(
         body,
@@ -86,20 +86,14 @@
 
 
 def gathered_dot(y_pos, parts, right, keep):
-    own, _, _, _, _ = parts
-    rows, depth = own.shape
+    rows, depth = parts[0].shape
     width = right.shape[0]
     total = 4 * rows
     mid = rows // 2
 
-    def body(pos, own_ref, left_ref, right_ref, top_ref, low_ref, w_ref, out, full):
-        for step, offset, ref in (
-            (0, 0, own_ref),
-            (3, 0, left_ref),
-            (1, 0, right_ref),
-            (2, 0, top_ref),
-            (2, mid, low_ref),
-        ):
+    def body(pos, *refs):
+        w_ref, out, full = refs[len(parts) :]
+        for (step, offset), ref in zip(((0, 0), (3, 0), (1, 0), (2, 0), (2, mid)), refs[: len(parts)]):
             at = lax.rem(pos[0] + step, 4) * rows + offset
             full[pl.ds(pl.multiple_of(at, mid), ref.shape[0]), :] = ref[...]
         out[...] = dot(full[...], w_ref[...], 1, 1).astype(BF)
@@ -117,7 +111,7 @@
         body,
         out_shape=out_shape,
         grid=(1,),
-        in_specs=[pl.BlockSpec(memory_space=pltpu.SMEM)] + [vmem] * 6,
+        in_specs=[pl.BlockSpec(memory_space=pltpu.SMEM)] + [vmem] * (len(parts) + 1),
         out_specs=out_specs,
         scratch_shapes=scratch,
         compiler_params=pltpu.CompilerParams(vmem_limit_bytes=24 << 20),
@@ -145,6 +139,13 @@
     top = own_top.astype(F32) + from_right[rows:].astype(F32) + far_left.astype(F32)
     low = own_low.astype(F32) + from_left[rows:].astype(F32) + far_right.astype(F32)
     return jnp.concatenate([top, low])
+
+
+def direct_gather(shard):
+    came = {}
+    for step in (2, 1, 3):
+        came[step] = chip_shift(shard, step)
+    return shard, came[1], came[3], came[2]
 
 
 def ring_gather(shard, chips):
@@ -270,7 +271,7 @@
     terms = ordered_dot(
         y_pos, arrived_grad, down_cols, ((2, 0), (1, 0), (3, 0), (0, 0)), (2 * half,) * 4
     )
-    gathered = ring_gather(hidden_shard, chips)
+    gathered = direct_gather(hidden_shard)
     gathered = tie_all(gathered, *terms)
     out_rows, hidden = gathered_dot(y_pos, gathered, down_cols, True)
     returned = exchange(out_rows)

time: 237 us -> 225 us (0.949)
  starting transfers between devices: 77.3 us -> 71.1 us
  waiting for transfers between devices: 105 us -> 99.9 us
    ppermute x15 -> x14, waiting for transfers between devices: 31.6 us -> 24.6 us  [chip_shift(): lax.ppermute(block, 'dp', [(i, (i + 2 * step) % count) for i in range(cou...]
    all_to_all x4, starting transfers between devices: 39.1 us -> 34 us  [exchange(): lax.all_to_all(block.reshape(experts, own_slots, pair_cols), 'expert', 0,...]
    ppermute x15 -> x14, starting transfers between devices: 20.1 us -> 17.3 us  [chip_shift(): lax.ppermute(block, 'dp', [(i, (i + 2 * step) % count) for i in range(cou...]
  transfers between devices with their start and end apart: 30 -> 29, of which waited for: 13 -> 13; matrix products, arithmetic and copies ran while one was open for 11% -> 11% of each run, Pallas kernels for 6% -> 7%
where the time goes in v7:
time: 225 us; the launch traced here: 224 us
  waiting for transfers between devices  99.9 us (44%)
  starting transfers between devices  71.1 us (32%)
  Pallas kernels  21.8 us (10%)
  other arithmetic  18.5 us (8%)
  matrix products  8.78 us (4%)
    ppermute x3, waiting for transfers between devices, expert_swap(): lax.ppermute(block, 'expert', [(i, i ^ count // 2) for i in range(count)])  54.7 us
    all_to_all x4, starting transfers between devices, exchange(): lax.all_to_all(block.reshape(experts, own_slots, pair_cols), 'expert', 0,...  34 us
    ppermute x14, waiting for transfers between devices, chip_shift(): lax.ppermute(block, 'dp', [(i, (i + 2 * step) % count) for i in range(cou...  24.6 us
    ppermute x14, starting transfers between devices, chip_shift(): lax.ppermute(block, 'dp', [(i, (i + 2 * step) % count) for i in range(cou...  17.3 us
    all_to_all x4, waiting for transfers between devices, exchange(): lax.all_to_all(block.reshape(experts, own_slots, pair_cols), 'expert', 0,...  15.5 us
    ppermute x8, starting transfers between devices, core_swap(): lax.ppermute(block, 'dp', [(i, i ^ 1) for i in range(lax.axis_size('dp'))])  14.2 us
    pallas_call x2, Pallas kernels, ordered_dot(): pl.pallas_call(body, out_shape=[pltpu.HBM((size, width), BF) for size in...  9.15 us
    dot_general x6, matrix products, dot(): lax.dot_general(a, b, (((ca,), (cb,)), ((), ())), preferred_element_type=...  8.78 us
  transfers between devices with their start and end apart: 29, of which 13 were waited for; matrix products, arithmetic and copies ran while one was open for 11% of the time, Pallas kernels for 7%

profile of v7, /device:TPU:1, one launch (start us, length us, event | category | flops | bytes accessed | tf_op | source)
XLA Modules:
  0.0 223.6 jit_solution(7193485758206967446)
XLA Ops:
  0.7 3.3 %collective-permute-start = (bf16[448,256]{1,0:T(8,128)(2,1)}, bf16[448,256]{1,0:T(8,128)(2,1)S(1)}, u32[]{:S(2)}, u32[]{:S(2)}) collective-permute-start(bf16[448,256]{1,0:T(8,128)(2,1)} %bitcast.65), channel_id=1, source_target_pairs={{0,32},{32,0},{64,96},{96,64},{128,160},{160,128},{192,224},{224,1... | collective-permute-start | bytes 688136 | tf_op jit(solution)/shard_map/ppermute | solution.py:21
  5.3 2.3 %convolution_convert_fusion = bf16[512,896]{1,0:T(8,128)(2,1)} fusion(bf16[448,256]{1,0:T(8,128)(2,1)S(1)} %collective-permute-done, bf16[448,256]{1,0:T(8,128)(2,1)} %bitcast.66, s32[512]{0:T(512)S(1)} %broadcast_select_fusion.1), kind=kOutput, calls=%fused_computation.9 | convolution fusion | flops 236388352 | bytes 1378304 | tf_op jit(solution)/shard_map/dot_general | solution.py:17
  7.6 9.4 %all-to-all-start = ((bf16[32,16,896]{2,1,0:T(8,128)(2,1)}), bf16[32,16,896]{2,1,0:T(8,128)(2,1)}, u32[]{:S(2)}, u32[]{:S(2)}) async-start(bf16[32,16,896]{2,1,0:T(8,128)(2,1)} %bitcast.4), calls=%async_computation | async-start | bytes 1835008 | tf_op jit(solution)/shard_map/all_to_all | solution.py:241
  19.2 3.7 %collective-permute-done.4 = bf16[448,256]{1,0:T(8,128)(2,1)S(1)} collective-permute-done((bf16[448,256]{1,0:T(8,128)(2,1)S(1)}, bf16[448,256]{1,0:T(8,128)(2,1)S(1)}, u32[]{:S(2)}, u32[]{:S(2)}) %collective-permute-start.4) | collective-permute-done | bytes 229408 | tf_op jit(solution)/shard_map/ppermute | solution.py:21
  22.9 1.5 multiply_convert_fusion
  24.4 5.9 %shard_map.146.right_ref.refs_5_ = bf16[896,2048]{1,0:T(8,128)(2,1)} custom-call(bf16[448,1024]{1,0:T(8,128)(2,1)S(1)} %bitcast.49, bf16[448,1024]{1,0:T(8,128)(2,1)S(1)} %bitcast.51, bf16[448,1024]{1,0:T(8,128)(2,1)S(1)} %collective-permute-done.1.gate_b, bf16[448,1024]{1,0:T(8,128)(2,1)} %collective-permute-done.2.up_b), custom_call_target="tpu_custom_call" | custom-call | bytes 7340032 | tf_op jit(solution)/shard_map/pallas_call | solution.py:186
  30.3 2.6 %pad_maximum_fusion.right_ref.refs_4_ = bf16[896,1024]{1,0:T(8,128)(2,1)} fusion(bf16[448,1024]{1,0:T(8,128)(2,1)} %collective-permute-done.3, bf16[448,1024]{1,0:T(8,128)(2,1)S(1)} %bitcast.59), kind=kLoop, calls=%fused_computation.4 | loop fusion | flops 3670016 | bytes 3670016 | tf_op jit(solution)/shard_map/concatenate | solution.py:162
  32.8 6.6 %all-to-all-done = bf16[32,16,896]{2,1,0:T(8,128)(2,1)} async-done(((bf16[32,16,896]{2,1,0:T(8,128)(2,1)}), bf16[32,16,896]{2,1,0:T(8,128)(2,1)}, u32[]{:S(2)}, u32[]{:S(2)}) %all-to-all-start) | async-done | bytes 917536 | tf_op jit(solution)/shard_map/all_to_all | solution.py:241
  39.4 5.7 %shard_map.147 = (bf16[128,2048]{1,0:T(8,128)(2,1)}, bf16[128,2048]{1,0:T(8,128)(2,1)}, bf16[256,2048]{1,0:T(8,128)(2,1)}) custom-call(s32[1]{0:T(128)} %bitcast.pos, bf16[512,896]{1,0:T(8,128)(2,1)} %bitcast.5.left_ref, bf16[896,2048]{1,0:T(8,128)(2,1)} %shard_map.146.right_ref.refs_5_), custom_call_target="tpu_custom_call" | custom-call | flops 1879048192 | bytes 6684672 | tf_op jit(solution)/shard_map/pallas_call | solution.py:66
  45.1 2.7 %collective-permute-start.5 = (bf16[128,2048]{1,0:T(8,128)(2,1)}, bf16[128,2048]{1,0:T(8,128)(2,1)S(1)}, u32[]{:S(2)}, u32[]{:S(2)}) collective-permute-start(bf16[128,2048]{1,0:T(8,128)(2,1)} %get-tuple-element.37), channel_id=1, source_target_pairs={{0,192},{32,224},{64,0},{96,32},{128,64},{160,96},{192,128},{224,1... | collective-permute-start | bytes 1572872 | tf_op jit(solution)/shard_map/ppermute | solution.py:26
  47.9 8.1 %all-to-all-start.1 = ((bf16[32,16,896]{2,1,0:T(8,128)(2,1)}), bf16[32,16,896]{2,1,0:T(8,128)(2,1)S(1)}, u32[]{:S(2)}, u32[]{:S(2)}) async-start(bf16[32,16,896]{2,1,0:T(8,128)(2,1)} %bitcast.12), calls=%async_computation.1 | async-start | bytes 1835008 | tf_op jit(solution)/shard_map/all_to_all | solution.py:241
  56.0 1.9 collective-permute-done.6
  58.2 2.7 %collective-permute-start.8 = (bf16[64,2048]{1,0:T(8,128)(2,1)S(1)}, bf16[64,2048]{1,0:T(8,128)(2,1)S(1)}, u32[]{:S(2)}, u32[]{:S(2)}) collective-permute-start(bf16[64,2048]{1,0:T(8,128)(2,1)S(1)} %get-tuple-element.40), channel_id=1, source_target_pairs={{0,192},{32,224},{64,0},{96,32},{128,64},{160,96},{192,128},{224,1... | collective-permute-start | bytes 786440 | tf_op jit(solution)/shard_map/ppermute | solution.py:26
  60.8 5.2 %collective-permute-done.7 = bf16[64,2048]{1,0:T(8,128)(2,1)S(1)} collective-permute-done((bf16[64,2048]{1,0:T(8,128)(2,1)S(1)}, bf16[64,2048]{1,0:T(8,128)(2,1)S(1)}, u32[]{:S(2)}, u32[]{:S(2)}) %collective-permute-start.7) | collective-permute-done | bytes 262176 | tf_op jit(solution)/shard_map/ppermute | solution.py:26
  66.6 2.7 %collective-permute-start.10 = (bf16[128,1024]{1,0:T(8,128)(2,1)S(1)}, bf16[128,1024]{1,0:T(8,128)(2,1)S(1)}, u32[]{:S(2)}, u32[]{:S(2)}) collective-permute-start(bf16[128,1024]{1,0:T(8,128)(2,1)S(1)} %multiply_convert_fusion.3.refs_0_), channel_id=1, source_target_pairs={{0,192},{32,224},{64,0},{96,32},{128,64},{160,96},{192,128},{224,1... | collective-permute-start | bytes 786440 | tf_op jit(solution)/shard_map/ppermute | solution.py:26
  69.2 8.9 %all-to-all-done.1 = bf16[32,16,896]{2,1,0:T(8,128)(2,1)S(1)} async-done(((bf16[32,16,896]{2,1,0:T(8,128)(2,1)}), bf16[32,16,896]{2,1,0:T(8,128)(2,1)S(1)}, u32[]{:S(2)}, u32[]{:S(2)}) %all-to-all-start.1) | async-done | bytes 917536 | tf_op jit(solution)/shard_map/all_to_all | solution.py:241
  78.1 3.4 %shard_map.148 = (bf16[128,1024]{1,0:T(8,128)(2,1)}, bf16[128,1024]{1,0:T(8,128)(2,1)}, bf16[128,1024]{1,0:T(8,128)(2,1)}, bf16[128,1024]{1,0:T(8,128)(2,1)}) custom-call(s32[1]{0:T(128)} %bitcast.pos, bf16[512,896]{1,0:T(8,128)(2,1)S(1)} %bitcast.46, bf16[896,1024]{1,0:T(8,128)(2,1)} %pad_maximum_fusion.right_ref.refs_4_), custom_call_target="tpu_custom_call" | custom-call | flops 939524096 | bytes 3801088 | tf_op jit(solution)/shard_map/pallas_call | solution.py:66
  81.5 2.3 %collective-permute-start.15 = (bf16[128,1024]{1,0:T(8,128)(2,1)}, bf16[128,1024]{1,0:T(8,128)(2,1)}, u32[]{:S(2)}, u32[]{:S(2)}) collective-permute-start(bf16[128,1024]{1,0:T(8,128)(2,1)} %get-tuple-element.46), channel_id=1, source_target_pairs={{0,192},{32,224},{64,0},{96,32},{128,64},{160,96},{192,128},{224,1... | collective-permute-start | bytes 786440 | tf_op jit(solution)/shard_map/ppermute | solution.py:26
  83.9 1.2 collective-permute-start.13
  85.1 3.2 %shard_map.149 = (bf16[512,896]{1,0:T(8,128)(2,1)}, bf16[512,1024]{1,0:T(8,128)(2,1)}) custom-call(s32[1]{0:T(128)} %bitcast.pos, bf16[128,1024]{1,0:T(8,128)(2,1)S(1)} %multiply_convert_fusion.3.refs_0_, bf16[128,1024]{1,0:T(8,128)(2,1)S(1)} %collective-permute-done.9.refs_1_, bf16[128,1024]{1,0:T(8,128)(2,1)S(1)} %collective-permute-done.10.refs_2_, ...), custom_call_target="tpu_custom_call" | custom-call | flops 939524096 | bytes 3801088 | tf_op jit(solution)/shard_map/pallas_call | solution.py:110
  88.3 8.0 %all-to-all-start.2 = ((bf16[32,16,896]{2,1,0:T(8,128)(2,1)}), bf16[32,16,896]{2,1,0:T(8,128)(2,1)S(1)}, u32[]{:S(2)}, u32[]{:S(2)}) async-start(bf16[32,16,896]{2,1,0:T(8,128)(2,1)} %bitcast.61), calls=%async_computation.2 | async-start | bytes 1835008 | tf_op jit(solution)/shard_map/all_to_all | solution.py:241
  96.4 1.5 collective-permute-done.13
  97.9 1.5 multiply_convert_fusion.2
  99.4 1.2 fusion.26
  100.8 4.1 %collective-permute-start.20 = (bf16[448,1024]{1,0:T(8,128)(2,1)S(1)}, bf16[448,1024]{1,0:T(8,128)(2,1)S(1)}, u32[]{:S(2)}, u32[]{:S(2)}) collective-permute-start(bf16[448,1024]{1,0:T(8,128)(2,1)S(1)} %slice.137), channel_id=1, source_target_pairs={{0,32},{32,0},{64,96},{96,64},{128,160},{160,128},{192,224},{224,1... | collective-permute-start | bytes 2752520 | tf_op jit(solution)/shard_map/ppermute | solution.py:21
  104.9 1.2 collective-permute-start.16
  106.1 1.5 collective-permute-start.17
  107.5 11.9 %collective-permute-done.16.refs_1_ = bf16[128,2048]{1,0:T(8,128)(2,1)S(1)} collective-permute-done((bf16[128,2048]{1,0:T(8,128)(2,1)S(1)}, bf16[128,2048]{1,0:T(8,128)(2,1)S(1)}, u32[]{:S(2)}, u32[]{:S(2)}) %collective-permute-start.16) | collective-permute-done | bytes 524320 | tf_op jit(solution)/shard_map/ppermute | solution.py:26
  119.6 2.7 %collective-permute-start.19 = (bf16[64,2048]{1,0:T(8,128)(2,1)S(1)}, bf16[64,2048]{1,0:T(8,128)(2,1)S(1)}, u32[]{:S(2)}, u32[]{:S(2)}) collective-permute-start(bf16[64,2048]{1,0:T(8,128)(2,1)S(1)} %slice.88), channel_id=1, source_target_pairs={{0,192},{32,224},{64,0},{96,32},{128,64},{160,96},{192,128},{224,1... | collective-permute-start | bytes 786440 | tf_op jit(solution)/shard_map/ppermute | solution.py:26
  122.4 1.2 fusion.3
  123.6 4.1 %collective-permute-done.18.refs_3_ = bf16[64,2048]{1,0:T(8,128)(2,1)S(1)} collective-permute-done((bf16[64,2048]{1,0:T(8,128)(2,1)S(1)}, bf16[64,2048]{1,0:T(8,128)(2,1)S(1)}, u32[]{:S(2)}, u32[]{:S(2)}) %collective-permute-start.18) | collective-permute-done | bytes 262176 | tf_op jit(solution)/shard_map/ppermute | solution.py:26
  127.7 3.5 %shard_map.150 = bf16[512,896]{1,0:T(8,128)(2,1)} custom-call(s32[1]{0:T(128)} %bitcast.pos, bf16[128,2048]{1,0:T(8,128)(2,1)S(1)} %pad_maximum_fusion.2.refs_0_, bf16[128,2048]{1,0:T(8,128)(2,1)S(1)} %collective-permute-done.16.refs_1_, bf16[128,2048]{1,0:T(8,128)(2,1)S(1)} %collective-permute-done.17.refs_2_, ...), custom_call_target="tpu_custom_call" | custom-call | flops 1879048192 | bytes 6684672 | tf_op jit(solution)/shard_map/pallas_call | solution.py:110
  131.2 8.4 %all-to-all-start.3 = ((bf16[32,16,896]{2,1,0:T(8,128)(2,1)}), bf16[32,16,896]{2,1,0:T(8,128)(2,1)}, u32[]{:S(2)}, u32[]{:S(2)}) async-start(bf16[32,16,896]{2,1,0:T(8,128)(2,1)} %bitcast.60), calls=%async_computation.3 | async-start | bytes 1835008 | tf_op jit(solution)/shard_map/all_to_all | solution.py:241
  139.7 1.1 convert_element_type.133
  140.7 2.7 %collective-permute-start.23 = (bf16[448,1024]{1,0:T(8,128)(2,1)}, bf16[448,1024]{1,0:T(8,128)(2,1)}, u32[]{:S(2)}, u32[]{:S(2)}) collective-permute-start(bf16[448,1024]{1,0:T(8,128)(2,1)} %convert_element_type.133), channel_id=1, source_target_pairs={{0,16},{1,17},{2,18},{3,19},{4,20},{5,21},{6,22},{7,23},{8,24},{9,... | collective-permute-start | bytes 2752520 | tf_op jit(solution)/shard_map/ppermute | solution.py:31
  143.4 1.1 convert_element_type.130
  145.2 2.2 %collective-permute-start.22 = (bf16[448,1024]{1,0:T(8,128)(2,1)}, bf16[448,1024]{1,0:T(8,128)(2,1)}, u32[]{:S(2)}, u32[]{:S(2)}) collective-permute-start(bf16[448,1024]{1,0:T(8,128)(2,1)} %fusion.3), channel_id=1, source_target_pairs={{0,16},{1,17},{2,18},{3,19},{4,20},{5,21},{6,22},{7,23},{8,24},{9,... | collective-permute-start | bytes 2752520 | tf_op jit(solution)/shard_map/ppermute | solution.py:31
  148.1 1.5 convolution_add_fusion
  149.6 1.1 slice.139
  150.8 3.6 %collective-permute-start.12 = (bf16[448,256]{1,0:T(8,128)(2,1)S(1)}, bf16[448,256]{1,0:T(8,128)(2,1)S(1)}, u32[]{:S(2)}, u32[]{:S(2)}) collective-permute-start(bf16[448,256]{1,0:T(8,128)(2,1)S(1)} %slice.139), channel_id=1, source_target_pairs={{0,32},{32,0},{64,96},{96,64},{128,160},{160,128},{192,224},{224,1... | collective-permute-start | bytes 688136 | tf_op jit(solution)/shard_map/ppermute | solution.py:21
  155.6 1.8 fusion.5
  157.4 15.4 %collective-permute-done.23 = bf16[448,1024]{1,0:T(8,128)(2,1)} collective-permute-done((bf16[448,1024]{1,0:T(8,128)(2,1)}, bf16[448,1024]{1,0:T(8,128)(2,1)}, u32[]{:S(2)}, u32[]{:S(2)}) %collective-permute-start.23) | collective-permute-done | bytes 917536 | tf_op jit(solution)/shard_map/ppermute | solution.py:31
  172.7 19.7 %collective-permute-done.21 = bf16[448,1024]{1,0:T(8,128)(2,1)} collective-permute-done((bf16[448,1024]{1,0:T(8,128)(2,1)}, bf16[448,1024]{1,0:T(8,128)(2,1)}, u32[]{:S(2)}, u32[]{:S(2)}) %collective-permute-start.21) | collective-permute-done | bytes 917536 | tf_op jit(solution)/shard_map/ppermute | solution.py:31
  192.4 19.7 %collective-permute-done.22 = bf16[448,1024]{1,0:T(8,128)(2,1)} collective-permute-done((bf16[448,1024]{1,0:T(8,128)(2,1)}, bf16[448,1024]{1,0:T(8,128)(2,1)}, u32[]{:S(2)}, u32[]{:S(2)}) %collective-permute-start.22) | collective-permute-done | bytes 917536 | tf_op jit(solution)/shard_map/ppermute | solution.py:31
  212.1 6.1 %divide_convert_fusion = (bf16[448,1024]{1,0:T(8,128)(2,1)}, f32[448,1024]{1,0:T(8,128)}, f32[448,1024]{1,0:T(8,128)}) fusion(bf16[448,1024]{1,0:T(8,128)(2,1)S(1)} %copy-done.13, f32[896,1024]{1,0:T(8,128)} %copy-done.5, bf16[448,1024]{1,0:T(8,128)(2,1)} %collective-permute-done.22, f32[1,1024,448]{1,2,0:T(8,128)S(1)} %copy-done.6, ...), kind=kLoop, calls=%fused_computation.5 | loop fusion | flops 8257536 | bytes 13762561 | tf_op jit(solution)/shard_map/convert_element_type | solution.py:299
  218.2 1.7 fusion.2
  219.9 1.9 collective-permute-start.24
  221.8 1.1 collective-permute-done.24
  (102 shorter events, 7.3 us)
Async XLA Ops:
  0.6 16.5 %copy-start.3 = (bf16[1,448,1024]{2,1,0:T(8,128)(2,1)S(1)}, bf16[1,448,1024]{2,1,0:T(8,128)(2,1)}, u32[]{:S(2)}) copy-start(bf16[1,448,1024]{2,1,0:T(8,128)(2,1)} %param.17) | copy-start | bytes 2752516
  0.7 17.2 %copy-start.4 = (bf16[1,448,1024]{2,1,0:T(8,128)(2,1)S(1)}, bf16[1,448,1024]{2,1,0:T(8,128)(2,1)}, u32[]{:S(2)}) copy-start(bf16[1,448,1024]{2,1,0:T(8,128)(2,1)} %param.18) | copy-start | bytes 2752516
  0.7 17.7 %copy-start.24 = (bf16[256,448]{0,1:T(8,128)(2,1)S(1)}, bf16[256,448]{0,1:T(8,128)(2,1)}, u32[]{:S(2)}) copy-start(bf16[256,448]{0,1:T(8,128)(2,1)} %param.12) | copy-start | bytes 688132
  0.7 17.8 %copy-start.18 = (f32[1,32,32]{2,1,0:T(8,128)S(1)}, f32[1,32,32]{2,1,0:T(8,128)}, u32[]{:S(2)}) copy-start(f32[1,32,32]{2,1,0:T(8,128)} %param.15) | copy-start | bytes 12292
  0.7 4.6 %collective-permute-start = (bf16[448,256]{1,0:T(8,128)(2,1)}, bf16[448,256]{1,0:T(8,128)(2,1)S(1)}, u32[]{:S(2)}, u32[]{:S(2)}) collective-permute-start(bf16[448,256]{1,0:T(8,128)(2,1)} %bitcast.65), channel_id=1, source_target_pairs={{0,32},{32,0},{64,96},{96,64},{128,160},{160,128},{192,224},{224,1... | collective-permute-start | bytes 688136 | tf_op jit(solution)/shard_map/ppermute | solution.py:21
  5.0 19.3 %copy-start.21 = (s32[512]{0:T(512)}, s32[512]{0:T(512)S(1)}, u32[]{:S(2)}) copy-start(s32[512]{0:T(512)S(1)} %broadcast_select_fusion.1) | copy-start | bytes 6148
  7.6 31.7 %all-to-all-start = ((bf16[32,16,896]{2,1,0:T(8,128)(2,1)}), bf16[32,16,896]{2,1,0:T(8,128)(2,1)}, u32[]{:S(2)}, u32[]{:S(2)}) async-start(bf16[32,16,896]{2,1,0:T(8,128)(2,1)} %bitcast.4), calls=%async_computation | async-start | bytes 1835008 | tf_op jit(solution)/shard_map/all_to_all | solution.py:241
  17.1 7.3 %collective-permute-start.1 = (bf16[448,1024]{1,0:T(8,128)(2,1)S(1)}, bf16[448,1024]{1,0:T(8,128)(2,1)S(1)}, u32[]{:S(2)}, u32[]{:S(2)}) collective-permute-start(bf16[448,1024]{1,0:T(8,128)(2,1)S(1)} %bitcast.48), channel_id=1, source_target_pairs={{0,32},{32,0},{64,96},{96,64},{128,160},{160,128},{192,224},{224,1... | collective-permute-start | bytes 2752520 | tf_op jit(solution)/shard_map/ppermute | solution.py:21
  17.9 6.5 %collective-permute-start.2 = (bf16[448,1024]{1,0:T(8,128)(2,1)S(1)}, bf16[448,1024]{1,0:T(8,128)(2,1)}, u32[]{:S(2)}, u32[]{:S(2)}) collective-permute-start(bf16[448,1024]{1,0:T(8,128)(2,1)S(1)} %bitcast.50), channel_id=1, source_target_pairs={{0,32},{32,0},{64,96},{96,64},{128,160},{160,128},{192,224},{224,1... | collective-permute-start | bytes 2752520 | tf_op jit(solution)/shard_map/ppermute | solution.py:21
  18.0 12.3 %collective-permute-start.3 = (bf16[448,1024]{1,0:T(8,128)(2,1)}, bf16[448,1024]{1,0:T(8,128)(2,1)}, u32[]{:S(2)}, u32[]{:S(2)}) collective-permute-start(bf16[448,1024]{1,0:T(8,128)(2,1)} %bitcast.58), channel_id=1, source_target_pairs={{0,32},{32,0},{64,96},{96,64},{128,160},{160,128},{192,224},{224,1... | collective-permute-start | bytes 2752520 | tf_op jit(solution)/shard_map/ppermute | solution.py:21
  18.4 4.5 %collective-permute-start.4 = (bf16[448,256]{1,0:T(8,128)(2,1)S(1)}, bf16[448,256]{1,0:T(8,128)(2,1)S(1)}, u32[]{:S(2)}, u32[]{:S(2)}) collective-permute-start(bf16[448,256]{1,0:T(8,128)(2,1)S(1)} %bitcast.67), channel_id=1, source_target_pairs={{0,32},{32,0},{64,96},{96,64},{128,160},{160,128},{192,224},{224,1... | collective-permute-start | bytes 688136 | tf_op jit(solution)/shard_map/ppermute | solution.py:21
  19.2 11.0 %copy-start.19 = (f32[512]{0:T(512)}, f32[512]{0:T(512)S(1)}, u32[]{:S(2)}) copy-start(f32[512]{0:T(512)S(1)} %get-tuple-element.67) | copy-start | bytes 6148
  24.4 5.9 %copy-start.16 = (bf16[1,1024,448]{1,2,0:T(8,128)(2,1)S(1)}, bf16[1,1024,448]{1,2,0:T(8,128)(2,1)}, u32[]{:S(2)}) copy-start(bf16[1,1024,448]{1,2,0:T(8,128)(2,1)} %param.19) | copy-start | bytes 2752516
  45.1 12.8 %copy-start.14 = (bf16[256,2048]{1,0:T(8,128)(2,1)S(1)}, bf16[256,2048]{1,0:T(8,128)(2,1)}, u32[]{:S(2)}) copy-start(bf16[256,2048]{1,0:T(8,128)(2,1)} %get-tuple-element.36) | copy-start | bytes 3145732
  45.1 10.9 %collective-permute-start.5 = (bf16[128,2048]{1,0:T(8,128)(2,1)}, bf16[128,2048]{1,0:T(8,128)(2,1)S(1)}, u32[]{:S(2)}, u32[]{:S(2)}) collective-permute-start(bf16[128,2048]{1,0:T(8,128)(2,1)} %get-tuple-element.37), channel_id=1, source_target_pairs={{0,192},{32,224},{64,0},{96,32},{128,64},{160,96},{192,128},{224,1... | collective-permute-start | bytes 1572872 | tf_op jit(solution)/shard_map/ppermute | solution.py:26
  47.9 10.1 %collective-permute-start.6 = (bf16[128,2048]{1,0:T(8,128)(2,1)}, bf16[128,2048]{1,0:T(8,128)(2,1)S(1)}, u32[]{:S(2)}, u32[]{:S(2)}) collective-permute-start(bf16[128,2048]{1,0:T(8,128)(2,1)} %get-tuple-element.38), channel_id=1, source_target_pairs={{0,64},{32,96},{64,128},{96,160},{128,192},{160,224},{192,0},{224,... | collective-permute-start | bytes 1572872 | tf_op jit(solution)/shard_map/ppermute | solution.py:26
  47.9 30.2 %all-to-all-start.1 = ((bf16[32,16,896]{2,1,0:T(8,128)(2,1)}), bf16[32,16,896]{2,1,0:T(8,128)(2,1)S(1)}, u32[]{:S(2)}, u32[]{:S(2)}) async-start(bf16[32,16,896]{2,1,0:T(8,128)(2,1)} %bitcast.12), calls=%async_computation.1 | async-start | bytes 1835008 | tf_op jit(solution)/shard_map/all_to_all | solution.py:241
  58.1 8.0 %collective-permute-start.7 = (bf16[64,2048]{1,0:T(8,128)(2,1)S(1)}, bf16[64,2048]{1,0:T(8,128)(2,1)S(1)}, u32[]{:S(2)}, u32[]{:S(2)}) collective-permute-start(bf16[64,2048]{1,0:T(8,128)(2,1)S(1)} %get-tuple-element.39), channel_id=1, source_target_pairs={{0,64},{32,96},{64,128},{96,160},{128,192},{160,224},{192,0},{224,... | collective-permute-start | bytes 786440 | tf_op jit(solution)/shard_map/ppermute | solution.py:26
  58.2 7.9 %collective-permute-start.8 = (bf16[64,2048]{1,0:T(8,128)(2,1)S(1)}, bf16[64,2048]{1,0:T(8,128)(2,1)S(1)}, u32[]{:S(2)}, u32[]{:S(2)}) collective-permute-start(bf16[64,2048]{1,0:T(8,128)(2,1)S(1)} %get-tuple-element.40), channel_id=1, source_target_pairs={{0,192},{32,224},{64,0},{96,32},{128,64},{160,96},{192,128},{224,1... | collective-permute-start | bytes 786440 | tf_op jit(solution)/shard_map/ppermute | solution.py:26
  66.5 18.7 %copy-start.2 = (bf16[896,1024]{1,0:T(8,128)(2,1)S(1)}, bf16[896,1024]{1,0:T(8,128)(2,1)}, u32[]{:S(2)}) copy-start(bf16[896,1024]{1,0:T(8,128)(2,1)} %pad_maximum_fusion.right_ref.refs_4_) | copy-start | bytes 5505028
  66.5 17.4 %collective-permute-start.9 = (bf16[128,1024]{1,0:T(8,128)(2,1)S(1)}, bf16[128,1024]{1,0:T(8,128)(2,1)S(1)}, u32[]{:S(2)}, u32[]{:S(2)}) collective-permute-start(bf16[128,1024]{1,0:T(8,128)(2,1)S(1)} %multiply_convert_fusion.3.refs_0_), channel_id=1, source_target_pairs={{0,64},{32,96},{64,128},{96,160},{128,192},{160,224},{192,0},{224,... | collective-permute-start | bytes 786440 | tf_op jit(solution)/shard_map/ppermute | solution.py:26
  66.6 18.6 %collective-permute-start.10 = (bf16[128,1024]{1,0:T(8,128)(2,1)S(1)}, bf16[128,1024]{1,0:T(8,128)(2,1)S(1)}, u32[]{:S(2)}, u32[]{:S(2)}) collective-permute-start(bf16[128,1024]{1,0:T(8,128)(2,1)S(1)} %multiply_convert_fusion.3.refs_0_), channel_id=1, source_target_pairs={{0,192},{32,224},{64,0},{96,32},{128,64},{160,96},{192,128},{224,1... | collective-permute-start | bytes 786440 | tf_op jit(solution)/shard_map/ppermute | solution.py:26
  69.2 15.9 %collective-permute-start.11 = (bf16[128,1024]{1,0:T(8,128)(2,1)S(1)}, bf16[128,1024]{1,0:T(8,128)(2,1)}, u32[]{:S(2)}, u32[]{:S(2)}) collective-permute-start(bf16[128,1024]{1,0:T(8,128)(2,1)S(1)} %multiply_convert_fusion.3.refs_0_), channel_id=1, source_target_pairs={{0,128},{32,160},{64,192},{96,224},{128,0},{160,32},{192,64},{224,... | collective-permute-start | bytes 786440 | tf_op jit(solution)/shard_map/ppermute | solution.py:26
  81.5 14.9 %collective-permute-start.15 = (bf16[128,1024]{1,0:T(8,128)(2,1)}, bf16[128,1024]{1,0:T(8,128)(2,1)}, u32[]{:S(2)}, u32[]{:S(2)}) collective-permute-start(bf16[128,1024]{1,0:T(8,128)(2,1)} %get-tuple-element.46), channel_id=1, source_target_pairs={{0,192},{32,224},{64,0},{96,32},{128,64},{160,96},{192,128},{224,1... | collective-permute-start | bytes 786440 | tf_op jit(solution)/shard_map/ppermute | solution.py:26
  83.9 12.6 %collective-permute-start.14 = (bf16[128,1024]{1,0:T(8,128)(2,1)}, bf16[128,1024]{1,0:T(8,128)(2,1)}, u32[]{:S(2)}, u32[]{:S(2)}) collective-permute-start(bf16[128,1024]{1,0:T(8,128)(2,1)} %get-tuple-element.45), channel_id=1, source_target_pairs={{0,64},{32,96},{64,128},{96,160},{128,192},{160,224},{192,0},{224,... | collective-permute-start | bytes 786440 | tf_op jit(solution)/shard_map/ppermute | solution.py:26
  83.9 14.0 %collective-permute-start.13 = (bf16[128,1024]{1,0:T(8,128)(2,1)}, bf16[128,1024]{1,0:T(8,128)(2,1)}, u32[]{:S(2)}, u32[]{:S(2)}) collective-permute-start(bf16[128,1024]{1,0:T(8,128)(2,1)} %get-tuple-element.44), channel_id=1, source_target_pairs={{0,128},{32,160},{64,192},{96,224},{128,0},{160,32},{192,64},{224,... | collective-permute-start | bytes 786440 | tf_op jit(solution)/shard_map/ppermute | solution.py:26
  88.3 9.6 %copy-start.9 = (f32[64,2048]{1,0:T(8,128)S(1)}, f32[64,2048]{1,0:T(8,128)}, u32[]{:S(2)}) copy-start(f32[64,2048]{1,0:T(8,128)} %copy-done.8) | copy-start | bytes 1572868
  88.3 9.6 %copy-start.11 = (f32[64,2048]{1,0:T(8,128)S(1)}, f32[64,2048]{1,0:T(8,128)}, u32[]{:S(2)}) copy-start(f32[64,2048]{1,0:T(8,128)} %copy-done.10) | copy-start | bytes 1572868
  88.3 9.6 %copy-start.17 = (bf16[128,1024]{1,0:T(8,128)(2,1)S(1)}, bf16[128,1024]{1,0:T(8,128)(2,1)}, u32[]{:S(2)}) copy-start(bf16[128,1024]{1,0:T(8,128)(2,1)} %get-tuple-element.47) | copy-start | bytes 786436
  88.3 42.9 %all-to-all-start.2 = ((bf16[32,16,896]{2,1,0:T(8,128)(2,1)}), bf16[32,16,896]{2,1,0:T(8,128)(2,1)S(1)}, u32[]{:S(2)}, u32[]{:S(2)}) async-start(bf16[32,16,896]{2,1,0:T(8,128)(2,1)} %bitcast.61), calls=%async_computation.2 | async-start | bytes 1835008 | tf_op jit(solution)/shard_map/all_to_all | solution.py:241
  100.6 23.0 %copy-start.5 = (f32[896,1024]{1,0:T(8,128)}, f32[896,1024]{1,0:T(8,128)S(1)}, u32[]{:S(2)}) copy-start(f32[896,1024]{1,0:T(8,128)S(1)} %fusion.26) | copy-start | bytes 11010052
  100.6 6.9 %copy-start.20 = (f32[512]{0:T(512)S(1)}, f32[512]{0:T(512)}, u32[]{:S(2)}) copy-start(f32[512]{0:T(512)} %copy-done.19) | copy-start | bytes 6148
  100.8 21.6 %collective-permute-start.20 = (bf16[448,1024]{1,0:T(8,128)(2,1)S(1)}, bf16[448,1024]{1,0:T(8,128)(2,1)S(1)}, u32[]{:S(2)}, u32[]{:S(2)}) collective-permute-start(bf16[448,1024]{1,0:T(8,128)(2,1)S(1)} %slice.137), channel_id=1, source_target_pairs={{0,32},{32,0},{64,96},{96,64},{128,160},{160,128},{192,224},{224,1... | collective-permute-start | bytes 2752520 | tf_op jit(solution)/shard_map/ppermute | solution.py:21
  104.9 14.6 %collective-permute-start.16 = (bf16[128,2048]{1,0:T(8,128)(2,1)S(1)}, bf16[128,2048]{1,0:T(8,128)(2,1)S(1)}, u32[]{:S(2)}, u32[]{:S(2)}) collective-permute-start(bf16[128,2048]{1,0:T(8,128)(2,1)S(1)} %pad_maximum_fusion.2.refs_0_), channel_id=1, source_target_pairs={{0,64},{32,96},{64,128},{96,160},{128,192},{160,224},{192,0},{224,... | collective-permute-start | bytes 1572872 | tf_op jit(solution)/shard_map/ppermute | solution.py:26
  106.1 13.5 %collective-permute-start.17 = (bf16[128,2048]{1,0:T(8,128)(2,1)S(1)}, bf16[128,2048]{1,0:T(8,128)(2,1)S(1)}, u32[]{:S(2)}, u32[]{:S(2)}) collective-permute-start(bf16[128,2048]{1,0:T(8,128)(2,1)S(1)} %pad_maximum_fusion.2.refs_0_), channel_id=1, source_target_pairs={{0,192},{32,224},{64,0},{96,32},{128,64},{160,96},{192,128},{224,1... | collective-permute-start | bytes 1572872 | tf_op jit(solution)/shard_map/ppermute | solution.py:26
  119.5 8.2 %collective-permute-start.18 = (bf16[64,2048]{1,0:T(8,128)(2,1)S(1)}, bf16[64,2048]{1,0:T(8,128)(2,1)S(1)}, u32[]{:S(2)}, u32[]{:S(2)}) collective-permute-start(bf16[64,2048]{1,0:T(8,128)(2,1)S(1)} %slice.87), channel_id=1, source_target_pairs={{0,64},{32,96},{64,128},{96,160},{128,192},{160,224},{192,0},{224,... | collective-permute-start | bytes 786440 | tf_op jit(solution)/shard_map/ppermute | solution.py:26
  119.6 8.1 %copy-start.1 = (bf16[896,2048]{1,0:T(8,128)(2,1)S(1)}, bf16[896,2048]{1,0:T(8,128)(2,1)}, u32[]{:S(2)}) copy-start(bf16[896,2048]{1,0:T(8,128)(2,1)} %shard_map.146.right_ref.refs_5_) | copy-start | bytes 11010052
  119.6 8.1 %collective-permute-start.19 = (bf16[64,2048]{1,0:T(8,128)(2,1)S(1)}, bf16[64,2048]{1,0:T(8,128)(2,1)S(1)}, u32[]{:S(2)}, u32[]{:S(2)}) collective-permute-start(bf16[64,2048]{1,0:T(8,128)(2,1)S(1)} %slice.88), channel_id=1, source_target_pairs={{0,192},{32,224},{64,0},{96,32},{128,64},{160,96},{192,128},{224,1... | collective-permute-start | bytes 786440 | tf_op jit(solution)/shard_map/ppermute | solution.py:26
  131.2 8.4 %copy-start.6 = (f32[1,1024,448]{1,2,0:T(8,128)S(1)}, f32[1,1024,448]{1,2,0:T(8,128)}, u32[]{:S(2)}) copy-start(f32[1,1024,448]{1,2,0:T(8,128)} %param.21) | copy-start | bytes 5505028
  131.2 86.9 %all-to-all-start.3 = ((bf16[32,16,896]{2,1,0:T(8,128)(2,1)}), bf16[32,16,896]{2,1,0:T(8,128)(2,1)}, u32[]{:S(2)}, u32[]{:S(2)}) async-start(bf16[32,16,896]{2,1,0:T(8,128)(2,1)} %bitcast.60), calls=%async_computation.3 | async-start | bytes 1835008 | tf_op jit(solution)/shard_map/all_to_all | solution.py:241
  140.7 6.7 %copy-start.22 = (s32[512]{0:T(512)S(1)}, s32[512]{0:T(512)}, u32[]{:S(2)}) copy-start(s32[512]{0:T(512)} %copy-done.21) | copy-start | bytes 6148
  140.7 32.0 %collective-permute-start.23 = (bf16[448,1024]{1,0:T(8,128)(2,1)}, bf16[448,1024]{1,0:T(8,128)(2,1)}, u32[]{:S(2)}, u32[]{:S(2)}) collective-permute-start(bf16[448,1024]{1,0:T(8,128)(2,1)} %convert_element_type.133), channel_id=1, source_target_pairs={{0,16},{1,17},{2,18},{3,19},{4,20},{5,21},{6,22},{7,23},{8,24},{9,... | collective-permute-start | bytes 2752520 | tf_op jit(solution)/shard_map/ppermute | solution.py:31
  144.5 47.9 %collective-permute-start.21 = (bf16[448,1024]{1,0:T(8,128)(2,1)}, bf16[448,1024]{1,0:T(8,128)(2,1)}, u32[]{:S(2)}, u32[]{:S(2)}) collective-permute-start(bf16[448,1024]{1,0:T(8,128)(2,1)} %convert_element_type.130), channel_id=1, source_target_pairs={{0,16},{1,17},{2,18},{3,19},{4,20},{5,21},{6,22},{7,23},{8,24},{9,... | collective-permute-start | bytes 2752520 | tf_op jit(solution)/shard_map/ppermute | solution.py:31
  145.2 66.8 %collective-permute-start.22 = (bf16[448,1024]{1,0:T(8,128)(2,1)}, bf16[448,1024]{1,0:T(8,128)(2,1)}, u32[]{:S(2)}, u32[]{:S(2)}) collective-permute-start(bf16[448,1024]{1,0:T(8,128)(2,1)} %fusion.3), channel_id=1, source_target_pairs={{0,16},{1,17},{2,18},{3,19},{4,20},{5,21},{6,22},{7,23},{8,24},{9,... | collective-permute-start | bytes 2752520 | tf_op jit(solution)/shard_map/ppermute | solution.py:31
  148.1 6.2 %copy-start.25 = (s32[16]{0:T(128)S(1)}, s32[16]{0:T(128)}, u32[]{:S(2)}) copy-start(s32[16]{0:T(128)} %param.16) | copy-start | bytes 196
  149.6 62.4 %copy-start.13 = (bf16[448,1024]{1,0:T(8,128)(2,1)S(1)}, bf16[448,1024]{1,0:T(8,128)(2,1)}, u32[]{:S(2)}) copy-start(bf16[448,1024]{1,0:T(8,128)(2,1)} %copy-done.12) | copy-start | bytes 2752516
  150.8 4.9 %collective-permute-start.12 = (bf16[448,256]{1,0:T(8,128)(2,1)S(1)}, bf16[448,256]{1,0:T(8,128)(2,1)S(1)}, u32[]{:S(2)}, u32[]{:S(2)}) collective-permute-start(bf16[448,256]{1,0:T(8,128)(2,1)S(1)} %slice.139), channel_id=1, source_target_pairs={{0,32},{32,0},{64,96},{96,64},{128,160},{160,128},{192,224},{224,1... | collective-permute-start | bytes 688136 | tf_op jit(solution)/shard_map/ppermute | solution.py:21
  219.9 3.0 %collective-permute-start.24 = (bf16[448,256]{1,0:T(8,128)(2,1)S(1)}, bf16[448,256]{1,0:T(8,128)(2,1)S(1)}, u32[]{:S(2)}, u32[]{:S(2)}) collective-permute-start(bf16[448,256]{1,0:T(8,128)(2,1)S(1)} %slice.138), channel_id=1, source_target_pairs={{0,32},{32,0},{64,96},{96,64},{128,160},{160,128},{192,224},{224,1... | collective-permute-start | bytes 688136 | tf_op jit(solution)/shard_map/ppermute | solution.py:21
  (7 other events, 22.8 us)

commit v8 on v7

--- a/solution.py
+++ b/solution.py
@@ -243,7 +243,7 @@
         ).reshape(rows, pair_cols)
 
     token_cols = pair_rows(tokens.T)
-    pick = (masked_route[:, None] == token_ids[None, :]).astype(BF)
+    pick = lax.optimization_barrier((masked_route[:, None] == token_ids[None, :]).astype(BF))
     arrived = exchange(dot(pick, token_cols, 1, 1).astype(BF))
     grad_cols = pair_rows(cotangent.T)
     grad_rows = (dot(pick, grad_cols, 1, 1) * weighted[:, None]).astype(BF)
@@ -305,8 +305,12 @@
         dot(returned, jnp.where(match, top[:, None], 0.0).astype(BF), 0, 0)
         + dot(returned, jnp.where(match, rest[:, None], 0.0).astype(BF), 0, 0),
     ).astype(BF)
-    returned_grad = tie(returned_grad, mixed, step_dir)
-    token_grad = pair_sum(dot(returned_grad, match.astype(BF), 0, 0)).astype(BF)
+    hits = lax.optimization_barrier(match.astype(BF))
+    returned_grad = tie(returned_grad, mixed, step_dir, hits)
+    far_part = dot(returned_grad[:, model_cols:], hits, 0, 0).astype(BF)
+    came = core_swap(far_part)
+    near_part = lax.optimization_barrier(dot(returned_grad[:, :model_cols], hits, 0, 0))
+    token_grad = (near_part + came.astype(F32)).astype(BF)
     return (mixed.T, token_grad.T, new_one.T[None], new_two.T[None], step_dir.T[None])
 
 

time: 225 us -> 225 us (level)
    dot_general x6 -> x7, matrix products: 8.78 us -> 10.2 us  [dot(): lax.dot_general(a, b, (((ca,), (cb,)), ((), ())), preferred_element_type=...]
  transfers between devices with their start and end apart: 29 -> 29, of which waited for: 13 -> 11; matrix products, arithmetic and copies ran while one was open for 11% -> 11% of each run, Pallas kernels for 7% -> 7%
where the time goes in v8:
time: 225 us; the launch traced here: 224 us
  waiting for transfers between devices  98.6 us (44%)
  starting transfers between devices  71 us (32%)
  Pallas kernels  21.8 us (10%)
  other arithmetic  18.6 us (8%)
  matrix products  10.2 us (5%)
    ppermute x3, waiting for transfers between devices, expert_swap(): lax.ppermute(block, 'expert', [(i, i ^ count // 2) for i in range(count)])  54.7 us
    all_to_all x4, starting transfers between devices, exchange(): lax.all_to_all(block.reshape(experts, own_slots, pair_cols), 'expert', 0,...  33.9 us
    ppermute x14, waiting for transfers between devices, chip_shift(): lax.ppermute(block, 'dp', [(i, (i + 2 * step) % count) for i in range(cou...  24.6 us
    ppermute x14, starting transfers between devices, chip_shift(): lax.ppermute(block, 'dp', [(i, (i + 2 * step) % count) for i in range(cou...  17.3 us
    all_to_all x4, waiting for transfers between devices, exchange(): lax.all_to_all(block.reshape(experts, own_slots, pair_cols), 'expert', 0,...  15.6 us
    ppermute x8, starting transfers between devices, core_swap(): lax.ppermute(block, 'dp', [(i, i ^ 1) for i in range(lax.axis_size('dp'))])  14.2 us
    dot_general x7, matrix products, dot(): lax.dot_general(a, b, (((ca,), (cb,)), ((), ())), preferred_element_type=...  10.2 us
    pallas_call x2, Pallas kernels, ordered_dot(): pl.pallas_call(body, out_shape=[pltpu.HBM((size, width), BF) for size in...  9.18 us
  transfers between devices with their start and end apart: 29, of which 11 were waited for; matrix products, arithmetic and copies ran while one was open for 11% of the time, Pallas kernels for 7%

profile of v8, /device:TPU:1, one launch (start us, length us, event | category | flops | bytes accessed | tf_op | source)
XLA Modules:
  0.0 223.8 jit_solution(18095417647526825595)
XLA Ops:
  0.6 3.3 %collective-permute-start = (bf16[448,256]{1,0:T(8,128)(2,1)}, bf16[448,256]{1,0:T(8,128)(2,1)S(1)}, u32[]{:S(2)}, u32[]{:S(2)}) collective-permute-start(bf16[448,256]{1,0:T(8,128)(2,1)} %bitcast.66), channel_id=1, source_target_pairs={{0,32},{32,0},{64,96},{96,64},{128,160},{160,128},{192,224},{224,1... | collective-permute-start | bytes 688136 | tf_op jit(solution)/shard_map/ppermute | solution.py:21
  5.3 2.5 %convolution_convert_fusion = bf16[512,896]{1,0:T(8,128)(2,1)} fusion(bf16[512,256]{1,0:T(8,128)(2,1)S(1)} %fusion.5, bf16[448,256]{1,0:T(8,128)(2,1)S(1)} %collective-permute-done, bf16[448,256]{1,0:T(8,128)(2,1)} %bitcast.67), kind=kOutput, calls=%fused_computation.9 | convolution fusion | flops 236257280 | bytes 1638400 | tf_op jit(solution)/shard_map/dot_general | solution.py:17
  7.8 9.4 %all-to-all-start = ((bf16[32,16,896]{2,1,0:T(8,128)(2,1)}), bf16[32,16,896]{2,1,0:T(8,128)(2,1)}, u32[]{:S(2)}, u32[]{:S(2)}) async-start(bf16[32,16,896]{2,1,0:T(8,128)(2,1)} %bitcast.4), calls=%async_computation | async-start | bytes 1835008 | tf_op jit(solution)/shard_map/all_to_all | solution.py:241
  19.3 3.7 %collective-permute-done.4 = bf16[448,256]{1,0:T(8,128)(2,1)S(1)} collective-permute-done((bf16[448,256]{1,0:T(8,128)(2,1)S(1)}, bf16[448,256]{1,0:T(8,128)(2,1)S(1)}, u32[]{:S(2)}, u32[]{:S(2)}) %collective-permute-start.4) | collective-permute-done | bytes 229408 | tf_op jit(solution)/shard_map/ppermute | solution.py:21
  23.0 1.4 multiply_convert_fusion
  24.4 5.9 %shard_map.146.right_ref.refs_5_ = bf16[896,2048]{1,0:T(8,128)(2,1)} custom-call(bf16[448,1024]{1,0:T(8,128)(2,1)S(1)} %bitcast.52, bf16[448,1024]{1,0:T(8,128)(2,1)S(1)} %bitcast.54, bf16[448,1024]{1,0:T(8,128)(2,1)S(1)} %collective-permute-done.1.gate_b, bf16[448,1024]{1,0:T(8,128)(2,1)} %collective-permute-done.2.up_b), custom_call_target="tpu_custom_call" | custom-call | bytes 7340032 | tf_op jit(solution)/shard_map/pallas_call | solution.py:186
  30.3 2.6 %pad_maximum_fusion.right_ref.refs_4_ = bf16[896,1024]{1,0:T(8,128)(2,1)} fusion(bf16[448,1024]{1,0:T(8,128)(2,1)} %collective-permute-done.3, bf16[448,1024]{1,0:T(8,128)(2,1)S(1)} %bitcast.62), kind=kLoop, calls=%fused_computation.4 | loop fusion | flops 3670016 | bytes 3670016 | tf_op jit(solution)/shard_map/concatenate | solution.py:162
  32.8 6.7 %all-to-all-done = bf16[32,16,896]{2,1,0:T(8,128)(2,1)} async-done(((bf16[32,16,896]{2,1,0:T(8,128)(2,1)}), bf16[32,16,896]{2,1,0:T(8,128)(2,1)}, u32[]{:S(2)}, u32[]{:S(2)}) %all-to-all-start) | async-done | bytes 917536 | tf_op jit(solution)/shard_map/all_to_all | solution.py:241
  39.6 5.7 %shard_map.147 = (bf16[128,2048]{1,0:T(8,128)(2,1)}, bf16[128,2048]{1,0:T(8,128)(2,1)}, bf16[256,2048]{1,0:T(8,128)(2,1)}) custom-call(s32[1]{0:T(128)} %bitcast.pos, bf16[512,896]{1,0:T(8,128)(2,1)} %bitcast.5.left_ref, bf16[896,2048]{1,0:T(8,128)(2,1)} %shard_map.146.right_ref.refs_5_), custom_call_target="tpu_custom_call" | custom-call | flops 1879048192 | bytes 6684672 | tf_op jit(solution)/shard_map/pallas_call | solution.py:66
  45.3 2.7 %collective-permute-start.5 = (bf16[128,2048]{1,0:T(8,128)(2,1)}, bf16[128,2048]{1,0:T(8,128)(2,1)S(1)}, u32[]{:S(2)}, u32[]{:S(2)}) collective-permute-start(bf16[128,2048]{1,0:T(8,128)(2,1)} %get-tuple-element.37), channel_id=1, source_target_pairs={{0,192},{32,224},{64,0},{96,32},{128,64},{160,96},{192,128},{224,1... | collective-permute-start | bytes 1572872 | tf_op jit(solution)/shard_map/ppermute | solution.py:26
  48.1 8.1 %all-to-all-start.1 = ((bf16[32,16,896]{2,1,0:T(8,128)(2,1)}), bf16[32,16,896]{2,1,0:T(8,128)(2,1)S(1)}, u32[]{:S(2)}, u32[]{:S(2)}) async-start(bf16[32,16,896]{2,1,0:T(8,128)(2,1)} %bitcast.12), calls=%async_computation.1 | async-start | bytes 1835008 | tf_op jit(solution)/shard_map/all_to_all | solution.py:241
  56.2 2.0 collective-permute-done.6
  58.4 2.7 %collective-permute-start.8 = (bf16[64,2048]{1,0:T(8,128)(2,1)S(1)}, bf16[64,2048]{1,0:T(8,128)(2,1)S(1)}, u32[]{:S(2)}, u32[]{:S(2)}) collective-permute-start(bf16[64,2048]{1,0:T(8,128)(2,1)S(1)} %get-tuple-element.40), channel_id=1, source_target_pairs={{0,192},{32,224},{64,0},{96,32},{128,64},{160,96},{192,128},{224,1... | collective-permute-start | bytes 786440 | tf_op jit(solution)/shard_map/ppermute | solution.py:26
  61.1 5.2 %collective-permute-done.7 = bf16[64,2048]{1,0:T(8,128)(2,1)S(1)} collective-permute-done((bf16[64,2048]{1,0:T(8,128)(2,1)S(1)}, bf16[64,2048]{1,0:T(8,128)(2,1)S(1)}, u32[]{:S(2)}, u32[]{:S(2)}) %collective-permute-start.7) | collective-permute-done | bytes 262176 | tf_op jit(solution)/shard_map/ppermute | solution.py:26
  66.8 2.7 %collective-permute-start.10 = (bf16[128,1024]{1,0:T(8,128)(2,1)S(1)}, bf16[128,1024]{1,0:T(8,128)(2,1)S(1)}, u32[]{:S(2)}, u32[]{:S(2)}) collective-permute-start(bf16[128,1024]{1,0:T(8,128)(2,1)S(1)} %multiply_convert_fusion.3.refs_0_), channel_id=1, source_target_pairs={{0,192},{32,224},{64,0},{96,32},{128,64},{160,96},{192,128},{224,1... | collective-permute-start | bytes 786440 | tf_op jit(solution)/shard_map/ppermute | solution.py:26
  69.4 8.9 %all-to-all-done.1 = bf16[32,16,896]{2,1,0:T(8,128)(2,1)S(1)} async-done(((bf16[32,16,896]{2,1,0:T(8,128)(2,1)}), bf16[32,16,896]{2,1,0:T(8,128)(2,1)S(1)}, u32[]{:S(2)}, u32[]{:S(2)}) %all-to-all-start.1) | async-done | bytes 917536 | tf_op jit(solution)/shard_map/all_to_all | solution.py:241
  78.3 3.4 %shard_map.148 = (bf16[128,1024]{1,0:T(8,128)(2,1)}, bf16[128,1024]{1,0:T(8,128)(2,1)}, bf16[128,1024]{1,0:T(8,128)(2,1)}, bf16[128,1024]{1,0:T(8,128)(2,1)}) custom-call(s32[1]{0:T(128)} %bitcast.pos, bf16[512,896]{1,0:T(8,128)(2,1)S(1)} %bitcast.49, bf16[896,1024]{1,0:T(8,128)(2,1)} %pad_maximum_fusion.right_ref.refs_4_), custom_call_target="tpu_custom_call" | custom-call | flops 939524096 | bytes 3801088 | tf_op jit(solution)/shard_map/pallas_call | solution.py:66
  81.7 2.3 %collective-permute-start.15 = (bf16[128,1024]{1,0:T(8,128)(2,1)}, bf16[128,1024]{1,0:T(8,128)(2,1)}, u32[]{:S(2)}, u32[]{:S(2)}) collective-permute-start(bf16[128,1024]{1,0:T(8,128)(2,1)} %get-tuple-element.46), channel_id=1, source_target_pairs={{0,192},{32,224},{64,0},{96,32},{128,64},{160,96},{192,128},{224,1... | collective-permute-start | bytes 786440 | tf_op jit(solution)/shard_map/ppermute | solution.py:26
  84.0 1.2 collective-permute-start.13
  85.3 3.2 %shard_map.149 = (bf16[512,896]{1,0:T(8,128)(2,1)}, bf16[512,1024]{1,0:T(8,128)(2,1)}) custom-call(s32[1]{0:T(128)} %bitcast.pos, bf16[128,1024]{1,0:T(8,128)(2,1)S(1)} %multiply_convert_fusion.3.refs_0_, bf16[128,1024]{1,0:T(8,128)(2,1)S(1)} %collective-permute-done.9.refs_1_, bf16[128,1024]{1,0:T(8,128)(2,1)S(1)} %collective-permute-done.10.refs_2_, ...), custom_call_target="tpu_custom_call" | custom-call | flops 939524096 | bytes 3801088 | tf_op jit(solution)/shard_map/pallas_call | solution.py:110
  88.5 8.0 %all-to-all-start.2 = ((bf16[32,16,896]{2,1,0:T(8,128)(2,1)}), bf16[32,16,896]{2,1,0:T(8,128)(2,1)S(1)}, u32[]{:S(2)}, u32[]{:S(2)}) async-start(bf16[32,16,896]{2,1,0:T(8,128)(2,1)} %bitcast.64), calls=%async_computation.2 | async-start | bytes 1835008 | tf_op jit(solution)/shard_map/all_to_all | solution.py:241
  96.6 1.4 collective-permute-done.13
  98.0 1.5 multiply_convert_fusion.2
  99.6 1.2 fusion.25
  100.9 4.1 %collective-permute-start.20 = (bf16[448,1024]{1,0:T(8,128)(2,1)S(1)}, bf16[448,1024]{1,0:T(8,128)(2,1)S(1)}, u32[]{:S(2)}, u32[]{:S(2)}) collective-permute-start(bf16[448,1024]{1,0:T(8,128)(2,1)S(1)} %slice.132), channel_id=1, source_target_pairs={{0,32},{32,0},{64,96},{96,64},{128,160},{160,128},{192,224},{224,1... | collective-permute-start | bytes 2752520 | tf_op jit(solution)/shard_map/ppermute | solution.py:21
  105.0 1.1 collective-permute-start.16
  106.1 1.6 collective-permute-start.17
  107.7 11.9 %collective-permute-done.16.refs_1_ = bf16[128,2048]{1,0:T(8,128)(2,1)S(1)} collective-permute-done((bf16[128,2048]{1,0:T(8,128)(2,1)S(1)}, bf16[128,2048]{1,0:T(8,128)(2,1)S(1)}, u32[]{:S(2)}, u32[]{:S(2)}) %collective-permute-start.16) | collective-permute-done | bytes 524320 | tf_op jit(solution)/shard_map/ppermute | solution.py:26
  119.8 2.7 %collective-permute-start.19 = (bf16[64,2048]{1,0:T(8,128)(2,1)S(1)}, bf16[64,2048]{1,0:T(8,128)(2,1)S(1)}, u32[]{:S(2)}, u32[]{:S(2)}) collective-permute-start(bf16[64,2048]{1,0:T(8,128)(2,1)S(1)} %slice.87), channel_id=1, source_target_pairs={{0,192},{32,224},{64,0},{96,32},{128,64},{160,96},{192,128},{224,1... | collective-permute-start | bytes 786440 | tf_op jit(solution)/shard_map/ppermute | solution.py:26
  122.5 1.2 fusion.6
  123.8 4.1 %collective-permute-done.18.refs_3_ = bf16[64,2048]{1,0:T(8,128)(2,1)S(1)} collective-permute-done((bf16[64,2048]{1,0:T(8,128)(2,1)S(1)}, bf16[64,2048]{1,0:T(8,128)(2,1)S(1)}, u32[]{:S(2)}, u32[]{:S(2)}) %collective-permute-start.18) | collective-permute-done | bytes 262176 | tf_op jit(solution)/shard_map/ppermute | solution.py:26
  127.9 3.5 %shard_map.150 = bf16[512,896]{1,0:T(8,128)(2,1)} custom-call(s32[1]{0:T(128)} %bitcast.pos, bf16[128,2048]{1,0:T(8,128)(2,1)S(1)} %pad_maximum_fusion.2.refs_0_, bf16[128,2048]{1,0:T(8,128)(2,1)S(1)} %collective-permute-done.16.refs_1_, bf16[128,2048]{1,0:T(8,128)(2,1)S(1)} %collective-permute-done.17.refs_2_, ...), custom_call_target="tpu_custom_call" | custom-call | flops 1879048192 | bytes 6684672 | tf_op jit(solution)/shard_map/pallas_call | solution.py:110
  131.4 8.3 %all-to-all-start.3 = ((bf16[32,16,896]{2,1,0:T(8,128)(2,1)}), bf16[32,16,896]{2,1,0:T(8,128)(2,1)}, u32[]{:S(2)}, u32[]{:S(2)}) async-start(bf16[32,16,896]{2,1,0:T(8,128)(2,1)} %bitcast.63), calls=%async_computation.3 | async-start | bytes 1835008 | tf_op jit(solution)/shard_map/all_to_all | solution.py:241
  139.7 1.1 convert_element_type.138
  140.8 2.7 %collective-permute-start.23 = (bf16[448,1024]{1,0:T(8,128)(2,1)}, bf16[448,1024]{1,0:T(8,128)(2,1)}, u32[]{:S(2)}, u32[]{:S(2)}) collective-permute-start(bf16[448,1024]{1,0:T(8,128)(2,1)} %convert_element_type.138), channel_id=1, source_target_pairs={{0,16},{1,17},{2,18},{3,19},{4,20},{5,21},{6,22},{7,23},{8,24},{9,... | collective-permute-start | bytes 2752520 | tf_op jit(solution)/shard_map/ppermute | solution.py:31
  143.5 1.1 convert_element_type.135
  145.3 2.2 collective-permute-start.22
  148.1 1.5 convolution_add_fusion
  149.7 1.1 slice.133
  150.8 3.6 %collective-permute-start.12 = (bf16[448,256]{1,0:T(8,128)(2,1)S(1)}, bf16[448,256]{1,0:T(8,128)(2,1)S(1)}, u32[]{:S(2)}, u32[]{:S(2)}) collective-permute-start(bf16[448,256]{1,0:T(8,128)(2,1)S(1)} %slice.133), channel_id=1, source_target_pairs={{0,32},{32,0},{64,96},{96,64},{128,160},{160,128},{192,224},{224,1... | collective-permute-start | bytes 688136 | tf_op jit(solution)/shard_map/ppermute | solution.py:21
  155.7 1.8 fusion.7
  157.4 15.3 %collective-permute-done.23 = bf16[448,1024]{1,0:T(8,128)(2,1)} collective-permute-done((bf16[448,1024]{1,0:T(8,128)(2,1)}, bf16[448,1024]{1,0:T(8,128)(2,1)}, u32[]{:S(2)}, u32[]{:S(2)}) %collective-permute-start.23) | collective-permute-done | bytes 917536 | tf_op jit(solution)/shard_map/ppermute | solution.py:31
  172.8 19.7 %collective-permute-done.21 = bf16[448,1024]{1,0:T(8,128)(2,1)} collective-permute-done((bf16[448,1024]{1,0:T(8,128)(2,1)}, bf16[448,1024]{1,0:T(8,128)(2,1)}, u32[]{:S(2)}, u32[]{:S(2)}) %collective-permute-start.21) | collective-permute-done | bytes 917536 | tf_op jit(solution)/shard_map/ppermute | solution.py:31
  192.4 19.7 %collective-permute-done.22 = bf16[448,1024]{1,0:T(8,128)(2,1)} collective-permute-done((bf16[448,1024]{1,0:T(8,128)(2,1)}, bf16[448,1024]{1,0:T(8,128)(2,1)}, u32[]{:S(2)}, u32[]{:S(2)}) %collective-permute-start.22) | collective-permute-done | bytes 917536 | tf_op jit(solution)/shard_map/ppermute | solution.py:31
  212.1 6.1 %divide_convert_fusion = (bf16[448,1024]{1,0:T(8,128)(2,1)}, f32[448,1024]{1,0:T(8,128)}, f32[448,1024]{1,0:T(8,128)}) fusion(bf16[448,1024]{1,0:T(8,128)(2,1)S(1)} %copy-done.13, f32[896,1024]{1,0:T(8,128)} %copy-done.5, bf16[448,1024]{1,0:T(8,128)(2,1)} %collective-permute-done.22, f32[1,1024,448]{1,2,0:T(8,128)S(1)} %copy-done.6, ...), kind=kLoop, calls=%fused_computation.5 | loop fusion | flops 8257536 | bytes 13762561 | tf_op jit(solution)/shard_map/convert_element_type | solution.py:299
  218.2 1.6 convolution_convert_fusion.1
  219.8 1.9 collective-permute-start.24
  221.7 1.4 fusion.3
  (107 shorter events, 7.1 us)
Async XLA Ops:
  0.6 4.6 %collective-permute-start = (bf16[448,256]{1,0:T(8,128)(2,1)}, bf16[448,256]{1,0:T(8,128)(2,1)S(1)}, u32[]{:S(2)}, u32[]{:S(2)}) collective-permute-start(bf16[448,256]{1,0:T(8,128)(2,1)} %bitcast.66), channel_id=1, source_target_pairs={{0,32},{32,0},{64,96},{96,64},{128,160},{160,128},{192,224},{224,1... | collective-permute-start | bytes 688136 | tf_op jit(solution)/shard_map/ppermute | solution.py:21
  5.0 12.3 %copy-start.3 = (bf16[1,448,1024]{2,1,0:T(8,128)(2,1)S(1)}, bf16[1,448,1024]{2,1,0:T(8,128)(2,1)}, u32[]{:S(2)}) copy-start(bf16[1,448,1024]{2,1,0:T(8,128)(2,1)} %param.17) | copy-start | bytes 2752516
  5.0 12.9 %copy-start.4 = (bf16[1,448,1024]{2,1,0:T(8,128)(2,1)S(1)}, bf16[1,448,1024]{2,1,0:T(8,128)(2,1)}, u32[]{:S(2)}) copy-start(bf16[1,448,1024]{2,1,0:T(8,128)(2,1)} %param.18) | copy-start | bytes 2752516
  5.0 13.4 %copy-start.26 = (bf16[256,448]{0,1:T(8,128)(2,1)S(1)}, bf16[256,448]{0,1:T(8,128)(2,1)}, u32[]{:S(2)}) copy-start(bf16[256,448]{0,1:T(8,128)(2,1)} %param.12) | copy-start | bytes 688132
  5.0 13.5 %copy-start.22 = (f32[1,32,32]{2,1,0:T(8,128)S(1)}, f32[1,32,32]{2,1,0:T(8,128)}, u32[]{:S(2)}) copy-start(f32[1,32,32]{2,1,0:T(8,128)} %param.15) | copy-start | bytes 12292
  5.2 19.2 %copy-start.15 = (bf16[512,256]{1,0:T(8,128)(2,1)}, bf16[512,256]{1,0:T(8,128)(2,1)S(1)}, u32[]{:S(2)}) copy-start(bf16[512,256]{1,0:T(8,128)(2,1)S(1)} %fusion.5) | copy-start | bytes 786436
  7.8 31.8 %all-to-all-start = ((bf16[32,16,896]{2,1,0:T(8,128)(2,1)}), bf16[32,16,896]{2,1,0:T(8,128)(2,1)}, u32[]{:S(2)}, u32[]{:S(2)}) async-start(bf16[32,16,896]{2,1,0:T(8,128)(2,1)} %bitcast.4), calls=%async_computation | async-start | bytes 1835008 | tf_op jit(solution)/shard_map/all_to_all | solution.py:241
  17.3 7.2 %collective-permute-start.1 = (bf16[448,1024]{1,0:T(8,128)(2,1)S(1)}, bf16[448,1024]{1,0:T(8,128)(2,1)S(1)}, u32[]{:S(2)}, u32[]{:S(2)}) collective-permute-start(bf16[448,1024]{1,0:T(8,128)(2,1)S(1)} %bitcast.51), channel_id=1, source_target_pairs={{0,32},{32,0},{64,96},{96,64},{128,160},{160,128},{192,224},{224,1... | collective-permute-start | bytes 2752520 | tf_op jit(solution)/shard_map/ppermute | solution.py:21
  18.0 6.5 %collective-permute-start.2 = (bf16[448,1024]{1,0:T(8,128)(2,1)S(1)}, bf16[448,1024]{1,0:T(8,128)(2,1)}, u32[]{:S(2)}, u32[]{:S(2)}) collective-permute-start(bf16[448,1024]{1,0:T(8,128)(2,1)S(1)} %bitcast.53), channel_id=1, source_target_pairs={{0,32},{32,0},{64,96},{96,64},{128,160},{160,128},{192,224},{224,1... | collective-permute-start | bytes 2752520 | tf_op jit(solution)/shard_map/ppermute | solution.py:21
  18.1 12.2 %collective-permute-start.3 = (bf16[448,1024]{1,0:T(8,128)(2,1)}, bf16[448,1024]{1,0:T(8,128)(2,1)}, u32[]{:S(2)}, u32[]{:S(2)}) collective-permute-start(bf16[448,1024]{1,0:T(8,128)(2,1)} %bitcast.61), channel_id=1, source_target_pairs={{0,32},{32,0},{64,96},{96,64},{128,160},{160,128},{192,224},{224,1... | collective-permute-start | bytes 2752520 | tf_op jit(solution)/shard_map/ppermute | solution.py:21
  18.5 4.5 %collective-permute-start.4 = (bf16[448,256]{1,0:T(8,128)(2,1)S(1)}, bf16[448,256]{1,0:T(8,128)(2,1)S(1)}, u32[]{:S(2)}, u32[]{:S(2)}) collective-permute-start(bf16[448,256]{1,0:T(8,128)(2,1)S(1)} %bitcast.70), channel_id=1, source_target_pairs={{0,32},{32,0},{64,96},{96,64},{128,160},{160,128},{192,224},{224,1... | collective-permute-start | bytes 688136 | tf_op jit(solution)/shard_map/ppermute | solution.py:21
  19.3 11.0 %copy-start.23 = (f32[512]{0:T(512)}, f32[512]{0:T(512)S(1)}, u32[]{:S(2)}) copy-start(f32[512]{0:T(512)S(1)} %get-tuple-element.67) | copy-start | bytes 6148
  45.3 12.9 %copy-start.14 = (bf16[256,2048]{1,0:T(8,128)(2,1)S(1)}, bf16[256,2048]{1,0:T(8,128)(2,1)}, u32[]{:S(2)}) copy-start(bf16[256,2048]{1,0:T(8,128)(2,1)} %get-tuple-element.36) | copy-start | bytes 3145732
  45.3 10.8 %collective-permute-start.5 = (bf16[128,2048]{1,0:T(8,128)(2,1)}, bf16[128,2048]{1,0:T(8,128)(2,1)S(1)}, u32[]{:S(2)}, u32[]{:S(2)}) collective-permute-start(bf16[128,2048]{1,0:T(8,128)(2,1)} %get-tuple-element.37), channel_id=1, source_target_pairs={{0,192},{32,224},{64,0},{96,32},{128,64},{160,96},{192,128},{224,1... | collective-permute-start | bytes 1572872 | tf_op jit(solution)/shard_map/ppermute | solution.py:26
  48.1 10.1 %collective-permute-start.6 = (bf16[128,2048]{1,0:T(8,128)(2,1)}, bf16[128,2048]{1,0:T(8,128)(2,1)S(1)}, u32[]{:S(2)}, u32[]{:S(2)}) collective-permute-start(bf16[128,2048]{1,0:T(8,128)(2,1)} %get-tuple-element.38), channel_id=1, source_target_pairs={{0,64},{32,96},{64,128},{96,160},{128,192},{160,224},{192,0},{224,... | collective-permute-start | bytes 1572872 | tf_op jit(solution)/shard_map/ppermute | solution.py:26
  48.1 30.2 %all-to-all-start.1 = ((bf16[32,16,896]{2,1,0:T(8,128)(2,1)}), bf16[32,16,896]{2,1,0:T(8,128)(2,1)S(1)}, u32[]{:S(2)}, u32[]{:S(2)}) async-start(bf16[32,16,896]{2,1,0:T(8,128)(2,1)} %bitcast.12), calls=%async_computation.1 | async-start | bytes 1835008 | tf_op jit(solution)/shard_map/all_to_all | solution.py:241
  58.3 7.9 %collective-permute-start.7 = (bf16[64,2048]{1,0:T(8,128)(2,1)S(1)}, bf16[64,2048]{1,0:T(8,128)(2,1)S(1)}, u32[]{:S(2)}, u32[]{:S(2)}) collective-permute-start(bf16[64,2048]{1,0:T(8,128)(2,1)S(1)} %get-tuple-element.39), channel_id=1, source_target_pairs={{0,64},{32,96},{64,128},{96,160},{128,192},{160,224},{192,0},{224,... | collective-permute-start | bytes 786440 | tf_op jit(solution)/shard_map/ppermute | solution.py:26
  58.4 7.8 %collective-permute-start.8 = (bf16[64,2048]{1,0:T(8,128)(2,1)S(1)}, bf16[64,2048]{1,0:T(8,128)(2,1)S(1)}, u32[]{:S(2)}, u32[]{:S(2)}) collective-permute-start(bf16[64,2048]{1,0:T(8,128)(2,1)S(1)} %get-tuple-element.40), channel_id=1, source_target_pairs={{0,192},{32,224},{64,0},{96,32},{128,64},{160,96},{192,128},{224,1... | collective-permute-start | bytes 786440 | tf_op jit(solution)/shard_map/ppermute | solution.py:26
  66.6 18.6 %copy-start.2 = (bf16[896,1024]{1,0:T(8,128)(2,1)S(1)}, bf16[896,1024]{1,0:T(8,128)(2,1)}, u32[]{:S(2)}) copy-start(bf16[896,1024]{1,0:T(8,128)(2,1)} %pad_maximum_fusion.right_ref.refs_4_) | copy-start | bytes 5505028
  66.7 17.4 %collective-permute-start.9 = (bf16[128,1024]{1,0:T(8,128)(2,1)S(1)}, bf16[128,1024]{1,0:T(8,128)(2,1)S(1)}, u32[]{:S(2)}, u32[]{:S(2)}) collective-permute-start(bf16[128,1024]{1,0:T(8,128)(2,1)S(1)} %multiply_convert_fusion.3.refs_0_), channel_id=1, source_target_pairs={{0,64},{32,96},{64,128},{96,160},{128,192},{160,224},{192,0},{224,... | collective-permute-start | bytes 786440 | tf_op jit(solution)/shard_map/ppermute | solution.py:26
  66.8 18.5 %collective-permute-start.10 = (bf16[128,1024]{1,0:T(8,128)(2,1)S(1)}, bf16[128,1024]{1,0:T(8,128)(2,1)S(1)}, u32[]{:S(2)}, u32[]{:S(2)}) collective-permute-start(bf16[128,1024]{1,0:T(8,128)(2,1)S(1)} %multiply_convert_fusion.3.refs_0_), channel_id=1, source_target_pairs={{0,192},{32,224},{64,0},{96,32},{128,64},{160,96},{192,128},{224,1... | collective-permute-start | bytes 786440 | tf_op jit(solution)/shard_map/ppermute | solution.py:26
  69.4 15.9 %collective-permute-start.11 = (bf16[128,1024]{1,0:T(8,128)(2,1)S(1)}, bf16[128,1024]{1,0:T(8,128)(2,1)}, u32[]{:S(2)}, u32[]{:S(2)}) collective-permute-start(bf16[128,1024]{1,0:T(8,128)(2,1)S(1)} %multiply_convert_fusion.3.refs_0_), channel_id=1, source_target_pairs={{0,128},{32,160},{64,192},{96,224},{128,0},{160,32},{192,64},{224,... | collective-permute-start | bytes 786440 | tf_op jit(solution)/shard_map/ppermute | solution.py:26
  81.7 14.9 %collective-permute-start.15 = (bf16[128,1024]{1,0:T(8,128)(2,1)}, bf16[128,1024]{1,0:T(8,128)(2,1)}, u32[]{:S(2)}, u32[]{:S(2)}) collective-permute-start(bf16[128,1024]{1,0:T(8,128)(2,1)} %get-tuple-element.46), channel_id=1, source_target_pairs={{0,192},{32,224},{64,0},{96,32},{128,64},{160,96},{192,128},{224,1... | collective-permute-start | bytes 786440 | tf_op jit(solution)/shard_map/ppermute | solution.py:26
  84.0 12.6 %collective-permute-start.14 = (bf16[128,1024]{1,0:T(8,128)(2,1)}, bf16[128,1024]{1,0:T(8,128)(2,1)}, u32[]{:S(2)}, u32[]{:S(2)}) collective-permute-start(bf16[128,1024]{1,0:T(8,128)(2,1)} %get-tuple-element.45), channel_id=1, source_target_pairs={{0,64},{32,96},{64,128},{96,160},{128,192},{160,224},{192,0},{224,... | collective-permute-start | bytes 786440 | tf_op jit(solution)/shard_map/ppermute | solution.py:26
  84.0 14.0 %collective-permute-start.13 = (bf16[128,1024]{1,0:T(8,128)(2,1)}, bf16[128,1024]{1,0:T(8,128)(2,1)}, u32[]{:S(2)}, u32[]{:S(2)}) collective-permute-start(bf16[128,1024]{1,0:T(8,128)(2,1)} %get-tuple-element.44), channel_id=1, source_target_pairs={{0,128},{32,160},{64,192},{96,224},{128,0},{160,32},{192,64},{224,... | collective-permute-start | bytes 786440 | tf_op jit(solution)/shard_map/ppermute | solution.py:26
  88.5 9.5 %copy-start.9 = (f32[64,2048]{1,0:T(8,128)S(1)}, f32[64,2048]{1,0:T(8,128)}, u32[]{:S(2)}) copy-start(f32[64,2048]{1,0:T(8,128)} %copy-done.8) | copy-start | bytes 1572868
  88.5 9.5 %copy-start.11 = (f32[64,2048]{1,0:T(8,128)S(1)}, f32[64,2048]{1,0:T(8,128)}, u32[]{:S(2)}) copy-start(f32[64,2048]{1,0:T(8,128)} %copy-done.10) | copy-start | bytes 1572868
  88.5 9.5 %copy-start.19 = (bf16[128,1024]{1,0:T(8,128)(2,1)S(1)}, bf16[128,1024]{1,0:T(8,128)(2,1)}, u32[]{:S(2)}) copy-start(bf16[128,1024]{1,0:T(8,128)(2,1)} %get-tuple-element.47) | copy-start | bytes 786436
  88.5 42.9 %all-to-all-start.2 = ((bf16[32,16,896]{2,1,0:T(8,128)(2,1)}), bf16[32,16,896]{2,1,0:T(8,128)(2,1)S(1)}, u32[]{:S(2)}, u32[]{:S(2)}) async-start(bf16[32,16,896]{2,1,0:T(8,128)(2,1)} %bitcast.64), calls=%async_computation.2 | async-start | bytes 1835008 | tf_op jit(solution)/shard_map/all_to_all | solution.py:241
  100.7 23.0 %copy-start.5 = (f32[896,1024]{1,0:T(8,128)}, f32[896,1024]{1,0:T(8,128)S(1)}, u32[]{:S(2)}) copy-start(f32[896,1024]{1,0:T(8,128)S(1)} %fusion.25) | copy-start | bytes 11010052
  100.7 7.0 %copy-start.24 = (f32[512]{0:T(512)S(1)}, f32[512]{0:T(512)}, u32[]{:S(2)}) copy-start(f32[512]{0:T(512)} %copy-done.23) | copy-start | bytes 6148
  100.9 21.6 %collective-permute-start.20 = (bf16[448,1024]{1,0:T(8,128)(2,1)S(1)}, bf16[448,1024]{1,0:T(8,128)(2,1)S(1)}, u32[]{:S(2)}, u32[]{:S(2)}) collective-permute-start(bf16[448,1024]{1,0:T(8,128)(2,1)S(1)} %slice.132), channel_id=1, source_target_pairs={{0,32},{32,0},{64,96},{96,64},{128,160},{160,128},{192,224},{224,1... | collective-permute-start | bytes 2752520 | tf_op jit(solution)/shard_map/ppermute | solution.py:21
  105.0 14.6 %collective-permute-start.16 = (bf16[128,2048]{1,0:T(8,128)(2,1)S(1)}, bf16[128,2048]{1,0:T(8,128)(2,1)S(1)}, u32[]{:S(2)}, u32[]{:S(2)}) collective-permute-start(bf16[128,2048]{1,0:T(8,128)(2,1)S(1)} %pad_maximum_fusion.2.refs_0_), channel_id=1, source_target_pairs={{0,64},{32,96},{64,128},{96,160},{128,192},{160,224},{192,0},{224,... | collective-permute-start | bytes 1572872 | tf_op jit(solution)/shard_map/ppermute | solution.py:26
  106.1 13.6 %collective-permute-start.17 = (bf16[128,2048]{1,0:T(8,128)(2,1)S(1)}, bf16[128,2048]{1,0:T(8,128)(2,1)S(1)}, u32[]{:S(2)}, u32[]{:S(2)}) collective-permute-start(bf16[128,2048]{1,0:T(8,128)(2,1)S(1)} %pad_maximum_fusion.2.refs_0_), channel_id=1, source_target_pairs={{0,192},{32,224},{64,0},{96,32},{128,64},{160,96},{192,128},{224,1... | collective-permute-start | bytes 1572872 | tf_op jit(solution)/shard_map/ppermute | solution.py:26
  119.6 8.2 %collective-permute-start.18 = (bf16[64,2048]{1,0:T(8,128)(2,1)S(1)}, bf16[64,2048]{1,0:T(8,128)(2,1)S(1)}, u32[]{:S(2)}, u32[]{:S(2)}) collective-permute-start(bf16[64,2048]{1,0:T(8,128)(2,1)S(1)} %slice.86), channel_id=1, source_target_pairs={{0,64},{32,96},{64,128},{96,160},{128,192},{160,224},{192,0},{224,... | collective-permute-start | bytes 786440 | tf_op jit(solution)/shard_map/ppermute | solution.py:26
  119.8 8.1 %copy-start.1 = (bf16[896,2048]{1,0:T(8,128)(2,1)S(1)}, bf16[896,2048]{1,0:T(8,128)(2,1)}, u32[]{:S(2)}) copy-start(bf16[896,2048]{1,0:T(8,128)(2,1)} %shard_map.146.right_ref.refs_5_) | copy-start | bytes 11010052
  119.8 8.1 %collective-permute-start.19 = (bf16[64,2048]{1,0:T(8,128)(2,1)S(1)}, bf16[64,2048]{1,0:T(8,128)(2,1)S(1)}, u32[]{:S(2)}, u32[]{:S(2)}) collective-permute-start(bf16[64,2048]{1,0:T(8,128)(2,1)S(1)} %slice.87), channel_id=1, source_target_pairs={{0,192},{32,224},{64,0},{96,32},{128,64},{160,96},{192,128},{224,1... | collective-permute-start | bytes 786440 | tf_op jit(solution)/shard_map/ppermute | solution.py:26
  131.4 8.3 %copy-start.6 = (f32[1,1024,448]{1,2,0:T(8,128)S(1)}, f32[1,1024,448]{1,2,0:T(8,128)}, u32[]{:S(2)}) copy-start(f32[1,1024,448]{1,2,0:T(8,128)} %param.21) | copy-start | bytes 5505028
  131.4 86.8 %all-to-all-start.3 = ((bf16[32,16,896]{2,1,0:T(8,128)(2,1)}), bf16[32,16,896]{2,1,0:T(8,128)(2,1)}, u32[]{:S(2)}, u32[]{:S(2)}) async-start(bf16[32,16,896]{2,1,0:T(8,128)(2,1)} %bitcast.63), calls=%async_computation.3 | async-start | bytes 1835008 | tf_op jit(solution)/shard_map/all_to_all | solution.py:241
  140.8 6.7 %copy-start.21 = (s32[512]{0:T(512)S(1)}, s32[512]{0:T(512)}, u32[]{:S(2)}) copy-start(s32[512]{0:T(512)} %copy-done.20) | copy-start | bytes 6148
  140.8 32.0 %collective-permute-start.23 = (bf16[448,1024]{1,0:T(8,128)(2,1)}, bf16[448,1024]{1,0:T(8,128)(2,1)}, u32[]{:S(2)}, u32[]{:S(2)}) collective-permute-start(bf16[448,1024]{1,0:T(8,128)(2,1)} %convert_element_type.138), channel_id=1, source_target_pairs={{0,16},{1,17},{2,18},{3,19},{4,20},{5,21},{6,22},{7,23},{8,24},{9,... | collective-permute-start | bytes 2752520 | tf_op jit(solution)/shard_map/ppermute | solution.py:31
  144.5 47.9 %collective-permute-start.21 = (bf16[448,1024]{1,0:T(8,128)(2,1)}, bf16[448,1024]{1,0:T(8,128)(2,1)}, u32[]{:S(2)}, u32[]{:S(2)}) collective-permute-start(bf16[448,1024]{1,0:T(8,128)(2,1)} %convert_element_type.135), channel_id=1, source_target_pairs={{0,16},{1,17},{2,18},{3,19},{4,20},{5,21},{6,22},{7,23},{8,24},{9,... | collective-permute-start | bytes 2752520 | tf_op jit(solution)/shard_map/ppermute | solution.py:31
  145.3 66.8 %collective-permute-start.22 = (bf16[448,1024]{1,0:T(8,128)(2,1)}, bf16[448,1024]{1,0:T(8,128)(2,1)}, u32[]{:S(2)}, u32[]{:S(2)}) collective-permute-start(bf16[448,1024]{1,0:T(8,128)(2,1)} %fusion.6), channel_id=1, source_target_pairs={{0,16},{1,17},{2,18},{3,19},{4,20},{5,21},{6,22},{7,23},{8,24},{9,... | collective-permute-start | bytes 2752520 | tf_op jit(solution)/shard_map/ppermute | solution.py:31
  148.1 6.3 %copy-start.27 = (s32[16]{0:T(128)S(1)}, s32[16]{0:T(128)}, u32[]{:S(2)}) copy-start(s32[16]{0:T(128)} %param.16) | copy-start | bytes 196
  149.7 62.4 %copy-start.13 = (bf16[448,1024]{1,0:T(8,128)(2,1)S(1)}, bf16[448,1024]{1,0:T(8,128)(2,1)}, u32[]{:S(2)}) copy-start(bf16[448,1024]{1,0:T(8,128)(2,1)} %copy-done.12) | copy-start | bytes 2752516
  150.8 4.9 %collective-permute-start.12 = (bf16[448,256]{1,0:T(8,128)(2,1)S(1)}, bf16[448,256]{1,0:T(8,128)(2,1)S(1)}, u32[]{:S(2)}, u32[]{:S(2)}) collective-permute-start(bf16[448,256]{1,0:T(8,128)(2,1)S(1)} %slice.133), channel_id=1, source_target_pairs={{0,32},{32,0},{64,96},{96,64},{128,160},{160,128},{192,224},{224,1... | collective-permute-start | bytes 688136 | tf_op jit(solution)/shard_map/ppermute | solution.py:21
  157.4 60.8 %copy-start.16 = (bf16[512,256]{1,0:T(8,128)(2,1)S(1)}, bf16[512,256]{1,0:T(8,128)(2,1)}, u32[]{:S(2)}) copy-start(bf16[512,256]{1,0:T(8,128)(2,1)} %copy-done.15) | copy-start | bytes 786436
  219.8 3.3 %collective-permute-start.24 = (bf16[448,256]{1,0:T(8,128)(2,1)S(1)}, bf16[448,256]{1,0:T(8,128)(2,1)S(1)}, u32[]{:S(2)}, u32[]{:S(2)}) collective-permute-start(bf16[448,256]{1,0:T(8,128)(2,1)S(1)} %convolution_convert_fusion.1), channel_id=1, source_target_pairs={{0,32},{32,0},{64,96},{96,64},{128,160},{160,128},{192,224},{224,1... | collective-permute-start | bytes 688136 | tf_op jit(solution)/shard_map/ppermute | solution.py:21
  (9 other events, 31.5 us)

commit v9 on v7

--- a/solution.py
+++ b/solution.py
@@ -39,11 +39,11 @@
     return lax.optimization_barrier(tuple(values) + others)[: len(values)]
 
 
-def ordered_dot(y_pos, left, right, units, sizes):
+def ordered_dot(y_pos, left, right, units, unit, sizes):
     rows, depth = left.shape
     width = right.shape[1]
-    unit = rows // len(units)
-    per_block = len(units) // 4
+    taken = len(units) * unit
+    per_block = rows // (4 * unit)
     tile = 512
 
     def body(pos, left_ref, right_ref, *refs):
@@ -74,12 +74,12 @@
                 pl.BlockSpec((depth, tile), lambda i, pos: (0, i)),
             ],
             out_specs=[pl.BlockSpec((size, tile), lambda i, pos: (0, i)) for size in sizes],
-            scratch_shapes=[pltpu.VMEM((rows, depth), BF)],
+            scratch_shapes=[pltpu.VMEM((taken, depth), BF)],
         ),
         compiler_params=pltpu.CompilerParams(vmem_limit_bytes=16 << 20),
         cost_estimate=pl.CostEstimate(
-            flops=2 * rows * depth * width,
-            bytes_accessed=2 * (rows * depth + depth * width + rows * width),
+            flops=2 * taken * depth * width,
+            bytes_accessed=2 * (rows * depth + depth * width + taken * width),
             transcendentals=0,
         ),
     )(y_pos.reshape(1), left, pltpu.with_memory_space_constraint(right, pltpu.HBM))
@@ -123,7 +123,8 @@
     )(y_pos.reshape(1), *parts, right)
 
 
-RING_UNITS = ((2, 0), (1, 1), (2, 1), (3, 0), (0, 0), (0, 1), (1, 0), (3, 1))
+RING_FIRST = ((2, 0), (1, 1), (2, 1), (3, 0))
+RING_REST = ((0, 0), (0, 1), (1, 0), (3, 1))
 
 
 def ring_sum(to_right, to_left, rest, chips):
@@ -262,14 +263,15 @@
     arrived_grad = exchange(grad_rows)
     hidden_units = down_weight.shape[1]
     half = rows // (2 * chips)
-    products = ordered_dot(y_pos, arrived, gate_up, RING_UNITS, (2 * half, 2 * half, 4 * half))
-    preact = ring_sum(*products, chips)
+    sent = ordered_dot(y_pos, arrived, gate_up, RING_FIRST, half, (2 * half, 2 * half))
+    (kept,) = ordered_dot(y_pos, arrived, gate_up, RING_REST, half, (4 * half,))
+    preact = ring_sum(*sent, kept, chips)
     gate_pre, up_pre = preact[:, :hidden_units], preact[:, hidden_units:]
     sig = jax.nn.sigmoid(gate_pre)
     hidden_shard = (gate_pre * sig * up_pre).astype(BF)
     arrived_grad = tie(arrived_grad, hidden_shard)
     terms = ordered_dot(
-        y_pos, arrived_grad, down_cols, ((2, 0), (1, 0), (3, 0), (0, 0)), (2 * half,) * 4
+        y_pos, arrived_grad, down_cols, ((2, 0), (1, 0), (3, 0), (0, 0)), 2 * half, (2 * half,) * 4
     )
     gathered = direct_gather(hidden_shard)
     gathered = tie_all(gathered, *terms)

time: 225 us -> 226 us (level)
  waiting for transfers between devices: 99.9 us -> 88.6 us
  starting transfers between devices: 71.1 us -> 76 us
  Pallas kernels: 21.8 us -> 24.9 us
    all_to_all x4, waiting for transfers between devices: 15.5 us -> 9.8 us  [exchange(): lax.all_to_all(block.reshape(experts, own_slots, pair_cols), 'expert', 0,...]
    ppermute x14, waiting for transfers between devices: 24.6 us -> 20 us  [chip_shift(): lax.ppermute(block, 'dp', [(i, (i + 2 * step) % count) for i in range(cou...]
    pallas_call x2 -> x3, Pallas kernels: 9.15 us -> 12.9 us  [ordered_dot(): pl.pallas_call(body, out_shape=[pltpu.HBM((size, width), BF) for size in...]
    unnamed x52 -> x44, local copies, waits for them, and re-layouts: 0.12 us -> 2.51 us
  transfers between devices with their start and end apart: 29 -> 29, of which waited for: 13 -> 11; matrix products, arithmetic and copies ran while one was open for 11% -> 12% of each run, Pallas kernels for 7% -> 9%
where the time goes in v9:
time: 226 us; the launch traced here: 225 us
  waiting for transfers between devices  88.6 us (39%)
  starting transfers between devices  76 us (34%)
  Pallas kernels  24.9 us (11%)
  other arithmetic  20.6 us (9%)
  matrix products  10.2 us (5%)
  local copies, waits for them, and re-layouts  3.2 us (1%)
    ppermute x3, waiting for transfers between devices, expert_swap(): lax.ppermute(block, 'expert', [(i, i ^ count // 2) for i in range(count)])  53.7 us
    all_to_all x4, starting transfers between devices, exchange(): lax.all_to_all(block.reshape(experts, own_slots, pair_cols), 'expert', 0,...  34.9 us
    ppermute x14, waiting for transfers between devices, chip_shift(): lax.ppermute(block, 'dp', [(i, (i + 2 * step) % count) for i in range(cou...  20 us
    ppermute x14, starting transfers between devices, chip_shift(): lax.ppermute(block, 'dp', [(i, (i + 2 * step) % count) for i in range(cou...  19.1 us
    ppermute x8, starting transfers between devices, core_swap(): lax.ppermute(block, 'dp', [(i, i ^ 1) for i in range(lax.axis_size('dp'))])  16.3 us
    pallas_call x3, Pallas kernels, ordered_dot(): pl.pallas_call(body, out_shape=[pltpu.HBM((size, width), BF) for size in...  12.9 us
    dot_general x6, matrix products, dot(): lax.dot_general(a, b, (((ca,), (cb,)), ((), ())), preferred_element_type=...  10.2 us
    all_to_all x4, waiting for transfers between devices, exchange(): lax.all_to_all(block.reshape(experts, own_slots, pair_cols), 'expert', 0,...  9.8 us
  transfers between devices with their start and end apart: 29, of which 11 were waited for; matrix products, arithmetic and copies ran while one was open for 12% of the time, Pallas kernels for 9%

profile of v9, /device:TPU:1, one launch (start us, length us, event | category | flops | bytes accessed | tf_op | source)
XLA Modules:
  0.0 225.2 jit_solution(7772185885512627276)
XLA Ops:
  0.7 3.3 %collective-permute-start = (bf16[448,256]{1,0:T(8,128)(2,1)}, bf16[448,256]{1,0:T(8,128)(2,1)S(1)}, u32[]{:S(2)}, u32[]{:S(2)}) collective-permute-start(bf16[448,256]{1,0:T(8,128)(2,1)} %bitcast.66), channel_id=1, source_target_pairs={{0,32},{32,0},{64,96},{96,64},{128,160},{160,128},{192,224},{224,1... | collective-permute-start | bytes 688136 | tf_op jit(solution)/shard_map/ppermute | solution.py:21
  5.3 2.3 %convolution_convert_fusion = bf16[512,896]{1,0:T(8,128)(2,1)} fusion(bf16[448,256]{1,0:T(8,128)(2,1)S(1)} %collective-permute-done, bf16[448,256]{1,0:T(8,128)(2,1)} %bitcast.67, s32[512]{0:T(512)S(1)} %broadcast_select_fusion.1), kind=kOutput, calls=%fused_computation.9 | convolution fusion | flops 236388352 | bytes 1378304 | tf_op jit(solution)/shard_map/dot_general | solution.py:17
  7.6 9.3 %all-to-all-start = ((bf16[32,16,896]{2,1,0:T(8,128)(2,1)}), bf16[32,16,896]{2,1,0:T(8,128)(2,1)S(1)}, u32[]{:S(2)}, u32[]{:S(2)}) async-start(bf16[32,16,896]{2,1,0:T(8,128)(2,1)} %bitcast.62), calls=%async_computation | async-start | bytes 1835008 | tf_op jit(solution)/shard_map/all_to_all | solution.py:242
  19.1 3.7 %collective-permute-done.4 = bf16[448,256]{1,0:T(8,128)(2,1)S(1)} collective-permute-done((bf16[448,256]{1,0:T(8,128)(2,1)S(1)}, bf16[448,256]{1,0:T(8,128)(2,1)S(1)}, u32[]{:S(2)}, u32[]{:S(2)}) %collective-permute-start.4) | collective-permute-done | bytes 229408 | tf_op jit(solution)/shard_map/ppermute | solution.py:21
  22.8 1.4 multiply_convert_fusion
  24.2 6.3 %shard_map.146.right_ref.refs_5_ = bf16[896,2048]{1,0:T(8,128)(2,1)} custom-call(bf16[448,1024]{1,0:T(8,128)(2,1)S(1)} %bitcast.51, bf16[448,1024]{1,0:T(8,128)(2,1)S(1)} %bitcast.53, bf16[448,1024]{1,0:T(8,128)(2,1)} %collective-permute-done.1.gate_b, bf16[448,1024]{1,0:T(8,128)(2,1)} %collective-permute-done.2.up_b), custom_call_target="tpu_custom_call" | custom-call | bytes 7340032 | tf_op jit(solution)/shard_map/pallas_call | solution.py:187
  30.5 2.6 %pad_maximum_fusion.right_ref.refs_4_ = bf16[896,1024]{1,0:T(8,128)(2,1)} fusion(bf16[448,1024]{1,0:T(8,128)(2,1)} %collective-permute-done.3, bf16[448,1024]{1,0:T(8,128)(2,1)S(1)} %bitcast.59), kind=kLoop, calls=%fused_computation.4 | loop fusion | flops 3670016 | bytes 3670016 | tf_op jit(solution)/shard_map/concatenate | solution.py:163
  33.1 6.2 %all-to-all-done = bf16[32,16,896]{2,1,0:T(8,128)(2,1)S(1)} async-done(((bf16[32,16,896]{2,1,0:T(8,128)(2,1)}), bf16[32,16,896]{2,1,0:T(8,128)(2,1)S(1)}, u32[]{:S(2)}, u32[]{:S(2)}) %all-to-all-start) | async-done | bytes 917536 | tf_op jit(solution)/shard_map/all_to_all | solution.py:242
  39.3 4.7 %shard_map.148 = (bf16[128,2048]{1,0:T(8,128)(2,1)}, bf16[128,2048]{1,0:T(8,128)(2,1)}) custom-call(s32[1]{0:T(128)} %bitcast.pos, bf16[512,896]{1,0:T(8,128)(2,1)S(1)} %bitcast.46, bf16[896,2048]{1,0:T(8,128)(2,1)} %shard_map.146.right_ref.refs_5_), custom_call_target="tpu_custom_call" | custom-call | flops 939524096 | bytes 5636096 | tf_op jit(solution)/shard_map/pallas_call | solution.py:66
  44.0 2.7 %collective-permute-start.5 = (bf16[128,2048]{1,0:T(8,128)(2,1)}, bf16[128,2048]{1,0:T(8,128)(2,1)S(1)}, u32[]{:S(2)}, u32[]{:S(2)}) collective-permute-start(bf16[128,2048]{1,0:T(8,128)(2,1)} %get-tuple-element.35), channel_id=1, source_target_pairs={{0,192},{32,224},{64,0},{96,32},{128,64},{160,96},{192,128},{224,1... | collective-permute-start | bytes 1572872 | tf_op jit(solution)/shard_map/ppermute | solution.py:26
  46.8 8.1 %all-to-all-start.1 = ((bf16[32,16,896]{2,1,0:T(8,128)(2,1)}), bf16[32,16,896]{2,1,0:T(8,128)(2,1)S(1)}, u32[]{:S(2)}, u32[]{:S(2)}) async-start(bf16[32,16,896]{2,1,0:T(8,128)(2,1)} %bitcast.12), calls=%async_computation.1 | async-start | bytes 1835008 | tf_op jit(solution)/shard_map/all_to_all | solution.py:242
  54.9 4.8 %shard_map.147 = bf16[256,2048]{1,0:T(8,128)(2,1)} custom-call(s32[1]{0:T(128)} %bitcast.pos, bf16[512,896]{1,0:T(8,128)(2,1)S(1)} %bitcast.47, bf16[896,2048]{1,0:T(8,128)(2,1)} %shard_map.146.right_ref.refs_5_), custom_call_target="tpu_custom_call" | custom-call | flops 939524096 | bytes 5636096 | tf_op jit(solution)/shard_map/pallas_call | solution.py:66
  59.7 1.4 add_convert_fusion
  61.2 2.7 %collective-permute-start.8 = (bf16[64,2048]{1,0:T(8,128)(2,1)S(1)}, bf16[64,2048]{1,0:T(8,128)(2,1)S(1)}, u32[]{:S(2)}, u32[]{:S(2)}) collective-permute-start(bf16[64,2048]{1,0:T(8,128)(2,1)S(1)} %get-tuple-element.38), channel_id=1, source_target_pairs={{0,192},{32,224},{64,0},{96,32},{128,64},{160,96},{192,128},{224,1... | collective-permute-start | bytes 786440 | tf_op jit(solution)/shard_map/ppermute | solution.py:26
  63.9 3.8 %collective-permute-done.7 = bf16[64,2048]{1,0:T(8,128)(2,1)S(1)} collective-permute-done((bf16[64,2048]{1,0:T(8,128)(2,1)S(1)}, bf16[64,2048]{1,0:T(8,128)(2,1)S(1)}, u32[]{:S(2)}, u32[]{:S(2)}) %collective-permute-start.7) | collective-permute-done | bytes 262176 | tf_op jit(solution)/shard_map/ppermute | solution.py:26
  67.7 1.2 convert_add_fusion.2
  69.0 1.4 collective-permute-start.9
  70.5 1.5 collective-permute-start.10
  72.0 1.5 collective-permute-start.11
  73.4 3.6 %all-to-all-done.1 = bf16[32,16,896]{2,1,0:T(8,128)(2,1)S(1)} async-done(((bf16[32,16,896]{2,1,0:T(8,128)(2,1)}), bf16[32,16,896]{2,1,0:T(8,128)(2,1)S(1)}, u32[]{:S(2)}, u32[]{:S(2)}) %all-to-all-start.1) | async-done | bytes 917536 | tf_op jit(solution)/shard_map/all_to_all | solution.py:242
  77.0 3.4 %shard_map.149 = (bf16[128,1024]{1,0:T(8,128)(2,1)}, bf16[128,1024]{1,0:T(8,128)(2,1)}, bf16[128,1024]{1,0:T(8,128)(2,1)}, bf16[128,1024]{1,0:T(8,128)(2,1)}) custom-call(s32[1]{0:T(128)} %bitcast.pos, bf16[512,896]{1,0:T(8,128)(2,1)S(1)} %bitcast.48, bf16[896,1024]{1,0:T(8,128)(2,1)} %pad_maximum_fusion.right_ref.refs_4_), custom_call_target="tpu_custom_call" | custom-call | flops 939524096 | bytes 3801088 | tf_op jit(solution)/shard_map/pallas_call | solution.py:66
  80.4 2.3 %collective-permute-start.15 = (bf16[128,1024]{1,0:T(8,128)(2,1)}, bf16[128,1024]{1,0:T(8,128)(2,1)S(1)}, u32[]{:S(2)}, u32[]{:S(2)}) collective-permute-start(bf16[128,1024]{1,0:T(8,128)(2,1)} %get-tuple-element.44), channel_id=1, source_target_pairs={{0,192},{32,224},{64,0},{96,32},{128,64},{160,96},{192,128},{224,1... | collective-permute-start | bytes 786440 | tf_op jit(solution)/shard_map/ppermute | solution.py:26
  82.7 1.2 collective-permute-start.13
  84.0 1.5 copy-done.2
  85.5 2.3 %shard_map.150 = (bf16[512,896]{1,0:T(8,128)(2,1)}, bf16[512,1024]{1,0:T(8,128)(2,1)}) custom-call(s32[1]{0:T(128)} %bitcast.pos, bf16[128,1024]{1,0:T(8,128)(2,1)S(1)} %multiply_convert_fusion.3.refs_0_, bf16[128,1024]{1,0:T(8,128)(2,1)S(1)} %collective-permute-done.9.refs_1_, bf16[128,1024]{1,0:T(8,128)(2,1)S(1)} %collective-permute-done.10.refs_2_, ...), custom_call_target="tpu_custom_call" | custom-call | flops 939524096 | bytes 3801088 | tf_op jit(solution)/shard_map/pallas_call | solution.py:110
  87.7 8.0 %all-to-all-start.2 = ((bf16[32,16,896]{2,1,0:T(8,128)(2,1)}), bf16[32,16,896]{2,1,0:T(8,128)(2,1)}, u32[]{:S(2)}, u32[]{:S(2)}) async-start(bf16[32,16,896]{2,1,0:T(8,128)(2,1)} %bitcast.61), calls=%async_computation.2 | async-start | bytes 1835008 | tf_op jit(solution)/shard_map/all_to_all | solution.py:242
  95.8 1.5 multiply_convert_fusion.2
  97.3 1.2 fusion.26
  98.7 6.5 %collective-permute-start.20 = (bf16[448,1024]{1,0:T(8,128)(2,1)S(1)}, bf16[448,1024]{1,0:T(8,128)(2,1)S(1)}, u32[]{:S(2)}, u32[]{:S(2)}) collective-permute-start(bf16[448,1024]{1,0:T(8,128)(2,1)S(1)} %slice.141), channel_id=1, source_target_pairs={{0,32},{32,0},{64,96},{96,64},{128,160},{160,128},{192,224},{224,1... | collective-permute-start | bytes 2752520 | tf_op jit(solution)/shard_map/ppermute | solution.py:21
  105.2 2.2 collective-permute-start.16
  107.8 12.0 %collective-permute-done.16.refs_1_ = bf16[128,2048]{1,0:T(8,128)(2,1)S(1)} collective-permute-done((bf16[128,2048]{1,0:T(8,128)(2,1)S(1)}, bf16[128,2048]{1,0:T(8,128)(2,1)S(1)}, u32[]{:S(2)}, u32[]{:S(2)}) %collective-permute-start.16) | collective-permute-done | bytes 524320 | tf_op jit(solution)/shard_map/ppermute | solution.py:26
  121.0 1.7 collective-permute-start.19
  122.8 1.3 fusion.3
  124.0 4.2 %collective-permute-done.18.refs_3_ = bf16[64,2048]{1,0:T(8,128)(2,1)S(1)} collective-permute-done((bf16[64,2048]{1,0:T(8,128)(2,1)S(1)}, bf16[64,2048]{1,0:T(8,128)(2,1)S(1)}, u32[]{:S(2)}, u32[]{:S(2)}) %collective-permute-start.18) | collective-permute-done | bytes 262176 | tf_op jit(solution)/shard_map/ppermute | solution.py:26
  128.2 3.5 %shard_map.151 = bf16[512,896]{1,0:T(8,128)(2,1)} custom-call(s32[1]{0:T(128)} %bitcast.pos, bf16[128,2048]{1,0:T(8,128)(2,1)S(1)} %pad_maximum_fusion.2.refs_0_, bf16[128,2048]{1,0:T(8,128)(2,1)S(1)} %collective-permute-done.16.refs_1_, bf16[128,2048]{1,0:T(8,128)(2,1)S(1)} %collective-permute-done.17.refs_2_, ...), custom_call_target="tpu_custom_call" | custom-call | flops 1879048192 | bytes 6684672 | tf_op jit(solution)/shard_map/pallas_call | solution.py:110
  131.7 9.5 %all-to-all-start.3 = ((bf16[32,16,896]{2,1,0:T(8,128)(2,1)}), bf16[32,16,896]{2,1,0:T(8,128)(2,1)}, u32[]{:S(2)}, u32[]{:S(2)}) async-start(bf16[32,16,896]{2,1,0:T(8,128)(2,1)} %bitcast.60), calls=%async_computation.3 | async-start | bytes 1835008 | tf_op jit(solution)/shard_map/all_to_all | solution.py:242
  142.3 2.7 %collective-permute-start.23 = (bf16[448,1024]{1,0:T(8,128)(2,1)}, bf16[448,1024]{1,0:T(8,128)(2,1)}, u32[]{:S(2)}, u32[]{:S(2)}) collective-permute-start(bf16[448,1024]{1,0:T(8,128)(2,1)} %convert_element_type.133), channel_id=1, source_target_pairs={{0,16},{1,17},{2,18},{3,19},{4,20},{5,21},{6,22},{7,23},{8,24},{9,... | collective-permute-start | bytes 2752520 | tf_op jit(solution)/shard_map/ppermute | solution.py:31
  146.8 2.2 collective-permute-start.22
  149.0 1.8 fusion.9
  150.9 1.8 convolution_add_fusion
  153.6 3.3 %collective-permute-start.12 = (bf16[448,256]{1,0:T(8,128)(2,1)S(1)}, bf16[448,256]{1,0:T(8,128)(2,1)S(1)}, u32[]{:S(2)}, u32[]{:S(2)}) collective-permute-start(bf16[448,256]{1,0:T(8,128)(2,1)S(1)} %slice.143), channel_id=1, source_target_pairs={{0,32},{32,0},{64,96},{96,64},{128,160},{160,128},{192,224},{224,1... | collective-permute-start | bytes 688136 | tf_op jit(solution)/shard_map/ppermute | solution.py:21
  158.2 1.8 fusion.5
  159.9 14.4 %collective-permute-done.23 = bf16[448,1024]{1,0:T(8,128)(2,1)} collective-permute-done((bf16[448,1024]{1,0:T(8,128)(2,1)}, bf16[448,1024]{1,0:T(8,128)(2,1)}, u32[]{:S(2)}, u32[]{:S(2)}) %collective-permute-start.23) | collective-permute-done | bytes 917536 | tf_op jit(solution)/shard_map/ppermute | solution.py:31
  174.3 19.7 %collective-permute-done.21 = bf16[448,1024]{1,0:T(8,128)(2,1)} collective-permute-done((bf16[448,1024]{1,0:T(8,128)(2,1)}, bf16[448,1024]{1,0:T(8,128)(2,1)}, u32[]{:S(2)}, u32[]{:S(2)}) %collective-permute-start.21) | collective-permute-done | bytes 917536 | tf_op jit(solution)/shard_map/ppermute | solution.py:31
  194.0 19.7 %collective-permute-done.22 = bf16[448,1024]{1,0:T(8,128)(2,1)} collective-permute-done((bf16[448,1024]{1,0:T(8,128)(2,1)}, bf16[448,1024]{1,0:T(8,128)(2,1)}, u32[]{:S(2)}, u32[]{:S(2)}) %collective-permute-start.22) | collective-permute-done | bytes 917536 | tf_op jit(solution)/shard_map/ppermute | solution.py:31
  213.6 6.0 %divide_convert_fusion = (bf16[448,1024]{1,0:T(8,128)(2,1)}, f32[448,1024]{1,0:T(8,128)}, f32[448,1024]{1,0:T(8,128)}) fusion(bf16[448,1024]{1,0:T(8,128)(2,1)S(1)} %collective-permute-done.20, f32[896,1024]{1,0:T(8,128)} %copy-done.5, bf16[448,1024]{1,0:T(8,128)(2,1)} %collective-permute-done.22, f32[1,1024,448]{1,2,0:T(8,128)S(1)} %copy-done.6, ...), kind=kLoop, calls=%fused_computation.5 | loop fusion | flops 8257536 | bytes 13762561 | tf_op jit(solution)/shard_map/convert_element_type | solution.py:301
  219.7 1.7 fusion.2
  221.4 1.9 collective-permute-start.24
  (95 shorter events, 11.9 us)
Async XLA Ops:
  0.6 4.2 %copy-start = (s32[1,32,32]{2,1,0:T(8,128)S(1)}, s32[1,32,32]{2,1,0:T(8,128)}, u32[]{:S(2)}) copy-start(s32[1,32,32]{2,1,0:T(8,128)} %param.13) | copy-start | bytes 12292
  0.6 16.3 %copy-start.3 = (bf16[1,448,1024]{2,1,0:T(8,128)(2,1)S(1)}, bf16[1,448,1024]{2,1,0:T(8,128)(2,1)}, u32[]{:S(2)}) copy-start(bf16[1,448,1024]{2,1,0:T(8,128)(2,1)} %param.17) | copy-start | bytes 2752516
  0.7 17.1 %copy-start.4 = (bf16[1,448,1024]{2,1,0:T(8,128)(2,1)S(1)}, bf16[1,448,1024]{2,1,0:T(8,128)(2,1)}, u32[]{:S(2)}) copy-start(bf16[1,448,1024]{2,1,0:T(8,128)(2,1)} %param.18) | copy-start | bytes 2752516
  0.7 17.6 %copy-start.20 = (bf16[256,448]{0,1:T(8,128)(2,1)S(1)}, bf16[256,448]{0,1:T(8,128)(2,1)}, u32[]{:S(2)}) copy-start(bf16[256,448]{0,1:T(8,128)(2,1)} %param.12) | copy-start | bytes 688132
  0.7 17.7 %copy-start.14 = (f32[1,32,32]{2,1,0:T(8,128)S(1)}, f32[1,32,32]{2,1,0:T(8,128)}, u32[]{:S(2)}) copy-start(f32[1,32,32]{2,1,0:T(8,128)} %param.15) | copy-start | bytes 12292
  0.7 4.6 %collective-permute-start = (bf16[448,256]{1,0:T(8,128)(2,1)}, bf16[448,256]{1,0:T(8,128)(2,1)S(1)}, u32[]{:S(2)}, u32[]{:S(2)}) collective-permute-start(bf16[448,256]{1,0:T(8,128)(2,1)} %bitcast.66), channel_id=1, source_target_pairs={{0,32},{32,0},{64,96},{96,64},{128,160},{160,128},{192,224},{224,1... | collective-permute-start | bytes 688136 | tf_op jit(solution)/shard_map/ppermute | solution.py:21
  5.0 19.2 %copy-start.17 = (s32[512]{0:T(512)}, s32[512]{0:T(512)S(1)}, u32[]{:S(2)}) copy-start(s32[512]{0:T(512)S(1)} %broadcast_select_fusion.1) | copy-start | bytes 6148
  7.6 31.6 %all-to-all-start = ((bf16[32,16,896]{2,1,0:T(8,128)(2,1)}), bf16[32,16,896]{2,1,0:T(8,128)(2,1)S(1)}, u32[]{:S(2)}, u32[]{:S(2)}) async-start(bf16[32,16,896]{2,1,0:T(8,128)(2,1)} %bitcast.62), calls=%async_computation | async-start | bytes 1835008 | tf_op jit(solution)/shard_map/all_to_all | solution.py:242
  17.0 7.2 %collective-permute-start.1 = (bf16[448,1024]{1,0:T(8,128)(2,1)S(1)}, bf16[448,1024]{1,0:T(8,128)(2,1)}, u32[]{:S(2)}, u32[]{:S(2)}) collective-permute-start(bf16[448,1024]{1,0:T(8,128)(2,1)S(1)} %bitcast.50), channel_id=1, source_target_pairs={{0,32},{32,0},{64,96},{96,64},{128,160},{160,128},{192,224},{224,1... | collective-permute-start | bytes 2752520 | tf_op jit(solution)/shard_map/ppermute | solution.py:21
  17.7 6.5 %collective-permute-start.2 = (bf16[448,1024]{1,0:T(8,128)(2,1)S(1)}, bf16[448,1024]{1,0:T(8,128)(2,1)}, u32[]{:S(2)}, u32[]{:S(2)}) collective-permute-start(bf16[448,1024]{1,0:T(8,128)(2,1)S(1)} %bitcast.52), channel_id=1, source_target_pairs={{0,32},{32,0},{64,96},{96,64},{128,160},{160,128},{192,224},{224,1... | collective-permute-start | bytes 2752520 | tf_op jit(solution)/shard_map/ppermute | solution.py:21
  17.8 12.6 %collective-permute-start.3 = (bf16[448,1024]{1,0:T(8,128)(2,1)}, bf16[448,1024]{1,0:T(8,128)(2,1)}, u32[]{:S(2)}, u32[]{:S(2)}) collective-permute-start(bf16[448,1024]{1,0:T(8,128)(2,1)} %bitcast.58), channel_id=1, source_target_pairs={{0,32},{32,0},{64,96},{96,64},{128,160},{160,128},{192,224},{224,1... | collective-permute-start | bytes 2752520 | tf_op jit(solution)/shard_map/ppermute | solution.py:21
  18.3 4.5 %collective-permute-start.4 = (bf16[448,256]{1,0:T(8,128)(2,1)S(1)}, bf16[448,256]{1,0:T(8,128)(2,1)S(1)}, u32[]{:S(2)}, u32[]{:S(2)}) collective-permute-start(bf16[448,256]{1,0:T(8,128)(2,1)S(1)} %bitcast.68), channel_id=1, source_target_pairs={{0,32},{32,0},{64,96},{96,64},{128,160},{160,128},{192,224},{224,1... | collective-permute-start | bytes 688136 | tf_op jit(solution)/shard_map/ppermute | solution.py:21
  19.1 11.4 %copy-start.15 = (f32[512]{0:T(512)}, f32[512]{0:T(512)S(1)}, u32[]{:S(2)}) copy-start(f32[512]{0:T(512)S(1)} %get-tuple-element.65) | copy-start | bytes 6148
  24.2 6.3 %copy-start.11 = (bf16[1,1024,448]{1,2,0:T(8,128)(2,1)S(1)}, bf16[1,1024,448]{1,2,0:T(8,128)(2,1)}, u32[]{:S(2)}) copy-start(bf16[1,1024,448]{1,2,0:T(8,128)(2,1)} %param.19) | copy-start | bytes 2752516
  44.0 15.6 %collective-permute-start.5 = (bf16[128,2048]{1,0:T(8,128)(2,1)}, bf16[128,2048]{1,0:T(8,128)(2,1)S(1)}, u32[]{:S(2)}, u32[]{:S(2)}) collective-permute-start(bf16[128,2048]{1,0:T(8,128)(2,1)} %get-tuple-element.35), channel_id=1, source_target_pairs={{0,192},{32,224},{64,0},{96,32},{128,64},{160,96},{192,128},{224,1... | collective-permute-start | bytes 1572872 | tf_op jit(solution)/shard_map/ppermute | solution.py:26
  46.8 12.9 %collective-permute-start.6 = (bf16[128,2048]{1,0:T(8,128)(2,1)}, bf16[128,2048]{1,0:T(8,128)(2,1)S(1)}, u32[]{:S(2)}, u32[]{:S(2)}) collective-permute-start(bf16[128,2048]{1,0:T(8,128)(2,1)} %get-tuple-element.36), channel_id=1, source_target_pairs={{0,64},{32,96},{64,128},{96,160},{128,192},{160,224},{192,0},{224,... | collective-permute-start | bytes 1572872 | tf_op jit(solution)/shard_map/ppermute | solution.py:26
  46.8 30.2 %all-to-all-start.1 = ((bf16[32,16,896]{2,1,0:T(8,128)(2,1)}), bf16[32,16,896]{2,1,0:T(8,128)(2,1)S(1)}, u32[]{:S(2)}, u32[]{:S(2)}) async-start(bf16[32,16,896]{2,1,0:T(8,128)(2,1)} %bitcast.12), calls=%async_computation.1 | async-start | bytes 1835008 | tf_op jit(solution)/shard_map/all_to_all | solution.py:242
  59.7 8.1 %copy-start.8 = (bf16[256,2048]{1,0:T(8,128)(2,1)S(1)}, bf16[256,2048]{1,0:T(8,128)(2,1)}, u32[]{:S(2)}) copy-start(bf16[256,2048]{1,0:T(8,128)(2,1)} %shard_map.147) | copy-start | bytes 3145732
  59.7 8.0 %copy-start.12 = (bf16[128,2048]{1,0:T(8,128)(2,1)}, bf16[128,2048]{1,0:T(8,128)(2,1)S(1)}, u32[]{:S(2)}) copy-start(bf16[128,2048]{1,0:T(8,128)(2,1)S(1)} %collective-permute-done.6) | copy-start | bytes 1572868
  61.1 6.7 %collective-permute-start.7 = (bf16[64,2048]{1,0:T(8,128)(2,1)S(1)}, bf16[64,2048]{1,0:T(8,128)(2,1)S(1)}, u32[]{:S(2)}, u32[]{:S(2)}) collective-permute-start(bf16[64,2048]{1,0:T(8,128)(2,1)S(1)} %get-tuple-element.37), channel_id=1, source_target_pairs={{0,64},{32,96},{64,128},{96,160},{128,192},{160,224},{192,0},{224,... | collective-permute-start | bytes 786440 | tf_op jit(solution)/shard_map/ppermute | solution.py:26
  61.2 6.6 %collective-permute-start.8 = (bf16[64,2048]{1,0:T(8,128)(2,1)S(1)}, bf16[64,2048]{1,0:T(8,128)(2,1)S(1)}, u32[]{:S(2)}, u32[]{:S(2)}) collective-permute-start(bf16[64,2048]{1,0:T(8,128)(2,1)S(1)} %get-tuple-element.38), channel_id=1, source_target_pairs={{0,192},{32,224},{64,0},{96,32},{128,64},{160,96},{192,128},{224,1... | collective-permute-start | bytes 786440 | tf_op jit(solution)/shard_map/ppermute | solution.py:26
  69.0 13.7 %collective-permute-start.9 = (bf16[128,1024]{1,0:T(8,128)(2,1)S(1)}, bf16[128,1024]{1,0:T(8,128)(2,1)S(1)}, u32[]{:S(2)}, u32[]{:S(2)}) collective-permute-start(bf16[128,1024]{1,0:T(8,128)(2,1)S(1)} %multiply_convert_fusion.3.refs_0_), channel_id=1, source_target_pairs={{0,64},{32,96},{64,128},{96,160},{128,192},{160,224},{192,0},{224,... | collective-permute-start | bytes 786440 | tf_op jit(solution)/shard_map/ppermute | solution.py:26
  70.5 13.5 %collective-permute-start.10 = (bf16[128,1024]{1,0:T(8,128)(2,1)S(1)}, bf16[128,1024]{1,0:T(8,128)(2,1)S(1)}, u32[]{:S(2)}, u32[]{:S(2)}) collective-permute-start(bf16[128,1024]{1,0:T(8,128)(2,1)S(1)} %multiply_convert_fusion.3.refs_0_), channel_id=1, source_target_pairs={{0,192},{32,224},{64,0},{96,32},{128,64},{160,96},{192,128},{224,1... | collective-permute-start | bytes 786440 | tf_op jit(solution)/shard_map/ppermute | solution.py:26
  72.0 12.0 %collective-permute-start.11 = (bf16[128,1024]{1,0:T(8,128)(2,1)S(1)}, bf16[128,1024]{1,0:T(8,128)(2,1)S(1)}, u32[]{:S(2)}, u32[]{:S(2)}) collective-permute-start(bf16[128,1024]{1,0:T(8,128)(2,1)S(1)} %multiply_convert_fusion.3.refs_0_), channel_id=1, source_target_pairs={{0,128},{32,160},{64,192},{96,224},{128,0},{160,32},{192,64},{224,... | collective-permute-start | bytes 786440 | tf_op jit(solution)/shard_map/ppermute | solution.py:26
  80.4 15.4 %collective-permute-start.15 = (bf16[128,1024]{1,0:T(8,128)(2,1)}, bf16[128,1024]{1,0:T(8,128)(2,1)S(1)}, u32[]{:S(2)}, u32[]{:S(2)}) collective-permute-start(bf16[128,1024]{1,0:T(8,128)(2,1)} %get-tuple-element.44), channel_id=1, source_target_pairs={{0,192},{32,224},{64,0},{96,32},{128,64},{160,96},{192,128},{224,1... | collective-permute-start | bytes 786440 | tf_op jit(solution)/shard_map/ppermute | solution.py:26
  82.7 13.1 %collective-permute-start.14 = (bf16[128,1024]{1,0:T(8,128)(2,1)}, bf16[128,1024]{1,0:T(8,128)(2,1)}, u32[]{:S(2)}, u32[]{:S(2)}) collective-permute-start(bf16[128,1024]{1,0:T(8,128)(2,1)} %get-tuple-element.43), channel_id=1, source_target_pairs={{0,64},{32,96},{64,128},{96,160},{128,192},{160,224},{192,0},{224,... | collective-permute-start | bytes 786440 | tf_op jit(solution)/shard_map/ppermute | solution.py:26
  82.7 13.1 %collective-permute-start.13 = (bf16[128,1024]{1,0:T(8,128)(2,1)}, bf16[128,1024]{1,0:T(8,128)(2,1)}, u32[]{:S(2)}, u32[]{:S(2)}) collective-permute-start(bf16[128,1024]{1,0:T(8,128)(2,1)} %get-tuple-element.42), channel_id=1, source_target_pairs={{0,128},{32,160},{64,192},{96,224},{128,0},{160,32},{192,64},{224,... | collective-permute-start | bytes 786440 | tf_op jit(solution)/shard_map/ppermute | solution.py:26
  85.5 10.3 %copy-start.13 = (bf16[128,1024]{1,0:T(8,128)(2,1)S(1)}, bf16[128,1024]{1,0:T(8,128)(2,1)}, u32[]{:S(2)}) copy-start(bf16[128,1024]{1,0:T(8,128)(2,1)} %get-tuple-element.45) | copy-start | bytes 786436
  87.7 44.0 %all-to-all-start.2 = ((bf16[32,16,896]{2,1,0:T(8,128)(2,1)}), bf16[32,16,896]{2,1,0:T(8,128)(2,1)}, u32[]{:S(2)}, u32[]{:S(2)}) async-start(bf16[32,16,896]{2,1,0:T(8,128)(2,1)} %bitcast.61), calls=%async_computation.2 | async-start | bytes 1835008 | tf_op jit(solution)/shard_map/all_to_all | solution.py:242
  98.5 25.5 %copy-start.5 = (f32[896,1024]{1,0:T(8,128)}, f32[896,1024]{1,0:T(8,128)S(1)}, u32[]{:S(2)}) copy-start(f32[896,1024]{1,0:T(8,128)S(1)} %fusion.26) | copy-start | bytes 11010052
  98.5 9.3 %copy-start.16 = (f32[512]{0:T(512)S(1)}, f32[512]{0:T(512)}, u32[]{:S(2)}) copy-start(f32[512]{0:T(512)} %copy-done.15) | copy-start | bytes 6148
  98.7 24.1 %collective-permute-start.20 = (bf16[448,1024]{1,0:T(8,128)(2,1)S(1)}, bf16[448,1024]{1,0:T(8,128)(2,1)S(1)}, u32[]{:S(2)}, u32[]{:S(2)}) collective-permute-start(bf16[448,1024]{1,0:T(8,128)(2,1)S(1)} %slice.141), channel_id=1, source_target_pairs={{0,32},{32,0},{64,96},{96,64},{128,160},{160,128},{192,224},{224,1... | collective-permute-start | bytes 2752520 | tf_op jit(solution)/shard_map/ppermute | solution.py:21
  105.2 14.7 %collective-permute-start.16 = (bf16[128,2048]{1,0:T(8,128)(2,1)S(1)}, bf16[128,2048]{1,0:T(8,128)(2,1)S(1)}, u32[]{:S(2)}, u32[]{:S(2)}) collective-permute-start(bf16[128,2048]{1,0:T(8,128)(2,1)S(1)} %pad_maximum_fusion.2.refs_0_), channel_id=1, source_target_pairs={{0,64},{32,96},{64,128},{96,160},{128,192},{160,224},{192,0},{224,... | collective-permute-start | bytes 1572872 | tf_op jit(solution)/shard_map/ppermute | solution.py:26
  107.4 13.6 %collective-permute-start.17 = (bf16[128,2048]{1,0:T(8,128)(2,1)S(1)}, bf16[128,2048]{1,0:T(8,128)(2,1)S(1)}, u32[]{:S(2)}, u32[]{:S(2)}) collective-permute-start(bf16[128,2048]{1,0:T(8,128)(2,1)S(1)} %pad_maximum_fusion.2.refs_0_), channel_id=1, source_target_pairs={{0,192},{32,224},{64,0},{96,32},{128,64},{160,96},{192,128},{224,1... | collective-permute-start | bytes 1572872 | tf_op jit(solution)/shard_map/ppermute | solution.py:26
  119.9 8.3 %collective-permute-start.18 = (bf16[64,2048]{1,0:T(8,128)(2,1)S(1)}, bf16[64,2048]{1,0:T(8,128)(2,1)S(1)}, u32[]{:S(2)}, u32[]{:S(2)}) collective-permute-start(bf16[64,2048]{1,0:T(8,128)(2,1)S(1)} %slice.91), channel_id=1, source_target_pairs={{0,64},{32,96},{64,128},{96,160},{128,192},{160,224},{192,0},{224,... | collective-permute-start | bytes 786440 | tf_op jit(solution)/shard_map/ppermute | solution.py:26
  121.0 7.2 %copy-start.1 = (bf16[896,2048]{1,0:T(8,128)(2,1)S(1)}, bf16[896,2048]{1,0:T(8,128)(2,1)}, u32[]{:S(2)}) copy-start(bf16[896,2048]{1,0:T(8,128)(2,1)} %shard_map.146.right_ref.refs_5_) | copy-start | bytes 11010052
  121.0 7.2 %collective-permute-start.19 = (bf16[64,2048]{1,0:T(8,128)(2,1)S(1)}, bf16[64,2048]{1,0:T(8,128)(2,1)S(1)}, u32[]{:S(2)}, u32[]{:S(2)}) collective-permute-start(bf16[64,2048]{1,0:T(8,128)(2,1)S(1)} %slice.92), channel_id=1, source_target_pairs={{0,192},{32,224},{64,0},{96,32},{128,64},{160,96},{192,128},{224,1... | collective-permute-start | bytes 786440 | tf_op jit(solution)/shard_map/ppermute | solution.py:26
  131.7 9.5 %copy-start.6 = (f32[1,1024,448]{1,2,0:T(8,128)S(1)}, f32[1,1024,448]{1,2,0:T(8,128)}, u32[]{:S(2)}) copy-start(f32[1,1024,448]{1,2,0:T(8,128)} %param.21) | copy-start | bytes 5505028
  131.7 87.9 %all-to-all-start.3 = ((bf16[32,16,896]{2,1,0:T(8,128)(2,1)}), bf16[32,16,896]{2,1,0:T(8,128)(2,1)}, u32[]{:S(2)}, u32[]{:S(2)}) async-start(bf16[32,16,896]{2,1,0:T(8,128)(2,1)} %bitcast.60), calls=%async_computation.3 | async-start | bytes 1835008 | tf_op jit(solution)/shard_map/all_to_all | solution.py:242
  141.2 3.8 %copy-start.7 = (f32[1,1024,448]{1,2,0:T(8,128)S(1)}, f32[1,1024,448]{1,2,0:T(8,128)}, u32[]{:S(2)}) copy-start(f32[1,1024,448]{1,2,0:T(8,128)} %param.20) | copy-start | bytes 5505028
  142.3 6.7 %copy-start.18 = (s32[512]{0:T(512)S(1)}, s32[512]{0:T(512)}, u32[]{:S(2)}) copy-start(s32[512]{0:T(512)} %copy-done.17) | copy-start | bytes 6148
  142.3 32.0 %collective-permute-start.23 = (bf16[448,1024]{1,0:T(8,128)(2,1)}, bf16[448,1024]{1,0:T(8,128)(2,1)}, u32[]{:S(2)}, u32[]{:S(2)}) collective-permute-start(bf16[448,1024]{1,0:T(8,128)(2,1)} %convert_element_type.133), channel_id=1, source_target_pairs={{0,16},{1,17},{2,18},{3,19},{4,20},{5,21},{6,22},{7,23},{8,24},{9,... | collective-permute-start | bytes 2752520 | tf_op jit(solution)/shard_map/ppermute | solution.py:31
  145.0 5.8 %copy-start.19 = (bf16[512]{0:T(512)(128)(2,1)S(1)}, bf16[512]{0:T(512)(128)(2,1)}, u32[]{:S(2)}) copy-start(bf16[512]{0:T(512)(128)(2,1)} %get-tuple-element.64) | copy-start | bytes 3076
  146.1 47.9 %collective-permute-start.21 = (bf16[448,1024]{1,0:T(8,128)(2,1)}, bf16[448,1024]{1,0:T(8,128)(2,1)}, u32[]{:S(2)}, u32[]{:S(2)}) collective-permute-start(bf16[448,1024]{1,0:T(8,128)(2,1)} %convert_element_type.130), channel_id=1, source_target_pairs={{0,16},{1,17},{2,18},{3,19},{4,20},{5,21},{6,22},{7,23},{8,24},{9,... | collective-permute-start | bytes 2752520 | tf_op jit(solution)/shard_map/ppermute | solution.py:31
  146.8 66.8 %collective-permute-start.22 = (bf16[448,1024]{1,0:T(8,128)(2,1)}, bf16[448,1024]{1,0:T(8,128)(2,1)}, u32[]{:S(2)}, u32[]{:S(2)}) collective-permute-start(bf16[448,1024]{1,0:T(8,128)(2,1)} %fusion.3), channel_id=1, source_target_pairs={{0,16},{1,17},{2,18},{3,19},{4,20},{5,21},{6,22},{7,23},{8,24},{9,... | collective-permute-start | bytes 2752520 | tf_op jit(solution)/shard_map/ppermute | solution.py:31
  150.8 6.1 %copy-start.21 = (s32[16]{0:T(128)S(1)}, s32[16]{0:T(128)}, u32[]{:S(2)}) copy-start(s32[16]{0:T(128)} %param.16) | copy-start | bytes 196
  153.6 4.6 %collective-permute-start.12 = (bf16[448,256]{1,0:T(8,128)(2,1)S(1)}, bf16[448,256]{1,0:T(8,128)(2,1)S(1)}, u32[]{:S(2)}, u32[]{:S(2)}) collective-permute-start(bf16[448,256]{1,0:T(8,128)(2,1)S(1)} %slice.143), channel_id=1, source_target_pairs={{0,32},{32,0},{64,96},{96,64},{128,160},{160,128},{192,224},{224,1... | collective-permute-start | bytes 688136 | tf_op jit(solution)/shard_map/ppermute | solution.py:21
  221.4 3.0 %collective-permute-start.24 = (bf16[448,256]{1,0:T(8,128)(2,1)S(1)}, bf16[448,256]{1,0:T(8,128)(2,1)S(1)}, u32[]{:S(2)}, u32[]{:S(2)}) collective-permute-start(bf16[448,256]{1,0:T(8,128)(2,1)S(1)} %slice.142), channel_id=1, source_target_pairs={{0,32},{32,0},{64,96},{96,64},{128,160},{160,128},{192,224},{224,1... | collective-permute-start | bytes 688136 | tf_op jit(solution)/shard_map/ppermute | solution.py:21
  (3 other events, 4.0 us)
